TPU v7x, 32 devices: a whole 2x2x4 slice. The times are simulated.
32 devices in a mesh: dp: 4 (over y, x), expert: 8 (over z, core).
Axes of the slice: x: 2, y: 2, z: 4, core: 2. Of those that a mesh axis runs over, the one named last changes fastest.
Arguments:
- tokens: bfloat16 [2, 2048, 1536], P(None, ('dp', 'expert')), may hold values from -6 to 6
- segments: int32 [2, 32, 64], P(None, ('dp', 'expert')), may hold values from 0 to 3, never falling along the last dimension, each value on 1 to 32 neighbouring positions
- routes: int32 [2, 2, 2048, 6], P(None, None, ('dp', 'expert')), may hold values from 0 to 15, all different within a row; in each aligned block of 64 rows (0 to 63, 64 to 127, ..., all dimensions but the last counted through in order) at most 36 rows name the same one
- norm_mamba: bfloat16 [1536], P(('dp', 'expert')), may hold values from 0.5 to 1.5
- w_in: bfloat16 [1536, 6400], P(('dp', 'expert')), may hold values from -0.15625 to 0.15625
- w_dt: bfloat16 [1536, 48], P(('dp', 'expert')), may hold values from -0.15625 to 0.15625
- conv_w: bfloat16 [4, 3328], P(None, ('dp', 'expert')), may hold values from -3 to 3
- conv_b: bfloat16 [3328], P(('dp', 'expert')), may hold values from -3 to 3
- dt_bias: float32 [48], replicated, may hold values from -4.6 to -2.3
- a_log: float32 [48], replicated, may hold values from 0 to 2.5
- skip_scale: float32 [48], replicated, may hold values from 0.5 to 1.5
- gate_norm: bfloat16 [3072], P(('dp', 'expert')), may hold values from 0.5 to 1.5
- w_mix_out: bfloat16 [3072, 1536], P(None, ('dp', 'expert')), may hold values from -0.109375 to 0.109375
- norm_moe_m: bfloat16 [1536], P(('dp', 'expert')), may hold values from 0.5 to 1.5
- router_m: bfloat16 [1536, 16], P(('dp', 'expert')), may hold values from -0.078125 to 0.078125
- shared_in_m: bfloat16 [1536, 2048], P(('dp', 'expert')), may hold values from -0.15625 to 0.15625
- shared_down_m: bfloat16 [1024, 1536], P(None, ('dp', 'expert')), may hold values from -0.25 to 0.25
- expert_in_m: bfloat16 [16, 1536, 1024], P('expert', 'dp'), may hold values from -0.15625 to 0.15625
- expert_down_m: bfloat16 [16, 512, 1536], P('expert', 'dp'), may hold values from -0.5 to 0.5
- norm_attn: bfloat16 [1536], P(('dp', 'expert')), may hold values from 0.5 to 1.5
- w_qkv: bfloat16 [1536, 2560], P(('dp', 'expert')), may hold values from -0.15625 to 0.15625
- w_out: bfloat16 [1536, 1536], P(None, ('dp', 'expert')), may hold values from -0.625 to 0.625
- norm_moe: bfloat16 [1536], P(('dp', 'expert')), may hold values from 0.5 to 1.5
- router: bfloat16 [1536, 16], P(('dp', 'expert')), may hold values from -0.078125 to 0.078125
- shared_in: bfloat16 [1536, 2048], P(('dp', 'expert')), may hold values from -0.15625 to 0.15625
- shared_down: bfloat16 [1024, 1536], P(None, ('dp', 'expert')), may hold values from -0.25 to 0.25
- expert_in: bfloat16 [16, 1536, 1024], P('expert', 'dp'), may hold values from -0.15625 to 0.15625
- expert_down: bfloat16 [16, 512, 1536], P('expert', 'dp'), may hold values from -0.5 to 0.5
- cotangent: bfloat16 [2, 2048, 1536], P(None, ('dp', 'expert')), may hold values from -6 to 6
Outputs:
- output: bfloat16 [2, 2048, 1536], P(None, ('dp', 'expert'))
- input_grad: float32 [2, 2048, 1536], P(None, ('dp', 'expert'))
- grad_norm_mamba: float32 [1536], P(('dp', 'expert'))
- grad_w_in: float32 [1536, 6400], P(('dp', 'expert'))
- grad_w_dt: float32 [1536, 48], P(('dp', 'expert'))
- grad_conv_w: float32 [4, 3328], P(None, ('dp', 'expert'))
- grad_conv_b: float32 [3328], P(('dp', 'expert'))
- grad_dt_bias: float32 [48], replicated
- grad_a_log: float32 [48], replicated
- grad_skip_scale: float32 [48], replicated
- grad_gate_norm: float32 [3072], P(('dp', 'expert'))
- grad_w_mix_out: float32 [3072, 1536], P(None, ('dp', 'expert'))
- grad_norm_moe_m: float32 [1536], P(('dp', 'expert'))
- grad_router_m: float32 [1536, 16], P(('dp', 'expert'))
- grad_shared_in_m: float32 [1536, 2048], P(('dp', 'expert'))
- grad_shared_down_m: float32 [1024, 1536], P(None, ('dp', 'expert'))
- grad_expert_in_m: float32 [16, 1536, 1024], P('expert', 'dp')
- grad_expert_down_m: float32 [16, 512, 1536], P('expert', 'dp')
- grad_norm_attn: float32 [1536], P(('dp', 'expert'))
- grad_w_qkv: float32 [1536, 2560], P(('dp', 'expert'))
- grad_w_out: float32 [1536, 1536], P(None, ('dp', 'expert'))
- grad_norm_moe: float32 [1536], P(('dp', 'expert'))
- grad_router: float32 [1536, 16], P(('dp', 'expert'))
- grad_shared_in: float32 [1536, 2048], P(('dp', 'expert'))
- grad_shared_down: float32 [1024, 1536], P(None, ('dp', 'expert'))
- grad_expert_in: float32 [16, 1536, 1024], P('expert', 'dp')
- grad_expert_down: float32 [16, 512, 1536], P('expert', 'dp')
Inputs may be any that keep to these rules, and one draw needn't show every extreme that they name: For each expert block, in each aligned block of 64 rows (one sequence) no expert is named by more than 36 routes, a bound that some block reaches. The 6 routes of a token differ. `segments`: within a sequence the numbers never fall; every segment has 1 to 32 positions.
All inputs are finite; a program needn't handle non-finite values.
Results may differ from a plain program's by a relative error of at most 0.039.
Values may be sent and summed in bfloat16 or wider, within the bound.
No kernel may reach another device: no remote copies, remote signals or barrier semaphores. Data moves between devices by JAX's collectives and lax.ppermute only.
A program may use at most 280 MiB of HBM per device.

v0:
```python
import jax
import jax.numpy as jnp
from jax import lax
from jax.sharding import Mesh, PartitionSpec as P

D = 1536
QH = 12
KVH = 4
HEAD = 128
EXP_FF = 512
SH_FF = 1024
TOP = 6
MH = 48
HP = 64
STATE = 128
CK = 4
DI = 3072

bf16 = jnp.bfloat16
f32 = jnp.float32
epsilon = 1e-05
masked_value = -1e30
highest = lax.Precision.HIGHEST
ALL = ("dp", "w", "z", "core")
EX = ("w", "z", "core")
TP = ("z", "core")
FS = ("dp", "w")
SWAP = [(0, 1), (1, 0)]


def dot(a, b, dims, out=f32):
    r = lax.dot_general(a, b, (dims, ((), ())), preferred_element_type=f32)
    return r if out == f32 else r.astype(out)


def nn(a, b, out=f32):
    return dot(a, b, ((1,), (0,)), out)


def nt(a, b, out=f32):
    return dot(a, b, ((1,), (1,)), out)


def tn(a, b, out=f32):
    return dot(a, b, ((0,), (0,)), out)


def ring(shift, axis="z"):
    n = lax.axis_size(axis)
    return [(i, (i + shift) % n) for i in range(n)]


def wide(x):
    parts = [x] + [lax.ppermute(x, "w", ring(s, "w")) for s in range(1, lax.axis_size("w"))]
    return parts[0] if len(parts) == 1 else jnp.concatenate(parts, axis=0)


def narrow(total):
    n = lax.axis_size("w")
    rows = total.shape[0] // n
    out = total[:rows]
    for s in range(1, n):
        part = total[s * rows : (s + 1) * rows].astype(bf16)
        out = out + lax.ppermute(part, "w", ring(-s, "w")).astype(f32)
    return out


def add_first(total, part):
    rows = part.shape[0]
    if rows == total.shape[0]:
        return total + part
    return jnp.concatenate([total[:rows] + part, total[rows:]], axis=0)


def fence(*trees):
    return lax.optimization_barrier(trees)


def gather_rows(x):
    n = lax.axis_size("z")
    parts = [x] + [lax.ppermute(x, "z", ring(s)) for s in range(1, n)]
    other = [lax.ppermute(p, "core", SWAP) for p in parts]
    return jnp.concatenate(parts + other, axis=0)


def return_rows(total):
    n = lax.axis_size("z")
    half = total.shape[0] // 2
    rows = half // n
    recv = lax.ppermute(total[half:].astype(bf16), "core", SWAP)
    mine = total[:half] + recv.astype(f32)
    out = mine[:rows]
    for s in range(1, n):
        part = mine[s * rows : (s + 1) * rows].astype(bf16)
        out = out + lax.ppermute(part, "z", ring(-s)).astype(f32)
    return out


def pair_gather(x):
    return jnp.concatenate([x, lax.ppermute(x, "core", SWAP)], axis=0)


def pair_return(total):
    half = total.shape[0] // 2
    recv = lax.ppermute(total[half:].astype(bf16), "core", SWAP)
    return total[:half] + recv.astype(f32)


def split_two(x):
    high = x.astype(bf16)
    return [high, (x - high.astype(f32)).astype(bf16)]


def row_scale(values):
    return lax.rsqrt(jnp.mean(values * values, axis=-1, keepdims=True) + epsilon)


def rms_forward(values, gain):
    scale = row_scale(values)
    normed = values * scale
    return normed, scale, (normed * gain).astype(bf16)


def rms_backward(grad_result, normed, scale, gain):
    grad_gain = jnp.sum(grad_result * normed, axis=0)
    grad_normed = grad_result * gain
    grad_values = scale * (
        grad_normed - normed * jnp.mean(grad_normed * normed, axis=-1, keepdims=True)
    )
    return grad_values, grad_gain


def lanes(parts, width):
    used = sum(p.shape[-1] for p in parts)
    rows = parts[0].shape[0]
    if used < width:
        parts = parts + [jnp.zeros((rows, width - used), bf16)]
    return jnp.concatenate(parts, axis=1)


def scan_piece(proj, dt_raw, seg, conv_w, conv_b, dt_bias, a_log, skip, heads):
    seqs, length, _ = proj.shape
    chan = heads * HP
    gate_z = proj[..., :chan]
    conv_in = proj[..., chan:]
    positions = lax.broadcasted_iota(jnp.int32, (length,), 0)
    conv_sum = jnp.zeros_like(conv_in) + conv_b
    for offset in range(CK):
        shifted = jnp.pad(conv_in, ((0, 0), (offset, 0), (0, 0)))[:, :length]
        seg_prev = jnp.pad(seg, ((0, 0), (offset, 0)))[:, :length]
        usable = (positions >= offset)[None] & (seg_prev == seg)
        conv_sum = conv_sum + jnp.where(usable[..., None], conv_w[offset] * shifted, 0.0)
    conv_act = jax.nn.silu(conv_sum)
    inputs = conv_act[..., :chan].reshape(seqs, length, heads, HP)
    b_state = conv_act[..., chan : chan + STATE]
    c_state = conv_act[..., chan + STATE :]
    step = jax.nn.softplus(dt_raw + dt_bias)
    rows_pos = lax.broadcasted_iota(jnp.int32, (length, length), 0)
    cols_pos = lax.broadcasted_iota(jnp.int32, (length, length), 1)
    lower = (cols_pos <= rows_pos).astype(f32)
    cum = jnp.einsum("ts,bsh->bht", lower, step * -jnp.exp(a_log), precision=highest)
    allowed = (seg[:, :, None] == seg[:, None, :]) & (cols_pos <= rows_pos)[None]
    allowed = allowed[:, None]
    gap = cum[..., :, None] - cum[..., None, :]
    decay = jnp.where(allowed, jnp.exp(jnp.where(allowed, gap, 0.0)), 0.0)
    cb = jnp.einsum("btn,bsn->bts", c_state, b_state, precision=highest)
    mix = decay * cb[:, None] * step.transpose(0, 2, 1)[:, :, None, :]
    scan = jnp.einsum("bhts,bshp->bthp", mix, inputs, precision=highest)
    scan = scan + skip[:, None] * inputs
    return scan.reshape(seqs, length, chan) * jax.nn.silu(gate_z)


def swiglu(gate, up):
    return gate * jax.nn.sigmoid(gate) * up


def swiglu_back(grad, gate, up):
    logistic = jax.nn.sigmoid(gate)
    grad_gate = grad * up * logistic * (1.0 + gate * (1.0 - logistic))
    return grad_gate.astype(bf16), (grad * gate * logistic).astype(bf16)


def gate_table(moe_in, mask, router):
    logits = nn(moe_in, router)
    picked = jnp.where(mask, logits, masked_value)
    peak = jnp.max(picked, axis=-1, keepdims=True)
    ex = jnp.where(mask, jnp.exp(picked - peak), 0.0)
    return ex / jnp.sum(ex, axis=-1, keepdims=True)


def moe_forward(own_in, mask, w):
    rows = own_in.shape[0]
    base_in = gather_rows(own_in)
    moe_in = wide(base_in)
    gates = gate_table(moe_in, mask, w["router"])
    count = w["expert_in"].shape[0]
    first = lax.axis_index(EX) * count
    local = lax.dynamic_slice(gates, (0, first), (gates.shape[0], count))
    pre = [nn(moe_in, w["expert_in"][e], bf16) for e in range(count)]
    pre_s = nn(base_in, w["shared_in"], bf16)
    total = None
    hidden = []
    for e in range(count):
        p = pre[e].astype(f32)
        act = swiglu(p[:, :EXP_FF], p[:, EXP_FF:])
        hid = (act * local[:, e : e + 1]).astype(bf16)
        hidden.append(hid)
        part = nn(hid, w["expert_down"][e])
        total = part if total is None else total + part
    half = pre_s.shape[1] // 2
    p = pre_s.astype(f32)
    hid_s = swiglu(p[:, :half], p[:, half:]).astype(bf16)
    total = add_first(total, nt(hid_s, w["shared_down_t"]))
    branch = return_rows(narrow(total))
    kept = (moe_in, base_in, gates[:rows], local, pre, pre_s, hidden, hid_s)
    return branch, kept


def moe_backward(base_z, kept, w, experts_total):
    moe_in, base_in, own_gates, local, pre, pre_s, hidden, hid_s = kept
    grad_z = wide(base_z)
    rows = own_gates.shape[0]
    count = len(pre)
    total = None
    first = lax.axis_index(EX) * count
    lane = lax.broadcasted_iota(jnp.int32, (1, experts_total), 1)
    table = jnp.zeros((grad_z.shape[0], experts_total), f32)
    pre_grads = []
    for e in range(count):
        p = pre[e].astype(f32)
        gate, up = p[:, :EXP_FF], p[:, EXP_FF:]
        grad_hid = nt(grad_z, w["expert_down"][e])
        share = local[:, e : e + 1]
        act = swiglu(gate, up)
        weighted = share * jnp.sum(grad_hid * act, axis=-1, keepdims=True)
        table = table + weighted * (lane == first + e).astype(f32)
        g_gate, g_up = swiglu_back(grad_hid * share, gate, up)
        g_pre = jnp.concatenate([g_gate, g_up], axis=1)
        pre_grads.append(g_pre)
        part = nt(g_pre, w["expert_in"][e])
        total = part if total is None else total + part
    half = pre_s.shape[1] // 2
    p = pre_s.astype(f32)
    grad_hid = nn(base_z, w["shared_down_t"])
    g_gate, g_up = swiglu_back(grad_hid, p[:, :half], p[:, half:])
    g_pre_s = jnp.concatenate([g_gate, g_up], axis=1)
    total = add_first(total, nt(g_pre_s, w["shared_in"]))
    extra = -(-experts_total // 128) * 128
    table = jnp.pad(table, ((0, 0), (0, extra - experts_total)))
    back = return_rows(narrow(jnp.concatenate([total, table], axis=1)))
    side = (moe_in, grad_z, hidden, hid_s, pre_grads, g_pre_s, base_in, base_z)
    return back, side


def moe_finish(back, kept, w, experts_total):
    own_gates = kept[2]
    weighted = back[:, D : D + experts_total]
    grad_logits = weighted - own_gates * jnp.sum(weighted, axis=-1, keepdims=True)
    grad_logits = grad_logits.astype(bf16)
    return back[:, :D] + nt(grad_logits, w["router"]), grad_logits


def cat(items):
    return jnp.concatenate(items, axis=0)


def moe_weight_grads(sides):
    moe_in = cat([s[0] for s in sides])
    grad_z = cat([s[1] for s in sides])
    count = len(sides[0][2])
    g_down = jnp.stack(
        [tn(cat([s[2][e] for s in sides]), grad_z, bf16) for e in range(count)]
    )
    g_in = jnp.stack([tn(moe_in, cat([s[4][e] for s in sides]), bf16) for e in range(count)])
    base_in = cat([s[6] for s in sides])
    g_sin = tn(base_in, cat([s[5] for s in sides]), bf16)
    g_sdown_t = tn(cat([s[7] for s in sides]), cat([s[3] for s in sides]), bf16)
    return g_in, g_down, g_sin, g_sdown_t


def attn_mask(seg):
    length = seg.shape[1]
    rows_pos = lax.broadcasted_iota(jnp.int32, (length, length), 0)
    cols_pos = lax.broadcasted_iota(jnp.int32, (length, length), 1)
    return (seg[:, :, None] == seg[:, None, :]) & (cols_pos <= rows_pos)[None]


def attn_forward(own_in, allowed, w_qkv, w_out_t):
    seqs, length, _ = allowed.shape
    kv = KVH // 2
    group = QH // KVH
    q_width = kv * group * HEAD
    kv_width = kv * HEAD
    attn_in = pair_gather(own_in)
    packed = nn(attn_in, w_qkv, bf16)
    q = packed[:, :q_width].reshape(seqs, length, kv, group, HEAD)
    k = packed[:, q_width : q_width + kv_width].reshape(seqs, length, kv, HEAD)
    v = packed[:, q_width + kv_width :].reshape(seqs, length, kv, HEAD)
    scores = jnp.einsum("bqhgd,bkhd->bhgqk", q, k, preferred_element_type=f32) * HEAD**-0.5
    scores = jnp.where(allowed[:, None, None], scores, masked_value)
    peak = jnp.max(scores, axis=-1, keepdims=True)
    ex = jnp.exp(scores - peak)
    probs = ex / jnp.sum(ex, axis=-1, keepdims=True)
    context = jnp.einsum("bhgqk,bkhd->bqhgd", probs.astype(bf16), v, preferred_element_type=f32)
    context = context.reshape(seqs * length, q_width).astype(bf16)
    branch = pair_return(nt(context, w_out_t))
    return branch, (attn_in, q, k, v, probs, context)


def attn_backward(own_grad, kept, w_qkv, w_out_t):
    attn_in, q, k, v, probs, context = kept
    seqs, length, kv, group, _ = q.shape
    grad = pair_gather(own_grad)
    grad_context = nn(grad, w_out_t, bf16).reshape(seqs, length, kv, group, HEAD)
    probs_low = probs.astype(bf16)
    grad_v = jnp.einsum("bhgqk,bqhgd->bkhd", probs_low, grad_context, preferred_element_type=f32)
    grad_p = jnp.einsum("bqhgd,bkhd->bhgqk", grad_context, v, preferred_element_type=f32)
    delta = jnp.sum(probs * grad_p, axis=-1, keepdims=True)
    grad_s = (probs * (grad_p - delta)).astype(bf16)
    scale = HEAD**-0.5
    grad_q = jnp.einsum("bhgqk,bkhd->bqhgd", grad_s, k, preferred_element_type=f32) * scale
    grad_k = jnp.einsum("bhgqk,bqhgd->bkhd", grad_s, q, preferred_element_type=f32) * scale
    rows = seqs * length
    grad_packed = jnp.concatenate(
        [grad_q.reshape(rows, -1), grad_k.reshape(rows, -1), grad_v.reshape(rows, -1)], axis=1
    ).astype(bf16)
    grad_in = pair_return(nt(grad_packed, w_qkv))
    return grad_in, (attn_in, grad_packed, context, grad)


def by_owner(x, count):
    return x.reshape(x.shape[0], count, x.shape[1] // count)


def body(
    tokens,
    segments,
    routes,
    norm_mamba,
    w_in,
    w_dt,
    conv_w,
    conv_b,
    dt_bias,
    a_log,
    skip_scale,
    gate_norm,
    w_mix_out,
    norm_moe_m,
    router_m,
    shared_in_m,
    shared_down_m,
    expert_in_m,
    expert_down_m,
    norm_attn,
    w_qkv,
    w_out,
    norm_moe,
    router,
    shared_in,
    shared_down,
    expert_in,
    expert_down,
    cotangent,
):
    micro, length, _ = tokens.shape
    n_tp = lax.axis_size("z") * lax.axis_size("core")
    n_ex = lax.axis_size("w") * n_tp
    n_all = lax.axis_size("dp") * n_ex
    rows = w_in.shape[0]
    local_experts = expert_in.shape[0]
    experts_total = local_experts * n_ex
    heads = MH // n_tp
    chan = heads * HP
    ff = SH_FF // n_tp
    slot = lax.axis_index(TP)
    conv_total = DI + 2 * STATE
    conv_here = conv_w.shape[1]
    gate_here = gate_norm.shape[0]
    vec_len = gate_here + (CK + 1) * conv_here
    vec_cols = -(-vec_len // rows)
    small_cols = 4 + 2 * experts_total + vec_cols
    step_width = -(-(heads + small_cols) // 128) * 128

    vec = jnp.concatenate([gate_norm, conv_b, conv_w.reshape(-1)])
    vec = jnp.pad(vec, (0, rows * vec_cols - vec_len)).reshape(rows, vec_cols)
    gains_own = jnp.stack([norm_mamba, norm_moe_m, norm_attn, norm_moe], axis=1)
    little = jnp.concatenate([gains_own, router_m, router, vec], axis=1)

    def for_all(x):
        return jnp.broadcast_to(x[:, None], (rows, n_tp, x.shape[1]))

    def columns(parts):
        packed = jnp.concatenate(parts, axis=2).transpose(1, 0, 2)
        moved = lax.all_to_all(packed, TP, split_axis=0, concat_axis=0, tiled=True)
        return lax.all_gather(moved.reshape(n_tp * rows, -1), FS, axis=0, tiled=True)

    def shared_pack(w_sin, w_sdown):
        return [
            by_owner(w_sin[:, :SH_FF], n_tp),
            by_owner(w_sin[:, SH_FF:], n_tp),
            by_owner(w_sdown.T, n_tp),
        ]

    blank = jnp.zeros((rows, n_tp, step_width - heads - small_cols), bf16)
    w_m = columns(
        [
            by_owner(w_in[:, :DI], n_tp),
            by_owner(w_in[:, DI : 2 * DI], n_tp),
            for_all(w_in[:, 2 * DI :]),
            by_owner(w_dt, n_tp),
            for_all(little),
            blank,
        ]
    )
    in_width = 2 * chan + 2 * STATE
    w_in_here = w_m[:, :in_width]
    w_step = w_m[:, in_width:]
    w_dt_here = w_step[:, :heads]
    small_all = w_step[:, heads : heads + small_cols]
    gain_mamba, gain_moe_m, gain_attn, gain_moe = [small_all[:, i].astype(f32) for i in range(4)]
    router_m_full = small_all[:, 4 : 4 + experts_total]
    router_full = small_all[:, 4 + experts_total : 4 + 2 * experts_total]
    vec_all = small_all[:, 4 + 2 * experts_total :].reshape(n_all, rows * vec_cols).astype(f32)
    gain_gate = vec_all[:, :gate_here].reshape(DI)
    bias_all = vec_all[:, gate_here : gate_here + conv_here].reshape(conv_total)
    taps_all = vec_all[:, gate_here + conv_here : vec_len].reshape(n_all, CK, conv_here)
    taps_all = taps_all.transpose(1, 0, 2).reshape(CK, conv_total)

    def channels(full_row):
        mine = lax.dynamic_slice_in_dim(full_row, slot * chan, chan, axis=-1)
        return jnp.concatenate([mine, full_row[..., DI:]], axis=-1)

    taps = channels(taps_all)
    bias = channels(bias_all)
    gain_here = lax.dynamic_slice_in_dim(gain_gate, slot * chan, chan)
    dt_here = lax.dynamic_slice_in_dim(dt_bias, slot * heads, heads)
    log_here = lax.dynamic_slice_in_dim(a_log, slot * heads, heads)
    skip_here = lax.dynamic_slice_in_dim(skip_scale, slot * heads, heads)

    w_s = columns(
        [by_owner(w_mix_out.T, n_tp)]
        + shared_pack(shared_in_m, shared_down_m)
        + shared_pack(shared_in, shared_down)
    )
    w_mix_t = w_s[:, :chan]
    at = chan

    moe_m = {
        "router": router_m_full,
        "shared_in": w_s[:, at : at + 2 * ff],
        "shared_down_t": w_s[:, at + 2 * ff : at + 3 * ff],
        "expert_in": lax.all_gather(expert_in_m, "dp", axis=1, tiled=True),
        "expert_down": lax.all_gather(expert_down_m, "dp", axis=1, tiled=True),
    }

    kv = KVH // 2
    q_width = QH // 2 * HEAD
    kv_width = kv * HEAD
    q_all, kv_all = QH * HEAD, KVH * HEAD
    attn_pack = jnp.concatenate(
        [
            by_owner(w_qkv[:, :q_all], 2),
            by_owner(w_qkv[:, q_all : q_all + kv_all], 2),
            by_owner(w_qkv[:, q_all + kv_all :], 2),
            by_owner(w_out.T, 2),
        ],
        axis=2,
    ).transpose(1, 0, 2)
    attn_pack = lax.all_to_all(attn_pack, "core", split_axis=0, concat_axis=0, tiled=True)
    attn_w = lax.all_gather(attn_pack.reshape(2 * rows, -1), "z", axis=0, tiled=True)
    attn_w = lax.all_gather(attn_w, FS, axis=0, tiled=True)
    w_qkv_here = attn_w[:, : q_width + 2 * kv_width]
    w_out_t = attn_w[:, q_width + 2 * kv_width :]

    moe_a = {
        "router": router_full,
        "shared_in": w_s[:, at + 3 * ff : at + 5 * ff],
        "shared_down_t": w_s[:, at + 5 * ff :],
        "expert_in": lax.all_gather(expert_in, "dp", axis=1, tiled=True),
        "expert_down": lax.all_gather(expert_down, "dp", axis=1, tiled=True),
    }

    expert_ids = jnp.arange(experts_total, dtype=jnp.int32)
    info_width = -(-(2 * experts_total + 1) // 128) * 128
    each = range(micro)
    x_own = [tokens[m].astype(f32) for m in each]
    seg_all, masks, allowed, mamba_kept, mix_kept, hidden_one = [], [], [], [], [], []
    for m in each:
        seg_own = segments[m, 0]
        hot = [
            jnp.any(routes[b, m][:, :, None] == expert_ids, axis=1).astype(bf16) for b in range(2)
        ]
        info = lanes(hot + [seg_own[:, None].astype(bf16)], info_width)
        rows_all = gather_rows(jnp.concatenate([tokens[m], info], axis=1))
        x_all = rows_all[:, :D].astype(f32)
        marks = wide(rows_all[:, D : D + 2 * experts_total]) > 0.5
        masks.append([marks[:, :experts_total], marks[:, experts_total:]])
        seg = rows_all[:, D + 2 * experts_total].astype(jnp.int32).reshape(n_tp, length)
        seg_all.append(seg)
        allowed.append(attn_mask(jnp.stack([seg[0], seg[n_tp // 2]])))

        normed_x, scale_x, mamba_in = rms_forward(x_all, gain_mamba)
        total_rows = mamba_in.shape[0]
        proj = nn(mamba_in, w_in_here, bf16)
        dt_raw = nn(mamba_in, w_dt_here)

        def piece(p, d, cw, cb, db, al, sk, seg=seg):
            return scan_piece(p, d, seg, cw, cb, db, al, sk, heads)

        gated, pullback = jax.vjp(
            piece,
            proj.astype(f32).reshape(n_tp, length, in_width),
            dt_raw.reshape(n_tp, length, heads),
            taps,
            bias,
            dt_here,
            log_here,
            skip_here,
        )
        gated = gated.reshape(total_rows, chan)
        gained = (gated * gain_here).astype(bf16)
        partial = nt(gained, w_mix_t)
        square = jnp.sum(gated * gated, axis=-1, keepdims=True)
        high = square.astype(bf16).astype(f32)
        extra = jnp.concatenate(
            [high, square - high, jnp.zeros((total_rows, 126), f32)], axis=1
        )
        back = return_rows(jnp.concatenate([partial, extra], axis=1))
        gate_scale = lax.rsqrt((back[:, D : D + 1] + back[:, D + 1 : D + 2]) / DI + epsilon)
        mix_branch = back[:, :D] * gate_scale
        hidden_one.append(x_own[m] + mix_branch)
        mamba_kept.append((normed_x[:length], scale_x[:length], mamba_in, pullback, gated, gained))
        mix_kept.append((mix_branch, gate_scale))

    one_kept, layer_one = [], []
    for m in each:
        normed, scale, own = rms_forward(hidden_one[m], gain_moe_m)
        branch, kept = moe_forward(own, masks[m][0], moe_m)
        layer_one.append(hidden_one[m] + branch)
        one_kept.append((normed, scale, kept))
    attn_kept, hidden_two = [], []
    for m in each:
        normed, scale, own = rms_forward(layer_one[m], gain_attn)
        branch, kept = attn_forward(own, allowed[m], w_qkv_here, w_out_t)
        hidden_two.append(layer_one[m] + branch)
        attn_kept.append((normed, scale, kept))
    cot_all = [gather_rows(cotangent[m]) for m in each]
    two_kept, results = [], []
    for m in each:
        normed, scale, own = rms_forward(hidden_two[m], gain_moe)
        branch, kept = moe_forward(own, masks[m][1], moe_a)
        results.append((hidden_two[m] + branch).astype(bf16))
        two_kept.append((normed, scale, kept))

    gains = [0.0, 0.0, 0.0, 0.0]

    def over_dp(g):
        return lax.psum_scatter(g, "dp", scatter_dimension=1, tiled=True).astype(f32)

    def moe_stage(grads, kept_all, w, gain):
        backs, sides = [], []
        for m in each:
            back, side = moe_backward(grads[m], kept_all[m][2], w, experts_total)
            backs.append(back)
            sides.append(side)
        weights = moe_weight_grads(sides)
        backs[-1], weights = fence(backs[-1], weights)
        grad_gain = 0.0
        values, logits = [], []
        for m in each:
            normed, scale, kept = kept_all[m]
            grad_in, grad_logits = moe_finish(backs[m], kept, w, experts_total)
            logits.append(grad_logits)
            grad_values, part = rms_backward(grad_in, normed, scale, gain)
            grad_gain = grad_gain + part
            values.append(grad_values)
        g_router = tn(cat([s[6][:length] for s in sides]), cat(logits))
        return values, weights, grad_gain, g_router

    values, (g_in_a, g_down_a, g_sin_a, g_sdown_a), gains[3], g_router = moe_stage(
        cot_all, two_kept, moe_a, gain_moe
    )
    out_expert_in = over_dp(g_in_a)
    out_expert_down = over_dp(g_down_a)
    grad_two = [cotangent[m].astype(f32) + values[m] for m in each]

    grad_layer, sides = [], []
    attn_back = []
    for m in each:
        grad_in, side = attn_backward(
            grad_two[m].astype(bf16), attn_kept[m][2], w_qkv_here, w_out_t
        )
        attn_back.append(grad_in)
        sides.append(side)
    attn_in = cat([s[0] for s in sides])
    grad_packed = cat([s[1] for s in sides])
    context = cat([s[2] for s in sides])
    grad_attn = cat([s[3] for s in sides])
    g_attn = jnp.concatenate([tn(attn_in, grad_packed, bf16), tn(grad_attn, context, bf16)], axis=1)
    attn_back[-1], g_attn = fence(attn_back[-1], g_attn)
    g_attn = lax.psum_scatter(g_attn, FS, scatter_dimension=0, tiled=True)
    g_attn = lax.psum_scatter(g_attn, "z", scatter_dimension=0, tiled=True)
    g_attn = lax.all_to_all(
        g_attn.reshape(2, rows, -1), "core", split_axis=0, concat_axis=0, tiled=True
    ).astype(f32)
    for m in each:
        normed, scale, _ = attn_kept[m]
        grad_values, part = rms_backward(attn_back[m], normed, scale, gain_attn)
        gains[2] = gains[2] + part
        grad_layer.append(grad_two[m] + grad_values)

    values, (g_in_m, g_down_m, g_sin_m, g_sdown_m), gains[1], g_router_m = moe_stage(
        [gather_rows(g.astype(bf16)) for g in grad_layer], one_kept, moe_m, gain_moe_m
    )
    out_expert_in_m = over_dp(g_in_m)
    out_expert_down_m = over_dp(g_down_m)
    grad_one = [grad_layer[m] + values[m] for m in each]

    small = None
    mamba_sides, mamba_back = [], []
    for m in each:
        mix_branch, gate_scale = mix_kept[m]
        normed_x, scale_x, mamba_in, pullback, gated, gained = mamba_kept[m]
        grad_mix = grad_one[m].astype(bf16)
        mean_term = jnp.sum(grad_mix.astype(f32) * mix_branch, axis=-1, keepdims=True) / DI
        extra = lanes(split_two(gate_scale) + split_two(mean_term), 128)
        rows_all = gather_rows(jnp.concatenate([grad_mix, extra], axis=1))
        mix_all = rows_all[:, :D]
        extra = rows_all[:, D:].astype(f32)
        scale_all = extra[:, 0:1] + extra[:, 1:2]
        mean_all = extra[:, 2:3] + extra[:, 3:4]
        grad_gated = nn(mix_all, w_mix_t, bf16).astype(f32)
        norm_gated = gated * scale_all
        grad_gate_norm = jnp.sum(grad_gated * norm_gated, axis=0)
        grad_rows = scale_all * (grad_gated * gain_here - norm_gated * mean_all)
        pulled = pullback(grad_rows.reshape(n_tp, length, chan))
        grad_proj = pulled[0].reshape(-1, in_width).astype(bf16)
        grad_step = pulled[1].reshape(-1, heads).astype(bf16)
        scaled_mix = (mix_all.astype(f32) * scale_all).astype(bf16)
        mamba_sides.append((mamba_in, grad_proj, grad_step, gained, scaled_mix))
        grads = (*pulled[2:], grad_gate_norm)
        small = grads if small is None else tuple(a + b for a, b in zip(small, grads))
        mamba_back.append(return_rows(nt(grad_proj, w_in_here) + nt(grad_step, w_dt_here)))

    def rows_back(packed):
        packed = lax.psum_scatter(packed, FS, scatter_dimension=0, tiled=True)
        return lax.all_to_all(
            packed.reshape(n_tp, rows, -1), TP, split_axis=0, concat_axis=0, tiled=True
        ).astype(f32)

    def owned(block):
        return block.transpose(1, 0, 2).reshape(rows, -1)

    g_mix = tn(
        cat([s[4] for s in mamba_sides]), cat([s[3] for s in mamba_sides]), bf16
    )
    g_s = rows_back(
        jnp.concatenate([g_mix, g_sin_m, g_sdown_m, g_sin_a, g_sdown_a], axis=1)
    )
    out_mix = owned(g_s[:, :, :chan]).T

    mamba_in = cat([s[0] for s in mamba_sides])
    g_proj = tn(mamba_in, cat([s[1] for s in mamba_sides]), bf16)
    g_step = tn(mamba_in, cat([s[2] for s in mamba_sides]), bf16)

    grads_in = []
    for m in each:
        normed_x, scale_x = mamba_kept[m][:2]
        grad_values, part = rms_backward(mamba_back[m], normed_x, scale_x, gain_mamba)
        gains[0] = gains[0] + part
        grads_in.append(grad_one[m] + grad_values)

    g_taps, g_bias, g_dt, g_log, g_skip, g_gate = small

    def spread(part, width):
        zeros = jnp.zeros(part.shape[:-1] + (width,), f32)
        return lax.dynamic_update_slice_in_dim(zeros, part[..., :chan], slot * chan, axis=-1)

    conv_grad = jnp.concatenate([g_bias[None], g_taps], axis=0)
    conv_grad = spread(conv_grad, conv_total) + jnp.pad(conv_grad[:, chan:], ((0, 0), (DI, 0)))
    conv_grad = conv_grad.reshape(CK + 1, n_all, conv_here).transpose(1, 0, 2).reshape(n_all, -1)
    vec_grad = jnp.concatenate([spread(g_gate, DI).reshape(n_all, gate_here), conv_grad], axis=1)
    vec_grad = jnp.pad(vec_grad, ((0, 0), (0, rows * vec_cols - vec_len))).reshape(D, vec_cols)
    little = jnp.concatenate(
        [g[:, None] for g in gains] + [g_router_m, g_router, vec_grad], axis=1
    ).astype(bf16)
    blank = jnp.zeros((D, step_width - heads - small_cols), bf16)
    g_m = rows_back(jnp.concatenate([g_proj, g_step, little, blank], axis=1))
    out_w_in = jnp.concatenate(
        [
            owned(g_m[:, :, :chan]),
            owned(g_m[:, :, chan : 2 * chan]),
            jnp.sum(g_m[:, :, 2 * chan : in_width], axis=0),
        ],
        axis=1,
    )
    out_w_dt = owned(g_m[:, :, in_width : in_width + heads])
    little = jnp.sum(g_m[:, :, in_width + heads : in_width + heads + small_cols], axis=0)
    vec = little[:, 4 + 2 * experts_total :].reshape(-1)
    out_gate = vec[:gate_here]
    out_conv_b = vec[gate_here : gate_here + conv_here]
    out_conv_w = vec[gate_here + conv_here : vec_len].reshape(CK, conv_here)

    head_grad = jnp.pad(jnp.stack([g_dt, g_log, g_skip]), ((0, 0), (0, 128 - heads)))[None]
    for axis in ("dp", "w"):
        own = head_grad
        for s in range(1, lax.axis_size(axis)):
            head_grad = head_grad + lax.ppermute(own, axis, ring(s, axis))
    for axis in ("z", "core"):
        n = lax.axis_size(axis)
        here = lax.axis_index(axis)
        parts = [head_grad] + [lax.ppermute(head_grad, axis, ring(s, axis)) for s in range(1, n)]
        ordered = 0.0
        for s, part in enumerate(parts):
            at_slot = jnp.arange(n)[:, None, None, None] == (here - s) % n
            ordered = ordered + jnp.where(at_slot, part[None], 0.0)
        head_grad = ordered.reshape((-1,) + ordered.shape[2:]) if axis == "z" else jnp.moveaxis(
            ordered, 0, 1
        ).reshape((-1,) + ordered.shape[2:])
    head_grad = head_grad[:, :, :heads].transpose(1, 0, 2).reshape(3, MH)

    cuts = (q_width, q_width + kv_width, q_width + 2 * kv_width)
    out_w_qkv = jnp.concatenate(
        [
            owned(g_attn[:, :, : cuts[0]]),
            owned(g_attn[:, :, cuts[0] : cuts[1]]),
            owned(g_attn[:, :, cuts[1] : cuts[2]]),
        ],
        axis=1,
    )
    out_w_out = owned(g_attn[:, :, cuts[2] :]).T

    def shared_out(block):
        g_sin = jnp.concatenate([owned(block[:, :, :ff]), owned(block[:, :, ff : 2 * ff])], axis=1)
        return g_sin, owned(block[:, :, 2 * ff :]).T

    out_sin_m, out_sdown_m = shared_out(g_s[:, :, chan : chan + 3 * ff])
    out_sin, out_sdown = shared_out(g_s[:, :, chan + 3 * ff :])

    return (
        jnp.stack(results),
        jnp.stack(grads_in),
        little[:, 0],
        out_w_in,
        out_w_dt,
        out_conv_w,
        out_conv_b,
        head_grad[0],
        head_grad[1],
        head_grad[2],
        out_gate,
        out_mix,
        little[:, 1],
        little[:, 4 : 4 + experts_total],
        out_sin_m,
        out_sdown_m,
        out_expert_in_m,
        out_expert_down_m,
        little[:, 2],
        out_w_qkv,
        out_w_out,
        little[:, 3],
        little[:, 4 + experts_total : 4 + 2 * experts_total],
        out_sin,
        out_sdown,
        out_expert_in,
        out_expert_down,
    )


def solution(mesh):
    n_dp, n_ex = mesh.shape["dp"], mesh.shape["expert"]
    outer = n_ex // 8
    fine = Mesh(mesh.devices.reshape(n_dp, outer, 4, 2), ALL)
    split = P(ALL)
    row = P(ALL, None)
    col = P(None, ALL)
    mid = P(None, ALL, None)
    part = P(EX, "dp", None)
    same = P()
    return jax.shard_map(
        body,
        mesh=fine,
        in_specs=(
            mid,
            mid,
            P(None, None, ALL, None),
            split,
            row,
            row,
            col,
            split,
            same,
            same,
            same,
            split,
            col,
            split,
            row,
            row,
            col,
            part,
            part,
            split,
            row,
            col,
            split,
            row,
            row,
            col,
            part,
            part,
            mid,
        ),
        out_specs=(
            mid,
            mid,
            split,
            row,
            row,
            col,
            split,
            same,
            same,
            same,
            split,
            col,
            split,
            row,
            row,
            col,
            part,
            part,
            split,
            row,
            col,
            split,
            row,
            row,
            col,
            part,
            part,
        ),
        check_vma=False,
    )
```

profile of v0, /device:TPU:0, one launch (start us, length us, event | category | flops | bytes accessed | tf_op | source)
XLA Modules:
  0.0 2011.2 jit_solution(14029155185068926951)
XLA Ops:
  17.4 49.4 %all_to_all.31 = bf16[8,48,1152]{2,1,0:T(8,128)(2,1)} all-to-all(bf16[8,48,1152]{2,1,0:T(8,128)(2,1)S(1)} %copy.873), channel_id=1, replica_groups=mesh['dp'=4,'w'=1,'z'=4,'core'=2] {'z','core'}, dimensions={0} | all-to-all | bytes 1769472 | tf_op jit(solution)/shard_map/all_to_all | solution.py:395
  67.5 26.2 %all_to_all.32 = bf16[8,48,1152]{2,1,0:T(8,128)(2,1)} all-to-all(bf16[8,48,1152]{2,1,0:T(8,128)(2,1)S(1)} %copy.883), channel_id=1, replica_groups=mesh['dp'=4,'w'=1,'z'=4,'core'=2] {'z','core'}, dimensions={0} | all-to-all | bytes 1769472 | tf_op jit(solution)/shard_map/all_to_all | solution.py:395
  109.3 18.6 collective-permute-start.35
  127.9 26.7 %collective-permute-done.1 = bf16[64,1664]{0,1:T(8,128)(2,1)S(1)} collective-permute-done((bf16[64,1664]{0,1:T(8,128)(2,1)S(1)}, bf16[64,1664]{0,1:T(8,128)(2,1)S(1)}, u32[]{:S(2)}, u32[]{:S(2)}) %collective-permute-start.1) | collective-permute-done | bytes 213024 | tf_op jit(solution)/shard_map/ppermute | solution.py:81
  155.8 16.7 collective-permute-done.36
  257.9 6.7 concatenate.283
  273.8 19.2 collective-permute-done.8
  293.1 16.1 collective-permute-done.9
  324.4 23.0 %collective-permute-done.12 = bf16[64,1536]{0,1:T(8,128)(2,1)S(1)} collective-permute-done((bf16[64,1536]{0,1:T(8,128)(2,1)S(1)}, bf16[64,1536]{0,1:T(8,128)(2,1)S(1)}, u32[]{:S(2)}, u32[]{:S(2)}) %collective-permute-start.12) | collective-permute-done | bytes 196640 | tf_op jit(solution)/shard_map/ppermute | solution.py:81
  349.3 10.5 collective-permute-start.71
  391.5 18.2 collective-permute-done.19
  409.8 23.0 %collective-permute-done.20 = bf16[64,1536]{0,1:T(8,128)(2,1)S(1)} collective-permute-done((bf16[64,1536]{0,1:T(8,128)(2,1)S(1)}, bf16[64,1536]{0,1:T(8,128)(2,1)S(1)}, u32[]{:S(2)}, u32[]{:S(2)}) %collective-permute-start.20) | collective-permute-done | bytes 196640 | tf_op jit(solution)/shard_map/ppermute | solution.py:95
  460.9 21.3 %collective-permute-done.25 = bf16[64,1536]{0,1:T(8,128)(2,1)} collective-permute-done((bf16[64,1536]{0,1:T(8,128)(2,1)}, bf16[64,1536]{0,1:T(8,128)(2,1)}, u32[]{:S(2)}, u32[]{:S(2)}) %collective-permute-start.25) | collective-permute-done | bytes 196640 | tf_op jit(solution)/shard_map/ppermute | solution.py:81
  524.7 7.9 concatenate.290
  542.2 9.2 collective-permute-start.80
  561.8 12.7 collective-permute-done.80
  574.5 16.6 collective-permute-done.79
  614.2 17.6 collective-permute-done.32
  631.8 13.6 collective-permute-done.33
  654.9 6.2 collective-permute-done.85
  661.1 23.4 %collective-permute-done.84 = bf16[64,1536]{0,1:T(8,128)(2,1)S(1)} collective-permute-done((bf16[64,1536]{0,1:T(8,128)(2,1)S(1)}, bf16[64,1536]{0,1:T(8,128)(2,1)S(1)}, u32[]{:S(2)}, u32[]{:S(2)}) %collective-permute-start.84) | collective-permute-done | bytes 196640 | tf_op jit(solution)/shard_map/ppermute | solution.py:81
  712.6 6.8 collective-permute-done.43
  719.4 25.6 %collective-permute-start.105 = (bf16[64,1536]{0,1:T(8,128)(2,1)}, bf16[64,1536]{0,1:T(8,128)(2,1)}, u32[]{:S(2)}, u32[]{:S(2)}) collective-permute-start(bf16[64,1536]{0,1:T(8,128)(2,1)} %bitcast.98), channel_id=1, source_target_pairs={{0,2},{2,4},{4,6},{6,0},{1,3},{3,5},{5,7},{7,1},{8,10},{10,12},{12... | collective-permute-start | bytes 589832 | tf_op jit(solution)/shard_map/ppermute | solution.py:81
  745.0 8.4 collective-permute-done.44
  759.1 19.4 collective-permute-done.91
  779.0 14.3 collective-permute-done.92
  807.4 8.3 concatenate.317
  823.8 42.4 %collective-permute-done.47 = bf16[64,1536]{0,1:T(8,128)(2,1)} collective-permute-done((bf16[64,1536]{0,1:T(8,128)(2,1)S(1)}, bf16[64,1536]{0,1:T(8,128)(2,1)}, u32[]{:S(2)}, u32[]{:S(2)}) %collective-permute-start.47) | collective-permute-done | bytes 196640 | tf_op jit(solution)/shard_map/ppermute | solution.py:81
  868.1 6.3 collective-permute-done.95
  899.8 8.3 concatenate.333
  924.6 6.3 fusion.262
  946.9 12.5 collective-permute-done.56
  959.4 14.7 collective-permute-done.55
  994.3 7.5 collective-permute-done.61
  1001.8 21.8 %collective-permute-done.60 = bf16[64,1536]{0,1:T(8,128)(2,1)S(1)} collective-permute-done((bf16[64,1536]{0,1:T(8,128)(2,1)S(1)}, bf16[64,1536]{0,1:T(8,128)(2,1)S(1)}, u32[]{:S(2)}, u32[]{:S(2)}) %collective-permute-start.60) | collective-permute-done | bytes 196640 | tf_op jit(solution)/shard_map/ppermute | solution.py:81
  1061.8 8.3 concatenate.313
  1070.1 7.7 fusion.3
  1077.9 12.0 fusion.2
  1129.5 12.4 collective-permute-done.115
  1141.9 16.5 collective-permute-done.114
  1189.2 10.0 collective-permute-done.68
  1208.6 7.9 collective-permute-done.120
  1216.5 23.5 %collective-permute-done.119 = bf16[64,1536]{0,1:T(8,128)(2,1)} collective-permute-done((bf16[64,1536]{0,1:T(8,128)(2,1)S(1)}, bf16[64,1536]{0,1:T(8,128)(2,1)}, u32[]{:S(2)}, u32[]{:S(2)}) %collective-permute-start.119) | collective-permute-done | bytes 196640 | tf_op jit(solution)/shard_map/ppermute | solution.py:81
  1247.4 8.3 concatenate.337
  1275.2 12.0 fusion.5
  1287.1 12.0 fusion.4
  1331.6 12.5 collective-permute-done.128
  1344.1 16.6 collective-permute-done.127
  1375.1 9.9 collective-permute-done.131
  1385.0 23.9 %collective-permute-done.130 = bf16[64,1664]{0,1:T(8,128)(2,1)} collective-permute-done((bf16[64,1664]{0,1:T(8,128)(2,1)}, bf16[64,1664]{0,1:T(8,128)(2,1)}, u32[]{:S(2)}, u32[]{:S(2)}) %collective-permute-start.130) | collective-permute-done | bytes 213024 | tf_op jit(solution)/shard_map/ppermute | solution.py:81
  1518.6 8.0 collective-permute-done.104
  1526.6 15.6 collective-permute-done.103
  1542.8 9.1 collective-permute-done.139
  1551.9 23.0 %collective-permute-done.138 = bf16[64,1536]{0,1:T(8,128)(2,1)S(1)} collective-permute-done((bf16[64,1536]{0,1:T(8,128)(2,1)S(1)}, bf16[64,1536]{0,1:T(8,128)(2,1)S(1)}, u32[]{:S(2)}, u32[]{:S(2)}) %collective-permute-start.138) | collective-permute-done | bytes 196640 | tf_op jit(solution)/shard_map/ppermute | solution.py:95
  1579.5 17.5 concatenate.352
  1601.0 8.7 copy.1131
  1625.4 10.3 collective-permute-done.145
  1635.7 7.7 collective-permute-done.144
  1654.3 65.8 %reduce-scatter.29.cloned.1.call-done = bf16[384,2048]{1,0:T(8,128)(2,1)} async-done(((bf16[1536,2048]{1,0:T(8,128)(2,1)}), bf16[384,2048]{1,0:T(8,128)(2,1)}) %reduce-scatter.29.cloned.1.call-update) | async-done | bytes 1572880
  1723.0 44.0 %reduce-scatter.23.cloned.1.call-done = bf16[2,128,1536]{2,1,0:T(8,128)(2,1)} async-done(((bf16[2,512,1536]{2,1,0:T(8,128)(2,1)}), bf16[2,128,1536]{2,1,0:T(8,128)(2,1)}) %reduce-scatter.23.cloned.1.call-update) | async-done | bytes 786448 | tf_op jit(solution)/shard_map/reduce_scatter | solution.py:559
  1769.4 44.5 %reduce-scatter.19.cloned.1.call-done = bf16[2,128,1536]{2,1,0:T(8,128)(2,1)} async-done(((bf16[2,512,1536]{2,1,0:T(8,128)(2,1)}), bf16[2,128,1536]{2,1,0:T(8,128)(2,1)}) %reduce-scatter.19.cloned.1.call-update) | async-done | bytes 786448 | tf_op jit(solution)/shard_map/reduce_scatter | solution.py:559
  1827.1 60.0 %reduce-scatter.21.cloned.1.call-done = bf16[2,384,1024]{2,1,0:T(8,128)(2,1)} async-done(((bf16[2,1536,1024]{2,1,0:T(8,128)(2,1)}), bf16[2,384,1024]{2,1,0:T(8,128)(2,1)}) %reduce-scatter.21.cloned.1.call-update) | async-done | bytes 1572880 | tf_op jit(solution)/shard_map/reduce_scatter | solution.py:559
  1890.5 69.6 %reduce-scatter.17.cloned.1.call-done = bf16[2,384,1024]{2,1,0:T(8,128)(2,1)} async-done(((bf16[2,1536,1024]{2,1,0:T(8,128)(2,1)}), bf16[2,384,1024]{2,1,0:T(8,128)(2,1)}) %reduce-scatter.17.cloned.1.call-update) | async-done | bytes 1572880 | tf_op jit(solution)/shard_map/reduce_scatter | solution.py:559
  1963.5 34.0 %reduce-scatter.31.cloned.1.call-done = bf16[96,2048]{1,0:T(8,128)(2,1)} async-done(((bf16[384,2048]{1,0:T(8,128)(2,1)}), bf16[96,2048]{1,0:T(8,128)(2,1)}) %reduce-scatter.31.cloned.1.call-update) | async-done | bytes 393232 | tf_op jit(solution)/shard_map/reduce_scatter | solution.py:603
  (1798 shorter events, 793.1 us)
Async XLA Ops:
  7.3 87.7 %all-gather.17.cloned.1.call-start = ((), (), s32[]{:S(2)}) async-start(), calls=%async_computation.18 | async-start | bytes 1966080 | tf_op jit(solution)/shard_map/all_gather | solution.py:471
  15.5 172.0 %all-gather.9.cloned.1.call-start = ((), (), s32[]{:S(2)}) async-start(), calls=%async_computation.14 | async-start | bytes 4423680 | tf_op jit(solution)/shard_map/all_gather | solution.py:396
  66.8 188.6 %all-gather.11.cloned.1.call-start = ((), (), s32[]{:S(2)}) async-start(), calls=%async_computation.15 | async-start | bytes 4423680 | tf_op jit(solution)/shard_map/all_gather | solution.py:396
  93.7 277.9 %all-gather.13.cloned.1.call-start = ((), (), s32[]{:S(2)}) async-start(), calls=%async_computation.16 | async-start | bytes 7864320 | tf_op jit(solution)/shard_map/all_gather | solution.py:453
  94.3 286.1 %all-gather.15.cloned.1.call-start = ((), (), s32[]{:S(2)}) async-start(), calls=%async_computation.17 | async-start | bytes 3932160 | tf_op jit(solution)/shard_map/all_gather | solution.py:454
  94.9 340.3 %all-gather.19.cloned.1.call-start = ((), (), s32[]{:S(2)}) async-start(), calls=%async_computation.19 | async-start | bytes 7864320 | tf_op jit(solution)/shard_map/all_gather | solution.py:472
  95.5 399.2 %all-gather.21.cloned.1.call-start = ((), (), s32[]{:S(2)}) async-start(), calls=%async_computation.20 | async-start | bytes 7864320 | tf_op jit(solution)/shard_map/all_gather | solution.py:480
  97.8 56.8 %collective-permute-start.1 = (bf16[64,1664]{0,1:T(8,128)(2,1)S(1)}, bf16[64,1664]{0,1:T(8,128)(2,1)S(1)}, u32[]{:S(2)}, u32[]{:S(2)}) collective-permute-start(bf16[64,1664]{0,1:T(8,128)(2,1)S(1)} %concatenate.280), channel_id=1, source_target_pairs={{0,4},{2,6},{4,0},{6,2},{1,5},{3,7},{5,1},{7,3},{8,12},{10,14},{12... | collective-permute-start | bytes 638984 | tf_op jit(solution)/shard_map/ppermute | solution.py:81
  98.3 56.3 %collective-permute-start = (bf16[64,1664]{0,1:T(8,128)(2,1)S(1)}, bf16[64,1664]{0,1:T(8,128)(2,1)S(1)}, u32[]{:S(2)}, u32[]{:S(2)}) collective-permute-start(bf16[64,1664]{0,1:T(8,128)(2,1)S(1)} %concatenate.280), channel_id=1, source_target_pairs={{0,2},{2,4},{4,6},{6,0},{1,3},{3,5},{5,7},{7,1},{8,10},{10,12},{12... | collective-permute-start | bytes 638984 | tf_op jit(solution)/shard_map/ppermute | solution.py:81
  99.4 55.8 %collective-permute-start.37 = (bf16[64,1664]{0,1:T(8,128)(2,1)S(1)}, bf16[64,1664]{0,1:T(8,128)(2,1)}, u32[]{:S(2)}, u32[]{:S(2)}) collective-permute-start(bf16[64,1664]{0,1:T(8,128)(2,1)S(1)} %concatenate.288), channel_id=1, source_target_pairs={{0,6},{2,0},{4,2},{6,4},{1,7},{3,1},{5,3},{7,5},{8,14},{10,8},{12,... | collective-permute-start | bytes 638984 | tf_op jit(solution)/shard_map/ppermute | solution.py:81
  103.0 400.5 %all-gather.23.cloned.1.call-start = ((), (), s32[]{:S(2)}) async-start(), calls=%async_computation.21 | async-start | bytes 3932160 | tf_op jit(solution)/shard_map/all_gather | solution.py:481
  104.2 68.3 %collective-permute-start.36 = (bf16[64,1664]{0,1:T(8,128)(2,1)S(1)}, bf16[64,1664]{0,1:T(8,128)(2,1)}, u32[]{:S(2)}, u32[]{:S(2)}) collective-permute-start(bf16[64,1664]{0,1:T(8,128)(2,1)S(1)} %concatenate.288), channel_id=1, source_target_pairs={{0,4},{2,6},{4,0},{6,2},{1,5},{3,7},{5,1},{7,3},{8,12},{10,14},{12... | collective-permute-start | bytes 638984 | tf_op jit(solution)/shard_map/ppermute | solution.py:81
  109.3 63.2 %collective-permute-start.35 = (bf16[64,1664]{0,1:T(8,128)(2,1)S(1)}, bf16[64,1664]{0,1:T(8,128)(2,1)}, u32[]{:S(2)}, u32[]{:S(2)}) collective-permute-start(bf16[64,1664]{0,1:T(8,128)(2,1)S(1)} %concatenate.288), channel_id=1, source_target_pairs={{0,2},{2,4},{4,6},{6,0},{1,3},{3,5},{5,7},{7,1},{8,10},{10,12},{12... | collective-permute-start | bytes 638984 | tf_op jit(solution)/shard_map/ppermute | solution.py:81
  272.6 36.6 %collective-permute-start.9 = (bf16[64,1664]{0,1:T(8,128)(2,1)S(1)}, bf16[64,1664]{0,1:T(8,128)(2,1)S(1)}, u32[]{:S(2)}, u32[]{:S(2)}) collective-permute-start(bf16[64,1664]{0,1:T(8,128)(2,1)S(1)} %get-tuple-element.409), channel_id=1, source_target_pairs={{0,4},{2,6},{4,0},{6,2},{1,5},{3,7},{5,1},{7,3},{8,12},{10,14},{12... | collective-permute-start | bytes 638984 | tf_op jit(solution)/shard_map/ppermute | solution.py:95
  313.5 33.9 %collective-permute-start.12 = (bf16[64,1536]{0,1:T(8,128)(2,1)S(1)}, bf16[64,1536]{0,1:T(8,128)(2,1)S(1)}, u32[]{:S(2)}, u32[]{:S(2)}) collective-permute-start(bf16[64,1536]{0,1:T(8,128)(2,1)S(1)} %multiply_convert_fusion.33), channel_id=1, source_target_pairs={{0,4},{2,6},{4,0},{6,2},{1,5},{3,7},{5,1},{7,3},{8,12},{10,14},{12... | collective-permute-start | bytes 589832 | tf_op jit(solution)/shard_map/ppermute | solution.py:81
  313.5 33.9 %collective-permute-start.11 = (bf16[64,1536]{0,1:T(8,128)(2,1)S(1)}, bf16[64,1536]{0,1:T(8,128)(2,1)S(1)}, u32[]{:S(2)}, u32[]{:S(2)}) collective-permute-start(bf16[64,1536]{0,1:T(8,128)(2,1)S(1)} %multiply_convert_fusion.33), channel_id=1, source_target_pairs={{0,2},{2,4},{4,6},{6,0},{1,3},{3,5},{5,7},{7,1},{8,10},{10,12},{12... | collective-permute-start | bytes 589832 | tf_op jit(solution)/shard_map/ppermute | solution.py:81
  315.1 128.9 %collective-permute-start.72 = (bf16[64,1536]{0,1:T(8,128)(2,1)S(1)}, bf16[64,1536]{0,1:T(8,128)(2,1)}, u32[]{:S(2)}, u32[]{:S(2)}) collective-permute-start(bf16[64,1536]{0,1:T(8,128)(2,1)S(1)} %bitcast.631), channel_id=1, source_target_pairs={{0,6},{2,0},{4,2},{6,4},{1,7},{3,1},{5,3},{7,5},{8,14},{10,8},{12,... | collective-permute-start | bytes 589832 | tf_op jit(solution)/shard_map/ppermute | solution.py:81
  318.7 1297.8 %reduce-scatter.27.cloned.1.call-start = ((), (), s32[]{:S(2)}) async-start(), calls=%async_computation.27 | async-start | bytes 4423680 | tf_op jit(solution)/shard_map/reduce_scatter | solution.py:647
  324.4 35.4 %collective-permute-start.17 = (bf16[64,1536]{0,1:T(8,128)(2,1)S(1)}, bf16[64,1536]{0,1:T(8,128)(2,1)S(1)}, u32[]{:S(2)}, u32[]{:S(2)}) collective-permute-start(bf16[64,1536]{0,1:T(8,128)(2,1)S(1)} %collective-permute-done.13), channel_id=1, source_target_pairs={{0,1},{1,0},{2,3},{3,2},{4,5},{5,4},{6,7},{7,6},{8,9},{9,8},{10,11... | collective-permute-start | bytes 589832 | tf_op jit(solution)/shard_map/ppermute | solution.py:82
  349.3 94.8 %collective-permute-start.71 = (bf16[64,1536]{0,1:T(8,128)(2,1)S(1)}, bf16[64,1536]{0,1:T(8,128)(2,1)}, u32[]{:S(2)}, u32[]{:S(2)}) collective-permute-start(bf16[64,1536]{0,1:T(8,128)(2,1)S(1)} %bitcast.632), channel_id=1, source_target_pairs={{0,4},{2,6},{4,0},{6,2},{1,5},{3,7},{5,1},{7,3},{8,12},{10,14},{12... | collective-permute-start | bytes 589832 | tf_op jit(solution)/shard_map/ppermute | solution.py:81
  390.9 41.9 %collective-permute-start.20 = (bf16[64,1536]{0,1:T(8,128)(2,1)S(1)}, bf16[64,1536]{0,1:T(8,128)(2,1)S(1)}, u32[]{:S(2)}, u32[]{:S(2)}) collective-permute-start(bf16[64,1536]{0,1:T(8,128)(2,1)S(1)} %get-tuple-element.438), channel_id=1, source_target_pairs={{0,4},{2,6},{4,0},{6,2},{1,5},{3,7},{5,1},{7,3},{8,12},{10,14},{12... | collective-permute-start | bytes 589832 | tf_op jit(solution)/shard_map/ppermute | solution.py:95
  409.6 34.9 %collective-permute-start.70 = (bf16[64,1536]{0,1:T(8,128)(2,1)S(1)}, bf16[64,1536]{0,1:T(8,128)(2,1)}, u32[]{:S(2)}, u32[]{:S(2)}) collective-permute-start(bf16[64,1536]{0,1:T(8,128)(2,1)S(1)} %bitcast.633), channel_id=1, source_target_pairs={{0,2},{2,4},{4,6},{6,0},{1,3},{3,5},{5,7},{7,1},{8,10},{10,12},{12... | collective-permute-start | bytes 589832 | tf_op jit(solution)/shard_map/ppermute | solution.py:81
  447.3 34.9 %collective-permute-start.25 = (bf16[64,1536]{0,1:T(8,128)(2,1)}, bf16[64,1536]{0,1:T(8,128)(2,1)}, u32[]{:S(2)}, u32[]{:S(2)}) collective-permute-start(bf16[64,1536]{0,1:T(8,128)(2,1)} %multiply_convert_fusion.31), channel_id=1, source_target_pairs={{0,4},{2,6},{4,0},{6,2},{1,5},{3,7},{5,1},{7,3},{8,12},{10,14},{12... | collective-permute-start | bytes 589832 | tf_op jit(solution)/shard_map/ppermute | solution.py:81
  447.4 34.8 %collective-permute-start.24 = (bf16[64,1536]{0,1:T(8,128)(2,1)}, bf16[64,1536]{0,1:T(8,128)(2,1)}, u32[]{:S(2)}, u32[]{:S(2)}) collective-permute-start(bf16[64,1536]{0,1:T(8,128)(2,1)} %multiply_convert_fusion.31), channel_id=1, source_target_pairs={{0,2},{2,4},{4,6},{6,0},{1,3},{3,5},{5,7},{7,1},{8,10},{10,12},{12... | collective-permute-start | bytes 589832 | tf_op jit(solution)/shard_map/ppermute | solution.py:81
  451.8 306.6 %collective-permute-start.107 = (bf16[64,1536]{0,1:T(8,128)(2,1)}, bf16[64,1536]{0,1:T(8,128)(2,1)}, u32[]{:S(2)}, u32[]{:S(2)}) collective-permute-start(bf16[64,1536]{0,1:T(8,128)(2,1)} %bitcast.98), channel_id=1, source_target_pairs={{0,6},{2,0},{4,2},{6,4},{1,7},{3,1},{5,3},{7,5},{8,14},{10,8},{12,... | collective-permute-start | bytes 589832 | tf_op jit(solution)/shard_map/ppermute | solution.py:81
  535.1 117.1 %collective-permute-start.42 = (bf16[256,1664]{0,1:T(8,128)(2,1)}, bf16[256,1664]{0,1:T(8,128)(2,1)}, u32[]{:S(2)}, u32[]{:S(2)}) collective-permute-start(bf16[256,1664]{0,1:T(8,128)(2,1)} %slice.2190), channel_id=1, source_target_pairs={{0,1},{1,0},{2,3},{3,2},{4,5},{5,4},{6,7},{7,6},{8,9},{9,8},{10,11... | collective-permute-start | bytes 2555912 | tf_op jit(solution)/shard_map/ppermute | solution.py:90
  551.4 39.7 %collective-permute-start.79 = (bf16[64,1664]{0,1:T(8,128)(2,1)S(1)}, bf16[64,1664]{0,1:T(8,128)(2,1)S(1)}, u32[]{:S(2)}, u32[]{:S(2)}) collective-permute-start(bf16[64,1664]{0,1:T(8,128)(2,1)S(1)} %get-tuple-element.403), channel_id=1, source_target_pairs={{0,4},{2,6},{4,0},{6,2},{1,5},{3,7},{5,1},{7,3},{8,12},{10,14},{12... | collective-permute-start | bytes 638984 | tf_op jit(solution)/shard_map/ppermute | solution.py:95
  686.9 71.6 %collective-permute-start.106 = (bf16[64,1536]{0,1:T(8,128)(2,1)}, bf16[64,1536]{0,1:T(8,128)(2,1)}, u32[]{:S(2)}, u32[]{:S(2)}) collective-permute-start(bf16[64,1536]{0,1:T(8,128)(2,1)} %bitcast.98), channel_id=1, source_target_pairs={{0,4},{2,6},{4,0},{6,2},{1,5},{3,7},{5,1},{7,3},{8,12},{10,14},{12... | collective-permute-start | bytes 589832 | tf_op jit(solution)/shard_map/ppermute | solution.py:81
  690.3 54.7 %collective-permute-start.45 = (bf16[64,1664]{0,1:T(8,128)(2,1)}, bf16[64,1664]{0,1:T(8,128)(2,1)}, u32[]{:S(2)}, u32[]{:S(2)}) collective-permute-start(bf16[64,1664]{0,1:T(8,128)(2,1)} %get-tuple-element.411), channel_id=1, source_target_pairs={{0,2},{2,4},{4,6},{6,0},{1,3},{3,5},{5,7},{7,1},{8,10},{10,12},{12... | collective-permute-start | bytes 638984 | tf_op jit(solution)/shard_map/ppermute | solution.py:95
  692.9 60.5 %collective-permute-start.44 = (bf16[64,1664]{0,1:T(8,128)(2,1)}, bf16[64,1664]{0,1:T(8,128)(2,1)}, u32[]{:S(2)}, u32[]{:S(2)}) collective-permute-start(bf16[64,1664]{0,1:T(8,128)(2,1)} %get-tuple-element.412), channel_id=1, source_target_pairs={{0,4},{2,6},{4,0},{6,2},{1,5},{3,7},{5,1},{7,3},{8,12},{10,14},{12... | collective-permute-start | bytes 638984 | tf_op jit(solution)/shard_map/ppermute | solution.py:95
  719.4 39.2 %collective-permute-start.105 = (bf16[64,1536]{0,1:T(8,128)(2,1)}, bf16[64,1536]{0,1:T(8,128)(2,1)}, u32[]{:S(2)}, u32[]{:S(2)}) collective-permute-start(bf16[64,1536]{0,1:T(8,128)(2,1)} %bitcast.98), channel_id=1, source_target_pairs={{0,2},{2,4},{4,6},{6,0},{1,3},{3,5},{5,7},{7,1},{8,10},{10,12},{12... | collective-permute-start | bytes 589832 | tf_op jit(solution)/shard_map/ppermute | solution.py:81
  758.5 34.8 %collective-permute-start.92 = (bf16[64,1664]{0,1:T(8,128)(2,1)S(1)}, bf16[64,1664]{0,1:T(8,128)(2,1)S(1)}, u32[]{:S(2)}, u32[]{:S(2)}) collective-permute-start(bf16[64,1664]{0,1:T(8,128)(2,1)S(1)} %get-tuple-element.397), channel_id=1, source_target_pairs={{0,4},{2,6},{4,0},{6,2},{1,5},{3,7},{5,1},{7,3},{8,12},{10,14},{12... | collective-permute-start | bytes 638984 | tf_op jit(solution)/shard_map/ppermute | solution.py:95
  758.5 46.3 %collective-permute-start.108 = (bf16[64,1536]{0,1:T(8,128)(2,1)}, bf16[64,1536]{0,1:T(8,128)(2,1)}, u32[]{:S(2)}, u32[]{:S(2)}) collective-permute-start(bf16[64,1536]{0,1:T(8,128)(2,1)} %bitcast.98), channel_id=1, source_target_pairs={{0,1},{1,0},{2,3},{3,2},{4,5},{5,4},{6,7},{7,6},{8,9},{9,8},{10,11... | collective-permute-start | bytes 589832 | tf_op jit(solution)/shard_map/ppermute | solution.py:82
  758.6 46.2 %collective-permute-start.111 = (bf16[64,1536]{0,1:T(8,128)(2,1)}, bf16[64,1536]{0,1:T(8,128)(2,1)}, u32[]{:S(2)}, u32[]{:S(2)}) collective-permute-start(bf16[64,1536]{0,1:T(8,128)(2,1)} %collective-permute-done.107), channel_id=1, source_target_pairs={{0,1},{1,0},{2,3},{3,2},{4,5},{5,4},{6,7},{7,6},{8,9},{9,8},{10,11... | collective-permute-start | bytes 589832 | tf_op jit(solution)/shard_map/ppermute | solution.py:82
  800.5 66.2 %collective-permute-start.96 = (bf16[64,1664]{0,1:T(8,128)(2,1)S(1)}, bf16[64,1664]{0,1:T(8,128)(2,1)}, u32[]{:S(2)}, u32[]{:S(2)}) collective-permute-start(bf16[64,1664]{0,1:T(8,128)(2,1)S(1)} %concatenate.306), channel_id=1, source_target_pairs={{0,6},{2,0},{4,2},{6,4},{1,7},{3,1},{5,3},{7,5},{8,14},{10,8},{12,... | collective-permute-start | bytes 638984 | tf_op jit(solution)/shard_map/ppermute | solution.py:81
  805.4 60.8 %collective-permute-start.47 = (bf16[64,1536]{0,1:T(8,128)(2,1)S(1)}, bf16[64,1536]{0,1:T(8,128)(2,1)}, u32[]{:S(2)}, u32[]{:S(2)}) collective-permute-start(bf16[64,1536]{0,1:T(8,128)(2,1)S(1)} %get-tuple-element.498), channel_id=1, source_target_pairs={{0,4},{2,6},{4,0},{6,2},{1,5},{3,7},{5,1},{7,3},{8,12},{10,14},{12... | collective-permute-start | bytes 589832 | tf_op jit(solution)/shard_map/ppermute | solution.py:81
  805.4 60.8 %collective-permute-start.46 = (bf16[64,1536]{0,1:T(8,128)(2,1)S(1)}, bf16[64,1536]{0,1:T(8,128)(2,1)}, u32[]{:S(2)}, u32[]{:S(2)}) collective-permute-start(bf16[64,1536]{0,1:T(8,128)(2,1)S(1)} %get-tuple-element.498), channel_id=1, source_target_pairs={{0,2},{2,4},{4,6},{6,0},{1,3},{3,5},{5,7},{7,1},{8,10},{10,12},{12... | collective-permute-start | bytes 589832 | tf_op jit(solution)/shard_map/ppermute | solution.py:81
  820.9 53.5 %collective-permute-start.95 = (bf16[64,1664]{0,1:T(8,128)(2,1)S(1)}, bf16[64,1664]{0,1:T(8,128)(2,1)}, u32[]{:S(2)}, u32[]{:S(2)}) collective-permute-start(bf16[64,1664]{0,1:T(8,128)(2,1)S(1)} %concatenate.306), channel_id=1, source_target_pairs={{0,4},{2,6},{4,0},{6,2},{1,5},{3,7},{5,1},{7,3},{8,12},{10,14},{12... | collective-permute-start | bytes 638984 | tf_op jit(solution)/shard_map/ppermute | solution.py:81
  823.8 50.6 %collective-permute-start.94 = (bf16[64,1664]{0,1:T(8,128)(2,1)S(1)}, bf16[64,1664]{0,1:T(8,128)(2,1)}, u32[]{:S(2)}, u32[]{:S(2)}) collective-permute-start(bf16[64,1664]{0,1:T(8,128)(2,1)S(1)} %concatenate.306), channel_id=1, source_target_pairs={{0,2},{2,4},{4,6},{6,0},{1,3},{3,5},{5,7},{7,1},{8,10},{10,12},{12... | collective-permute-start | bytes 638984 | tf_op jit(solution)/shard_map/ppermute | solution.py:81
  874.4 33.7 %collective-permute-start.97 = (bf16[64,1664]{0,1:T(8,128)(2,1)S(1)}, bf16[64,1664]{0,1:T(8,128)(2,1)}, u32[]{:S(2)}, u32[]{:S(2)}) collective-permute-start(bf16[64,1664]{0,1:T(8,128)(2,1)S(1)} %concatenate.306), channel_id=1, source_target_pairs={{0,1},{1,0},{2,3},{3,2},{4,5},{5,4},{6,7},{7,6},{8,9},{9,8},{10,11... | collective-permute-start | bytes 638984 | tf_op jit(solution)/shard_map/ppermute | solution.py:82
  874.4 33.7 %collective-permute-start.100 = (bf16[64,1664]{0,1:T(8,128)(2,1)}, bf16[64,1664]{0,1:T(8,128)(2,1)}, u32[]{:S(2)}, u32[]{:S(2)}) collective-permute-start(bf16[64,1664]{0,1:T(8,128)(2,1)} %collective-permute-done.96), channel_id=1, source_target_pairs={{0,1},{1,0},{2,3},{3,2},{4,5},{5,4},{6,7},{7,6},{8,9},{9,8},{10,11... | collective-permute-start | bytes 638984 | tf_op jit(solution)/shard_map/ppermute | solution.py:82
  874.9 33.2 %collective-permute-start.99 = (bf16[64,1664]{0,1:T(8,128)(2,1)}, bf16[64,1664]{0,1:T(8,128)(2,1)}, u32[]{:S(2)}, u32[]{:S(2)}) collective-permute-start(bf16[64,1664]{0,1:T(8,128)(2,1)} %collective-permute-done.95), channel_id=1, source_target_pairs={{0,1},{1,0},{2,3},{3,2},{4,5},{5,4},{6,7},{7,6},{8,9},{9,8},{10,11... | collective-permute-start | bytes 638984 | tf_op jit(solution)/shard_map/ppermute | solution.py:82
  937.2 37.0 %collective-permute-start.55 = (bf16[64,1536]{0,1:T(8,128)(2,1)}, bf16[64,1536]{0,1:T(8,128)(2,1)}, u32[]{:S(2)}, u32[]{:S(2)}) collective-permute-start(bf16[64,1536]{0,1:T(8,128)(2,1)} %get-tuple-element.444), channel_id=1, source_target_pairs={{0,4},{2,6},{4,0},{6,2},{1,5},{3,7},{5,1},{7,3},{8,12},{10,14},{12... | collective-permute-start | bytes 589832 | tf_op jit(solution)/shard_map/ppermute | solution.py:95
  989.4 34.1 %collective-permute-start.60 = (bf16[64,1536]{0,1:T(8,128)(2,1)S(1)}, bf16[64,1536]{0,1:T(8,128)(2,1)S(1)}, u32[]{:S(2)}, u32[]{:S(2)}) collective-permute-start(bf16[64,1536]{0,1:T(8,128)(2,1)S(1)} %multiply_convert_fusion.28), channel_id=1, source_target_pairs={{0,4},{2,6},{4,0},{6,2},{1,5},{3,7},{5,1},{7,3},{8,12},{10,14},{12... | collective-permute-start | bytes 589832 | tf_op jit(solution)/shard_map/ppermute | solution.py:81
  989.5 34.1 %collective-permute-start.59 = (bf16[64,1536]{0,1:T(8,128)(2,1)S(1)}, bf16[64,1536]{0,1:T(8,128)(2,1)S(1)}, u32[]{:S(2)}, u32[]{:S(2)}) collective-permute-start(bf16[64,1536]{0,1:T(8,128)(2,1)S(1)} %multiply_convert_fusion.28), channel_id=1, source_target_pairs={{0,2},{2,4},{4,6},{6,0},{1,3},{3,5},{5,7},{7,1},{8,10},{10,12},{12... | collective-permute-start | bytes 589832 | tf_op jit(solution)/shard_map/ppermute | solution.py:81
  994.3 33.7 %collective-permute-start.62 = (bf16[64,1536]{0,1:T(8,128)(2,1)S(1)}, bf16[64,1536]{0,1:T(8,128)(2,1)S(1)}, u32[]{:S(2)}, u32[]{:S(2)}) collective-permute-start(bf16[64,1536]{0,1:T(8,128)(2,1)S(1)} %multiply_convert_fusion.28), channel_id=1, source_target_pairs={{0,1},{1,0},{2,3},{3,2},{4,5},{5,4},{6,7},{7,6},{8,9},{9,8},{10,11... | collective-permute-start | bytes 589832 | tf_op jit(solution)/shard_map/ppermute | solution.py:82
  1119.7 38.7 %collective-permute-start.114 = (bf16[64,1664]{0,1:T(8,128)(2,1)S(1)}, bf16[64,1664]{0,1:T(8,128)(2,1)S(1)}, u32[]{:S(2)}, u32[]{:S(2)}) collective-permute-start(bf16[64,1664]{0,1:T(8,128)(2,1)S(1)} %get-tuple-element.406), channel_id=1, source_target_pairs={{0,4},{2,6},{4,0},{6,2},{1,5},{3,7},{5,1},{7,3},{8,12},{10,14},{12... | collective-permute-start | bytes 638984 | tf_op jit(solution)/shard_map/ppermute | solution.py:95
  1208.6 38.8 %collective-permute-start.121 = (bf16[64,1536]{0,1:T(8,128)(2,1)S(1)}, bf16[64,1536]{0,1:T(8,128)(2,1)}, u32[]{:S(2)}, u32[]{:S(2)}) collective-permute-start(bf16[64,1536]{0,1:T(8,128)(2,1)S(1)} %get-tuple-element.301), channel_id=1, source_target_pairs={{0,1},{1,0},{2,3},{3,2},{4,5},{5,4},{6,7},{7,6},{8,9},{9,8},{10,11... | collective-permute-start | bytes 589832 | tf_op jit(solution)/shard_map/ppermute | solution.py:82
  1321.9 38.8 %collective-permute-start.127 = (bf16[64,1664]{0,1:T(8,128)(2,1)S(1)}, bf16[64,1664]{0,1:T(8,128)(2,1)S(1)}, u32[]{:S(2)}, u32[]{:S(2)}) collective-permute-start(bf16[64,1664]{0,1:T(8,128)(2,1)S(1)} %get-tuple-element.400), channel_id=1, source_target_pairs={{0,4},{2,6},{4,0},{6,2},{1,5},{3,7},{5,1},{7,3},{8,12},{10,14},{12... | collective-permute-start | bytes 638984 | tf_op jit(solution)/shard_map/ppermute | solution.py:95
  1372.1 36.8 %collective-permute-start.130 = (bf16[64,1664]{0,1:T(8,128)(2,1)}, bf16[64,1664]{0,1:T(8,128)(2,1)}, u32[]{:S(2)}, u32[]{:S(2)}) collective-permute-start(bf16[64,1664]{0,1:T(8,128)(2,1)} %concatenate.341), channel_id=1, source_target_pairs={{0,4},{2,6},{4,0},{6,2},{1,5},{3,7},{5,1},{7,3},{8,12},{10,14},{12... | collective-permute-start | bytes 638984 | tf_op jit(solution)/shard_map/ppermute | solution.py:81
  1372.1 36.8 %collective-permute-start.129 = (bf16[64,1664]{0,1:T(8,128)(2,1)}, bf16[64,1664]{0,1:T(8,128)(2,1)}, u32[]{:S(2)}, u32[]{:S(2)}) collective-permute-start(bf16[64,1664]{0,1:T(8,128)(2,1)} %concatenate.341), channel_id=1, source_target_pairs={{0,2},{2,4},{4,6},{6,0},{1,3},{3,5},{5,7},{7,1},{8,10},{10,12},{12... | collective-permute-start | bytes 638984 | tf_op jit(solution)/shard_map/ppermute | solution.py:81
  1375.1 42.0 %collective-permute-start.132 = (bf16[64,1664]{0,1:T(8,128)(2,1)}, bf16[64,1664]{0,1:T(8,128)(2,1)}, u32[]{:S(2)}, u32[]{:S(2)}) collective-permute-start(bf16[64,1664]{0,1:T(8,128)(2,1)} %concatenate.341), channel_id=1, source_target_pairs={{0,1},{1,0},{2,3},{3,2},{4,5},{5,4},{6,7},{7,6},{8,9},{9,8},{10,11... | collective-permute-start | bytes 638984 | tf_op jit(solution)/shard_map/ppermute | solution.py:82
  1454.3 192.6 %reduce-scatter.25.cloned.1.call-start = ((), (), s32[]{:S(2)}) async-start(), calls=%async_computation.26 | async-start | bytes 4423680 | tf_op jit(solution)/shard_map/reduce_scatter | solution.py:647
  1505.0 37.2 %collective-permute-start.103 = (bf16[64,1536]{0,1:T(8,128)(2,1)S(1)}, bf16[64,1536]{0,1:T(8,128)(2,1)S(1)}, u32[]{:S(2)}, u32[]{:S(2)}) collective-permute-start(bf16[64,1536]{0,1:T(8,128)(2,1)S(1)} %get-tuple-element.419), channel_id=1, source_target_pairs={{0,4},{2,6},{4,0},{6,2},{1,5},{3,7},{5,1},{7,3},{8,12},{10,14},{12... | collective-permute-start | bytes 589832 | tf_op jit(solution)/shard_map/ppermute | solution.py:95
  1509.3 33.4 %collective-permute-start.137 = (bf16[64,1536]{0,1:T(8,128)(2,1)S(1)}, bf16[64,1536]{0,1:T(8,128)(2,1)S(1)}, u32[]{:S(2)}, u32[]{:S(2)}) collective-permute-start(bf16[64,1536]{0,1:T(8,128)(2,1)S(1)} %get-tuple-element.420), channel_id=1, source_target_pairs={{0,6},{2,0},{4,2},{6,4},{1,7},{3,1},{5,3},{7,5},{8,14},{10,8},{12,... | collective-permute-start | bytes 589832 | tf_op jit(solution)/shard_map/ppermute | solution.py:95
  1510.3 41.6 %collective-permute-start.139 = (bf16[64,1536]{0,1:T(8,128)(2,1)S(1)}, bf16[64,1536]{0,1:T(8,128)(2,1)S(1)}, u32[]{:S(2)}, u32[]{:S(2)}) collective-permute-start(bf16[64,1536]{0,1:T(8,128)(2,1)S(1)} %get-tuple-element.421), channel_id=1, source_target_pairs={{0,2},{2,4},{4,6},{6,0},{1,3},{3,5},{5,7},{7,1},{8,10},{10,12},{12... | collective-permute-start | bytes 589832 | tf_op jit(solution)/shard_map/ppermute | solution.py:95
  1514.9 60.0 %collective-permute-start.138 = (bf16[64,1536]{0,1:T(8,128)(2,1)S(1)}, bf16[64,1536]{0,1:T(8,128)(2,1)S(1)}, u32[]{:S(2)}, u32[]{:S(2)}) collective-permute-start(bf16[64,1536]{0,1:T(8,128)(2,1)S(1)} %get-tuple-element.422), channel_id=1, source_target_pairs={{0,4},{2,6},{4,0},{6,2},{1,5},{3,7},{5,1},{7,3},{8,12},{10,14},{12... | collective-permute-start | bytes 589832 | tf_op jit(solution)/shard_map/ppermute | solution.py:95
  1600.9 119.2 %reduce-scatter.29.cloned.1.call-start = ((), (), s32[]{:S(2)}) async-start(), calls=%async_computation.28 | async-start | bytes 7864320
  1609.7 157.3 %reduce-scatter.23.cloned.1.call-start = ((), (), s32[]{:S(2)}) async-start(), calls=%async_computation.25 | async-start | bytes 3932160 | tf_op jit(solution)/shard_map/reduce_scatter | solution.py:559
  1610.3 203.6 %reduce-scatter.19.cloned.1.call-start = ((), (), s32[]{:S(2)}) async-start(), calls=%async_computation.23 | async-start | bytes 3932160 | tf_op jit(solution)/shard_map/reduce_scatter | solution.py:559
  1611.0 276.0 %reduce-scatter.21.cloned.1.call-start = ((), (), s32[]{:S(2)}) async-start(), calls=%async_computation.24 | async-start | bytes 7864320 | tf_op jit(solution)/shard_map/reduce_scatter | solution.py:559
  1611.7 348.4 %reduce-scatter.17.cloned.1.call-start = ((), (), s32[]{:S(2)}) async-start(), calls=%async_computation.22 | async-start | bytes 7864320 | tf_op jit(solution)/shard_map/reduce_scatter | solution.py:559
  1646.9 173.6 %all-to-all-start.3 = ((bf16[8,48,1152]{2,1,0:T(8,128)(2,1)}), bf16[8,48,1152]{2,1,0:T(8,128)(2,1)S(1)}, u32[]{:S(2)}, u32[]{:S(2)}) async-start(bf16[8,48,1152]{2,1,0:T(8,128)(2,1)} %bitcast.667), calls=%async_computation.3 | async-start | bytes 1769472 | tf_op jit(solution)/shard_map/all_to_all | solution.py:648
  1651.5 346.1 %reduce-scatter.31.cloned.1.call-start = ((), (), s32[]{:S(2)}) async-start(), calls=%async_computation.29 | async-start | bytes 1966080 | tf_op jit(solution)/shard_map/reduce_scatter | solution.py:603
  (559 other events, 6317.8 us)
Sparse Core Ops, SparseCore 0:
  15.6 56.7 all-gather.16
  74.3 46.1 all-gather.8
  122.3 47.2 all-gather.10
  171.3 70.1 all-gather.12
  243.2 43.9 all-gather.14
  288.9 70.1 all-gather.18
  360.9 70.1 all-gather.20
  433.0 43.9 all-gather.22
  1454.4 48.3 reduce-scatter.26
  1601.0 45.7 reduce-scatter.24
  1649.9 70.2 reduce-scatter.28
  1723.0 43.9 reduce-scatter.22
  1769.9 43.9 reduce-scatter.18
  1816.7 70.2 reduce-scatter.20
  1889.9 70.1 reduce-scatter.16
  1962.2 35.2 reduce-scatter.30
where the time goes:
time: 2030 us; the launch traced here: 2010 us
  waiting for transfers between devices  974 us (48%)
  matrix products  303 us (15%)
  local copies, waits for them, and re-layouts  286 us (14%)
  starting transfers between devices  185 us (9%)
  other arithmetic  156 us (8%)
  blocking collectives  85.4 us (4%)
  between operations  21.5 us (1%)
    ppermute x36, waiting for transfers between devices, return_rows(): out = out + lax.ppermute(part, 'z', ring(-s)).astype(f32)  359 us
    ppermute x36, waiting for transfers between devices, gather_rows(): parts = [x] + [lax.ppermute(x, 'z', ring(s)) for s in range(1, n)]  271 us
    dot_general x95, matrix products, dot(): r = lax.dot_general(a, b, (dims, ((), ())), preferred_element_type=f32)  250 us
    reduce_scatter x4, waiting for transfers between devices, over_dp(): lax.psum_scatter(g, 'dp', scatter_dimension=1, tiled=True).astype(f32)  218 us
    ppermute x36, starting transfers between devices, gather_rows(): parts = [x] + [lax.ppermute(x, 'z', ring(s)) for s in range(1, n)]  100 us
    all_to_all x2, blocking collectives, columns(): moved = lax.all_to_all(packed, TP, split_axis=0, concat_axis=0, tiled=True)  75.5 us
    unnamed x17, waiting for transfers between devices  69.8 us
    unnamed x947, local copies, waits for them, and re-layouts  63.5 us
  transfers between devices with their start and end apart: 165, of which 61 were waited for; matrix products, arithmetic and copies ran while one was open for 25% of the time, Pallas kernels for 0%

commit v1 on v0

--- a/solution.py
+++ b/solution.py
@@ -73,6 +73,8 @@
 
 
 def fence(*trees):
+    if lax.axis_size("w") > 1:
+        return trees
     return lax.optimization_barrier(trees)
 
 
@@ -199,12 +201,10 @@
     pre = [nn(moe_in, w["expert_in"][e], bf16) for e in range(count)]
     pre_s = nn(base_in, w["shared_in"], bf16)
     total = None
-    hidden = []
     for e in range(count):
         p = pre[e].astype(f32)
         act = swiglu(p[:, :EXP_FF], p[:, EXP_FF:])
         hid = (act * local[:, e : e + 1]).astype(bf16)
-        hidden.append(hid)
         part = nn(hid, w["expert_down"][e])
         total = part if total is None else total + part
     half = pre_s.shape[1] // 2
@@ -212,12 +212,13 @@
     hid_s = swiglu(p[:, :half], p[:, half:]).astype(bf16)
     total = add_first(total, nt(hid_s, w["shared_down_t"]))
     branch = return_rows(narrow(total))
-    kept = (moe_in, base_in, gates[:rows], local, pre, pre_s, hidden, hid_s)
+    kept = (moe_in, base_in, gates[:rows], local, pre, pre_s)
     return branch, kept
 
 
 def moe_backward(base_z, kept, w, experts_total):
-    moe_in, base_in, own_gates, local, pre, pre_s, hidden, hid_s = kept
+    moe_in, base_in, own_gates, local, pre, pre_s = kept
+    pre, pre_s, _ = fence(pre, pre_s, base_z)
     grad_z = wide(base_z)
     rows = own_gates.shape[0]
     count = len(pre)
@@ -225,13 +226,14 @@
     first = lax.axis_index(EX) * count
     lane = lax.broadcasted_iota(jnp.int32, (1, experts_total), 1)
     table = jnp.zeros((grad_z.shape[0], experts_total), f32)
-    pre_grads = []
+    pre_grads, hidden = [], []
     for e in range(count):
         p = pre[e].astype(f32)
         gate, up = p[:, :EXP_FF], p[:, EXP_FF:]
         grad_hid = nt(grad_z, w["expert_down"][e])
         share = local[:, e : e + 1]
         act = swiglu(gate, up)
+        hidden.append((act * share).astype(bf16))
         weighted = share * jnp.sum(grad_hid * act, axis=-1, keepdims=True)
         table = table + weighted * (lane == first + e).astype(f32)
         g_gate, g_up = swiglu_back(grad_hid * share, gate, up)
@@ -242,6 +244,7 @@
     half = pre_s.shape[1] // 2
     p = pre_s.astype(f32)
     grad_hid = nn(base_z, w["shared_down_t"])
+    hid_s = swiglu(p[:, :half], p[:, half:]).astype(bf16)
     g_gate, g_up = swiglu_back(grad_hid, p[:, :half], p[:, half:])
     g_pre_s = jnp.concatenate([g_gate, g_up], axis=1)
     total = add_first(total, nt(g_pre_s, w["shared_in"]))
@@ -260,21 +263,22 @@
     return back[:, :D] + nt(grad_logits, w["router"]), grad_logits
 
 
-def cat(items):
-    return jnp.concatenate(items, axis=0)
+def tn_sum(pairs, out=bf16):
+    if lax.axis_size("w") > 1:
+        return tn(*[jnp.concatenate(side, axis=0) for side in zip(*pairs)], out)
+    total = None
+    for a, b in pairs:
+        part = tn(a, b)
+        total = part if total is None else total + part
+    return total.astype(out)
 
 
 def moe_weight_grads(sides):
-    moe_in = cat([s[0] for s in sides])
-    grad_z = cat([s[1] for s in sides])
     count = len(sides[0][2])
-    g_down = jnp.stack(
-        [tn(cat([s[2][e] for s in sides]), grad_z, bf16) for e in range(count)]
-    )
-    g_in = jnp.stack([tn(moe_in, cat([s[4][e] for s in sides]), bf16) for e in range(count)])
-    base_in = cat([s[6] for s in sides])
-    g_sin = tn(base_in, cat([s[5] for s in sides]), bf16)
-    g_sdown_t = tn(cat([s[7] for s in sides]), cat([s[3] for s in sides]), bf16)
+    g_down = jnp.stack([tn_sum([(s[2][e], s[1]) for s in sides]) for e in range(count)])
+    g_in = jnp.stack([tn_sum([(s[0], s[4][e]) for s in sides]) for e in range(count)])
+    g_sin = tn_sum([(s[6], s[5]) for s in sides])
+    g_sdown_t = tn_sum([(s[7], s[3]) for s in sides])
     return g_in, g_down, g_sin, g_sdown_t
 
 
@@ -390,10 +394,14 @@
     def for_all(x):
         return jnp.broadcast_to(x[:, None], (rows, n_tp, x.shape[1]))
 
-    def columns(parts):
+    def moved_columns(parts, *after):
         packed = jnp.concatenate(parts, axis=2).transpose(1, 0, 2)
+        packed = fence(packed, *after)[0]
         moved = lax.all_to_all(packed, TP, split_axis=0, concat_axis=0, tiled=True)
-        return lax.all_gather(moved.reshape(n_tp * rows, -1), FS, axis=0, tiled=True)
+        return moved.reshape(n_tp * rows, -1)
+
+    def whole_rows(moved):
+        return lax.all_gather(moved, FS, axis=0, tiled=True)
 
     def shared_pack(w_sin, w_sdown):
         return [
@@ -403,7 +411,7 @@
         ]
 
     blank = jnp.zeros((rows, n_tp, step_width - heads - small_cols), bf16)
-    w_m = columns(
+    moved_m = moved_columns(
         [
             by_owner(w_in[:, :DI], n_tp),
             by_owner(w_in[:, DI : 2 * DI], n_tp),
@@ -413,6 +421,14 @@
             blank,
         ]
     )
+    w_m = whole_rows(moved_m)
+    moved_s = moved_columns(
+        [by_owner(w_mix_out.T, n_tp)]
+        + shared_pack(shared_in_m, shared_down_m)
+        + shared_pack(shared_in, shared_down),
+        moved_m,
+    )
+    w_s = whole_rows(moved_s)
     in_width = 2 * chan + 2 * STATE
     w_in_here = w_m[:, :in_width]
     w_step = w_m[:, in_width:]
@@ -438,11 +454,6 @@
     log_here = lax.dynamic_slice_in_dim(a_log, slot * heads, heads)
     skip_here = lax.dynamic_slice_in_dim(skip_scale, slot * heads, heads)
 
-    w_s = columns(
-        [by_owner(w_mix_out.T, n_tp)]
-        + shared_pack(shared_in_m, shared_down_m)
-        + shared_pack(shared_in, shared_down)
-    )
     w_mix_t = w_s[:, :chan]
     at = chan
 
@@ -467,6 +478,7 @@
         ],
         axis=2,
     ).transpose(1, 0, 2)
+    attn_pack, _ = fence(attn_pack, (w_m, moved_s))
     attn_pack = lax.all_to_all(attn_pack, "core", split_axis=0, concat_axis=0, tiled=True)
     attn_w = lax.all_gather(attn_pack.reshape(2 * rows, -1), "z", axis=0, tiled=True)
     attn_w = lax.all_gather(attn_w, FS, axis=0, tiled=True)
@@ -492,7 +504,8 @@
             jnp.any(routes[b, m][:, :, None] == expert_ids, axis=1).astype(bf16) for b in range(2)
         ]
         info = lanes(hot + [seg_own[:, None].astype(bf16)], info_width)
-        rows_all = gather_rows(jnp.concatenate([tokens[m], info], axis=1))
+        x_info, _ = fence(jnp.concatenate([tokens[m], info], axis=1), moved_m)
+        rows_all = gather_rows(x_info)
         x_all = rows_all[:, :D].astype(f32)
         marks = wide(rows_all[:, D : D + 2 * experts_total]) > 0.5
         masks.append([marks[:, :experts_total], marks[:, experts_total:]])
@@ -530,9 +543,11 @@
         gate_scale = lax.rsqrt((back[:, D : D + 1] + back[:, D + 1 : D + 2]) / DI + epsilon)
         mix_branch = back[:, :D] * gate_scale
         hidden_one.append(x_own[m] + mix_branch)
-        mamba_kept.append((normed_x[:length], scale_x[:length], mamba_in, pullback, gated, gained))
+        mamba_kept.append((rows_all, scale_x[:length], mamba_in, pullback, gated, gained))
         mix_kept.append((mix_branch, gate_scale))
 
+    cot_all = [gather_rows(cotangent[m]) for m in each]
+    hidden_one[-1], cot_all = fence(hidden_one[-1], cot_all)
     one_kept, layer_one = [], []
     for m in each:
         normed, scale, own = rms_forward(hidden_one[m], gain_moe_m)
@@ -545,7 +560,6 @@
         branch, kept = attn_forward(own, allowed[m], w_qkv_here, w_out_t)
         hidden_two.append(layer_one[m] + branch)
         attn_kept.append((normed, scale, kept))
-    cot_all = [gather_rows(cotangent[m]) for m in each]
     two_kept, results = [], []
     for m in each:
         normed, scale, own = rms_forward(hidden_two[m], gain_moe)
@@ -556,16 +570,18 @@
     gains = [0.0, 0.0, 0.0, 0.0]
 
     def over_dp(g):
-        return lax.psum_scatter(g, "dp", scatter_dimension=1, tiled=True).astype(f32)
-
-    def moe_stage(grads, kept_all, w, gain):
-        backs, sides = [], []
+        return lax.psum_scatter(g, "dp", scatter_dimension=1, tiled=True)
+
+    def moe_stage(grads, kept_all, w, gain, *before):
+        backs, sides, own_rows = [], [], []
         for m in each:
             back, side = moe_backward(grads[m], kept_all[m][2], w, experts_total)
             backs.append(back)
             sides.append(side)
+            own_rows.append(side[6][:length])
         weights = moe_weight_grads(sides)
-        backs[-1], weights = fence(backs[-1], weights)
+        backs[-1], weights = lax.optimization_barrier((backs[-1], weights))
+        backs[-1], before = fence(backs[-1], before)
         grad_gain = 0.0
         values, logits = [], []
         for m in each:
@@ -575,14 +591,14 @@
             grad_values, part = rms_backward(grad_in, normed, scale, gain)
             grad_gain = grad_gain + part
             values.append(grad_values)
-        g_router = tn(cat([s[6][:length] for s in sides]), cat(logits))
-        return values, weights, grad_gain, g_router
-
-    values, (g_in_a, g_down_a, g_sin_a, g_sdown_a), gains[3], g_router = moe_stage(
+        g_router = tn_sum(list(zip(own_rows, logits)), f32)
+        return values, weights, grad_gain, g_router, before
+
+    values, (g_in_a, g_down_a, g_sin_a, g_sdown_a), gains[3], g_router, _ = moe_stage(
         cot_all, two_kept, moe_a, gain_moe
     )
-    out_expert_in = over_dp(g_in_a)
-    out_expert_down = over_dp(g_down_a)
+    sum_in_a = over_dp(g_in_a)
+    sum_down_a = over_dp(g_down_a)
     grad_two = [cotangent[m].astype(f32) + values[m] for m in each]
 
     grad_layer, sides = [], []
@@ -593,13 +609,13 @@
         )
         attn_back.append(grad_in)
         sides.append(side)
-    attn_in = cat([s[0] for s in sides])
-    grad_packed = cat([s[1] for s in sides])
-    context = cat([s[2] for s in sides])
-    grad_attn = cat([s[3] for s in sides])
-    g_attn = jnp.concatenate([tn(attn_in, grad_packed, bf16), tn(grad_attn, context, bf16)], axis=1)
-    attn_back[-1], g_attn = fence(attn_back[-1], g_attn)
+    g_attn = jnp.concatenate(
+        [tn_sum([(s[0], s[1]) for s in sides]), tn_sum([(s[3], s[2]) for s in sides])], axis=1
+    )
+    attn_back[-1], g_attn = lax.optimization_barrier((attn_back[-1], g_attn))
+    attn_back[-1], sum_in_a = fence(attn_back[-1], sum_in_a)
     g_attn = lax.psum_scatter(g_attn, FS, scatter_dimension=0, tiled=True)
+    g_part = g_attn
     g_attn = lax.psum_scatter(g_attn, "z", scatter_dimension=0, tiled=True)
     g_attn = lax.all_to_all(
         g_attn.reshape(2, rows, -1), "core", split_axis=0, concat_axis=0, tiled=True
@@ -610,18 +626,28 @@
         gains[2] = gains[2] + part
         grad_layer.append(grad_two[m] + grad_values)
 
-    values, (g_in_m, g_down_m, g_sin_m, g_sdown_m), gains[1], g_router_m = moe_stage(
-        [gather_rows(g.astype(bf16)) for g in grad_layer], one_kept, moe_m, gain_moe_m
-    )
-    out_expert_in_m = over_dp(g_in_m)
-    out_expert_down_m = over_dp(g_down_m)
+    values, (g_in_m, g_down_m, g_sin_m, g_sdown_m), gains[1], g_router_m, before = moe_stage(
+        [gather_rows(g.astype(bf16)) for g in grad_layer],
+        one_kept,
+        moe_m,
+        gain_moe_m,
+        sum_down_a,
+        g_part,
+    )
+    sum_down_a = before[0]
+    sum_in_m = over_dp(g_in_m)
+    sum_down_m = over_dp(g_down_m)
     grad_one = [grad_layer[m] + values[m] for m in each]
 
     small = None
-    mamba_sides, mamba_back = [], []
+    mamba_sides, mamba_back, mixes, own_normed = [], [], [], []
     for m in each:
         mix_branch, gate_scale = mix_kept[m]
-        normed_x, scale_x, mamba_in, pullback, gated, gained = mamba_kept[m]
+        x_rows, _, mamba_in, pullback, gated, gained = mamba_kept[m]
+        x_rows, _ = fence(x_rows, grad_one[m])
+        x_rows = x_rows[:, :D].astype(f32)
+        normed_x = x_rows * row_scale(x_rows)
+        own_normed.append(normed_x[:length])
         grad_mix = grad_one[m].astype(bf16)
         mean_term = jnp.sum(grad_mix.astype(f32) * mix_branch, axis=-1, keepdims=True) / DI
         extra = lanes(split_two(gate_scale) + split_two(mean_term), 128)
@@ -630,6 +656,11 @@
         extra = rows_all[:, D:].astype(f32)
         scale_all = extra[:, 0:1] + extra[:, 1:2]
         mean_all = extra[:, 2:3] + extra[:, 3:4]
+        scaled_mix = (mix_all.astype(f32) * scale_all).astype(bf16)
+        mixes.append(scaled_mix)
+        if m == micro - 1:
+            g_mix = tn_sum([(x, k[5]) for x, k in zip(mixes, mamba_kept)])
+            mix_all, g_mix = fence(mix_all, g_mix)
         grad_gated = nn(mix_all, w_mix_t, bf16).astype(f32)
         norm_gated = gated * scale_all
         grad_gate_norm = jnp.sum(grad_gated * norm_gated, axis=0)
@@ -637,11 +668,12 @@
         pulled = pullback(grad_rows.reshape(n_tp, length, chan))
         grad_proj = pulled[0].reshape(-1, in_width).astype(bf16)
         grad_step = pulled[1].reshape(-1, heads).astype(bf16)
-        scaled_mix = (mix_all.astype(f32) * scale_all).astype(bf16)
-        mamba_sides.append((mamba_in, grad_proj, grad_step, gained, scaled_mix))
+        mamba_sides.append((mamba_in, grad_proj, grad_step))
         grads = (*pulled[2:], grad_gate_norm)
         small = grads if small is None else tuple(a + b for a, b in zip(small, grads))
-        mamba_back.append(return_rows(nt(grad_proj, w_in_here) + nt(grad_step, w_dt_here)))
+        total = nt(grad_proj, w_in_here) + nt(grad_step, w_dt_here)
+        gains[0] = gains[0] + jnp.sum(total * normed_x, axis=0)
+        mamba_back.append(return_rows(total))
 
     def rows_back(packed):
         packed = lax.psum_scatter(packed, FS, scatter_dimension=0, tiled=True)
@@ -652,23 +684,23 @@
     def owned(block):
         return block.transpose(1, 0, 2).reshape(rows, -1)
 
-    g_mix = tn(
-        cat([s[4] for s in mamba_sides]), cat([s[3] for s in mamba_sides]), bf16
-    )
     g_s = rows_back(
         jnp.concatenate([g_mix, g_sin_m, g_sdown_m, g_sin_a, g_sdown_a], axis=1)
     )
     out_mix = owned(g_s[:, :, :chan]).T
 
-    mamba_in = cat([s[0] for s in mamba_sides])
-    g_proj = tn(mamba_in, cat([s[1] for s in mamba_sides]), bf16)
-    g_step = tn(mamba_in, cat([s[2] for s in mamba_sides]), bf16)
+    g_proj = tn_sum([(s[0], s[1]) for s in mamba_sides])
+    g_step = tn_sum([(s[0], s[2]) for s in mamba_sides])
+    g_proj, sum_in_m = fence(g_proj, sum_in_m)
+    out_expert_in = sum_in_a.astype(f32)
+    out_expert_down = sum_down_a.astype(f32)
+    out_expert_in_m = sum_in_m.astype(f32)
+    out_expert_down_m = sum_down_m.astype(f32)
 
     grads_in = []
     for m in each:
-        normed_x, scale_x = mamba_kept[m][:2]
-        grad_values, part = rms_backward(mamba_back[m], normed_x, scale_x, gain_mamba)
-        gains[0] = gains[0] + part
+        scale_x = mamba_kept[m][1]
+        grad_values, _ = rms_backward(mamba_back[m], own_normed[m], scale_x, gain_mamba)
         grads_in.append(grad_one[m] + grad_values)
 
     g_taps, g_bias, g_dt, g_log, g_skip, g_gate = small

time: 2030 us -> 1820 us (0.90)
  waiting for transfers between devices: 974 us -> 877 us
  starting transfers between devices: 185 us -> 123 us
  blocking collectives: 85.4 us -> 40.3 us
    reduce_scatter x4, waiting for transfers between devices: 218 us -> 11.1 us  [over_dp(): return lax.psum_scatter(g, 'dp', scatter_dimension=1, tiled=True)]
    ppermute x36, waiting for transfers between devices: 271 us -> 370 us  [gather_rows(): parts = [x] + [lax.ppermute(x, 'z', ring(s)) for s in range(1, n)]]
    unnamed x17, waiting for transfers between devices: 69.8 us -> 2.62 us
    ppermute x36, starting transfers between devices: 100 us -> 43.8 us  [gather_rows(): parts = [x] + [lax.ppermute(x, 'z', ring(s)) for s in range(1, n)]]
    all_to_all x2 -> x1, blocking collectives: 75.5 us -> 29.4 us  [moved_columns(): moved = lax.all_to_all(packed, TP, split_axis=0, concat_axis=0, tiled=True)]
    all_gather x1, waiting for transfers between devices: 0.02 us -> 35.3 us  [body(): lax.all_gather(attn_pack.reshape(2 * rows, -1), 'z', axis=0, tiled=True)]
    reduce_scatter x1, waiting for transfers between devices: 34 us -> 0.01 us  [body(): g_attn = lax.psum_scatter(g_attn, 'z', scatter_dimension=0, tiled=True)]
    concatenate x8 -> x4, local copies, waits for them, and re-layouts: 34.4 us -> 1.22 us  [the longest x2 0.81 us: body(): x_info, _ = fence(jnp.concatenate([tokens[m], info], axis=1), moved_m)]
  transfers between devices with their start and end apart: 165 -> 166, of which waited for: 61 -> 75; matrix products, arithmetic and copies ran while one was open for 25% -> 30% of each run, Pallas kernels for 0% -> 0%
where the time goes in v1:
time: 1820 us; the launch traced here: 1810 us
  waiting for transfers between devices  877 us (48%)
  matrix products  310 us (17%)
  local copies, waits for them, and re-layouts  285 us (16%)
  other arithmetic  151 us (8%)
  starting transfers between devices  123 us (7%)
  blocking collectives  40.3 us (2%)
  between operations  20.3 us (1%)
    ppermute x36, waiting for transfers between devices, gather_rows(): parts = [x] + [lax.ppermute(x, 'z', ring(s)) for s in range(1, n)]  370 us
    ppermute x36, waiting for transfers between devices, return_rows(): out = out + lax.ppermute(part, 'z', ring(-s)).astype(f32)  368 us
    dot_general x114, matrix products, dot(): r = lax.dot_general(a, b, (dims, ((), ())), preferred_element_type=f32)  250 us
    unnamed x876, local copies, waits for them, and re-layouts  69.9 us
    concatenate x12, local copies, waits for them, and re-layouts, gather_rows(): return jnp.concatenate(parts + other, axis=0)  59.4 us
    ppermute x36, starting transfers between devices, return_rows(): out = out + lax.ppermute(part, 'z', ring(-s)).astype(f32)  49.6 us
    ppermute x36, starting transfers between devices, gather_rows(): parts = [x] + [lax.ppermute(x, 'z', ring(s)) for s in range(1, n)]  43.8 us
  transfers between devices with their start and end apart: 166, of which 75 were waited for; matrix products, arithmetic and copies ran while one was open for 30% of the time, Pallas kernels for 0%

profile of v1, /device:TPU:0, one launch (start us, length us, event | category | flops | bytes accessed | tf_op | source)
XLA Modules:
  0.0 1806.8 jit_solution(11225228415668615441)
XLA Ops:
  14.2 29.4 %all_to_all.30 = bf16[8,48,1152]{2,1,0:T(8,128)(2,1)} all-to-all(bf16[8,48,1152]{2,1,0:T(8,128)(2,1)S(1)} %copy.1190), channel_id=1, replica_groups=mesh['dp'=4,'w'=1,'z'=4,'core'=2] {'z','core'}, dimensions={0} | all-to-all | bytes 1769472 | tf_op jit(solution)/shard_map/all_to_all | solution.py:400
  50.2 22.4 %all-to-all-done.1 = bf16[8,48,1152]{2,1,0:T(8,128)(2,1)S(1)} async-done(((bf16[8,48,1152]{2,1,0:T(8,128)(2,1)}), bf16[8,48,1152]{2,1,0:T(8,128)(2,1)S(1)}, u32[]{:S(2)}, u32[]{:S(2)}) %all-to-all-start.1) | async-done | bytes 884768 | tf_op jit(solution)/shard_map/all_to_all | solution.py:400
  72.6 17.4 all-gather.9.cloned.1.call-done
  96.9 35.3 %all-gather.17.cloned.1.call-done = bf16[384,2048]{1,0:T(8,128)(2,1)} async-done(((bf16[96,2048]{1,0:T(8,128)(2,1)}), bf16[384,2048]{1,0:T(8,128)(2,1)}) %all-gather.17.cloned.1.call-update) | async-done | bytes 1572880 | tf_op jit(solution)/shard_map/all_gather | solution.py:483
  141.2 6.4 collective-permute-done.2
  147.5 26.5 %collective-permute-done.1 = bf16[64,1664]{0,1:T(8,128)(2,1)S(1)} collective-permute-done((bf16[64,1664]{0,1:T(8,128)(2,1)S(1)}, bf16[64,1664]{0,1:T(8,128)(2,1)S(1)}, u32[]{:S(2)}, u32[]{:S(2)}) %collective-permute-start.1) | collective-permute-done | bytes 213024 | tf_op jit(solution)/shard_map/ppermute | solution.py:83
  177.7 32.5 %collective-permute-done.36 = bf16[64,1664]{0,1:T(8,128)(2,1)} collective-permute-done((bf16[64,1664]{0,1:T(8,128)(2,1)S(1)}, bf16[64,1664]{0,1:T(8,128)(2,1)}, u32[]{:S(2)}, u32[]{:S(2)}) %collective-permute-start.36) | collective-permute-done | bytes 213024 | tf_op jit(solution)/shard_map/ppermute | solution.py:83
  278.8 6.2 bitcast_add_fusion.2
  289.5 6.2 bitcast_add_fusion.3
  309.0 25.9 %collective-permute-done.54 = bf16[64,1536]{0,1:T(8,128)(2,1)} collective-permute-done((bf16[64,1536]{0,1:T(8,128)(2,1)}, bf16[64,1536]{0,1:T(8,128)(2,1)}, u32[]{:S(2)}, u32[]{:S(2)}) %collective-permute-start.54) | collective-permute-done | bytes 196640 | tf_op jit(solution)/shard_map/ppermute | solution.py:83
  340.7 10.2 concatenate.182
  369.5 19.5 %collective-permute-done.8 = bf16[64,1664]{0,1:T(8,128)(2,1)S(1)} collective-permute-done((bf16[64,1664]{0,1:T(8,128)(2,1)S(1)}, bf16[64,1664]{0,1:T(8,128)(2,1)S(1)}, u32[]{:S(2)}, u32[]{:S(2)}) %collective-permute-start.8) | collective-permute-done | bytes 213024 | tf_op jit(solution)/shard_map/ppermute | solution.py:97
  389.0 15.7 collective-permute-done.9
  410.1 8.8 collective-permute-done.13
  419.0 23.4 %collective-permute-done.12 = bf16[64,1536]{0,1:T(8,128)(2,1)S(1)} collective-permute-done((bf16[64,1536]{0,1:T(8,128)(2,1)S(1)}, bf16[64,1536]{0,1:T(8,128)(2,1)S(1)}, u32[]{:S(2)}, u32[]{:S(2)}) %collective-permute-start.12) | collective-permute-done | bytes 196640 | tf_op jit(solution)/shard_map/ppermute | solution.py:83
  477.2 10.0 concatenate.189
  502.5 11.6 collective-permute-done.21
  514.1 15.0 collective-permute-done.20
  544.2 9.6 collective-permute-done.43
  553.8 15.0 collective-permute-done.44
  576.6 8.4 collective-permute-done.26
  585.0 23.1 %collective-permute-done.25 = bf16[64,1536]{0,1:T(8,128)(2,1)S(1)} collective-permute-done((bf16[64,1536]{0,1:T(8,128)(2,1)S(1)}, bf16[64,1536]{0,1:T(8,128)(2,1)S(1)}, u32[]{:S(2)}, u32[]{:S(2)}) %collective-permute-start.25) | collective-permute-done | bytes 196640 | tf_op jit(solution)/shard_map/ppermute | solution.py:83
  665.7 12.6 collective-permute-done.87
  678.4 16.6 collective-permute-done.86
  723.7 17.6 collective-permute-done.32
  741.2 13.4 collective-permute-done.33
  762.5 8.9 collective-permute-done.92
  771.4 23.4 %collective-permute-done.91 = bf16[64,1536]{0,1:T(8,128)(2,1)S(1)} collective-permute-done((bf16[64,1536]{0,1:T(8,128)(2,1)S(1)}, bf16[64,1536]{0,1:T(8,128)(2,1)S(1)}, u32[]{:S(2)}, u32[]{:S(2)}) %collective-permute-start.91) | collective-permute-done | bytes 196640 | tf_op jit(solution)/shard_map/ppermute | solution.py:83
  797.2 5.5 concatenate.201
  828.6 7.0 collective-permute-done.98
  835.5 12.3 collective-permute-done.100
  847.8 16.4 collective-permute-done.99
  871.1 10.4 collective-permute-done.62
  881.5 21.5 %collective-permute-done.61 = bf16[64,1536]{0,1:T(8,128)(2,1)S(1)} collective-permute-done((bf16[64,1536]{0,1:T(8,128)(2,1)S(1)}, bf16[64,1536]{0,1:T(8,128)(2,1)S(1)}, u32[]{:S(2)}, u32[]{:S(2)}) %collective-permute-start.61) | collective-permute-done | bytes 196640 | tf_op jit(solution)/shard_map/ppermute | solution.py:83
  934.4 6.1 collective-permute-done.68
  940.5 11.8 collective-permute-done.70
  952.3 15.0 collective-permute-done.69
  988.0 10.4 collective-permute-done.75
  998.4 21.8 %collective-permute-done.74 = bf16[64,1536]{0,1:T(8,128)(2,1)S(1)} collective-permute-done((bf16[64,1536]{0,1:T(8,128)(2,1)S(1)}, bf16[64,1536]{0,1:T(8,128)(2,1)S(1)}, u32[]{:S(2)}, u32[]{:S(2)}) %collective-permute-start.74) | collective-permute-done | bytes 196640 | tf_op jit(solution)/shard_map/ppermute | solution.py:83
  1080.8 6.5 pad_maximum_fusion
  1101.8 12.4 collective-permute-done.115
  1114.3 16.2 collective-permute-done.114
  1164.5 8.8 copy.1446
  1188.3 11.1 reduce-scatter.13.cloned.1.call-done
  1206.9 14.4 collective-permute-done.82
  1228.7 9.0 collective-permute-done.120
  1237.7 23.0 %collective-permute-done.119 = bf16[64,1536]{0,1:T(8,128)(2,1)} collective-permute-done((bf16[64,1536]{0,1:T(8,128)(2,1)S(1)}, bf16[64,1536]{0,1:T(8,128)(2,1)}, u32[]{:S(2)}, u32[]{:S(2)}) %collective-permute-start.119) | collective-permute-done | bytes 196640 | tf_op jit(solution)/shard_map/ppermute | solution.py:83
  1311.0 6.3 pad_maximum_fusion.2
  1325.5 5.6 collective-permute-done.126
  1331.2 12.3 collective-permute-done.128
  1343.4 16.2 collective-permute-done.127
  1367.3 10.2 collective-permute-done.103
  1377.6 23.7 %collective-permute-done.102 = bf16[64,1664]{0,1:T(8,128)(2,1)S(1)} collective-permute-done((bf16[64,1664]{0,1:T(8,128)(2,1)S(1)}, bf16[64,1664]{0,1:T(8,128)(2,1)S(1)}, u32[]{:S(2)}, u32[]{:S(2)}) %collective-permute-start.102) | collective-permute-done | bytes 213024 | tf_op jit(solution)/shard_map/ppermute | solution.py:83
  1433.4 6.3 fusion.205
  1471.2 14.9 collective-permute-done.131
  1486.1 37.6 %collective-permute-done.130 = bf16[64,1664]{0,1:T(8,128)(2,1)} collective-permute-done((bf16[64,1664]{0,1:T(8,128)(2,1)}, bf16[64,1664]{0,1:T(8,128)(2,1)}, u32[]{:S(2)}, u32[]{:S(2)}) %collective-permute-start.130) | collective-permute-done | bytes 213024 | tf_op jit(solution)/shard_map/ppermute | solution.py:83
  1552.9 6.3 fusion.207
  1614.1 7.9 concatenate.224
  1681.9 15.8 collective-permute-done.110
  1697.6 9.6 collective-permute-done.139
  1707.2 23.0 %collective-permute-done.138 = bf16[64,1536]{0,1:T(8,128)(2,1)} collective-permute-done((bf16[64,1536]{0,1:T(8,128)(2,1)}, bf16[64,1536]{0,1:T(8,128)(2,1)}, u32[]{:S(2)}, u32[]{:S(2)}) %collective-permute-start.138) | collective-permute-done | bytes 196640 | tf_op jit(solution)/shard_map/ppermute | solution.py:97
  1733.5 6.1 all_to_all.32
  1750.9 16.1 all-to-all-done.4
  1781.2 12.3 all-to-all-done.3
  (1747 shorter events, 846.0 us)
Async XLA Ops:
  7.2 82.7 %all-gather.9.cloned.1.call-start = ((), (), s32[]{:S(2)}) async-start(), calls=%async_computation.14 | async-start | bytes 4423680 | tf_op jit(solution)/shard_map/all_gather | solution.py:404
  49.6 82.5 %all-gather.17.cloned.1.call-start = ((), (), s32[]{:S(2)}) async-start(), calls=%async_computation.18 | async-start | bytes 1966080 | tf_op jit(solution)/shard_map/all_gather | solution.py:483
  94.9 241.0 %all-gather.11.cloned.1.call-start = ((), (), s32[]{:S(2)}) async-start(), calls=%async_computation.15 | async-start | bytes 4423680 | tf_op jit(solution)/shard_map/all_gather | solution.py:404
  95.6 358.3 %all-gather.13.cloned.1.call-start = ((), (), s32[]{:S(2)}) async-start(), calls=%async_computation.16 | async-start | bytes 7864320 | tf_op jit(solution)/shard_map/all_gather | solution.py:464
  96.2 366.7 %all-gather.15.cloned.1.call-start = ((), (), s32[]{:S(2)}) async-start(), calls=%async_computation.17 | async-start | bytes 3932160 | tf_op jit(solution)/shard_map/all_gather | solution.py:465
  96.8 436.2 %all-gather.19.cloned.1.call-start = ((), (), s32[]{:S(2)}) async-start(), calls=%async_computation.19 | async-start | bytes 7864320 | tf_op jit(solution)/shard_map/all_gather | solution.py:484
  132.2 486.4 %all-gather.21.cloned.1.call-start = ((), (), s32[]{:S(2)}) async-start(), calls=%async_computation.20 | async-start | bytes 7864320 | tf_op jit(solution)/shard_map/all_gather | solution.py:492
  132.9 499.6 %all-gather.23.cloned.1.call-start = ((), (), s32[]{:S(2)}) async-start(), calls=%async_computation.21 | async-start | bytes 3932160 | tf_op jit(solution)/shard_map/all_gather | solution.py:493
  135.4 38.7 %collective-permute-start.1 = (bf16[64,1664]{0,1:T(8,128)(2,1)S(1)}, bf16[64,1664]{0,1:T(8,128)(2,1)S(1)}, u32[]{:S(2)}, u32[]{:S(2)}) collective-permute-start(bf16[64,1664]{0,1:T(8,128)(2,1)S(1)} %concatenate.179), channel_id=1, source_target_pairs={{0,4},{2,6},{4,0},{6,2},{1,5},{3,7},{5,1},{7,3},{8,12},{10,14},{12... | collective-permute-start | bytes 638984 | tf_op jit(solution)/shard_map/ppermute | solution.py:83
  136.0 38.1 %collective-permute-start = (bf16[64,1664]{0,1:T(8,128)(2,1)S(1)}, bf16[64,1664]{0,1:T(8,128)(2,1)}, u32[]{:S(2)}, u32[]{:S(2)}) collective-permute-start(bf16[64,1664]{0,1:T(8,128)(2,1)S(1)} %concatenate.179), channel_id=1, source_target_pairs={{0,2},{2,4},{4,6},{6,0},{1,3},{3,5},{5,7},{7,1},{8,10},{10,12},{12... | collective-permute-start | bytes 638984 | tf_op jit(solution)/shard_map/ppermute | solution.py:83
  138.1 36.5 %collective-permute-start.37 = (bf16[64,1664]{0,1:T(8,128)(2,1)S(1)}, bf16[64,1664]{0,1:T(8,128)(2,1)}, u32[]{:S(2)}, u32[]{:S(2)}) collective-permute-start(bf16[64,1664]{0,1:T(8,128)(2,1)S(1)} %concatenate.187), channel_id=1, source_target_pairs={{0,6},{2,0},{4,2},{6,4},{1,7},{3,1},{5,3},{7,5},{8,14},{10,8},{12,... | collective-permute-start | bytes 638984 | tf_op jit(solution)/shard_map/ppermute | solution.py:83
  140.6 69.6 %collective-permute-start.36 = (bf16[64,1664]{0,1:T(8,128)(2,1)S(1)}, bf16[64,1664]{0,1:T(8,128)(2,1)}, u32[]{:S(2)}, u32[]{:S(2)}) collective-permute-start(bf16[64,1664]{0,1:T(8,128)(2,1)S(1)} %concatenate.187), channel_id=1, source_target_pairs={{0,4},{2,6},{4,0},{6,2},{1,5},{3,7},{5,1},{7,3},{8,12},{10,14},{12... | collective-permute-start | bytes 638984 | tf_op jit(solution)/shard_map/ppermute | solution.py:83
  147.5 62.7 %collective-permute-start.35 = (bf16[64,1664]{0,1:T(8,128)(2,1)S(1)}, bf16[64,1664]{0,1:T(8,128)(2,1)}, u32[]{:S(2)}, u32[]{:S(2)}) collective-permute-start(bf16[64,1664]{0,1:T(8,128)(2,1)S(1)} %concatenate.187), channel_id=1, source_target_pairs={{0,2},{2,4},{4,6},{6,0},{1,3},{3,5},{5,7},{7,1},{8,10},{10,12},{12... | collective-permute-start | bytes 638984 | tf_op jit(solution)/shard_map/ppermute | solution.py:83
  174.1 36.6 %collective-permute-start.6 = (bf16[64,1664]{0,1:T(8,128)(2,1)S(1)}, bf16[64,1664]{0,1:T(8,128)(2,1)}, u32[]{:S(2)}, u32[]{:S(2)}) collective-permute-start(bf16[64,1664]{0,1:T(8,128)(2,1)S(1)} %collective-permute-done.2), channel_id=1, source_target_pairs={{0,1},{1,0},{2,3},{3,2},{4,5},{5,4},{6,7},{7,6},{8,9},{9,8},{10,11... | collective-permute-start | bytes 638984 | tf_op jit(solution)/shard_map/ppermute | solution.py:84
  174.1 36.7 %collective-permute-start.5 = (bf16[64,1664]{0,1:T(8,128)(2,1)S(1)}, bf16[64,1664]{0,1:T(8,128)(2,1)}, u32[]{:S(2)}, u32[]{:S(2)}) collective-permute-start(bf16[64,1664]{0,1:T(8,128)(2,1)S(1)} %collective-permute-done.1), channel_id=1, source_target_pairs={{0,1},{1,0},{2,3},{3,2},{4,5},{5,4},{6,7},{7,6},{8,9},{9,8},{10,11... | collective-permute-start | bytes 638984 | tf_op jit(solution)/shard_map/ppermute | solution.py:84
  174.6 37.2 %collective-permute-start.4 = (bf16[64,1664]{0,1:T(8,128)(2,1)}, bf16[64,1664]{0,1:T(8,128)(2,1)}, u32[]{:S(2)}, u32[]{:S(2)}) collective-permute-start(bf16[64,1664]{0,1:T(8,128)(2,1)} %collective-permute-done), channel_id=1, source_target_pairs={{0,1},{1,0},{2,3},{3,2},{4,5},{5,4},{6,7},{7,6},{8,9},{9,8},{10,11... | collective-permute-start | bytes 638984 | tf_op jit(solution)/shard_map/ppermute | solution.py:84
  211.8 95.8 %collective-permute-start.49 = (bf16[64,1536]{0,1:T(8,128)(2,1)}, bf16[64,1536]{0,1:T(8,128)(2,1)}, u32[]{:S(2)}, u32[]{:S(2)}) collective-permute-start(bf16[64,1536]{0,1:T(8,128)(2,1)} %bitcast.57), channel_id=1, source_target_pairs={{0,1},{1,0},{2,3},{3,2},{4,5},{5,4},{6,7},{7,6},{8,9},{9,8},{10,11... | collective-permute-start | bytes 589832 | tf_op jit(solution)/shard_map/ppermute | solution.py:84
  217.0 90.7 %collective-permute-start.48 = (bf16[64,1536]{0,1:T(8,128)(2,1)}, bf16[64,1536]{0,1:T(8,128)(2,1)}, u32[]{:S(2)}, u32[]{:S(2)}) collective-permute-start(bf16[64,1536]{0,1:T(8,128)(2,1)} %bitcast.57), channel_id=1, source_target_pairs={{0,6},{2,0},{4,2},{6,4},{1,7},{3,1},{5,3},{7,5},{8,14},{10,8},{12,... | collective-permute-start | bytes 589832 | tf_op jit(solution)/shard_map/ppermute | solution.py:83
  217.0 91.4 %collective-permute-start.47 = (bf16[64,1536]{0,1:T(8,128)(2,1)}, bf16[64,1536]{0,1:T(8,128)(2,1)}, u32[]{:S(2)}, u32[]{:S(2)}) collective-permute-start(bf16[64,1536]{0,1:T(8,128)(2,1)} %bitcast.57), channel_id=1, source_target_pairs={{0,4},{2,6},{4,0},{6,2},{1,5},{3,7},{5,1},{7,3},{8,12},{10,14},{12... | collective-permute-start | bytes 589832 | tf_op jit(solution)/shard_map/ppermute | solution.py:83
  219.0 89.3 %collective-permute-start.46 = (bf16[64,1536]{0,1:T(8,128)(2,1)}, bf16[64,1536]{0,1:T(8,128)(2,1)}, u32[]{:S(2)}, u32[]{:S(2)}) collective-permute-start(bf16[64,1536]{0,1:T(8,128)(2,1)} %bitcast.57), channel_id=1, source_target_pairs={{0,2},{2,4},{4,6},{6,0},{1,3},{3,5},{5,7},{7,1},{8,10},{10,12},{12... | collective-permute-start | bytes 589832 | tf_op jit(solution)/shard_map/ppermute | solution.py:83
  221.0 87.9 %collective-permute-start.55 = (bf16[64,1536]{0,1:T(8,128)(2,1)}, bf16[64,1536]{0,1:T(8,128)(2,1)}, u32[]{:S(2)}, u32[]{:S(2)}) collective-permute-start(bf16[64,1536]{0,1:T(8,128)(2,1)} %bitcast.58), channel_id=1, source_target_pairs={{0,6},{2,0},{4,2},{6,4},{1,7},{3,1},{5,3},{7,5},{8,14},{10,8},{12,... | collective-permute-start | bytes 589832 | tf_op jit(solution)/shard_map/ppermute | solution.py:83
  308.9 50.0 %collective-permute-start.56 = (bf16[64,1536]{0,1:T(8,128)(2,1)}, bf16[64,1536]{0,1:T(8,128)(2,1)}, u32[]{:S(2)}, u32[]{:S(2)}) collective-permute-start(bf16[64,1536]{0,1:T(8,128)(2,1)} %bitcast.58), channel_id=1, source_target_pairs={{0,1},{1,0},{2,3},{3,2},{4,5},{5,4},{6,7},{7,6},{8,9},{9,8},{10,11... | collective-permute-start | bytes 589832 | tf_op jit(solution)/shard_map/ppermute | solution.py:84
  353.5 845.9 %reduce-scatter.13.cloned.1.call-start = ((), (), s32[]{:S(2)}) async-start(), calls=%async_computation.22 | async-start | bytes 7864320 | tf_op jit(solution)/shard_map/reduce_scatter | solution.py:573
  368.6 36.1 %collective-permute-start.9 = (bf16[64,1664]{0,1:T(8,128)(2,1)S(1)}, bf16[64,1664]{0,1:T(8,128)(2,1)S(1)}, u32[]{:S(2)}, u32[]{:S(2)}) collective-permute-start(bf16[64,1664]{0,1:T(8,128)(2,1)S(1)} %get-tuple-element.511), channel_id=1, source_target_pairs={{0,4},{2,6},{4,0},{6,2},{1,5},{3,7},{5,1},{7,3},{8,12},{10,14},{12... | collective-permute-start | bytes 638984 | tf_op jit(solution)/shard_map/ppermute | solution.py:97
  409.4 33.0 %collective-permute-start.12 = (bf16[64,1536]{0,1:T(8,128)(2,1)S(1)}, bf16[64,1536]{0,1:T(8,128)(2,1)S(1)}, u32[]{:S(2)}, u32[]{:S(2)}) collective-permute-start(bf16[64,1536]{0,1:T(8,128)(2,1)S(1)} %multiply_convert_fusion.33), channel_id=1, source_target_pairs={{0,4},{2,6},{4,0},{6,2},{1,5},{3,7},{5,1},{7,3},{8,12},{10,14},{12... | collective-permute-start | bytes 589832 | tf_op jit(solution)/shard_map/ppermute | solution.py:83
  409.4 33.0 %collective-permute-start.11 = (bf16[64,1536]{0,1:T(8,128)(2,1)S(1)}, bf16[64,1536]{0,1:T(8,128)(2,1)S(1)}, u32[]{:S(2)}, u32[]{:S(2)}) collective-permute-start(bf16[64,1536]{0,1:T(8,128)(2,1)S(1)} %multiply_convert_fusion.33), channel_id=1, source_target_pairs={{0,2},{2,4},{4,6},{6,0},{1,3},{3,5},{5,7},{7,1},{8,10},{10,12},{12... | collective-permute-start | bytes 589832 | tf_op jit(solution)/shard_map/ppermute | solution.py:83
  410.1 32.9 %collective-permute-start.14 = (bf16[64,1536]{0,1:T(8,128)(2,1)S(1)}, bf16[64,1536]{0,1:T(8,128)(2,1)S(1)}, u32[]{:S(2)}, u32[]{:S(2)}) collective-permute-start(bf16[64,1536]{0,1:T(8,128)(2,1)S(1)} %multiply_convert_fusion.33), channel_id=1, source_target_pairs={{0,1},{1,0},{2,3},{3,2},{4,5},{5,4},{6,7},{7,6},{8,9},{9,8},{10,11... | collective-permute-start | bytes 589832 | tf_op jit(solution)/shard_map/ppermute | solution.py:84
  493.3 35.8 %collective-permute-start.20 = (bf16[64,1536]{0,1:T(8,128)(2,1)S(1)}, bf16[64,1536]{0,1:T(8,128)(2,1)S(1)}, u32[]{:S(2)}, u32[]{:S(2)}) collective-permute-start(bf16[64,1536]{0,1:T(8,128)(2,1)S(1)} %get-tuple-element.540), channel_id=1, source_target_pairs={{0,4},{2,6},{4,0},{6,2},{1,5},{3,7},{5,1},{7,3},{8,12},{10,14},{12... | collective-permute-start | bytes 589832 | tf_op jit(solution)/shard_map/ppermute | solution.py:97
  533.0 35.7 %collective-permute-start.44 = (bf16[64,1664]{0,1:T(8,128)(2,1)S(1)}, bf16[64,1664]{0,1:T(8,128)(2,1)}, u32[]{:S(2)}, u32[]{:S(2)}) collective-permute-start(bf16[64,1664]{0,1:T(8,128)(2,1)S(1)} %get-tuple-element.514), channel_id=1, source_target_pairs={{0,4},{2,6},{4,0},{6,2},{1,5},{3,7},{5,1},{7,3},{8,12},{10,14},{12... | collective-permute-start | bytes 638984 | tf_op jit(solution)/shard_map/ppermute | solution.py:97
  575.4 32.7 %collective-permute-start.25 = (bf16[64,1536]{0,1:T(8,128)(2,1)S(1)}, bf16[64,1536]{0,1:T(8,128)(2,1)S(1)}, u32[]{:S(2)}, u32[]{:S(2)}) collective-permute-start(bf16[64,1536]{0,1:T(8,128)(2,1)S(1)} %multiply_convert_fusion.31), channel_id=1, source_target_pairs={{0,4},{2,6},{4,0},{6,2},{1,5},{3,7},{5,1},{7,3},{8,12},{10,14},{12... | collective-permute-start | bytes 589832 | tf_op jit(solution)/shard_map/ppermute | solution.py:83
  575.4 32.7 %collective-permute-start.24 = (bf16[64,1536]{0,1:T(8,128)(2,1)S(1)}, bf16[64,1536]{0,1:T(8,128)(2,1)S(1)}, u32[]{:S(2)}, u32[]{:S(2)}) collective-permute-start(bf16[64,1536]{0,1:T(8,128)(2,1)S(1)} %multiply_convert_fusion.31), channel_id=1, source_target_pairs={{0,2},{2,4},{4,6},{6,0},{1,3},{3,5},{5,7},{7,1},{8,10},{10,12},{12... | collective-permute-start | bytes 589832 | tf_op jit(solution)/shard_map/ppermute | solution.py:83
  576.6 33.0 %collective-permute-start.27 = (bf16[64,1536]{0,1:T(8,128)(2,1)S(1)}, bf16[64,1536]{0,1:T(8,128)(2,1)S(1)}, u32[]{:S(2)}, u32[]{:S(2)}) collective-permute-start(bf16[64,1536]{0,1:T(8,128)(2,1)S(1)} %multiply_convert_fusion.31), channel_id=1, source_target_pairs={{0,1},{1,0},{2,3},{3,2},{4,5},{5,4},{6,7},{7,6},{8,9},{9,8},{10,11... | collective-permute-start | bytes 589832 | tf_op jit(solution)/shard_map/ppermute | solution.py:84
  656.0 38.9 %collective-permute-start.86 = (bf16[64,1664]{0,1:T(8,128)(2,1)S(1)}, bf16[64,1664]{0,1:T(8,128)(2,1)S(1)}, u32[]{:S(2)}, u32[]{:S(2)}) collective-permute-start(bf16[64,1664]{0,1:T(8,128)(2,1)S(1)} %get-tuple-element.505), channel_id=1, source_target_pairs={{0,4},{2,6},{4,0},{6,2},{1,5},{3,7},{5,1},{7,3},{8,12},{10,14},{12... | collective-permute-start | bytes 638984 | tf_op jit(solution)/shard_map/ppermute | solution.py:97
  660.9 38.4 %collective-permute-start.31 = (bf16[256,1536]{0,1:T(8,128)(2,1)S(1)}, bf16[256,1536]{0,1:T(8,128)(2,1)S(1)}, u32[]{:S(2)}, u32[]{:S(2)}) collective-permute-start(bf16[256,1536]{0,1:T(8,128)(2,1)S(1)} %slice.2424), channel_id=1, source_target_pairs={{0,1},{1,0},{2,3},{3,2},{4,5},{5,4},{6,7},{7,6},{8,9},{9,8},{10,11... | collective-permute-start | bytes 2359304 | tf_op jit(solution)/shard_map/ppermute | solution.py:92
  761.8 32.9 %collective-permute-start.91 = (bf16[64,1536]{0,1:T(8,128)(2,1)S(1)}, bf16[64,1536]{0,1:T(8,128)(2,1)S(1)}, u32[]{:S(2)}, u32[]{:S(2)}) collective-permute-start(bf16[64,1536]{0,1:T(8,128)(2,1)S(1)} %get-tuple-element.405), channel_id=1, source_target_pairs={{0,4},{2,6},{4,0},{6,2},{1,5},{3,7},{5,1},{7,3},{8,12},{10,14},{12... | collective-permute-start | bytes 589832 | tf_op jit(solution)/shard_map/ppermute | solution.py:83
  761.8 32.9 %collective-permute-start.90 = (bf16[64,1536]{0,1:T(8,128)(2,1)S(1)}, bf16[64,1536]{0,1:T(8,128)(2,1)S(1)}, u32[]{:S(2)}, u32[]{:S(2)}) collective-permute-start(bf16[64,1536]{0,1:T(8,128)(2,1)S(1)} %get-tuple-element.405), channel_id=1, source_target_pairs={{0,2},{2,4},{4,6},{6,0},{1,3},{3,5},{5,7},{7,1},{8,10},{10,12},{12... | collective-permute-start | bytes 589832 | tf_op jit(solution)/shard_map/ppermute | solution.py:83
  762.5 32.8 %collective-permute-start.93 = (bf16[64,1536]{0,1:T(8,128)(2,1)S(1)}, bf16[64,1536]{0,1:T(8,128)(2,1)S(1)}, u32[]{:S(2)}, u32[]{:S(2)}) collective-permute-start(bf16[64,1536]{0,1:T(8,128)(2,1)S(1)} %get-tuple-element.405), channel_id=1, source_target_pairs={{0,1},{1,0},{2,3},{3,2},{4,5},{5,4},{6,7},{7,6},{8,9},{9,8},{10,11... | collective-permute-start | bytes 589832 | tf_op jit(solution)/shard_map/ppermute | solution.py:84
  825.7 38.5 %collective-permute-start.99 = (bf16[64,1664]{0,1:T(8,128)(2,1)S(1)}, bf16[64,1664]{0,1:T(8,128)(2,1)S(1)}, u32[]{:S(2)}, u32[]{:S(2)}) collective-permute-start(bf16[64,1664]{0,1:T(8,128)(2,1)S(1)} %get-tuple-element.499), channel_id=1, source_target_pairs={{0,4},{2,6},{4,0},{6,2},{1,5},{3,7},{5,1},{7,3},{8,12},{10,14},{12... | collective-permute-start | bytes 638984 | tf_op jit(solution)/shard_map/ppermute | solution.py:97
  869.9 33.1 %collective-permute-start.61 = (bf16[64,1536]{0,1:T(8,128)(2,1)S(1)}, bf16[64,1536]{0,1:T(8,128)(2,1)S(1)}, u32[]{:S(2)}, u32[]{:S(2)}) collective-permute-start(bf16[64,1536]{0,1:T(8,128)(2,1)S(1)} %get-tuple-element.599), channel_id=1, source_target_pairs={{0,4},{2,6},{4,0},{6,2},{1,5},{3,7},{5,1},{7,3},{8,12},{10,14},{12... | collective-permute-start | bytes 589832 | tf_op jit(solution)/shard_map/ppermute | solution.py:83
  869.9 33.1 %collective-permute-start.60 = (bf16[64,1536]{0,1:T(8,128)(2,1)S(1)}, bf16[64,1536]{0,1:T(8,128)(2,1)S(1)}, u32[]{:S(2)}, u32[]{:S(2)}) collective-permute-start(bf16[64,1536]{0,1:T(8,128)(2,1)S(1)} %get-tuple-element.599), channel_id=1, source_target_pairs={{0,2},{2,4},{4,6},{6,0},{1,3},{3,5},{5,7},{7,1},{8,10},{10,12},{12... | collective-permute-start | bytes 589832 | tf_op jit(solution)/shard_map/ppermute | solution.py:83
  931.4 35.9 %collective-permute-start.69 = (bf16[64,1536]{0,1:T(8,128)(2,1)S(1)}, bf16[64,1536]{0,1:T(8,128)(2,1)S(1)}, u32[]{:S(2)}, u32[]{:S(2)}) collective-permute-start(bf16[64,1536]{0,1:T(8,128)(2,1)S(1)} %get-tuple-element.546), channel_id=1, source_target_pairs={{0,4},{2,6},{4,0},{6,2},{1,5},{3,7},{5,1},{7,3},{8,12},{10,14},{12... | collective-permute-start | bytes 589832 | tf_op jit(solution)/shard_map/ppermute | solution.py:97
  986.5 33.7 %collective-permute-start.74 = (bf16[64,1536]{0,1:T(8,128)(2,1)S(1)}, bf16[64,1536]{0,1:T(8,128)(2,1)S(1)}, u32[]{:S(2)}, u32[]{:S(2)}) collective-permute-start(bf16[64,1536]{0,1:T(8,128)(2,1)S(1)} %multiply_convert_fusion.28), channel_id=1, source_target_pairs={{0,4},{2,6},{4,0},{6,2},{1,5},{3,7},{5,1},{7,3},{8,12},{10,14},{12... | collective-permute-start | bytes 589832 | tf_op jit(solution)/shard_map/ppermute | solution.py:83
  986.5 33.7 %collective-permute-start.73 = (bf16[64,1536]{0,1:T(8,128)(2,1)S(1)}, bf16[64,1536]{0,1:T(8,128)(2,1)S(1)}, u32[]{:S(2)}, u32[]{:S(2)}) collective-permute-start(bf16[64,1536]{0,1:T(8,128)(2,1)S(1)} %multiply_convert_fusion.28), channel_id=1, source_target_pairs={{0,2},{2,4},{4,6},{6,0},{1,3},{3,5},{5,7},{7,1},{8,10},{10,12},{12... | collective-permute-start | bytes 589832 | tf_op jit(solution)/shard_map/ppermute | solution.py:83
  988.0 32.7 %collective-permute-start.76 = (bf16[64,1536]{0,1:T(8,128)(2,1)S(1)}, bf16[64,1536]{0,1:T(8,128)(2,1)S(1)}, u32[]{:S(2)}, u32[]{:S(2)}) collective-permute-start(bf16[64,1536]{0,1:T(8,128)(2,1)S(1)} %multiply_convert_fusion.28), channel_id=1, source_target_pairs={{0,1},{1,0},{2,3},{3,2},{4,5},{5,4},{6,7},{7,6},{8,9},{9,8},{10,11... | collective-permute-start | bytes 589832 | tf_op jit(solution)/shard_map/ppermute | solution.py:84
  1091.8 38.7 %collective-permute-start.114 = (bf16[64,1664]{0,1:T(8,128)(2,1)S(1)}, bf16[64,1664]{0,1:T(8,128)(2,1)S(1)}, u32[]{:S(2)}, u32[]{:S(2)}) collective-permute-start(bf16[64,1664]{0,1:T(8,128)(2,1)S(1)} %get-tuple-element.508), channel_id=1, source_target_pairs={{0,4},{2,6},{4,0},{6,2},{1,5},{3,7},{5,1},{7,3},{8,12},{10,14},{12... | collective-permute-start | bytes 638984 | tf_op jit(solution)/shard_map/ppermute | solution.py:97
  1130.7 320.3 %reduce-scatter.25.cloned.1.call-start = ((), (), s32[]{:S(2)}) async-start(), calls=%async_computation.28 | async-start | bytes 7864320
  1173.3 278.0 %reduce-scatter.15.cloned.1.call-start = ((), (), s32[]{:S(2)}) async-start(), calls=%async_computation.23 | async-start | bytes 3932160 | tf_op jit(solution)/shard_map/reduce_scatter | solution.py:573
  1187.7 33.6 %collective-permute-start.82 = (bf16[64,1536]{0,1:T(8,128)(2,1)S(1)}, bf16[64,1536]{0,1:T(8,128)(2,1)}, u32[]{:S(2)}, u32[]{:S(2)}) collective-permute-start(bf16[64,1536]{0,1:T(8,128)(2,1)S(1)} %get-tuple-element.543), channel_id=1, source_target_pairs={{0,4},{2,6},{4,0},{6,2},{1,5},{3,7},{5,1},{7,3},{8,12},{10,14},{12... | collective-permute-start | bytes 589832 | tf_op jit(solution)/shard_map/ppermute | solution.py:97
  1261.2 352.1 %reduce-scatter.17.cloned.1.call-start = ((), (), s32[]{:S(2)}) async-start(), calls=%async_computation.24 | async-start | bytes 7864320 | tf_op jit(solution)/shard_map/reduce_scatter | solution.py:573
  1321.3 38.3 %collective-permute-start.127 = (bf16[64,1664]{0,1:T(8,128)(2,1)S(1)}, bf16[64,1664]{0,1:T(8,128)(2,1)S(1)}, u32[]{:S(2)}, u32[]{:S(2)}) collective-permute-start(bf16[64,1664]{0,1:T(8,128)(2,1)S(1)} %get-tuple-element.502), channel_id=1, source_target_pairs={{0,4},{2,6},{4,0},{6,2},{1,5},{3,7},{5,1},{7,3},{8,12},{10,14},{12... | collective-permute-start | bytes 638984 | tf_op jit(solution)/shard_map/ppermute | solution.py:97
  1360.8 372.7 %reduce-scatter.27.cloned.1.call-start = ((), (), s32[]{:S(2)}) async-start(), calls=%async_computation.29 | async-start | bytes 1966080 | tf_op jit(solution)/shard_map/reduce_scatter | solution.py:619
  1363.8 38.6 %collective-permute-start.104 = (bf16[64,1664]{0,1:T(8,128)(2,1)S(1)}, bf16[64,1664]{0,1:T(8,128)(2,1)S(1)}, u32[]{:S(2)}, u32[]{:S(2)}) collective-permute-start(bf16[64,1664]{0,1:T(8,128)(2,1)S(1)} %concatenate.206), channel_id=1, source_target_pairs={{0,1},{1,0},{2,3},{3,2},{4,5},{5,4},{6,7},{7,6},{8,9},{9,8},{10,11... | collective-permute-start | bytes 638984 | tf_op jit(solution)/shard_map/ppermute | solution.py:84
  1365.0 36.4 %collective-permute-start.102 = (bf16[64,1664]{0,1:T(8,128)(2,1)S(1)}, bf16[64,1664]{0,1:T(8,128)(2,1)S(1)}, u32[]{:S(2)}, u32[]{:S(2)}) collective-permute-start(bf16[64,1664]{0,1:T(8,128)(2,1)S(1)} %concatenate.206), channel_id=1, source_target_pairs={{0,4},{2,6},{4,0},{6,2},{1,5},{3,7},{5,1},{7,3},{8,12},{10,14},{12... | collective-permute-start | bytes 638984 | tf_op jit(solution)/shard_map/ppermute | solution.py:83
  1365.0 36.4 %collective-permute-start.101 = (bf16[64,1664]{0,1:T(8,128)(2,1)S(1)}, bf16[64,1664]{0,1:T(8,128)(2,1)S(1)}, u32[]{:S(2)}, u32[]{:S(2)}) collective-permute-start(bf16[64,1664]{0,1:T(8,128)(2,1)S(1)} %concatenate.206), channel_id=1, source_target_pairs={{0,2},{2,4},{4,6},{6,0},{1,3},{3,5},{5,7},{7,1},{8,10},{10,12},{12... | collective-permute-start | bytes 638984 | tf_op jit(solution)/shard_map/ppermute | solution.py:83
  1451.0 288.6 %reduce-scatter.21.cloned.1.call-start = ((), (), s32[]{:S(2)}) async-start(), calls=%async_computation.26 | async-start | bytes 4423680 | tf_op jit(solution)/shard_map/reduce_scatter | solution.py:679
  1460.8 63.9 %collective-permute-start.132 = (bf16[64,1664]{0,1:T(8,128)(2,1)}, bf16[64,1664]{0,1:T(8,128)(2,1)}, u32[]{:S(2)}, u32[]{:S(2)}) collective-permute-start(bf16[64,1664]{0,1:T(8,128)(2,1)} %concatenate.220), channel_id=1, source_target_pairs={{0,1},{1,0},{2,3},{3,2},{4,5},{5,4},{6,7},{7,6},{8,9},{9,8},{10,11... | collective-permute-start | bytes 638984 | tf_op jit(solution)/shard_map/ppermute | solution.py:84
  1461.0 62.7 %collective-permute-start.130 = (bf16[64,1664]{0,1:T(8,128)(2,1)}, bf16[64,1664]{0,1:T(8,128)(2,1)}, u32[]{:S(2)}, u32[]{:S(2)}) collective-permute-start(bf16[64,1664]{0,1:T(8,128)(2,1)} %concatenate.220), channel_id=1, source_target_pairs={{0,4},{2,6},{4,0},{6,2},{1,5},{3,7},{5,1},{7,3},{8,12},{10,14},{12... | collective-permute-start | bytes 638984 | tf_op jit(solution)/shard_map/ppermute | solution.py:83
  1464.9 58.8 %collective-permute-start.129 = (bf16[64,1664]{0,1:T(8,128)(2,1)}, bf16[64,1664]{0,1:T(8,128)(2,1)}, u32[]{:S(2)}, u32[]{:S(2)}) collective-permute-start(bf16[64,1664]{0,1:T(8,128)(2,1)} %concatenate.220), channel_id=1, source_target_pairs={{0,2},{2,4},{4,6},{6,0},{1,3},{3,5},{5,7},{7,1},{8,10},{10,12},{12... | collective-permute-start | bytes 638984 | tf_op jit(solution)/shard_map/ppermute | solution.py:83
  1486.1 38.6 %collective-permute-start.135 = (bf16[64,1664]{0,1:T(8,128)(2,1)}, bf16[64,1664]{0,1:T(8,128)(2,1)}, u32[]{:S(2)}, u32[]{:S(2)}) collective-permute-start(bf16[64,1664]{0,1:T(8,128)(2,1)} %collective-permute-done.131), channel_id=1, source_target_pairs={{0,1},{1,0},{2,3},{3,2},{4,5},{5,4},{6,7},{7,6},{8,9},{9,8},{10,11... | collective-permute-start | bytes 638984 | tf_op jit(solution)/shard_map/ppermute | solution.py:84
  1569.1 197.8 %reduce-scatter.19.cloned.1.call-start = ((), (), s32[]{:S(2)}) async-start(), calls=%async_computation.25 | async-start | bytes 4423680 | tf_op jit(solution)/shard_map/reduce_scatter | solution.py:679
  1622.1 149.3 %reduce-scatter.23.cloned.1.call-start = ((), (), s32[]{:S(2)}) async-start(), calls=%async_computation.27 | async-start | bytes 3932160 | tf_op jit(solution)/shard_map/reduce_scatter | solution.py:573
  1661.6 36.1 %collective-permute-start.110 = (bf16[64,1536]{0,1:T(8,128)(2,1)}, bf16[64,1536]{0,1:T(8,128)(2,1)}, u32[]{:S(2)}, u32[]{:S(2)}) collective-permute-start(bf16[64,1536]{0,1:T(8,128)(2,1)} %get-tuple-element.524), channel_id=1, source_target_pairs={{0,4},{2,6},{4,0},{6,2},{1,5},{3,7},{5,1},{7,3},{8,12},{10,14},{12... | collective-permute-start | bytes 589832 | tf_op jit(solution)/shard_map/ppermute | solution.py:97
  1668.1 39.0 %collective-permute-start.139 = (bf16[64,1536]{0,1:T(8,128)(2,1)}, bf16[64,1536]{0,1:T(8,128)(2,1)}, u32[]{:S(2)}, u32[]{:S(2)}) collective-permute-start(bf16[64,1536]{0,1:T(8,128)(2,1)} %get-tuple-element.520), channel_id=1, source_target_pairs={{0,2},{2,4},{4,6},{6,0},{1,3},{3,5},{5,7},{7,1},{8,10},{10,12},{12... | collective-permute-start | bytes 589832 | tf_op jit(solution)/shard_map/ppermute | solution.py:97
  1671.4 58.8 %collective-permute-start.138 = (bf16[64,1536]{0,1:T(8,128)(2,1)}, bf16[64,1536]{0,1:T(8,128)(2,1)}, u32[]{:S(2)}, u32[]{:S(2)}) collective-permute-start(bf16[64,1536]{0,1:T(8,128)(2,1)} %get-tuple-element.521), channel_id=1, source_target_pairs={{0,4},{2,6},{4,0},{6,2},{1,5},{3,7},{5,1},{7,3},{8,12},{10,14},{12... | collective-permute-start | bytes 589832 | tf_op jit(solution)/shard_map/ppermute | solution.py:97
  (527 other events, 7042.4 us)
Sparse Core Ops, SparseCore 0:
  43.8 46.1 all-gather.8
  95.0 37.0 all-gather.16
  134.0 46.0 all-gather.10
  181.8 70.1 all-gather.12
  253.7 43.9 all-gather.14
  299.4 70.1 all-gather.18
  371.5 70.1 all-gather.20
  443.5 43.9 all-gather.22
  1130.8 68.4 reduce-scatter.12
  1202.2 70.1 reduce-scatter.24
  1275.4 43.9 reduce-scatter.14
  1360.9 68.8 reduce-scatter.16
  1451.1 66.1 reduce-scatter.26
  1569.2 45.4 reduce-scatter.20
  1622.2 45.3 reduce-scatter.18
  1670.4 43.9 reduce-scatter.22

commit v2 on v1

--- a/solution.py
+++ b/solution.py
@@ -1,6 +1,7 @@
 import jax
 import jax.numpy as jnp
 from jax import lax
+from jax.experimental.layout import Layout, with_layout_constraint
 from jax.sharding import Mesh, PartitionSpec as P
 
 D = 1536
@@ -78,33 +79,43 @@
     return lax.optimization_barrier(trees)
 
 
+def by_rows(x):
+    if lax.axis_size("w") > 1:
+        return x
+    return with_layout_constraint(x, Layout(major_to_minor=tuple(range(x.ndim))))
+
+
+def send(x, axis, pairs):
+    return by_rows(lax.ppermute(by_rows(x), axis, pairs))
+
+
 def gather_rows(x):
     n = lax.axis_size("z")
-    parts = [x] + [lax.ppermute(x, "z", ring(s)) for s in range(1, n)]
-    other = [lax.ppermute(p, "core", SWAP) for p in parts]
-    return jnp.concatenate(parts + other, axis=0)
+    parts = [x] + [send(x, "z", ring(s)) for s in range(1, n)]
+    other = [send(p, "core", SWAP) for p in parts]
+    return by_rows(jnp.concatenate(parts + other, axis=0))
 
 
 def return_rows(total):
     n = lax.axis_size("z")
     half = total.shape[0] // 2
     rows = half // n
-    recv = lax.ppermute(total[half:].astype(bf16), "core", SWAP)
+    recv = send(total[half:].astype(bf16), "core", SWAP)
     mine = total[:half] + recv.astype(f32)
     out = mine[:rows]
     for s in range(1, n):
         part = mine[s * rows : (s + 1) * rows].astype(bf16)
-        out = out + lax.ppermute(part, "z", ring(-s)).astype(f32)
+        out = out + send(part, "z", ring(-s)).astype(f32)
     return out
 
 
 def pair_gather(x):
-    return jnp.concatenate([x, lax.ppermute(x, "core", SWAP)], axis=0)
+    return by_rows(jnp.concatenate([x, send(x, "core", SWAP)], axis=0))
 
 
 def pair_return(total):
     half = total.shape[0] // 2
-    recv = lax.ppermute(total[half:].astype(bf16), "core", SWAP)
+    recv = send(total[half:].astype(bf16), "core", SWAP)
     return total[:half] + recv.astype(f32)
 
 

time: 1820 us -> 1370 us (0.75)
  waiting for transfers between devices: 877 us -> 343 us
  starting transfers between devices: 123 us -> 221 us
  local copies, waits for them, and re-layouts: 285 us -> 241 us
  matrix products: 310 us -> 329 us
    ppermute x140, waiting for transfers between devices: 757 us -> 247 us  [send(): return by_rows(lax.ppermute(by_rows(x), axis, pairs))]
    ppermute x140, starting transfers between devices: 105 us -> 189 us  [send(): return by_rows(lax.ppermute(by_rows(x), axis, pairs))]
    concatenate x12, local copies, waits for them, and re-layouts: 59.4 us -> 4.1 us  [gather_rows(): return by_rows(jnp.concatenate(parts + other, axis=0))]
    dot_general x114, matrix products: 250 us -> 271 us  [dot(): r = lax.dot_general(a, b, (dims, ((), ())), preferred_element_type=f32)]
    unnamed x876 -> x879, local copies, waits for them, and re-layouts: 69.9 us -> 88.4 us
  transfers between devices with their start and end apart: 166 -> 166, of which waited for: 75 -> 49; matrix products, arithmetic and copies ran while one was open for 30% -> 51% of each run, Pallas kernels for 0% -> 0%
where the time goes in v2:
time: 1370 us; the launch traced here: 1350 us
  waiting for transfers between devices  343 us (25%)
  matrix products  329 us (24%)
  local copies, waits for them, and re-layouts  241 us (18%)
  starting transfers between devices  221 us (16%)
  other arithmetic  161 us (12%)
  blocking collectives  39.3 us (3%)
  between operations  20.6 us (2%)
    dot_general x114, matrix products, dot(): r = lax.dot_general(a, b, (dims, ((), ())), preferred_element_type=f32)  271 us
    ppermute x140, waiting for transfers between devices, send(): return by_rows(lax.ppermute(by_rows(x), axis, pairs))  247 us
    ppermute x140, starting transfers between devices, send(): return by_rows(lax.ppermute(by_rows(x), axis, pairs))  189 us
    unnamed x879, local copies, waits for them, and re-layouts  88.4 us
    all_gather x1, waiting for transfers between devices, body(): lax.all_gather(attn_pack.reshape(2 * rows, -1), 'z', axis=0, tiled=True)  35.3 us
    dot_general x6, matrix products, scan_piece(): scan = jnp.einsum('bhts,bshp->bthp', mix, inputs, precision=highest)  32 us
    all_to_all x1, blocking collectives, moved_columns(): moved = lax.all_to_all(packed, TP, split_axis=0, concat_axis=0, tiled=True)  29.4 us
  transfers between devices with their start and end apart: 166, of which 49 were waited for; matrix products, arithmetic and copies ran while one was open for 51% of the time, Pallas kernels for 0%

profile of v2, /device:TPU:0, one launch (start us, length us, event | category | flops | bytes accessed | tf_op | source)
XLA Modules:
  0.0 1354.7 jit_solution(7209939251068578977)
XLA Ops:
  10.3 29.4 %all_to_all.30 = bf16[8,48,1152]{2,1,0:T(8,128)(2,1)} all-to-all(bf16[8,48,1152]{2,1,0:T(8,128)(2,1)S(1)} %copy.1189), channel_id=1, replica_groups=mesh['dp'=4,'w'=1,'z'=4,'core'=2] {'z','core'}, dimensions={0} | all-to-all | bytes 1769472 | tf_op jit(solution)/shard_map/all_to_all | solution.py:411
  46.2 22.4 %all-to-all-done.1 = bf16[8,48,1152]{2,1,0:T(8,128)(2,1)S(1)} async-done(((bf16[8,48,1152]{2,1,0:T(8,128)(2,1)}), bf16[8,48,1152]{2,1,0:T(8,128)(2,1)S(1)}, u32[]{:S(2)}, u32[]{:S(2)}) %all-to-all-start.1) | async-done | bytes 884768 | tf_op jit(solution)/shard_map/all_to_all | solution.py:411
  68.6 17.5 %all-gather.9.cloned.1.call-done = bf16[1536,1152]{1,0:T(8,128)(2,1)} async-done(((bf16[384,1152]{1,0:T(8,128)(2,1)}), bf16[1536,1152]{1,0:T(8,128)(2,1)}) %all-gather.9.cloned.1.call-update) | async-done | bytes 3538960 | tf_op jit(solution)/shard_map/all_gather | solution.py:415
  86.2 4.8 all_to_all.31
  92.9 35.3 %all-gather.17.cloned.1.call-done = bf16[384,2048]{1,0:T(8,128)(2,1)} async-done(((bf16[96,2048]{1,0:T(8,128)(2,1)}), bf16[384,2048]{1,0:T(8,128)(2,1)}) %all-gather.17.cloned.1.call-update) | async-done | bytes 1572880 | tf_op jit(solution)/shard_map/all_gather | solution.py:494
  139.5 7.1 collective-permute-start.54
  147.3 6.1 collective-permute-done.47
  153.4 4.7 collective-permute-start.55
  182.3 8.0 collective-permute-done.1
  190.3 5.6 collective-permute-start.37
  196.7 11.2 collective-permute-done.36
  264.1 6.2 bitcast_add_fusion.2
  287.1 6.2 bitcast_add_fusion.3
  302.5 4.3 fusion.230
  307.6 4.4 concatenate.189
  319.3 4.3 concatenate.182
  327.7 5.7 collective-permute-start.43
  339.2 13.8 %collective-permute-start.9 = (bf16[64,1664]{1,0:T(8,128)(2,1)S(1)}, bf16[64,1664]{1,0:T(8,128)(2,1)S(1)}, u32[]{:S(2)}, u32[]{:S(2)}) collective-permute-start(bf16[64,1664]{1,0:T(8,128)(2,1)S(1)} %get-tuple-element.537), channel_id=1, source_target_pairs={{0,4},{2,6},{4,0},{6,2},{1,5},{3,7},{5,1},{7,3},{8,12},{10,14},{12... | collective-permute-start | bytes 638984 | tf_op jit(solution)/shard_map/ppermute | solution.py:89
  352.9 9.8 collective-permute-done.44
  363.7 7.6 collective-permute-done.9
  378.6 4.5 collective-permute-done.60
  383.1 14.4 %collective-permute-done.61 = bf16[64,1536]{1,0:T(8,128)(2,1)S(1)} collective-permute-done((bf16[64,1536]{1,0:T(8,128)(2,1)S(1)}, bf16[64,1536]{1,0:T(8,128)(2,1)S(1)}, u32[]{:S(2)}, u32[]{:S(2)}) %collective-permute-start.61) | collective-permute-done | bytes 196640 | tf_op jit(solution)/shard_map/ppermute | solution.py:89
  398.7 8.5 collective-permute-done.12
  413.2 6.0 fusion.658
  461.1 10.4 collective-permute-start.21
  471.5 12.1 collective-permute-done.69
  483.8 7.7 collective-permute-done.20
  516.9 5.0 collective-permute-done.24
  522.6 7.6 collective-permute-done.25
  538.0 8.6 collective-permute-done.74
  556.5 5.6 fusion.677
  562.2 4.9 fusion.678
  568.6 5.1 multiply_reduce_fusion.21
  660.8 5.2 fusion.3
  666.0 5.0 fusion.4
  683.2 6.1 pad_maximum_fusion
  700.8 13.7 %collective-permute-done.114 = bf16[64,1664]{1,0:T(8,128)(2,1)S(1)} collective-permute-done((bf16[64,1664]{1,0:T(8,128)(2,1)S(1)}, bf16[64,1664]{1,0:T(8,128)(2,1)S(1)}, u32[]{:S(2)}, u32[]{:S(2)}) %collective-permute-start.114) | collective-permute-done | bytes 213024 | tf_op jit(solution)/shard_map/ppermute | solution.py:89
  726.3 5.6 collective-permute-done.85
  731.8 20.3 %collective-permute-start.34 = (bf16[64,1536]{1,0:T(8,128)(2,1)S(1)}, bf16[64,1536]{1,0:T(8,128)(2,1)S(1)}, u32[]{:S(2)}, u32[]{:S(2)}) collective-permute-start(bf16[64,1536]{1,0:T(8,128)(2,1)S(1)} %get-tuple-element.560), channel_id=1, source_target_pairs={{0,2},{2,4},{4,6},{6,0},{1,3},{3,5},{5,7},{7,1},{8,10},{10,12},{12... | collective-permute-start | bytes 589832 | tf_op jit(solution)/shard_map/ppermute | solution.py:89
  763.1 8.7 collective-permute-done.82
  820.7 8.7 copy.1396
  850.9 9.4 collective-permute-start.91
  860.4 11.6 collective-permute-start.92
  894.1 5.0 multiply_convert_fusion.9
  900.1 4.9 multiply_convert_fusion.23
  905.8 4.9 multiply_convert_fusion.21
  950.2 6.1 pad_maximum_fusion.2
  958.3 6.3 collective-permute-start.126
  970.3 13.1 collective-permute-done.127
  984.4 4.1 fusion.46
  1014.9 9.9 collective-permute-done.99
  1049.7 4.3 collective-permute-done.130
  1061.6 24.4 %collective-permute-done.102 = bf16[64,1664]{1,0:T(8,128)(2,1)S(1)} collective-permute-done((bf16[64,1664]{1,0:T(8,128)(2,1)S(1)}, bf16[64,1664]{1,0:T(8,128)(2,1)S(1)}, u32[]{:S(2)}, u32[]{:S(2)}) %collective-permute-start.102) | collective-permute-done | bytes 213024 | tf_op jit(solution)/shard_map/ppermute | solution.py:89
  1122.3 5.4 bitcast_add_fusion
  1144.1 6.4 fusion.195
  1154.8 4.5 fusion.193
  1164.3 5.1 multiply_reduce_fusion.9
  1205.7 8.4 concatenate.224
  1230.0 9.7 collective-permute-start.143
  1269.5 5.1 all_to_all.32
  1274.6 5.1 all-to-all-start.4
  1279.7 24.5 %collective-permute-done.110 = bf16[64,1536]{1,0:T(8,128)(2,1)} collective-permute-done((bf16[64,1536]{1,0:T(8,128)(2,1)}, bf16[64,1536]{1,0:T(8,128)(2,1)}, u32[]{:S(2)}, u32[]{:S(2)}) %collective-permute-start.110) | collective-permute-done | bytes 196640 | tf_op jit(solution)/shard_map/ppermute | solution.py:89
  1312.9 5.4 all-to-all-start.3
  1328.5 12.8 all-to-all-done.3
  (1763 shorter events, 749.6 us)
Async XLA Ops:
  7.3 78.7 %all-gather.9.cloned.1.call-start = ((), (), s32[]{:S(2)}) async-start(), calls=%async_computation.14 | async-start | bytes 4423680 | tf_op jit(solution)/shard_map/all_gather | solution.py:415
  41.9 26.7 %all-to-all-start.1 = ((bf16[8,48,1152]{2,1,0:T(8,128)(2,1)}), bf16[8,48,1152]{2,1,0:T(8,128)(2,1)S(1)}, u32[]{:S(2)}, u32[]{:S(2)}) async-start(bf16[8,48,1152]{2,1,0:T(8,128)(2,1)} %copy.1202), calls=%async_computation.1 | async-start | bytes 1769472 | tf_op jit(solution)/shard_map/all_to_all | solution.py:411
  45.6 82.6 %all-gather.17.cloned.1.call-start = ((), (), s32[]{:S(2)}) async-start(), calls=%async_computation.18 | async-start | bytes 1966080 | tf_op jit(solution)/shard_map/all_gather | solution.py:494
  91.0 211.6 %all-gather.11.cloned.1.call-start = ((), (), s32[]{:S(2)}) async-start(), calls=%async_computation.15 | async-start | bytes 4423680 | tf_op jit(solution)/shard_map/all_gather | solution.py:415
  91.7 321.5 %all-gather.13.cloned.1.call-start = ((), (), s32[]{:S(2)}) async-start(), calls=%async_computation.16 | async-start | bytes 7864320 | tf_op jit(solution)/shard_map/all_gather | solution.py:475
  92.3 333.0 %all-gather.15.cloned.1.call-start = ((), (), s32[]{:S(2)}) async-start(), calls=%async_computation.17 | async-start | bytes 3932160 | tf_op jit(solution)/shard_map/all_gather | solution.py:476
  92.9 400.9 %all-gather.19.cloned.1.call-start = ((), (), s32[]{:S(2)}) async-start(), calls=%async_computation.19 | async-start | bytes 7864320 | tf_op jit(solution)/shard_map/all_gather | solution.py:495
  128.3 428.3 %all-gather.21.cloned.1.call-start = ((), (), s32[]{:S(2)}) async-start(), calls=%async_computation.20 | async-start | bytes 7864320 | tf_op jit(solution)/shard_map/all_gather | solution.py:503
  129.1 439.6 %all-gather.23.cloned.1.call-start = ((), (), s32[]{:S(2)}) async-start(), calls=%async_computation.21 | async-start | bytes 3932160 | tf_op jit(solution)/shard_map/all_gather | solution.py:504
  129.7 23.8 %collective-permute-start.47 = (bf16[64,1536]{1,0:T(8,128)(2,1)S(1)}, bf16[64,1536]{1,0:T(8,128)(2,1)S(1)}, u32[]{:S(2)}, u32[]{:S(2)}) collective-permute-start(bf16[64,1536]{1,0:T(8,128)(2,1)S(1)} %get-tuple-element.583), channel_id=1, source_target_pairs={{0,4},{2,6},{4,0},{6,2},{1,5},{3,7},{5,1},{7,3},{8,12},{10,14},{12... | collective-permute-start | bytes 589832 | tf_op jit(solution)/shard_map/ppermute | solution.py:89
  131.0 27.8 %collective-permute-start.48 = (bf16[64,1536]{1,0:T(8,128)(2,1)S(1)}, bf16[64,1536]{1,0:T(8,128)(2,1)S(1)}, u32[]{:S(2)}, u32[]{:S(2)}) collective-permute-start(bf16[64,1536]{1,0:T(8,128)(2,1)S(1)} %get-tuple-element.583), channel_id=1, source_target_pairs={{0,6},{2,0},{4,2},{6,4},{1,7},{3,1},{5,3},{7,5},{8,14},{10,8},{12,... | collective-permute-start | bytes 589832 | tf_op jit(solution)/shard_map/ppermute | solution.py:89
  133.4 26.2 %collective-permute-start.49 = (bf16[64,1536]{1,0:T(8,128)(2,1)S(1)}, bf16[64,1536]{1,0:T(8,128)(2,1)S(1)}, u32[]{:S(2)}, u32[]{:S(2)}) collective-permute-start(bf16[64,1536]{1,0:T(8,128)(2,1)S(1)} %get-tuple-element.583), channel_id=1, source_target_pairs={{0,1},{1,0},{2,3},{3,2},{4,5},{5,4},{6,7},{7,6},{8,9},{9,8},{10,11... | collective-permute-start | bytes 589832 | tf_op jit(solution)/shard_map/ppermute | solution.py:89
  133.4 27.4 %collective-permute-start.53 = (bf16[64,1536]{1,0:T(8,128)(2,1)S(1)}, bf16[64,1536]{1,0:T(8,128)(2,1)S(1)}, u32[]{:S(2)}, u32[]{:S(2)}) collective-permute-start(bf16[64,1536]{1,0:T(8,128)(2,1)S(1)} %get-tuple-element.582), channel_id=1, source_target_pairs={{0,2},{2,4},{4,6},{6,0},{1,3},{3,5},{5,7},{7,1},{8,10},{10,12},{12... | collective-permute-start | bytes 589832 | tf_op jit(solution)/shard_map/ppermute | solution.py:89
  133.7 701.4 %reduce-scatter.13.cloned.1.call-start = ((), (), s32[]{:S(2)}) async-start(), calls=%async_computation.22 | async-start | bytes 7864320 | tf_op jit(solution)/shard_map/reduce_scatter | solution.py:584
  181.2 26.7 %collective-permute-start.36 = (bf16[64,1664]{1,0:T(8,128)(2,1)}, bf16[64,1664]{1,0:T(8,128)(2,1)S(1)}, u32[]{:S(2)}, u32[]{:S(2)}) collective-permute-start(bf16[64,1664]{1,0:T(8,128)(2,1)} %concatenate.187), channel_id=1, source_target_pairs={{0,4},{2,6},{4,0},{6,2},{1,5},{3,7},{5,1},{7,3},{8,12},{10,14},{12... | collective-permute-start | bytes 638984 | tf_op jit(solution)/shard_map/ppermute | solution.py:89
  333.5 29.2 %collective-permute-start.44 = (bf16[64,1664]{1,0:T(8,128)(2,1)S(1)}, bf16[64,1664]{1,0:T(8,128)(2,1)S(1)}, u32[]{:S(2)}, u32[]{:S(2)}) collective-permute-start(bf16[64,1664]{1,0:T(8,128)(2,1)S(1)} %get-tuple-element.540), channel_id=1, source_target_pairs={{0,4},{2,6},{4,0},{6,2},{1,5},{3,7},{5,1},{7,3},{8,12},{10,14},{12... | collective-permute-start | bytes 638984 | tf_op jit(solution)/shard_map/ppermute | solution.py:89
  333.8 28.9 %collective-permute-start.45 = (bf16[64,1664]{1,0:T(8,128)(2,1)S(1)}, bf16[64,1664]{1,0:T(8,128)(2,1)S(1)}, u32[]{:S(2)}, u32[]{:S(2)}) collective-permute-start(bf16[64,1664]{1,0:T(8,128)(2,1)S(1)} %get-tuple-element.539), channel_id=1, source_target_pairs={{0,2},{2,4},{4,6},{6,0},{1,3},{3,5},{5,7},{7,1},{8,10},{10,12},{12... | collective-permute-start | bytes 638984 | tf_op jit(solution)/shard_map/ppermute | solution.py:89
  334.4 29.3 %collective-permute-start.10 = (bf16[64,1664]{1,0:T(8,128)(2,1)S(1)}, bf16[64,1664]{1,0:T(8,128)(2,1)S(1)}, u32[]{:S(2)}, u32[]{:S(2)}) collective-permute-start(bf16[64,1664]{1,0:T(8,128)(2,1)S(1)} %get-tuple-element.536), channel_id=1, source_target_pairs={{0,2},{2,4},{4,6},{6,0},{1,3},{3,5},{5,7},{7,1},{8,10},{10,12},{12... | collective-permute-start | bytes 638984 | tf_op jit(solution)/shard_map/ppermute | solution.py:89
  337.3 26.4 %collective-permute-start.8 = (bf16[64,1664]{1,0:T(8,128)(2,1)S(1)}, bf16[64,1664]{1,0:T(8,128)(2,1)S(1)}, u32[]{:S(2)}, u32[]{:S(2)}) collective-permute-start(bf16[64,1664]{1,0:T(8,128)(2,1)S(1)} %get-tuple-element.535), channel_id=1, source_target_pairs={{0,6},{2,0},{4,2},{6,4},{1,7},{3,1},{5,3},{7,5},{8,14},{10,8},{12,... | collective-permute-start | bytes 638984 | tf_op jit(solution)/shard_map/ppermute | solution.py:89
  339.2 32.2 %collective-permute-start.9 = (bf16[64,1664]{1,0:T(8,128)(2,1)S(1)}, bf16[64,1664]{1,0:T(8,128)(2,1)S(1)}, u32[]{:S(2)}, u32[]{:S(2)}) collective-permute-start(bf16[64,1664]{1,0:T(8,128)(2,1)S(1)} %get-tuple-element.537), channel_id=1, source_target_pairs={{0,4},{2,6},{4,0},{6,2},{1,5},{3,7},{5,1},{7,3},{8,12},{10,14},{12... | collective-permute-start | bytes 638984 | tf_op jit(solution)/shard_map/ppermute | solution.py:89
  373.5 24.0 %collective-permute-start.61 = (bf16[64,1536]{1,0:T(8,128)(2,1)S(1)}, bf16[64,1536]{1,0:T(8,128)(2,1)S(1)}, u32[]{:S(2)}, u32[]{:S(2)}) collective-permute-start(bf16[64,1536]{1,0:T(8,128)(2,1)S(1)} %get-tuple-element.633), channel_id=1, source_target_pairs={{0,4},{2,6},{4,0},{6,2},{1,5},{3,7},{5,1},{7,3},{8,12},{10,14},{12... | collective-permute-start | bytes 589832 | tf_op jit(solution)/shard_map/ppermute | solution.py:89
  383.1 24.1 %collective-permute-start.12 = (bf16[64,1536]{1,0:T(8,128)(2,1)S(1)}, bf16[64,1536]{1,0:T(8,128)(2,1)S(1)}, u32[]{:S(2)}, u32[]{:S(2)}) collective-permute-start(bf16[64,1536]{1,0:T(8,128)(2,1)S(1)} %get-tuple-element.452), channel_id=1, source_target_pairs={{0,4},{2,6},{4,0},{6,2},{1,5},{3,7},{5,1},{7,3},{8,12},{10,14},{12... | collective-permute-start | bytes 589832 | tf_op jit(solution)/shard_map/ppermute | solution.py:89
  407.7 24.9 %collective-permute-start.15 = (bf16[64,1536]{1,0:T(8,128)(2,1)S(1)}, bf16[64,1536]{1,0:T(8,128)(2,1)}, u32[]{:S(2)}, u32[]{:S(2)}) collective-permute-start(bf16[64,1536]{1,0:T(8,128)(2,1)S(1)} %collective-permute-done.11), channel_id=1, source_target_pairs={{0,1},{1,0},{2,3},{3,2},{4,5},{5,4},{6,7},{7,6},{8,9},{9,8},{10,11... | collective-permute-start | bytes 589832 | tf_op jit(solution)/shard_map/ppermute | solution.py:89
  408.8 24.8 %collective-permute-start.16 = (bf16[64,1536]{1,0:T(8,128)(2,1)S(1)}, bf16[64,1536]{1,0:T(8,128)(2,1)}, u32[]{:S(2)}, u32[]{:S(2)}) collective-permute-start(bf16[64,1536]{1,0:T(8,128)(2,1)S(1)} %collective-permute-done.12), channel_id=1, source_target_pairs={{0,1},{1,0},{2,3},{3,2},{4,5},{5,4},{6,7},{7,6},{8,9},{9,8},{10,11... | collective-permute-start | bytes 589832 | tf_op jit(solution)/shard_map/ppermute | solution.py:89
  409.3 25.3 %collective-permute-start.17 = (bf16[64,1536]{1,0:T(8,128)(2,1)}, bf16[64,1536]{1,0:T(8,128)(2,1)}, u32[]{:S(2)}, u32[]{:S(2)}) collective-permute-start(bf16[64,1536]{1,0:T(8,128)(2,1)} %collective-permute-done.13), channel_id=1, source_target_pairs={{0,1},{1,0},{2,3},{3,2},{4,5},{5,4},{6,7},{7,6},{8,9},{9,8},{10,11... | collective-permute-start | bytes 589832 | tf_op jit(solution)/shard_map/ppermute | solution.py:89
  454.6 29.0 %collective-permute-start.69 = (bf16[64,1536]{1,0:T(8,128)(2,1)S(1)}, bf16[64,1536]{1,0:T(8,128)(2,1)S(1)}, u32[]{:S(2)}, u32[]{:S(2)}) collective-permute-start(bf16[64,1536]{1,0:T(8,128)(2,1)S(1)} %get-tuple-element.570), channel_id=1, source_target_pairs={{0,4},{2,6},{4,0},{6,2},{1,5},{3,7},{5,1},{7,3},{8,12},{10,14},{12... | collective-permute-start | bytes 589832 | tf_op jit(solution)/shard_map/ppermute | solution.py:89
  456.8 26.7 %collective-permute-start.70 = (bf16[64,1536]{1,0:T(8,128)(2,1)S(1)}, bf16[64,1536]{1,0:T(8,128)(2,1)S(1)}, u32[]{:S(2)}, u32[]{:S(2)}) collective-permute-start(bf16[64,1536]{1,0:T(8,128)(2,1)S(1)} %get-tuple-element.569), channel_id=1, source_target_pairs={{0,2},{2,4},{4,6},{6,0},{1,3},{3,5},{5,7},{7,1},{8,10},{10,12},{12... | collective-permute-start | bytes 589832 | tf_op jit(solution)/shard_map/ppermute | solution.py:89
  457.1 26.7 %collective-permute-start.19 = (bf16[64,1536]{1,0:T(8,128)(2,1)S(1)}, bf16[64,1536]{1,0:T(8,128)(2,1)S(1)}, u32[]{:S(2)}, u32[]{:S(2)}) collective-permute-start(bf16[64,1536]{1,0:T(8,128)(2,1)S(1)} %get-tuple-element.562), channel_id=1, source_target_pairs={{0,6},{2,0},{4,2},{6,4},{1,7},{3,1},{5,3},{7,5},{8,14},{10,8},{12,... | collective-permute-start | bytes 589832 | tf_op jit(solution)/shard_map/ppermute | solution.py:89
  461.0 30.5 %collective-permute-start.20 = (bf16[64,1536]{1,0:T(8,128)(2,1)S(1)}, bf16[64,1536]{1,0:T(8,128)(2,1)S(1)}, u32[]{:S(2)}, u32[]{:S(2)}) collective-permute-start(bf16[64,1536]{1,0:T(8,128)(2,1)S(1)} %get-tuple-element.564), channel_id=1, source_target_pairs={{0,4},{2,6},{4,0},{6,2},{1,5},{3,7},{5,1},{7,3},{8,12},{10,14},{12... | collective-permute-start | bytes 589832 | tf_op jit(solution)/shard_map/ppermute | solution.py:89
  461.1 30.4 %collective-permute-start.21 = (bf16[64,1536]{1,0:T(8,128)(2,1)S(1)}, bf16[64,1536]{1,0:T(8,128)(2,1)S(1)}, u32[]{:S(2)}, u32[]{:S(2)}) collective-permute-start(bf16[64,1536]{1,0:T(8,128)(2,1)S(1)} %get-tuple-element.563), channel_id=1, source_target_pairs={{0,2},{2,4},{4,6},{6,0},{1,3},{3,5},{5,7},{7,1},{8,10},{10,12},{12... | collective-permute-start | bytes 589832 | tf_op jit(solution)/shard_map/ppermute | solution.py:89
  521.8 24.8 %collective-permute-start.74 = (bf16[64,1536]{1,0:T(8,128)(2,1)}, bf16[64,1536]{1,0:T(8,128)(2,1)}, u32[]{:S(2)}, u32[]{:S(2)}) collective-permute-start(bf16[64,1536]{1,0:T(8,128)(2,1)} %get-tuple-element.627), channel_id=1, source_target_pairs={{0,4},{2,6},{4,0},{6,2},{1,5},{3,7},{5,1},{7,3},{8,12},{10,14},{12... | collective-permute-start | bytes 589832 | tf_op jit(solution)/shard_map/ppermute | solution.py:89
  548.2 46.7 %collective-permute-start.77 = (bf16[64,1536]{1,0:T(8,128)(2,1)}, bf16[64,1536]{1,0:T(8,128)(2,1)}, u32[]{:S(2)}, u32[]{:S(2)}) collective-permute-start(bf16[64,1536]{1,0:T(8,128)(2,1)} %collective-permute-done.73), channel_id=1, source_target_pairs={{0,1},{1,0},{2,3},{3,2},{4,5},{5,4},{6,7},{7,6},{8,9},{9,8},{10,11... | collective-permute-start | bytes 589832 | tf_op jit(solution)/shard_map/ppermute | solution.py:89
  550.4 45.5 %collective-permute-start.78 = (bf16[64,1536]{1,0:T(8,128)(2,1)}, bf16[64,1536]{1,0:T(8,128)(2,1)}, u32[]{:S(2)}, u32[]{:S(2)}) collective-permute-start(bf16[64,1536]{1,0:T(8,128)(2,1)} %collective-permute-done.74), channel_id=1, source_target_pairs={{0,1},{1,0},{2,3},{3,2},{4,5},{5,4},{6,7},{7,6},{8,9},{9,8},{10,11... | collective-permute-start | bytes 589832 | tf_op jit(solution)/shard_map/ppermute | solution.py:89
  551.1 45.8 %collective-permute-start.79 = (bf16[64,1536]{1,0:T(8,128)(2,1)}, bf16[64,1536]{1,0:T(8,128)(2,1)}, u32[]{:S(2)}, u32[]{:S(2)}) collective-permute-start(bf16[64,1536]{1,0:T(8,128)(2,1)} %collective-permute-done.75), channel_id=1, source_target_pairs={{0,1},{1,0},{2,3},{3,2},{4,5},{5,4},{6,7},{7,6},{8,9},{9,8},{10,11... | collective-permute-start | bytes 589832 | tf_op jit(solution)/shard_map/ppermute | solution.py:89
  594.9 120.5 %collective-permute-start.31 = (bf16[256,1536]{1,0:T(8,128)(2,1)}, bf16[256,1536]{1,0:T(8,128)(2,1)}, u32[]{:S(2)}, u32[]{:S(2)}) collective-permute-start(bf16[256,1536]{1,0:T(8,128)(2,1)} %slice.2496), channel_id=1, source_target_pairs={{0,1},{1,0},{2,3},{3,2},{4,5},{5,4},{6,7},{7,6},{8,9},{9,8},{10,11... | collective-permute-start | bytes 2359304 | tf_op jit(solution)/shard_map/ppermute | solution.py:89
  635.0 84.6 %collective-permute-start.80 = (bf16[256,1536]{1,0:T(8,128)(2,1)}, bf16[256,1536]{1,0:T(8,128)(2,1)}, u32[]{:S(2)}, u32[]{:S(2)}) collective-permute-start(bf16[256,1536]{1,0:T(8,128)(2,1)} %slice.2494), channel_id=1, source_target_pairs={{0,1},{1,0},{2,3},{3,2},{4,5},{5,4},{6,7},{7,6},{8,9},{9,8},{10,11... | collective-permute-start | bytes 2359304 | tf_op jit(solution)/shard_map/ppermute | solution.py:89
  660.3 29.1 %collective-permute-start.112 = (bf16[256,1664]{1,0:T(8,128)(2,1)}, bf16[256,1664]{1,0:T(8,128)(2,1)}, u32[]{:S(2)}, u32[]{:S(2)}) collective-permute-start(bf16[256,1664]{1,0:T(8,128)(2,1)} %slice.2487), channel_id=1, source_target_pairs={{0,1},{1,0},{2,3},{3,2},{4,5},{5,4},{6,7},{7,6},{8,9},{9,8},{10,11... | collective-permute-start | bytes 2555912 | tf_op jit(solution)/shard_map/ppermute | solution.py:89
  715.4 291.9 %reduce-scatter.25.cloned.1.call-start = ((), (), s32[]{:S(2)}) async-start(), calls=%async_computation.28 | async-start | bytes 7864320
  717.6 43.1 %collective-permute-start.32 = (bf16[64,1536]{1,0:T(8,128)(2,1)S(1)}, bf16[64,1536]{1,0:T(8,128)(2,1)S(1)}, u32[]{:S(2)}, u32[]{:S(2)}) collective-permute-start(bf16[64,1536]{1,0:T(8,128)(2,1)S(1)} %get-tuple-element.559), channel_id=1, source_target_pairs={{0,6},{2,0},{4,2},{6,4},{1,7},{3,1},{5,3},{7,5},{8,14},{10,8},{12,... | collective-permute-start | bytes 589832 | tf_op jit(solution)/shard_map/ppermute | solution.py:89
  717.6 45.5 %collective-permute-start.33 = (bf16[64,1536]{1,0:T(8,128)(2,1)S(1)}, bf16[64,1536]{1,0:T(8,128)(2,1)S(1)}, u32[]{:S(2)}, u32[]{:S(2)}) collective-permute-start(bf16[64,1536]{1,0:T(8,128)(2,1)S(1)} %get-tuple-element.561), channel_id=1, source_target_pairs={{0,4},{2,6},{4,0},{6,2},{1,5},{3,7},{5,1},{7,3},{8,12},{10,14},{12... | collective-permute-start | bytes 589832 | tf_op jit(solution)/shard_map/ppermute | solution.py:89
  724.9 30.7 %collective-permute-start.86 = (bf16[64,1664]{1,0:T(8,128)(2,1)S(1)}, bf16[64,1664]{1,0:T(8,128)(2,1)S(1)}, u32[]{:S(2)}, u32[]{:S(2)}) collective-permute-start(bf16[64,1664]{1,0:T(8,128)(2,1)S(1)} %get-tuple-element.531), channel_id=1, source_target_pairs={{0,4},{2,6},{4,0},{6,2},{1,5},{3,7},{5,1},{7,3},{8,12},{10,14},{12... | collective-permute-start | bytes 638984 | tf_op jit(solution)/shard_map/ppermute | solution.py:89
  726.2 29.4 %collective-permute-start.87 = (bf16[64,1664]{1,0:T(8,128)(2,1)S(1)}, bf16[64,1664]{1,0:T(8,128)(2,1)S(1)}, u32[]{:S(2)}, u32[]{:S(2)}) collective-permute-start(bf16[64,1664]{1,0:T(8,128)(2,1)S(1)} %get-tuple-element.530), channel_id=1, source_target_pairs={{0,2},{2,4},{4,6},{6,0},{1,3},{3,5},{5,7},{7,1},{8,10},{10,12},{12... | collective-permute-start | bytes 638984 | tf_op jit(solution)/shard_map/ppermute | solution.py:89
  731.8 31.3 %collective-permute-start.34 = (bf16[64,1536]{1,0:T(8,128)(2,1)S(1)}, bf16[64,1536]{1,0:T(8,128)(2,1)S(1)}, u32[]{:S(2)}, u32[]{:S(2)}) collective-permute-start(bf16[64,1536]{1,0:T(8,128)(2,1)S(1)} %get-tuple-element.560), channel_id=1, source_target_pairs={{0,2},{2,4},{4,6},{6,0},{1,3},{3,5},{5,7},{7,1},{8,10},{10,12},{12... | collective-permute-start | bytes 589832 | tf_op jit(solution)/shard_map/ppermute | solution.py:89
  829.4 178.0 %reduce-scatter.15.cloned.1.call-start = ((), (), s32[]{:S(2)}) async-start(), calls=%async_computation.23 | async-start | bytes 3932160 | tf_op jit(solution)/shard_map/reduce_scatter | solution.py:584
  835.0 370.6 %reduce-scatter.17.cloned.1.call-start = ((), (), s32[]{:S(2)}) async-start(), calls=%async_computation.24 | async-start | bytes 7864320 | tf_op jit(solution)/shard_map/reduce_scatter | solution.py:584
  844.1 27.8 %collective-permute-start.120 = (bf16[64,1536]{1,0:T(8,128)(2,1)S(1)}, bf16[64,1536]{1,0:T(8,128)(2,1)S(1)}, u32[]{:S(2)}, u32[]{:S(2)}) collective-permute-start(bf16[64,1536]{1,0:T(8,128)(2,1)S(1)} %get-tuple-element.435), channel_id=1, source_target_pairs={{0,6},{2,0},{4,2},{6,4},{1,7},{3,1},{5,3},{7,5},{8,14},{10,8},{12,... | collective-permute-start | bytes 589832 | tf_op jit(solution)/shard_map/ppermute | solution.py:89
  847.1 25.0 %collective-permute-start.121 = (bf16[64,1536]{1,0:T(8,128)(2,1)S(1)}, bf16[64,1536]{1,0:T(8,128)(2,1)S(1)}, u32[]{:S(2)}, u32[]{:S(2)}) collective-permute-start(bf16[64,1536]{1,0:T(8,128)(2,1)S(1)} %get-tuple-element.435), channel_id=1, source_target_pairs={{0,1},{1,0},{2,3},{3,2},{4,5},{5,4},{6,7},{7,6},{8,9},{9,8},{10,11... | collective-permute-start | bytes 589832 | tf_op jit(solution)/shard_map/ppermute | solution.py:89
  849.1 23.6 %collective-permute-start.90 = (bf16[64,1536]{1,0:T(8,128)(2,1)S(1)}, bf16[64,1536]{1,0:T(8,128)(2,1)S(1)}, u32[]{:S(2)}, u32[]{:S(2)}) collective-permute-start(bf16[64,1536]{1,0:T(8,128)(2,1)S(1)} %get-tuple-element.430), channel_id=1, source_target_pairs={{0,2},{2,4},{4,6},{6,0},{1,3},{3,5},{5,7},{7,1},{8,10},{10,12},{12... | collective-permute-start | bytes 589832 | tf_op jit(solution)/shard_map/ppermute | solution.py:89
  850.9 24.7 %collective-permute-start.91 = (bf16[64,1536]{1,0:T(8,128)(2,1)S(1)}, bf16[64,1536]{1,0:T(8,128)(2,1)S(1)}, u32[]{:S(2)}, u32[]{:S(2)}) collective-permute-start(bf16[64,1536]{1,0:T(8,128)(2,1)S(1)} %get-tuple-element.430), channel_id=1, source_target_pairs={{0,4},{2,6},{4,0},{6,2},{1,5},{3,7},{5,1},{7,3},{8,12},{10,14},{12... | collective-permute-start | bytes 589832 | tf_op jit(solution)/shard_map/ppermute | solution.py:89
  926.8 29.5 %collective-permute-start.125 = (bf16[256,1664]{1,0:T(8,128)(2,1)}, bf16[256,1664]{1,0:T(8,128)(2,1)}, u32[]{:S(2)}, u32[]{:S(2)}) collective-permute-start(bf16[256,1664]{1,0:T(8,128)(2,1)} %slice.2486), channel_id=1, source_target_pairs={{0,1},{1,0},{2,3},{3,2},{4,5},{5,4},{6,7},{7,6},{8,9},{9,8},{10,11... | collective-permute-start | bytes 2555912 | tf_op jit(solution)/shard_map/ppermute | solution.py:89
  984.3 285.2 %reduce-scatter.27.cloned.1.call-start = ((), (), s32[]{:S(2)}) async-start(), calls=%async_computation.29 | async-start | bytes 1966080 | tf_op jit(solution)/shard_map/reduce_scatter | solution.py:630
  1007.3 267.2 %reduce-scatter.21.cloned.1.call-start = ((), (), s32[]{:S(2)}) async-start(), calls=%async_computation.26 | async-start | bytes 4423680 | tf_op jit(solution)/shard_map/reduce_scatter | solution.py:690
  1047.1 38.9 %collective-permute-start.102 = (bf16[64,1664]{1,0:T(8,128)(2,1)S(1)}, bf16[64,1664]{1,0:T(8,128)(2,1)S(1)}, u32[]{:S(2)}, u32[]{:S(2)}) collective-permute-start(bf16[64,1664]{1,0:T(8,128)(2,1)S(1)} %copy-done.146), channel_id=1, source_target_pairs={{0,4},{2,6},{4,0},{6,2},{1,5},{3,7},{5,1},{7,3},{8,12},{10,14},{12... | collective-permute-start | bytes 638984 | tf_op jit(solution)/shard_map/ppermute | solution.py:89
  1054.0 32.1 %collective-permute-start.103 = (bf16[64,1664]{1,0:T(8,128)(2,1)S(1)}, bf16[64,1664]{1,0:T(8,128)(2,1)S(1)}, u32[]{:S(2)}, u32[]{:S(2)}) collective-permute-start(bf16[64,1664]{1,0:T(8,128)(2,1)S(1)} %copy-done.146), channel_id=1, source_target_pairs={{0,6},{2,0},{4,2},{6,4},{1,7},{3,1},{5,3},{7,5},{8,14},{10,8},{12,... | collective-permute-start | bytes 638984 | tf_op jit(solution)/shard_map/ppermute | solution.py:89
  1058.0 28.7 %collective-permute-start.104 = (bf16[64,1664]{1,0:T(8,128)(2,1)S(1)}, bf16[64,1664]{1,0:T(8,128)(2,1)S(1)}, u32[]{:S(2)}, u32[]{:S(2)}) collective-permute-start(bf16[64,1664]{1,0:T(8,128)(2,1)S(1)} %copy-done.146), channel_id=1, source_target_pairs={{0,1},{1,0},{2,3},{3,2},{4,5},{5,4},{6,7},{7,6},{8,9},{9,8},{10,11... | collective-permute-start | bytes 638984 | tf_op jit(solution)/shard_map/ppermute | solution.py:89
  1059.0 27.7 %collective-permute-start.133 = (bf16[64,1664]{1,0:T(8,128)(2,1)}, bf16[64,1664]{1,0:T(8,128)(2,1)S(1)}, u32[]{:S(2)}, u32[]{:S(2)}) collective-permute-start(bf16[64,1664]{1,0:T(8,128)(2,1)} %collective-permute-done.129), channel_id=1, source_target_pairs={{0,1},{1,0},{2,3},{3,2},{4,5},{5,4},{6,7},{7,6},{8,9},{9,8},{10,11... | collective-permute-start | bytes 638984 | tf_op jit(solution)/shard_map/ppermute | solution.py:89
  1060.6 26.8 %collective-permute-start.134 = (bf16[64,1664]{1,0:T(8,128)(2,1)}, bf16[64,1664]{1,0:T(8,128)(2,1)S(1)}, u32[]{:S(2)}, u32[]{:S(2)}) collective-permute-start(bf16[64,1664]{1,0:T(8,128)(2,1)} %collective-permute-done.130), channel_id=1, source_target_pairs={{0,1},{1,0},{2,3},{3,2},{4,5},{5,4},{6,7},{7,6},{8,9},{9,8},{10,11... | collective-permute-start | bytes 638984 | tf_op jit(solution)/shard_map/ppermute | solution.py:89
  1163.6 149.3 %reduce-scatter.19.cloned.1.call-start = ((), (), s32[]{:S(2)}) async-start(), calls=%async_computation.25 | async-start | bytes 4423680 | tf_op jit(solution)/shard_map/reduce_scatter | solution.py:690
  1214.1 105.7 %reduce-scatter.23.cloned.1.call-start = ((), (), s32[]{:S(2)}) async-start(), calls=%async_computation.27 | async-start | bytes 3932160 | tf_op jit(solution)/shard_map/reduce_scatter | solution.py:584
  1226.9 28.1 %collective-permute-start.136 = (bf16[256,1536]{1,0:T(8,128)(2,1)}, bf16[256,1536]{1,0:T(8,128)(2,1)}, u32[]{:S(2)}, u32[]{:S(2)}) collective-permute-start(bf16[256,1536]{1,0:T(8,128)(2,1)} %slice.2492), channel_id=1, source_target_pairs={{0,1},{1,0},{2,3},{3,2},{4,5},{5,4},{6,7},{7,6},{8,9},{9,8},{10,11... | collective-permute-start | bytes 2359304 | tf_op jit(solution)/shard_map/ppermute | solution.py:89
  1266.5 37.6 %collective-permute-start.110 = (bf16[64,1536]{1,0:T(8,128)(2,1)}, bf16[64,1536]{1,0:T(8,128)(2,1)}, u32[]{:S(2)}, u32[]{:S(2)}) collective-permute-start(bf16[64,1536]{1,0:T(8,128)(2,1)} %get-tuple-element.550), channel_id=1, source_target_pairs={{0,4},{2,6},{4,0},{6,2},{1,5},{3,7},{5,1},{7,3},{8,12},{10,14},{12... | collective-permute-start | bytes 589832 | tf_op jit(solution)/shard_map/ppermute | solution.py:89
  1267.6 36.5 %collective-permute-start.111 = (bf16[64,1536]{1,0:T(8,128)(2,1)}, bf16[64,1536]{1,0:T(8,128)(2,1)}, u32[]{:S(2)}, u32[]{:S(2)}) collective-permute-start(bf16[64,1536]{1,0:T(8,128)(2,1)} %get-tuple-element.549), channel_id=1, source_target_pairs={{0,2},{2,4},{4,6},{6,0},{1,3},{3,5},{5,7},{7,1},{8,10},{10,12},{12... | collective-permute-start | bytes 589832 | tf_op jit(solution)/shard_map/ppermute | solution.py:89
  1274.6 38.3 %all-to-all-start.4 = ((bf16[8,48,1152]{2,1,0:T(8,128)(2,1)}), bf16[8,48,1152]{2,1,0:T(8,128)(2,1)S(1)}, u32[]{:S(2)}, u32[]{:S(2)}) async-start(bf16[8,48,1152]{2,1,0:T(8,128)(2,1)} %bitcast.650), calls=%async_computation.9 | async-start | bytes 1769472 | tf_op jit(solution)/shard_map/all_to_all | solution.py:691
  1312.9 28.4 %all-to-all-start.3 = ((bf16[8,48,1152]{2,1,0:T(8,128)(2,1)}), bf16[8,48,1152]{2,1,0:T(8,128)(2,1)S(1)}, u32[]{:S(2)}, u32[]{:S(2)}) async-start(bf16[8,48,1152]{2,1,0:T(8,128)(2,1)} %bitcast.651), calls=%async_computation.7 | async-start | bytes 1769472 | tf_op jit(solution)/shard_map/all_to_all | solution.py:691
  (494 other events, 4097.7 us)
Sparse Core Ops, SparseCore 0:
  39.9 46.1 all-gather.8
  91.1 37.0 all-gather.16
  130.6 46.1 all-gather.10
  178.6 70.1 all-gather.12
  250.4 43.9 all-gather.14
  296.2 70.1 all-gather.18
  368.2 70.1 all-gather.20
  440.3 43.9 all-gather.22
  715.5 69.6 reduce-scatter.12
  829.5 70.5 reduce-scatter.24
  903.1 43.9 reduce-scatter.14
  984.4 70.1 reduce-scatter.16
  1056.9 42.0 reduce-scatter.26
  1163.7 56.0 reduce-scatter.20
  1222.7 47.2 reduce-scatter.18
  1272.8 43.9 reduce-scatter.22

commit v3 on v2

--- a/solution.py
+++ b/solution.py
@@ -1,6 +1,10 @@
+import functools
+
 import jax
 import jax.numpy as jnp
 from jax import lax
+from jax.experimental import pallas as pl
+from jax.experimental.pallas import tpu as pltpu
 from jax.experimental.layout import Layout, with_layout_constraint
 from jax.sharding import Mesh, PartitionSpec as P
 
@@ -151,36 +155,210 @@
     return jnp.concatenate(parts, axis=1)
 
 
-def scan_piece(proj, dt_raw, seg, conv_w, conv_b, dt_bias, a_log, skip, heads):
-    seqs, length, _ = proj.shape
-    chan = heads * HP
-    gate_z = proj[..., :chan]
-    conv_in = proj[..., chan:]
-    positions = lax.broadcasted_iota(jnp.int32, (length,), 0)
-    conv_sum = jnp.zeros_like(conv_in) + conv_b
-    for offset in range(CK):
-        shifted = jnp.pad(conv_in, ((0, 0), (offset, 0), (0, 0)))[:, :length]
-        seg_prev = jnp.pad(seg, ((0, 0), (offset, 0)))[:, :length]
-        usable = (positions >= offset)[None] & (seg_prev == seg)
-        conv_sum = conv_sum + jnp.where(usable[..., None], conv_w[offset] * shifted, 0.0)
-    conv_act = jax.nn.silu(conv_sum)
-    inputs = conv_act[..., :chan].reshape(seqs, length, heads, HP)
-    b_state = conv_act[..., chan : chan + STATE]
-    c_state = conv_act[..., chan + STATE :]
-    step = jax.nn.softplus(dt_raw + dt_bias)
+def scan_core(proj, step_raw, seg_col, seg_row, taps, bias, heads_par):
+    length = proj.shape[0]
+    chan = proj.shape[1] - 2 * STATE
+    chan = chan // 2
+    z = proj[:, :chan].astype(f32)
+    conv_in = proj[:, chan:].astype(f32)
+    place = lax.broadcasted_iota(jnp.int32, (length, 1), 0)
+    shifted, masks = [], []
+    conv_sum = bias
+    for k in range(CK):
+        if k == 0:
+            moved, mask = conv_in, None
+            conv_sum = conv_sum + taps[0:1] * moved
+        else:
+            same = pltpu.roll(seg_col, k, 0) == seg_col
+            mask = jnp.where(same & (place >= k), 1.0, 0.0)
+            moved = pltpu.roll(conv_in, k, 0) * mask
+            conv_sum = conv_sum + taps[k : k + 1] * moved
+        shifted.append(moved)
+        masks.append(mask)
+    logistic = jax.nn.sigmoid(conv_sum)
+    act = conv_sum * logistic
+    pre = step_raw + heads_par[0:1]
+    step = jnp.maximum(pre, 0.0) + jnp.log1p(jnp.exp(-jnp.abs(pre)))
+    decay_rate = heads_par[1:2]
     rows_pos = lax.broadcasted_iota(jnp.int32, (length, length), 0)
     cols_pos = lax.broadcasted_iota(jnp.int32, (length, length), 1)
-    lower = (cols_pos <= rows_pos).astype(f32)
-    cum = jnp.einsum("ts,bsh->bht", lower, step * -jnp.exp(a_log), precision=highest)
-    allowed = (seg[:, :, None] == seg[:, None, :]) & (cols_pos <= rows_pos)[None]
-    allowed = allowed[:, None]
-    gap = cum[..., :, None] - cum[..., None, :]
-    decay = jnp.where(allowed, jnp.exp(jnp.where(allowed, gap, 0.0)), 0.0)
-    cb = jnp.einsum("btn,bsn->bts", c_state, b_state, precision=highest)
-    mix = decay * cb[:, None] * step.transpose(0, 2, 1)[:, :, None, :]
-    scan = jnp.einsum("bhts,bshp->bthp", mix, inputs, precision=highest)
-    scan = scan + skip[:, None] * inputs
-    return scan.reshape(seqs, length, chan) * jax.nn.silu(gate_z)
+    lower = jnp.where(cols_pos <= rows_pos, 1.0, 0.0)
+    cum = lax.dot_general(
+        lower, step * decay_rate, (((1,), (0,)), ((), ())), precision=highest, preferred_element_type=f32
+    )
+    allowed = (seg_col == seg_row) & (cols_pos <= rows_pos)
+    b_low = act[:, chan : chan + STATE].astype(bf16)
+    c_low = act[:, chan + STATE :].astype(bf16)
+    cb = nt(c_low, b_low)
+    return dict(
+        chan=chan, z=z, conv_in=conv_in, shifted=shifted, masks=masks, conv_sum=conv_sum,
+        logistic=logistic, act=act, pre=pre, step=step, rate=decay_rate, lower=lower, cum=cum,
+        cum_t=cum.T, step_t=step.T, allowed=allowed, b=b_low, c=c_low, cb=cb,
+    )
+
+
+def head_table(s, h):
+    gap = s["cum"][:, h : h + 1] - s["cum_t"][h : h + 1, :]
+    decay = jnp.exp(jnp.where(s["allowed"], gap, masked_value))
+    return decay, s["step_t"][h : h + 1, :]
+
+
+def pair_scan(s, heads, low):
+    lane = lax.broadcasted_iota(jnp.int32, (1, 2 * HP), 1)
+    blocks, mixes, tables = [], [], []
+    for j in range(heads // 2):
+        both = low[:, j * 2 * HP : (j + 1) * 2 * HP]
+        outs = []
+        for h in (2 * j, 2 * j + 1):
+            decay, step_row = head_table(s, h)
+            mix = (decay * s["cb"] * step_row).astype(bf16)
+            outs.append(nn(mix, both))
+            mixes.append(mix)
+            tables.append((decay, step_row))
+        blocks.append(jnp.where(lane < HP, outs[0], outs[1]))
+    return jnp.concatenate(blocks, axis=1), mixes, tables
+
+
+def scan_forward_kernel(heads, proj_ref, step_ref, col_ref, row_ref, conv_ref, chan_ref, head_ref, gained_ref, square_ref):
+    s = scan_core(
+        proj_ref[...], step_ref[...], col_ref[...], row_ref[0], conv_ref[0:CK], conv_ref[CK : CK + 1], head_ref[...]
+    )
+    chan = s["chan"]
+    inputs = s["act"][:, :chan]
+    scan, _, _ = pair_scan(s, heads, inputs.astype(bf16))
+    scan = scan + chan_ref[1:2] * inputs
+    gated = scan * s["z"] * jax.nn.sigmoid(s["z"])
+    gained_ref[...] = (gated * chan_ref[0:1]).astype(bf16)
+    square_ref[...] = jnp.broadcast_to(jnp.sum(gated * gated, axis=1, keepdims=True), square_ref.shape)
+
+
+def scan_backward_kernel(
+    heads, proj_ref, step_ref, col_ref, row_ref, conv_ref, chan_ref, head_ref, grad_ref, extra_ref,
+    dproj_ref, dstep_ref, dconv_ref, dchan_ref, dhead_ref, flat_ref,
+):
+    @pl.when(pl.program_id(0) == 0)
+    def _():
+        dconv_ref[...] = jnp.zeros_like(dconv_ref)
+        dchan_ref[...] = jnp.zeros_like(dchan_ref)
+        dhead_ref[...] = jnp.zeros_like(dhead_ref)
+
+    taps = conv_ref[0:CK]
+    s = scan_core(proj_ref[...], step_ref[...], col_ref[...], row_ref[0], taps, conv_ref[CK : CK + 1], head_ref[...])
+    chan, length = s["chan"], s["z"].shape[0]
+    gain, skip = chan_ref[0:1], chan_ref[1:2]
+    inputs = s["act"][:, :chan]
+    low = inputs.astype(bf16)
+    scan, mixes, tables = pair_scan(s, heads, low)
+    scan = scan + skip * inputs
+    z = s["z"]
+    sig = jax.nn.sigmoid(z)
+    silu = z * sig
+    gated = scan * silu
+    extra = extra_ref[...].astype(f32)
+    scale = extra[:, 0:1] + extra[:, 1:2]
+    mean = extra[:, 2:3] + extra[:, 3:4]
+    grad = grad_ref[...].astype(f32)
+    normed = gated * scale
+    d_gated = scale * (grad * gain - normed * mean)
+    d_scan = d_gated * silu
+    d_z = d_gated * scan * sig * (1.0 + z * (1.0 - sig))
+    d_low = d_scan.astype(bf16)
+    lane = lax.broadcasted_iota(jnp.int32, (1, 2 * HP), 1)
+    spot = lax.broadcasted_iota(jnp.int32, (1, s["step"].shape[1]), 1)
+    d_cb = jnp.zeros((length, length), f32)
+    d_cum = jnp.zeros(s["step"].shape, f32)
+    flat_ref[...] = jnp.zeros_like(flat_ref)
+    blocks = []
+    for j in range(heads // 2):
+        cut = slice(j * 2 * HP, (j + 1) * 2 * HP)
+        both, d_both = low[:, cut], d_low[:, cut]
+        outs = []
+        for i, h in enumerate((2 * j, 2 * j + 1)):
+            decay, step_row = tables[h]
+            outs.append(tn(mixes[h], d_both))
+            keep = (lane < HP) if i == 0 else (lane >= HP)
+            d_mix = nt(jnp.where(keep, d_both, jnp.zeros_like(d_both)), both)
+            part = d_mix * decay
+            d_cb = d_cb + part * step_row
+            part = part * s["cb"]
+            flat_ref[h : h + 1, 0:length] = jnp.sum(part, axis=0, keepdims=True)
+            column = jnp.sum(part * step_row, axis=1, keepdims=True)
+            d_cum = d_cum + jnp.where(spot == h, column, 0.0)
+        blocks.append(jnp.where(lane < HP, outs[0], outs[1]))
+    d_inputs = jnp.concatenate(blocks, axis=1) + skip * d_scan
+    from_rows = flat_ref[...].T[0:length]
+    d_cum = d_cum - s["step"] * from_rows
+    d_rate = lax.dot_general(
+        s["lower"], d_cum, (((0,), (0,)), ((), ())), precision=highest, preferred_element_type=f32
+    )
+    d_step = from_rows + d_rate * s["rate"]
+    d_pre = jnp.where(spot < heads, d_step * jax.nn.sigmoid(s["pre"]), 0.0)
+    d_cb_low = d_cb.astype(bf16)
+    d_act = jnp.concatenate([d_inputs, tn(d_cb_low, s["c"]), nn(d_cb_low, s["b"])], axis=1)
+    logistic = s["logistic"]
+    d_sum = d_act * logistic * (1.0 + s["conv_sum"] * (1.0 - logistic))
+    d_in = taps[0:1] * d_sum
+    for k in range(1, CK):
+        back = d_sum * s["masks"][k] * taps[k : k + 1]
+        d_in = d_in + pltpu.roll(back, length - k, 0)
+    dproj_ref[...] = jnp.concatenate([d_z, d_in], axis=1).astype(bf16)
+    dstep_ref[...] = d_pre.astype(bf16)
+    for k in range(CK):
+        dconv_ref[k : k + 1] += jnp.sum(d_sum * s["shifted"][k], axis=0, keepdims=True)
+    dconv_ref[CK : CK + 1] += jnp.sum(d_sum, axis=0, keepdims=True)
+    dchan_ref[0:1] += jnp.sum(grad * normed, axis=0, keepdims=True)
+    dchan_ref[1:2] += jnp.sum(d_scan * inputs, axis=0, keepdims=True)
+    dhead_ref[0:1] += jnp.sum(d_pre, axis=0, keepdims=True)
+    dhead_ref[1:2] += jnp.sum(d_rate * s["step"] * s["rate"], axis=0, keepdims=True)
+
+
+def scan_specs(length, width, lanes_, conv, chan):
+    def whole(shape):
+        return pl.BlockSpec(shape, lambda i: (0,) * len(shape))
+
+    rows = lambda w: pl.BlockSpec((length, w), lambda i: (i, 0))
+    return rows, whole, [
+        rows(width), rows(lanes_), rows(1), pl.BlockSpec((1, 1, length), lambda i: (i, 0, 0)),
+        whole((8, conv)), whole((8, chan)), whole((8, lanes_)),
+    ]
+
+
+def scan_forward(heads, length, proj, step, seg_col, seg_row, conv_par, chan_par, head_par):
+    total, width = proj.shape
+    chan = heads * HP
+    rows, whole, specs = scan_specs(length, width, step.shape[1], width - chan, chan)
+    return pl.pallas_call(
+        functools.partial(scan_forward_kernel, heads),
+        grid=(total // length,),
+        in_specs=specs,
+        out_specs=[rows(chan), rows(128)],
+        out_shape=[jax.ShapeDtypeStruct((total, chan), bf16), jax.ShapeDtypeStruct((total, 128), f32)],
+        compiler_params=pltpu.CompilerParams(vmem_limit_bytes=32 << 20),
+        name="scan_forward",
+    )(proj, step, seg_col, seg_row, conv_par, chan_par, head_par)
+
+
+def scan_backward(heads, length, proj, step, seg_col, seg_row, conv_par, chan_par, head_par, grad, extra):
+    total, width = proj.shape
+    chan = heads * HP
+    lanes_ = step.shape[1]
+    rows, whole, specs = scan_specs(length, width, lanes_, width - chan, chan)
+    return pl.pallas_call(
+        functools.partial(scan_backward_kernel, heads),
+        grid=(total // length,),
+        in_specs=specs + [rows(chan), rows(128)],
+        out_specs=[rows(width), rows(lanes_), whole((8, width - chan)), whole((8, chan)), whole((8, lanes_))],
+        out_shape=[
+            jax.ShapeDtypeStruct((total, width), bf16),
+            jax.ShapeDtypeStruct((total, lanes_), bf16),
+            jax.ShapeDtypeStruct((8, width - chan), f32),
+            jax.ShapeDtypeStruct((8, chan), f32),
+            jax.ShapeDtypeStruct((8, lanes_), f32),
+        ],
+        scratch_shapes=[pltpu.VMEM((128, 128), f32)],
+        compiler_params=pltpu.CompilerParams(vmem_limit_bytes=32 << 20),
+        name="scan_backward",
+    )(proj, step, seg_col, seg_row, conv_par, chan_par, head_par, grad, extra)
 
 
 def swiglu(gate, up):
@@ -211,6 +389,8 @@
     local = lax.dynamic_slice(gates, (0, first), (gates.shape[0], count))
     pre = [nn(moe_in, w["expert_in"][e], bf16) for e in range(count)]
     pre_s = nn(base_in, w["shared_in"], bf16)
+    if lax.axis_size("w") > 1:
+        pre, pre_s = lax.optimization_barrier((pre, pre_s))
     total = None
     for e in range(count):
         p = pre[e].astype(f32)
@@ -229,7 +409,7 @@
 
 def moe_backward(base_z, kept, w, experts_total):
     moe_in, base_in, own_gates, local, pre, pre_s = kept
-    pre, pre_s, _ = fence(pre, pre_s, base_z)
+    pre, pre_s, _ = lax.optimization_barrier((pre, pre_s, base_z))
     grad_z = wide(base_z)
     rows = own_gates.shape[0]
     count = len(pre)
@@ -433,17 +613,29 @@
         ]
     )
     w_m = whole_rows(moved_m)
+
+    expert_ids = jnp.arange(experts_total, dtype=jnp.int32)
+    info_width = -(-(2 * experts_total + 1) // 128) * 128
+    each = range(micro)
+    rows_in = []
+    for m in each:
+        hot = [
+            jnp.any(routes[b, m][:, :, None] == expert_ids, axis=1).astype(bf16) for b in range(2)
+        ]
+        info = lanes(hot + [segments[m, 0][:, None].astype(bf16)], info_width)
+        x_info, _ = fence(jnp.concatenate([tokens[m], info], axis=1), moved_m)
+        rows_in.append(gather_rows(x_info))
     moved_s = moved_columns(
         [by_owner(w_mix_out.T, n_tp)]
         + shared_pack(shared_in_m, shared_down_m)
         + shared_pack(shared_in, shared_down),
-        moved_m,
+        rows_in[0],
     )
     w_s = whole_rows(moved_s)
     in_width = 2 * chan + 2 * STATE
     w_in_here = w_m[:, :in_width]
     w_step = w_m[:, in_width:]
-    w_dt_here = w_step[:, :heads]
+    w_dt_here = w_step[:, :128]
     small_all = w_step[:, heads : heads + small_cols]
     gain_mamba, gain_moe_m, gain_attn, gain_moe = [small_all[:, i].astype(f32) for i in range(4)]
     router_m_full = small_all[:, 4 : 4 + experts_total]
@@ -466,6 +658,7 @@
     skip_here = lax.dynamic_slice_in_dim(skip_scale, slot * heads, heads)
 
     w_mix_t = w_s[:, :chan]
+    expert_in_m, expert_down_m, _ = fence(expert_in_m, expert_down_m, moved_s)
     at = chan
 
     moe_m = {
@@ -480,6 +673,54 @@
     q_width = QH // 2 * HEAD
     kv_width = kv * HEAD
     q_all, kv_all = QH * HEAD, KVH * HEAD
+    moe_a = {
+        "router": router_full,
+        "shared_in": w_s[:, at + 3 * ff : at + 5 * ff],
+        "shared_down_t": w_s[:, at + 5 * ff :],
+        "expert_in": lax.all_gather(expert_in, "dp", axis=1, tiled=True),
+        "expert_down": lax.all_gather(expert_down, "dp", axis=1, tiled=True),
+    }
+
+    def eight(parts):
+        block = jnp.concatenate([p.reshape(-1, p.shape[-1]) for p in parts], axis=0)
+        return jnp.pad(block, ((0, 8 - block.shape[0]), (0, 0)))
+
+    conv_par = eight([taps, bias])
+    chan_par = eight([gain_here, jnp.repeat(skip_here, HP)])
+    head_par = jnp.pad(eight([dt_here, -jnp.exp(log_here)]), ((0, 0), (0, 128 - heads)))
+    x_own = [tokens[m].astype(f32) for m in each]
+    masks, allowed, mamba_kept, mix_kept, hidden_one = [], [], [], [], []
+    proj_all, cot_all = [], []
+    for m in each:
+        rows_all = rows_in[m]
+        x_all = rows_all[:, :D].astype(f32)
+        marks = wide(rows_all[:, D : D + 2 * experts_total]) > 0.5
+        masks.append([marks[:, :experts_total], marks[:, experts_total:]])
+        seg_col = rows_all[:, D + 2 * experts_total :][:, :1].astype(f32)
+        seg_row = seg_col.reshape(n_tp, 1, length)
+        seg = seg_row[:, 0].astype(jnp.int32)
+        allowed.append(attn_mask(jnp.stack([seg[0], seg[n_tp // 2]])))
+
+        _, scale_x, mamba_in = rms_forward(x_all, gain_mamba)
+        total_rows = mamba_in.shape[0]
+        proj = nn(mamba_in, w_in_here, bf16)
+        dt_raw = nn(mamba_in, w_dt_here)
+        proj_all.append(proj)
+        cot, _ = fence(cotangent[m], proj)
+        cot_all.append(gather_rows(cot))
+        pars = (seg_col, seg_row, conv_par, chan_par, head_par)
+        gained, square = scan_forward(heads, length, proj, dt_raw, *pars)
+        partial = nt(gained, w_mix_t)
+        high = square.astype(bf16).astype(f32)
+        lane = lax.broadcasted_iota(jnp.int32, square.shape, 1)
+        extra = jnp.where(lane == 0, high, jnp.where(lane == 1, square - high, 0.0))
+        back = return_rows(jnp.concatenate([partial, extra], axis=1))
+        gate_scale = lax.rsqrt((back[:, D : D + 1] + back[:, D + 1 : D + 2]) / DI + epsilon)
+        mix_branch = back[:, :D] * gate_scale
+        hidden_one.append(x_own[m] + mix_branch)
+        mamba_kept.append((rows_all, scale_x[:length], mamba_in, (proj, dt_raw, *pars), gained))
+        mix_kept.append((mix_branch, gate_scale))
+
     attn_pack = jnp.concatenate(
         [
             by_owner(w_qkv[:, :q_all], 2),
@@ -489,75 +730,13 @@
         ],
         axis=2,
     ).transpose(1, 0, 2)
-    attn_pack, _ = fence(attn_pack, (w_m, moved_s))
+    attn_pack, _ = fence(attn_pack, hidden_one[0])
     attn_pack = lax.all_to_all(attn_pack, "core", split_axis=0, concat_axis=0, tiled=True)
     attn_w = lax.all_gather(attn_pack.reshape(2 * rows, -1), "z", axis=0, tiled=True)
     attn_w = lax.all_gather(attn_w, FS, axis=0, tiled=True)
     w_qkv_here = attn_w[:, : q_width + 2 * kv_width]
     w_out_t = attn_w[:, q_width + 2 * kv_width :]
 
-    moe_a = {
-        "router": router_full,
-        "shared_in": w_s[:, at + 3 * ff : at + 5 * ff],
-        "shared_down_t": w_s[:, at + 5 * ff :],
-        "expert_in": lax.all_gather(expert_in, "dp", axis=1, tiled=True),
-        "expert_down": lax.all_gather(expert_down, "dp", axis=1, tiled=True),
-    }
-
-    expert_ids = jnp.arange(experts_total, dtype=jnp.int32)
-    info_width = -(-(2 * experts_total + 1) // 128) * 128
-    each = range(micro)
-    x_own = [tokens[m].astype(f32) for m in each]
-    seg_all, masks, allowed, mamba_kept, mix_kept, hidden_one = [], [], [], [], [], []
-    for m in each:
-        seg_own = segments[m, 0]
-        hot = [
-            jnp.any(routes[b, m][:, :, None] == expert_ids, axis=1).astype(bf16) for b in range(2)
-        ]
-        info = lanes(hot + [seg_own[:, None].astype(bf16)], info_width)
-        x_info, _ = fence(jnp.concatenate([tokens[m], info], axis=1), moved_m)
-        rows_all = gather_rows(x_info)
-        x_all = rows_all[:, :D].astype(f32)
-        marks = wide(rows_all[:, D : D + 2 * experts_total]) > 0.5
-        masks.append([marks[:, :experts_total], marks[:, experts_total:]])
-        seg = rows_all[:, D + 2 * experts_total].astype(jnp.int32).reshape(n_tp, length)
-        seg_all.append(seg)
-        allowed.append(attn_mask(jnp.stack([seg[0], seg[n_tp // 2]])))
-
-        normed_x, scale_x, mamba_in = rms_forward(x_all, gain_mamba)
-        total_rows = mamba_in.shape[0]
-        proj = nn(mamba_in, w_in_here, bf16)
-        dt_raw = nn(mamba_in, w_dt_here)
-
-        def piece(p, d, cw, cb, db, al, sk, seg=seg):
-            return scan_piece(p, d, seg, cw, cb, db, al, sk, heads)
-
-        gated, pullback = jax.vjp(
-            piece,
-            proj.astype(f32).reshape(n_tp, length, in_width),
-            dt_raw.reshape(n_tp, length, heads),
-            taps,
-            bias,
-            dt_here,
-            log_here,
-            skip_here,
-        )
-        gated = gated.reshape(total_rows, chan)
-        gained = (gated * gain_here).astype(bf16)
-        partial = nt(gained, w_mix_t)
-        square = jnp.sum(gated * gated, axis=-1, keepdims=True)
-        high = square.astype(bf16).astype(f32)
-        extra = jnp.concatenate(
-            [high, square - high, jnp.zeros((total_rows, 126), f32)], axis=1
-        )
-        back = return_rows(jnp.concatenate([partial, extra], axis=1))
-        gate_scale = lax.rsqrt((back[:, D : D + 1] + back[:, D + 1 : D + 2]) / DI + epsilon)
-        mix_branch = back[:, :D] * gate_scale
-        hidden_one.append(x_own[m] + mix_branch)
-        mamba_kept.append((rows_all, scale_x[:length], mamba_in, pullback, gated, gained))
-        mix_kept.append((mix_branch, gate_scale))
-
-    cot_all = [gather_rows(cotangent[m]) for m in each]
     hidden_one[-1], cot_all = fence(hidden_one[-1], cot_all)
     one_kept, layer_one = [], []
     for m in each:
@@ -583,15 +762,24 @@
     def over_dp(g):
         return lax.psum_scatter(g, "dp", scatter_dimension=1, tiled=True)
 
+    saving = lax.axis_size("w") > 1
+
     def moe_stage(grads, kept_all, w, gain, *before):
+        grads = list(grads)
         backs, sides, own_rows = [], [], []
         for m in each:
             back, side = moe_backward(grads[m], kept_all[m][2], w, experts_total)
             backs.append(back)
             sides.append(side)
             own_rows.append(side[6][:length])
-        weights = moe_weight_grads(sides)
-        backs[-1], weights = lax.optimization_barrier((backs[-1], weights))
+            if saving:
+                newer = moe_weight_grads(sides[-1:])
+                hold = (back, newer, grads[m + 1 :])
+                backs[-1], newer, grads[m + 1 :] = lax.optimization_barrier(hold)
+                weights = newer if m == 0 else [a + b for a, b in zip(weights, newer)]
+        if not saving:
+            weights = moe_weight_grads(sides)
+            backs[-1], weights = lax.optimization_barrier((backs[-1], weights))
         backs[-1], before = fence(backs[-1], before)
         grad_gain = 0.0
         values, logits = [], []
@@ -654,7 +842,7 @@
     mamba_sides, mamba_back, mixes, own_normed = [], [], [], []
     for m in each:
         mix_branch, gate_scale = mix_kept[m]
-        x_rows, _, mamba_in, pullback, gated, gained = mamba_kept[m]
+        x_rows, _, mamba_in, scan_args, _ = mamba_kept[m]
         x_rows, _ = fence(x_rows, grad_one[m])
         x_rows = x_rows[:, :D].astype(f32)
         normed_x = x_rows * row_scale(x_rows)
@@ -664,24 +852,19 @@
         extra = lanes(split_two(gate_scale) + split_two(mean_term), 128)
         rows_all = gather_rows(jnp.concatenate([grad_mix, extra], axis=1))
         mix_all = rows_all[:, :D]
-        extra = rows_all[:, D:].astype(f32)
-        scale_all = extra[:, 0:1] + extra[:, 1:2]
-        mean_all = extra[:, 2:3] + extra[:, 3:4]
+        extra_all = rows_all[:, D:]
+        scale_all = extra_all[:, 0:1].astype(f32) + extra_all[:, 1:2].astype(f32)
         scaled_mix = (mix_all.astype(f32) * scale_all).astype(bf16)
         mixes.append(scaled_mix)
         if m == micro - 1:
-            g_mix = tn_sum([(x, k[5]) for x, k in zip(mixes, mamba_kept)])
+            g_mix = tn_sum([(x, k[4]) for x, k in zip(mixes, mamba_kept)])
             mix_all, g_mix = fence(mix_all, g_mix)
-        grad_gated = nn(mix_all, w_mix_t, bf16).astype(f32)
-        norm_gated = gated * scale_all
-        grad_gate_norm = jnp.sum(grad_gated * norm_gated, axis=0)
-        grad_rows = scale_all * (grad_gated * gain_here - norm_gated * mean_all)
-        pulled = pullback(grad_rows.reshape(n_tp, length, chan))
-        grad_proj = pulled[0].reshape(-1, in_width).astype(bf16)
-        grad_step = pulled[1].reshape(-1, heads).astype(bf16)
+        grad_gated = nn(mix_all, w_mix_t, bf16)
+        grad_proj, grad_step, *grads = scan_backward(
+            heads, length, *scan_args, grad_gated, extra_all
+        )
         mamba_sides.append((mamba_in, grad_proj, grad_step))
-        grads = (*pulled[2:], grad_gate_norm)
-        small = grads if small is None else tuple(a + b for a, b in zip(small, grads))
+        small = grads if small is None else [a + b for a, b in zip(small, grads)]
         total = nt(grad_proj, w_in_here) + nt(grad_step, w_dt_here)
         gains[0] = gains[0] + jnp.sum(total * normed_x, axis=0)
         mamba_back.append(return_rows(total))
@@ -701,7 +884,7 @@
     out_mix = owned(g_s[:, :, :chan]).T
 
     g_proj = tn_sum([(s[0], s[1]) for s in mamba_sides])
-    g_step = tn_sum([(s[0], s[2]) for s in mamba_sides])
+    g_step = tn_sum([(s[0], s[2]) for s in mamba_sides])[:, :heads]
     g_proj, sum_in_m = fence(g_proj, sum_in_m)
     out_expert_in = sum_in_a.astype(f32)
     out_expert_down = sum_down_a.astype(f32)
@@ -714,13 +897,16 @@
         grad_values, _ = rms_backward(mamba_back[m], own_normed[m], scale_x, gain_mamba)
         grads_in.append(grad_one[m] + grad_values)
 
-    g_taps, g_bias, g_dt, g_log, g_skip, g_gate = small
+    conv_sums, chan_sums, head_sums = small
+    g_gate = chan_sums[0]
+    g_skip = jnp.sum(chan_sums[1].reshape(heads, HP), axis=1)
+    head_grad = jnp.stack([head_sums[0, :heads], head_sums[1, :heads], g_skip])
 
     def spread(part, width):
         zeros = jnp.zeros(part.shape[:-1] + (width,), f32)
         return lax.dynamic_update_slice_in_dim(zeros, part[..., :chan], slot * chan, axis=-1)
 
-    conv_grad = jnp.concatenate([g_bias[None], g_taps], axis=0)
+    conv_grad = jnp.concatenate([conv_sums[CK : CK + 1], conv_sums[:CK]], axis=0)
     conv_grad = spread(conv_grad, conv_total) + jnp.pad(conv_grad[:, chan:], ((0, 0), (DI, 0)))
     conv_grad = conv_grad.reshape(CK + 1, n_all, conv_here).transpose(1, 0, 2).reshape(n_all, -1)
     vec_grad = jnp.concatenate([spread(g_gate, DI).reshape(n_all, gate_here), conv_grad], axis=1)
@@ -745,23 +931,15 @@
     out_conv_b = vec[gate_here : gate_here + conv_here]
     out_conv_w = vec[gate_here + conv_here : vec_len].reshape(CK, conv_here)
 
-    head_grad = jnp.pad(jnp.stack([g_dt, g_log, g_skip]), ((0, 0), (0, 128 - heads)))[None]
-    for axis in ("dp", "w"):
-        own = head_grad
-        for s in range(1, lax.axis_size(axis)):
-            head_grad = head_grad + lax.ppermute(own, axis, ring(s, axis))
-    for axis in ("z", "core"):
-        n = lax.axis_size(axis)
-        here = lax.axis_index(axis)
-        parts = [head_grad] + [lax.ppermute(head_grad, axis, ring(s, axis)) for s in range(1, n)]
-        ordered = 0.0
-        for s, part in enumerate(parts):
-            at_slot = jnp.arange(n)[:, None, None, None] == (here - s) % n
-            ordered = ordered + jnp.where(at_slot, part[None], 0.0)
-        head_grad = ordered.reshape((-1,) + ordered.shape[2:]) if axis == "z" else jnp.moveaxis(
-            ordered, 0, 1
-        ).reshape((-1,) + ordered.shape[2:])
-    head_grad = head_grad[:, :, :heads].transpose(1, 0, 2).reshape(3, MH)
+    head_grad = lax.dynamic_update_slice(jnp.zeros((8, 128), f32), head_grad, (0, slot * heads))
+    for axis in ALL:
+        size = lax.axis_size(axis)
+        step = 1
+        while step < size:
+            pairs = [(i, i ^ step) for i in range(size)]
+            head_grad = head_grad + send(head_grad, axis, pairs)
+            step *= 2
+    head_grad = head_grad[:3, :MH]
 
     cuts = (q_width, q_width + kv_width, q_width + 2 * kv_width)
     out_w_qkv = jnp.concatenate(

time: 1370 us -> 1290 us (0.942)
  waiting for transfers between devices: 343 us -> 466 us
  local copies, waits for them, and re-layouts: 241 us -> 142 us
  other arithmetic: 161 us -> 110 us
  matrix products: 329 us -> 279 us
  blocking collectives: 39.3 us -> 9.88 us
  Pallas kernels: 0 us -> 27.9 us
    ppermute x140 -> x145, waiting for transfers between devices: 247 us -> 298 us  [send(): return by_rows(lax.ppermute(by_rows(x), axis, pairs))]
    dot_general x16 -> x0, matrix products: 46.9 us -> none  [the longest x6 32 us: scan_piece(): scan = jnp.einsum('bhts,bshp->bthp', mix, inputs, precision=highest)]
    all_gather x1, waiting for transfers between devices: 0.01 us -> 36.5 us  [body(): lax.all_gather(expert_down, 'dp', axis=1, tiled=True)]
    reshape x12 -> x4, local copies, waits for them, and re-layouts: 30.1 us -> 0.17 us  [the longest x2 0.16 us: body(): seg_row = seg_col.reshape(n_tp, 1, length)]
    all_to_all x1 -> x0, blocking collectives: 29.4 us -> none  [moved_columns(): moved = lax.all_to_all(packed, TP, split_axis=0, concat_axis=0, tiled=True)]
    pallas_call x0 -> x4, Pallas kernels: none -> 27.9 us  [the longest x2 18.3 us: scan_backward(): pl.pallas_call(functools.partial(scan_backward_kernel, heads), grid=(tota...]
    reduce_sum x8 -> x1, other arithmetic: 19 us -> 0.12 us  [body(): g_skip = jnp.sum(chan_sums[1].reshape(heads, HP), axis=1)]
    ppermute x140 -> x145, starting transfers between devices: 189 us -> 207 us  [send(): return by_rows(lax.ppermute(by_rows(x), axis, pairs))]
  transfers between devices with their start and end apart: 166 -> 165, of which waited for: 49 -> 60; matrix products, arithmetic and copies ran while one was open for 51% -> 37% of each run, Pallas kernels for 0% -> 2%
where the time goes in v3:
time: 1290 us; the launch traced here: 1280 us
  waiting for transfers between devices  466 us (36%)
  matrix products  279 us (22%)
  starting transfers between devices  227 us (18%)
  local copies, waits for them, and re-layouts  142 us (11%)
  other arithmetic  110 us (9%)
  Pallas kernels  27.9 us (2%)
  between operations  20.2 us (2%)
    ppermute x145, waiting for transfers between devices, send(): return by_rows(lax.ppermute(by_rows(x), axis, pairs))  298 us
    dot_general x114, matrix products, dot(): r = lax.dot_general(a, b, (dims, ((), ())), preferred_element_type=f32)  270 us
    ppermute x145, starting transfers between devices, send(): return by_rows(lax.ppermute(by_rows(x), axis, pairs))  207 us
    unnamed x742, local copies, waits for them, and re-layouts  76.3 us
    all_gather x1, waiting for transfers between devices, body(): lax.all_gather(expert_down, 'dp', axis=1, tiled=True)  36.5 us
    all_gather x1, waiting for transfers between devices, body(): lax.all_gather(attn_pack.reshape(2 * rows, -1), 'z', axis=0, tiled=True)  36.3 us
  transfers between devices with their start and end apart: 165, of which 60 were waited for; matrix products, arithmetic and copies ran while one was open for 37% of the time, Pallas kernels for 2%

profile of v3, /device:TPU:0, one launch (start us, length us, event | category | flops | bytes accessed | tf_op | source)
XLA Modules:
  0.0 1281.6 jit_solution(14155295369109530043)
XLA Ops:
  11.2 6.5 all-to-all-start
  17.8 22.9 %all-to-all-done = bf16[8,48,1152]{2,1,0:T(8,128)(2,1)S(1)} async-done(((bf16[8,48,1152]{2,1,0:T(8,128)(2,1)}), bf16[8,48,1152]{2,1,0:T(8,128)(2,1)S(1)}, u32[]{:S(2)}, u32[]{:S(2)}) %all-to-all-start) | async-done | bytes 884768 | tf_op jit(solution)/shard_map/all_to_all | solution.py:591
  46.6 6.2 collective-permute-done
  52.8 7.8 collective-permute-done.1
  63.6 5.1 all-to-all-start.1
  76.2 16.9 %collective-permute-done.35 = bf16[64,1664]{1,0:T(8,128)(2,1)S(1)} collective-permute-done((bf16[64,1664]{1,0:T(8,128)(2,1)S(1)}, bf16[64,1664]{1,0:T(8,128)(2,1)S(1)}, u32[]{:S(2)}, u32[]{:S(2)}) %collective-permute-start.35) | collective-permute-done | bytes 213024 | tf_op jit(solution)/shard_map/ppermute | solution.py:93
  93.1 12.8 %collective-permute-done.36 = bf16[64,1664]{1,0:T(8,128)(2,1)S(1)} collective-permute-done((bf16[64,1664]{1,0:T(8,128)(2,1)S(1)}, bf16[64,1664]{1,0:T(8,128)(2,1)S(1)}, u32[]{:S(2)}, u32[]{:S(2)}) %collective-permute-start.36) | collective-permute-done | bytes 213024 | tf_op jit(solution)/shard_map/ppermute | solution.py:93
  134.4 4.8 scan_forward.3
  141.8 4.8 scan_forward.2
  147.7 12.2 all-gather.11.cloned.1.call-done
  181.7 16.8 %collective-permute-done.44 = bf16[64,1664]{1,0:T(8,128)(2,1)S(1)} collective-permute-done((bf16[64,1664]{1,0:T(8,128)(2,1)S(1)}, bf16[64,1664]{1,0:T(8,128)(2,1)S(1)}, u32[]{:S(2)}, u32[]{:S(2)}) %collective-permute-start.44) | collective-permute-done | bytes 213024 | tf_op jit(solution)/shard_map/ppermute | solution.py:93
  199.5 12.3 collective-permute-done.9
  213.7 4.8 all_to_all.30
  219.8 36.3 %all-gather.17.cloned.1.call-done = bf16[384,2048]{1,0:T(8,128)(2,1)} async-done(((bf16[96,2048]{1,0:T(8,128)(2,1)}), bf16[384,2048]{1,0:T(8,128)(2,1)}) %all-gather.17.cloned.1.call-update) | async-done | bytes 1572880 | tf_op jit(solution)/shard_map/all_gather | solution.py:735
  266.7 5.2 collective-permute-done.53
  271.9 7.7 collective-permute-start.47
  279.6 6.8 collective-permute-done.54
  286.4 4.7 collective-permute-start.48
  311.6 7.5 collective-permute-done.61
  319.1 6.0 collective-permute-start.13
  325.9 9.8 collective-permute-done.12
  348.6 5.5 fusion.533
  357.6 14.9 %all-gather.15.cloned.1.call-done = bf16[2,512,1536]{2,1,0:T(8,128)(2,1)} async-done(((bf16[2,128,1536]{2,1,0:T(8,128)(2,1)}), bf16[2,512,1536]{2,1,0:T(8,128)(2,1)}) %all-gather.15.cloned.1.call-update) | async-done | bytes 3145744 | tf_op jit(solution)/shard_map/all_gather | solution.py:669
  401.5 12.0 collective-permute-done.69
  413.8 14.8 %collective-permute-done.20 = bf16[64,1536]{1,0:T(8,128)(2,1)S(1)} collective-permute-done((bf16[64,1536]{1,0:T(8,128)(2,1)S(1)}, bf16[64,1536]{1,0:T(8,128)(2,1)S(1)}, u32[]{:S(2)}, u32[]{:S(2)}) %collective-permute-start.20) | collective-permute-done | bytes 196640 | tf_op jit(solution)/shard_map/ppermute | solution.py:93
  430.8 13.6 %all-gather.19.cloned.1.call-done = bf16[1536,2048]{1,0:T(8,128)(2,1)} async-done(((bf16[384,2048]{1,0:T(8,128)(2,1)}), bf16[1536,2048]{1,0:T(8,128)(2,1)}) %all-gather.19.cloned.1.call-update) | async-done | bytes 6291472 | tf_op jit(solution)/shard_map/all_gather | solution.py:736
  471.4 8.9 collective-permute-start.74
  481.0 11.0 collective-permute-start.75
  504.6 11.9 all-gather.21.cloned.1.call-done
  516.5 5.6 fusion.550
  525.8 36.5 %all-gather.23.cloned.1.call-done = bf16[2,512,1536]{2,1,0:T(8,128)(2,1)} async-done(((bf16[2,128,1536]{2,1,0:T(8,128)(2,1)}), bf16[2,512,1536]{2,1,0:T(8,128)(2,1)}) %all-gather.23.cloned.1.call-update) | async-done | bytes 3145744 | tf_op jit(solution)/shard_map/all_gather | solution.py:681
  635.7 4.6 fusion.167
  652.3 6.3 fusion.3
  671.5 6.1 pad_maximum_fusion
  688.6 13.3 %collective-permute-done.114 = bf16[64,1664]{1,0:T(8,128)(2,1)S(1)} collective-permute-done((bf16[64,1664]{1,0:T(8,128)(2,1)S(1)}, bf16[64,1664]{1,0:T(8,128)(2,1)S(1)}, u32[]{:S(2)}, u32[]{:S(2)}) %collective-permute-start.114) | collective-permute-done | bytes 213024 | tf_op jit(solution)/shard_map/ppermute | solution.py:93
  713.2 5.9 collective-permute-done.85
  719.1 21.2 %collective-permute-start.34 = (bf16[64,1536]{1,0:T(8,128)(2,1)S(1)}, bf16[64,1536]{1,0:T(8,128)(2,1)S(1)}, u32[]{:S(2)}, u32[]{:S(2)}) collective-permute-start(bf16[64,1536]{1,0:T(8,128)(2,1)S(1)} %get-tuple-element.536), channel_id=1, source_target_pairs={{0,2},{2,4},{4,6},{6,0},{1,3},{3,5},{5,7},{7,1},{8,10},{10,12},{12... | collective-permute-start | bytes 589832 | tf_op jit(solution)/shard_map/ppermute | solution.py:93
  751.0 8.9 collective-permute-done.82
  797.4 8.7 copy.1140
  826.2 9.1 collective-permute-start.91
  835.3 9.4 collective-permute-start.92
  845.6 5.3 collective-permute-done.91
  867.7 4.9 multiply_convert_fusion.9
  872.8 4.3 multiply_convert_fusion.23
  877.2 4.9 multiply_convert_fusion.21
  920.7 6.1 pad_maximum_fusion.2
  929.0 6.0 collective-permute-start.126
  940.7 12.9 %collective-permute-done.127 = bf16[64,1664]{1,0:T(8,128)(2,1)S(1)} collective-permute-done((bf16[64,1664]{1,0:T(8,128)(2,1)S(1)}, bf16[64,1664]{1,0:T(8,128)(2,1)S(1)}, u32[]{:S(2)}, u32[]{:S(2)}) %collective-permute-start.127) | collective-permute-done | bytes 213024 | tf_op jit(solution)/shard_map/ppermute | solution.py:93
  958.9 4.7 convolution_add_fusion.21
  982.4 4.3 collective-permute-done.100
  990.1 9.8 collective-permute-done.99
  1016.2 4.1 collective-permute-done.129
  1021.0 8.3 collective-permute-done.130
  1036.0 32.1 %collective-permute-done.102 = bf16[64,1664]{1,0:T(8,128)(2,1)S(1)} collective-permute-done((bf16[64,1664]{1,0:T(8,128)(2,1)S(1)}, bf16[64,1664]{1,0:T(8,128)(2,1)S(1)}, u32[]{:S(2)}, u32[]{:S(2)}) %collective-permute-start.102) | collective-permute-done | bytes 213024 | tf_op jit(solution)/shard_map/ppermute | solution.py:93
  1090.8 9.2 scan_backward.3
  1102.4 9.2 scan_backward.2
  1116.5 6.2 multiply_reduce_fusion
  1122.8 4.7 multiply_reduce_fusion.1
  1139.5 8.3 concatenate.236
  1159.3 8.8 collective-permute-start.142
  1194.4 8.7 collective-permute-start.111
  1203.6 5.1 all_to_all.31
  1215.2 18.0 %collective-permute-done.110 = bf16[64,1536]{1,0:T(8,128)(2,1)} collective-permute-done((bf16[64,1536]{1,0:T(8,128)(2,1)}, bf16[64,1536]{1,0:T(8,128)(2,1)}, u32[]{:S(2)}, u32[]{:S(2)}) %collective-permute-start.110) | collective-permute-done | bytes 196640 | tf_op jit(solution)/shard_map/ppermute | solution.py:93
  1255.5 12.7 all-to-all-done.3
  (1541 shorter events, 616.4 us)
Async XLA Ops:
  11.2 29.5 %all-to-all-start = ((bf16[8,48,1152]{2,1,0:T(8,128)(2,1)}), bf16[8,48,1152]{2,1,0:T(8,128)(2,1)S(1)}, u32[]{:S(2)}, u32[]{:S(2)}) async-start(bf16[8,48,1152]{2,1,0:T(8,128)(2,1)} %copy.974), calls=%async_computation | async-start | bytes 1769472 | tf_op jit(solution)/shard_map/all_to_all | solution.py:591
  17.6 105.0 %all-gather.9.cloned.1.call-start = ((), (), s32[]{:S(2)}) async-start(), calls=%async_computation.14 | async-start | bytes 4423680 | tf_op jit(solution)/shard_map/all_gather | solution.py:595
  63.6 45.0 %all-to-all-start.1 = ((bf16[8,48,1152]{2,1,0:T(8,128)(2,1)}), bf16[8,48,1152]{2,1,0:T(8,128)(2,1)S(1)}, u32[]{:S(2)}, u32[]{:S(2)}) async-start(bf16[8,48,1152]{2,1,0:T(8,128)(2,1)} %copy.977), calls=%async_computation.1 | async-start | bytes 1769472 | tf_op jit(solution)/shard_map/all_to_all | solution.py:591
  68.7 91.2 %all-gather.11.cloned.1.call-start = ((), (), s32[]{:S(2)}) async-start(), calls=%async_computation.15 | async-start | bytes 4423680 | tf_op jit(solution)/shard_map/all_gather | solution.py:595
  71.9 34.0 %collective-permute-start.36 = (bf16[64,1664]{1,0:T(8,128)(2,1)S(1)}, bf16[64,1664]{1,0:T(8,128)(2,1)S(1)}, u32[]{:S(2)}, u32[]{:S(2)}) collective-permute-start(bf16[64,1664]{1,0:T(8,128)(2,1)S(1)} %concatenate.199), channel_id=1, source_target_pairs={{0,4},{2,6},{4,0},{6,2},{1,5},{3,7},{5,1},{7,3},{8,12},{10,14},{12... | collective-permute-start | bytes 638984 | tf_op jit(solution)/shard_map/ppermute | solution.py:93
  74.0 31.9 %collective-permute-start.37 = (bf16[64,1664]{1,0:T(8,128)(2,1)S(1)}, bf16[64,1664]{1,0:T(8,128)(2,1)S(1)}, u32[]{:S(2)}, u32[]{:S(2)}) collective-permute-start(bf16[64,1664]{1,0:T(8,128)(2,1)S(1)} %concatenate.199), channel_id=1, source_target_pairs={{0,6},{2,0},{4,2},{6,4},{1,7},{3,1},{5,3},{7,5},{8,14},{10,8},{12,... | collective-permute-start | bytes 638984 | tf_op jit(solution)/shard_map/ppermute | solution.py:93
  75.5 34.3 %collective-permute-start.38 = (bf16[64,1664]{1,0:T(8,128)(2,1)S(1)}, bf16[64,1664]{1,0:T(8,128)(2,1)}, u32[]{:S(2)}, u32[]{:S(2)}) collective-permute-start(bf16[64,1664]{1,0:T(8,128)(2,1)S(1)} %concatenate.199), channel_id=1, source_target_pairs={{0,1},{1,0},{2,3},{3,2},{4,5},{5,4},{6,7},{7,6},{8,9},{9,8},{10,11... | collective-permute-start | bytes 638984 | tf_op jit(solution)/shard_map/ppermute | solution.py:93
  109.5 146.6 %all-gather.17.cloned.1.call-start = ((), (), s32[]{:S(2)}) async-start(), calls=%async_computation.18 | async-start | bytes 1966080 | tf_op jit(solution)/shard_map/all_gather | solution.py:735
  174.6 23.9 %collective-permute-start.44 = (bf16[64,1664]{1,0:T(8,128)(2,1)S(1)}, bf16[64,1664]{1,0:T(8,128)(2,1)S(1)}, u32[]{:S(2)}, u32[]{:S(2)}) collective-permute-start(bf16[64,1664]{1,0:T(8,128)(2,1)S(1)} %get-tuple-element.516), channel_id=1, source_target_pairs={{0,4},{2,6},{4,0},{6,2},{1,5},{3,7},{5,1},{7,3},{8,12},{10,14},{12... | collective-permute-start | bytes 638984 | tf_op jit(solution)/shard_map/ppermute | solution.py:93
  174.6 23.9 %collective-permute-start.45 = (bf16[64,1664]{1,0:T(8,128)(2,1)S(1)}, bf16[64,1664]{1,0:T(8,128)(2,1)S(1)}, u32[]{:S(2)}, u32[]{:S(2)}) collective-permute-start(bf16[64,1664]{1,0:T(8,128)(2,1)S(1)} %get-tuple-element.515), channel_id=1, source_target_pairs={{0,2},{2,4},{4,6},{6,0},{1,3},{3,5},{5,7},{7,1},{8,10},{10,12},{12... | collective-permute-start | bytes 638984 | tf_op jit(solution)/shard_map/ppermute | solution.py:93
  176.0 23.5 %collective-permute-start.10 = (bf16[64,1664]{1,0:T(8,128)(2,1)S(1)}, bf16[64,1664]{1,0:T(8,128)(2,1)S(1)}, u32[]{:S(2)}, u32[]{:S(2)}) collective-permute-start(bf16[64,1664]{1,0:T(8,128)(2,1)S(1)} %get-tuple-element.512), channel_id=1, source_target_pairs={{0,2},{2,4},{4,6},{6,0},{1,3},{3,5},{5,7},{7,1},{8,10},{10,12},{12... | collective-permute-start | bytes 638984 | tf_op jit(solution)/shard_map/ppermute | solution.py:93
  180.3 31.6 %collective-permute-start.9 = (bf16[64,1664]{1,0:T(8,128)(2,1)S(1)}, bf16[64,1664]{1,0:T(8,128)(2,1)S(1)}, u32[]{:S(2)}, u32[]{:S(2)}) collective-permute-start(bf16[64,1664]{1,0:T(8,128)(2,1)S(1)} %get-tuple-element.513), channel_id=1, source_target_pairs={{0,4},{2,6},{4,0},{6,2},{1,5},{3,7},{5,1},{7,3},{8,12},{10,14},{12... | collective-permute-start | bytes 638984 | tf_op jit(solution)/shard_map/ppermute | solution.py:93
  218.5 130.1 %all-gather.13.cloned.1.call-start = ((), (), s32[]{:S(2)}) async-start(), calls=%async_computation.16 | async-start | bytes 7864320 | tf_op jit(solution)/shard_map/all_gather | solution.py:668
  219.1 153.4 %all-gather.15.cloned.1.call-start = ((), (), s32[]{:S(2)}) async-start(), calls=%async_computation.17 | async-start | bytes 3932160 | tf_op jit(solution)/shard_map/all_gather | solution.py:669
  219.7 224.7 %all-gather.19.cloned.1.call-start = ((), (), s32[]{:S(2)}) async-start(), calls=%async_computation.19 | async-start | bytes 7864320 | tf_op jit(solution)/shard_map/all_gather | solution.py:736
  256.1 260.4 %all-gather.21.cloned.1.call-start = ((), (), s32[]{:S(2)}) async-start(), calls=%async_computation.20 | async-start | bytes 7864320 | tf_op jit(solution)/shard_map/all_gather | solution.py:680
  256.9 305.5 %all-gather.23.cloned.1.call-start = ((), (), s32[]{:S(2)}) async-start(), calls=%async_computation.21 | async-start | bytes 3932160 | tf_op jit(solution)/shard_map/all_gather | solution.py:681
  257.6 555.1 %reduce-scatter.13.cloned.1.call-start = ((), (), s32[]{:S(2)}) async-start(), calls=%async_computation.22 | async-start | bytes 7864320 | tf_op jit(solution)/shard_map/reduce_scatter | solution.py:763
  262.7 23.7 %collective-permute-start.54 = (bf16[64,1536]{1,0:T(8,128)(2,1)S(1)}, bf16[64,1536]{1,0:T(8,128)(2,1)S(1)}, u32[]{:S(2)}, u32[]{:S(2)}) collective-permute-start(bf16[64,1536]{1,0:T(8,128)(2,1)S(1)} %get-tuple-element.97), channel_id=1, source_target_pairs={{0,4},{2,6},{4,0},{6,2},{1,5},{3,7},{5,1},{7,3},{8,12},{10,14},{12... | collective-permute-start | bytes 589832 | tf_op jit(solution)/shard_map/ppermute | solution.py:93
  264.1 27.1 %collective-permute-start.55 = (bf16[64,1536]{1,0:T(8,128)(2,1)S(1)}, bf16[64,1536]{1,0:T(8,128)(2,1)S(1)}, u32[]{:S(2)}, u32[]{:S(2)}) collective-permute-start(bf16[64,1536]{1,0:T(8,128)(2,1)S(1)} %get-tuple-element.97), channel_id=1, source_target_pairs={{0,6},{2,0},{4,2},{6,4},{1,7},{3,1},{5,3},{7,5},{8,14},{10,8},{12,... | collective-permute-start | bytes 589832 | tf_op jit(solution)/shard_map/ppermute | solution.py:93
  266.5 24.8 %collective-permute-start.56 = (bf16[64,1536]{1,0:T(8,128)(2,1)S(1)}, bf16[64,1536]{1,0:T(8,128)(2,1)S(1)}, u32[]{:S(2)}, u32[]{:S(2)}) collective-permute-start(bf16[64,1536]{1,0:T(8,128)(2,1)S(1)} %get-tuple-element.97), channel_id=1, source_target_pairs={{0,1},{1,0},{2,3},{3,2},{4,5},{5,4},{6,7},{7,6},{8,9},{9,8},{10,11... | collective-permute-start | bytes 589832 | tf_op jit(solution)/shard_map/ppermute | solution.py:93
  266.5 25.4 %collective-permute-start.46 = (bf16[64,1536]{1,0:T(8,128)(2,1)S(1)}, bf16[64,1536]{1,0:T(8,128)(2,1)S(1)}, u32[]{:S(2)}, u32[]{:S(2)}) collective-permute-start(bf16[64,1536]{1,0:T(8,128)(2,1)S(1)} %get-tuple-element.96), channel_id=1, source_target_pairs={{0,2},{2,4},{4,6},{6,0},{1,3},{3,5},{5,7},{7,1},{8,10},{10,12},{12... | collective-permute-start | bytes 589832 | tf_op jit(solution)/shard_map/ppermute | solution.py:93
  271.9 24.2 %collective-permute-start.47 = (bf16[64,1536]{1,0:T(8,128)(2,1)S(1)}, bf16[64,1536]{1,0:T(8,128)(2,1)S(1)}, u32[]{:S(2)}, u32[]{:S(2)}) collective-permute-start(bf16[64,1536]{1,0:T(8,128)(2,1)S(1)} %get-tuple-element.96), channel_id=1, source_target_pairs={{0,4},{2,6},{4,0},{6,2},{1,5},{3,7},{5,1},{7,3},{8,12},{10,14},{12... | collective-permute-start | bytes 589832 | tf_op jit(solution)/shard_map/ppermute | solution.py:93
  310.7 25.0 %collective-permute-start.12 = (bf16[64,1536]{1,0:T(8,128)(2,1)S(1)}, bf16[64,1536]{1,0:T(8,128)(2,1)S(1)}, u32[]{:S(2)}, u32[]{:S(2)}) collective-permute-start(bf16[64,1536]{1,0:T(8,128)(2,1)S(1)} %get-tuple-element.444), channel_id=1, source_target_pairs={{0,4},{2,6},{4,0},{6,2},{1,5},{3,7},{5,1},{7,3},{8,12},{10,14},{12... | collective-permute-start | bytes 589832 | tf_op jit(solution)/shard_map/ppermute | solution.py:93
  398.9 29.7 %collective-permute-start.20 = (bf16[64,1536]{1,0:T(8,128)(2,1)S(1)}, bf16[64,1536]{1,0:T(8,128)(2,1)S(1)}, u32[]{:S(2)}, u32[]{:S(2)}) collective-permute-start(bf16[64,1536]{1,0:T(8,128)(2,1)S(1)} %get-tuple-element.540), channel_id=1, source_target_pairs={{0,4},{2,6},{4,0},{6,2},{1,5},{3,7},{5,1},{7,3},{8,12},{10,14},{12... | collective-permute-start | bytes 589832 | tf_op jit(solution)/shard_map/ppermute | solution.py:93
  400.0 28.6 %collective-permute-start.21 = (bf16[64,1536]{1,0:T(8,128)(2,1)S(1)}, bf16[64,1536]{1,0:T(8,128)(2,1)S(1)}, u32[]{:S(2)}, u32[]{:S(2)}) collective-permute-start(bf16[64,1536]{1,0:T(8,128)(2,1)S(1)} %get-tuple-element.539), channel_id=1, source_target_pairs={{0,2},{2,4},{4,6},{6,0},{1,3},{3,5},{5,7},{7,1},{8,10},{10,12},{12... | collective-permute-start | bytes 589832 | tf_op jit(solution)/shard_map/ppermute | solution.py:93
  466.2 26.5 %collective-permute-start.26 = (bf16[64,1536]{1,0:T(8,128)(2,1)S(1)}, bf16[64,1536]{1,0:T(8,128)(2,1)S(1)}, u32[]{:S(2)}, u32[]{:S(2)}) collective-permute-start(bf16[64,1536]{1,0:T(8,128)(2,1)S(1)} %get-tuple-element.436), channel_id=1, source_target_pairs={{0,6},{2,0},{4,2},{6,4},{1,7},{3,1},{5,3},{7,5},{8,14},{10,8},{12,... | collective-permute-start | bytes 589832 | tf_op jit(solution)/shard_map/ppermute | solution.py:93
  467.6 25.8 %collective-permute-start.27 = (bf16[64,1536]{1,0:T(8,128)(2,1)S(1)}, bf16[64,1536]{1,0:T(8,128)(2,1)S(1)}, u32[]{:S(2)}, u32[]{:S(2)}) collective-permute-start(bf16[64,1536]{1,0:T(8,128)(2,1)S(1)} %get-tuple-element.436), channel_id=1, source_target_pairs={{0,1},{1,0},{2,3},{3,2},{4,5},{5,4},{6,7},{7,6},{8,9},{9,8},{10,11... | collective-permute-start | bytes 589832 | tf_op jit(solution)/shard_map/ppermute | solution.py:93
  467.6 27.0 %collective-permute-start.73 = (bf16[64,1536]{1,0:T(8,128)(2,1)S(1)}, bf16[64,1536]{1,0:T(8,128)(2,1)}, u32[]{:S(2)}, u32[]{:S(2)}) collective-permute-start(bf16[64,1536]{1,0:T(8,128)(2,1)S(1)} %get-tuple-element.585), channel_id=1, source_target_pairs={{0,2},{2,4},{4,6},{6,0},{1,3},{3,5},{5,7},{7,1},{8,10},{10,12},{12... | collective-permute-start | bytes 589832 | tf_op jit(solution)/shard_map/ppermute | solution.py:93
  471.4 24.9 %collective-permute-start.74 = (bf16[64,1536]{1,0:T(8,128)(2,1)S(1)}, bf16[64,1536]{1,0:T(8,128)(2,1)}, u32[]{:S(2)}, u32[]{:S(2)}) collective-permute-start(bf16[64,1536]{1,0:T(8,128)(2,1)S(1)} %get-tuple-element.585), channel_id=1, source_target_pairs={{0,4},{2,6},{4,0},{6,2},{1,5},{3,7},{5,1},{7,3},{8,12},{10,14},{12... | collective-permute-start | bytes 589832 | tf_op jit(solution)/shard_map/ppermute | solution.py:93
  497.2 87.7 %collective-permute-start.77 = (bf16[64,1536]{1,0:T(8,128)(2,1)}, bf16[64,1536]{1,0:T(8,128)(2,1)}, u32[]{:S(2)}, u32[]{:S(2)}) collective-permute-start(bf16[64,1536]{1,0:T(8,128)(2,1)} %collective-permute-done.73), channel_id=1, source_target_pairs={{0,1},{1,0},{2,3},{3,2},{4,5},{5,4},{6,7},{7,6},{8,9},{9,8},{10,11... | collective-permute-start | bytes 589832 | tf_op jit(solution)/shard_map/ppermute | solution.py:93
  498.7 87.1 %collective-permute-start.78 = (bf16[64,1536]{1,0:T(8,128)(2,1)}, bf16[64,1536]{1,0:T(8,128)(2,1)}, u32[]{:S(2)}, u32[]{:S(2)}) collective-permute-start(bf16[64,1536]{1,0:T(8,128)(2,1)} %collective-permute-done.74), channel_id=1, source_target_pairs={{0,1},{1,0},{2,3},{3,2},{4,5},{5,4},{6,7},{7,6},{8,9},{9,8},{10,11... | collective-permute-start | bytes 589832 | tf_op jit(solution)/shard_map/ppermute | solution.py:93
  498.9 88.0 %collective-permute-start.79 = (bf16[64,1536]{1,0:T(8,128)(2,1)}, bf16[64,1536]{1,0:T(8,128)(2,1)}, u32[]{:S(2)}, u32[]{:S(2)}) collective-permute-start(bf16[64,1536]{1,0:T(8,128)(2,1)} %collective-permute-done.75), channel_id=1, source_target_pairs={{0,1},{1,0},{2,3},{3,2},{4,5},{5,4},{6,7},{7,6},{8,9},{9,8},{10,11... | collective-permute-start | bytes 589832 | tf_op jit(solution)/shard_map/ppermute | solution.py:93
  584.9 117.9 %collective-permute-start.31 = (bf16[256,1536]{1,0:T(8,128)(2,1)}, bf16[256,1536]{1,0:T(8,128)(2,1)}, u32[]{:S(2)}, u32[]{:S(2)}) collective-permute-start(bf16[256,1536]{1,0:T(8,128)(2,1)} %slice.2261), channel_id=1, source_target_pairs={{0,1},{1,0},{2,3},{3,2},{4,5},{5,4},{6,7},{7,6},{8,9},{9,8},{10,11... | collective-permute-start | bytes 2359304 | tf_op jit(solution)/shard_map/ppermute | solution.py:93
  623.8 83.9 %collective-permute-start.80 = (bf16[256,1536]{1,0:T(8,128)(2,1)}, bf16[256,1536]{1,0:T(8,128)(2,1)}, u32[]{:S(2)}, u32[]{:S(2)}) collective-permute-start(bf16[256,1536]{1,0:T(8,128)(2,1)} %slice.2259), channel_id=1, source_target_pairs={{0,1},{1,0},{2,3},{3,2},{4,5},{5,4},{6,7},{7,6},{8,9},{9,8},{10,11... | collective-permute-start | bytes 2359304 | tf_op jit(solution)/shard_map/ppermute | solution.py:93
  651.7 26.0 %collective-permute-start.112 = (bf16[256,1664]{1,0:T(8,128)(2,1)}, bf16[256,1664]{1,0:T(8,128)(2,1)S(1)}, u32[]{:S(2)}, u32[]{:S(2)}) collective-permute-start(bf16[256,1664]{1,0:T(8,128)(2,1)} %slice.2254), channel_id=1, source_target_pairs={{0,1},{1,0},{2,3},{3,2},{4,5},{5,4},{6,7},{7,6},{8,9},{9,8},{10,11... | collective-permute-start | bytes 2555912 | tf_op jit(solution)/shard_map/ppermute | solution.py:93
  702.7 279.4 %reduce-scatter.25.cloned.1.call-start = ((), (), s32[]{:S(2)}) async-start(), calls=%async_computation.28 | async-start | bytes 7864320
  704.9 43.6 %collective-permute-start.32 = (bf16[64,1536]{1,0:T(8,128)(2,1)S(1)}, bf16[64,1536]{1,0:T(8,128)(2,1)S(1)}, u32[]{:S(2)}, u32[]{:S(2)}) collective-permute-start(bf16[64,1536]{1,0:T(8,128)(2,1)S(1)} %get-tuple-element.535), channel_id=1, source_target_pairs={{0,6},{2,0},{4,2},{6,4},{1,7},{3,1},{5,3},{7,5},{8,14},{10,8},{12,... | collective-permute-start | bytes 589832 | tf_op jit(solution)/shard_map/ppermute | solution.py:93
  705.0 46.0 %collective-permute-start.33 = (bf16[64,1536]{1,0:T(8,128)(2,1)S(1)}, bf16[64,1536]{1,0:T(8,128)(2,1)S(1)}, u32[]{:S(2)}, u32[]{:S(2)}) collective-permute-start(bf16[64,1536]{1,0:T(8,128)(2,1)S(1)} %get-tuple-element.537), channel_id=1, source_target_pairs={{0,4},{2,6},{4,0},{6,2},{1,5},{3,7},{5,1},{7,3},{8,12},{10,14},{12... | collective-permute-start | bytes 589832 | tf_op jit(solution)/shard_map/ppermute | solution.py:93
  711.7 32.1 %collective-permute-start.86 = (bf16[64,1664]{1,0:T(8,128)(2,1)S(1)}, bf16[64,1664]{1,0:T(8,128)(2,1)S(1)}, u32[]{:S(2)}, u32[]{:S(2)}) collective-permute-start(bf16[64,1664]{1,0:T(8,128)(2,1)S(1)} %get-tuple-element.507), channel_id=1, source_target_pairs={{0,4},{2,6},{4,0},{6,2},{1,5},{3,7},{5,1},{7,3},{8,12},{10,14},{12... | collective-permute-start | bytes 638984 | tf_op jit(solution)/shard_map/ppermute | solution.py:93
  713.2 30.6 %collective-permute-start.87 = (bf16[64,1664]{1,0:T(8,128)(2,1)S(1)}, bf16[64,1664]{1,0:T(8,128)(2,1)S(1)}, u32[]{:S(2)}, u32[]{:S(2)}) collective-permute-start(bf16[64,1664]{1,0:T(8,128)(2,1)S(1)} %get-tuple-element.506), channel_id=1, source_target_pairs={{0,2},{2,4},{4,6},{6,0},{1,3},{3,5},{5,7},{7,1},{8,10},{10,12},{12... | collective-permute-start | bytes 638984 | tf_op jit(solution)/shard_map/ppermute | solution.py:93
  719.1 31.9 %collective-permute-start.34 = (bf16[64,1536]{1,0:T(8,128)(2,1)S(1)}, bf16[64,1536]{1,0:T(8,128)(2,1)S(1)}, u32[]{:S(2)}, u32[]{:S(2)}) collective-permute-start(bf16[64,1536]{1,0:T(8,128)(2,1)S(1)} %get-tuple-element.536), channel_id=1, source_target_pairs={{0,2},{2,4},{4,6},{6,0},{1,3},{3,5},{5,7},{7,1},{8,10},{10,12},{12... | collective-permute-start | bytes 589832 | tf_op jit(solution)/shard_map/ppermute | solution.py:93
  806.1 176.1 %reduce-scatter.15.cloned.1.call-start = ((), (), s32[]{:S(2)}) async-start(), calls=%async_computation.23 | async-start | bytes 3932160 | tf_op jit(solution)/shard_map/reduce_scatter | solution.py:763
  812.6 326.8 %reduce-scatter.17.cloned.1.call-start = ((), (), s32[]{:S(2)}) async-start(), calls=%async_computation.24 | async-start | bytes 7864320 | tf_op jit(solution)/shard_map/reduce_scatter | solution.py:763
  819.2 25.6 %collective-permute-start.120 = (bf16[64,1536]{1,0:T(8,128)(2,1)S(1)}, bf16[64,1536]{1,0:T(8,128)(2,1)S(1)}, u32[]{:S(2)}, u32[]{:S(2)}) collective-permute-start(bf16[64,1536]{1,0:T(8,128)(2,1)S(1)} %get-tuple-element.427), channel_id=1, source_target_pairs={{0,6},{2,0},{4,2},{6,4},{1,7},{3,1},{5,3},{7,5},{8,14},{10,8},{12,... | collective-permute-start | bytes 589832 | tf_op jit(solution)/shard_map/ppermute | solution.py:93
  826.2 24.7 %collective-permute-start.91 = (bf16[64,1536]{1,0:T(8,128)(2,1)S(1)}, bf16[64,1536]{1,0:T(8,128)(2,1)S(1)}, u32[]{:S(2)}, u32[]{:S(2)}) collective-permute-start(bf16[64,1536]{1,0:T(8,128)(2,1)S(1)} %get-tuple-element.422), channel_id=1, source_target_pairs={{0,4},{2,6},{4,0},{6,2},{1,5},{3,7},{5,1},{7,3},{8,12},{10,14},{12... | collective-permute-start | bytes 589832 | tf_op jit(solution)/shard_map/ppermute | solution.py:93
  897.3 29.6 %collective-permute-start.125 = (bf16[256,1664]{1,0:T(8,128)(2,1)}, bf16[256,1664]{1,0:T(8,128)(2,1)}, u32[]{:S(2)}, u32[]{:S(2)}) collective-permute-start(bf16[256,1664]{1,0:T(8,128)(2,1)} %slice.2253), channel_id=1, source_target_pairs={{0,1},{1,0},{2,3},{3,2},{4,5},{5,4},{6,7},{7,6},{8,9},{9,8},{10,11... | collective-permute-start | bytes 2555912 | tf_op jit(solution)/shard_map/ppermute | solution.py:93
  953.8 249.8 %reduce-scatter.27.cloned.1.call-start = ((), (), s32[]{:S(2)}) async-start(), calls=%async_computation.29 | async-start | bytes 1966080 | tf_op jit(solution)/shard_map/reduce_scatter | solution.py:818
  982.2 226.6 %reduce-scatter.21.cloned.1.call-start = ((), (), s32[]{:S(2)}) async-start(), calls=%async_computation.26 | async-start | bytes 4423680 | tf_op jit(solution)/shard_map/reduce_scatter | solution.py:873
  1020.3 47.8 %collective-permute-start.102 = (bf16[64,1664]{1,0:T(8,128)(2,1)S(1)}, bf16[64,1664]{1,0:T(8,128)(2,1)S(1)}, u32[]{:S(2)}, u32[]{:S(2)}) collective-permute-start(bf16[64,1664]{1,0:T(8,128)(2,1)S(1)} %concatenate.218), channel_id=1, source_target_pairs={{0,4},{2,6},{4,0},{6,2},{1,5},{3,7},{5,1},{7,3},{8,12},{10,14},{12... | collective-permute-start | bytes 638984 | tf_op jit(solution)/shard_map/ppermute | solution.py:93
  1029.3 38.9 %collective-permute-start.103 = (bf16[64,1664]{1,0:T(8,128)(2,1)S(1)}, bf16[64,1664]{1,0:T(8,128)(2,1)S(1)}, u32[]{:S(2)}, u32[]{:S(2)}) collective-permute-start(bf16[64,1664]{1,0:T(8,128)(2,1)S(1)} %concatenate.218), channel_id=1, source_target_pairs={{0,6},{2,0},{4,2},{6,4},{1,7},{3,1},{5,3},{7,5},{8,14},{10,8},{12,... | collective-permute-start | bytes 638984 | tf_op jit(solution)/shard_map/ppermute | solution.py:93
  1033.2 35.6 %collective-permute-start.104 = (bf16[64,1664]{1,0:T(8,128)(2,1)S(1)}, bf16[64,1664]{1,0:T(8,128)(2,1)S(1)}, u32[]{:S(2)}, u32[]{:S(2)}) collective-permute-start(bf16[64,1664]{1,0:T(8,128)(2,1)S(1)} %concatenate.218), channel_id=1, source_target_pairs={{0,1},{1,0},{2,3},{3,2},{4,5},{5,4},{6,7},{7,6},{8,9},{9,8},{10,11... | collective-permute-start | bytes 638984 | tf_op jit(solution)/shard_map/ppermute | solution.py:93
  1033.9 35.0 %collective-permute-start.133 = (bf16[64,1664]{1,0:T(8,128)(2,1)S(1)}, bf16[64,1664]{1,0:T(8,128)(2,1)S(1)}, u32[]{:S(2)}, u32[]{:S(2)}) collective-permute-start(bf16[64,1664]{1,0:T(8,128)(2,1)S(1)} %collective-permute-done.129), channel_id=1, source_target_pairs={{0,1},{1,0},{2,3},{3,2},{4,5},{5,4},{6,7},{7,6},{8,9},{9,8},{10,11... | collective-permute-start | bytes 638984 | tf_op jit(solution)/shard_map/ppermute | solution.py:93
  1036.0 34.2 %collective-permute-start.134 = (bf16[64,1664]{1,0:T(8,128)(2,1)S(1)}, bf16[64,1664]{1,0:T(8,128)(2,1)S(1)}, u32[]{:S(2)}, u32[]{:S(2)}) collective-permute-start(bf16[64,1664]{1,0:T(8,128)(2,1)S(1)} %collective-permute-done.130), channel_id=1, source_target_pairs={{0,1},{1,0},{2,3},{3,2},{4,5},{5,4},{6,7},{7,6},{8,9},{9,8},{10,11... | collective-permute-start | bytes 638984 | tf_op jit(solution)/shard_map/ppermute | solution.py:93
  1082.3 159.4 %reduce-scatter.19.cloned.1.call-start = ((), (), s32[]{:S(2)}) async-start(), calls=%async_computation.25 | async-start | bytes 4423680 | tf_op jit(solution)/shard_map/reduce_scatter | solution.py:873
  1147.9 98.9 %reduce-scatter.23.cloned.1.call-start = ((), (), s32[]{:S(2)}) async-start(), calls=%async_computation.27 | async-start | bytes 3932160 | tf_op jit(solution)/shard_map/reduce_scatter | solution.py:763
  1150.7 30.8 %collective-permute-start.136 = (bf16[256,1536]{1,0:T(8,128)(2,1)}, bf16[256,1536]{1,0:T(8,128)(2,1)}, u32[]{:S(2)}, u32[]{:S(2)}) collective-permute-start(bf16[256,1536]{1,0:T(8,128)(2,1)} %slice.2257), channel_id=1, source_target_pairs={{0,1},{1,0},{2,3},{3,2},{4,5},{5,4},{6,7},{7,6},{8,9},{9,8},{10,11... | collective-permute-start | bytes 2359304 | tf_op jit(solution)/shard_map/ppermute | solution.py:93
  1186.4 28.8 %collective-permute-start.138 = (bf16[64,1536]{1,0:T(8,128)(2,1)}, bf16[64,1536]{1,0:T(8,128)(2,1)S(1)}, u32[]{:S(2)}, u32[]{:S(2)}) collective-permute-start(bf16[64,1536]{1,0:T(8,128)(2,1)} %get-tuple-element.523), channel_id=1, source_target_pairs={{0,4},{2,6},{4,0},{6,2},{1,5},{3,7},{5,1},{7,3},{8,12},{10,14},{12... | collective-permute-start | bytes 589832 | tf_op jit(solution)/shard_map/ppermute | solution.py:93
  1188.4 26.8 %collective-permute-start.139 = (bf16[64,1536]{1,0:T(8,128)(2,1)}, bf16[64,1536]{1,0:T(8,128)(2,1)}, u32[]{:S(2)}, u32[]{:S(2)}) collective-permute-start(bf16[64,1536]{1,0:T(8,128)(2,1)} %get-tuple-element.522), channel_id=1, source_target_pairs={{0,2},{2,4},{4,6},{6,0},{1,3},{3,5},{5,7},{7,1},{8,10},{10,12},{12... | collective-permute-start | bytes 589832 | tf_op jit(solution)/shard_map/ppermute | solution.py:93
  1190.6 24.6 %collective-permute-start.109 = (bf16[64,1536]{1,0:T(8,128)(2,1)}, bf16[64,1536]{1,0:T(8,128)(2,1)}, u32[]{:S(2)}, u32[]{:S(2)}) collective-permute-start(bf16[64,1536]{1,0:T(8,128)(2,1)} %get-tuple-element.524), channel_id=1, source_target_pairs={{0,6},{2,0},{4,2},{6,4},{1,7},{3,1},{5,3},{7,5},{8,14},{10,8},{12,... | collective-permute-start | bytes 589832 | tf_op jit(solution)/shard_map/ppermute | solution.py:93
  1194.4 38.8 %collective-permute-start.110 = (bf16[64,1536]{1,0:T(8,128)(2,1)}, bf16[64,1536]{1,0:T(8,128)(2,1)}, u32[]{:S(2)}, u32[]{:S(2)}) collective-permute-start(bf16[64,1536]{1,0:T(8,128)(2,1)} %get-tuple-element.526), channel_id=1, source_target_pairs={{0,4},{2,6},{4,0},{6,2},{1,5},{3,7},{5,1},{7,3},{8,12},{10,14},{12... | collective-permute-start | bytes 589832 | tf_op jit(solution)/shard_map/ppermute | solution.py:93
  1194.4 38.8 %collective-permute-start.111 = (bf16[64,1536]{1,0:T(8,128)(2,1)}, bf16[64,1536]{1,0:T(8,128)(2,1)}, u32[]{:S(2)}, u32[]{:S(2)}) collective-permute-start(bf16[64,1536]{1,0:T(8,128)(2,1)} %get-tuple-element.525), channel_id=1, source_target_pairs={{0,2},{2,4},{4,6},{6,0},{1,3},{3,5},{5,7},{7,1},{8,10},{10,12},{12... | collective-permute-start | bytes 589832 | tf_op jit(solution)/shard_map/ppermute | solution.py:93
  1208.7 32.9 %all-to-all-start.4 = ((bf16[8,48,1152]{2,1,0:T(8,128)(2,1)}), bf16[8,48,1152]{2,1,0:T(8,128)(2,1)S(1)}, u32[]{:S(2)}, u32[]{:S(2)}) async-start(bf16[8,48,1152]{2,1,0:T(8,128)(2,1)} %bitcast.532), calls=%async_computation.9 | async-start | bytes 1769472 | tf_op jit(solution)/shard_map/all_to_all | solution.py:874
  1241.7 26.6 %all-to-all-start.3 = ((bf16[8,48,1152]{2,1,0:T(8,128)(2,1)}), bf16[8,48,1152]{2,1,0:T(8,128)(2,1)S(1)}, u32[]{:S(2)}, u32[]{:S(2)}) async-start(bf16[8,48,1152]{2,1,0:T(8,128)(2,1)} %bitcast.533), calls=%async_computation.7 | async-start | bytes 1769472 | tf_op jit(solution)/shard_map/all_to_all | solution.py:874
  (421 other events, 4829.4 us)
Sparse Core Ops, SparseCore 0:
  41.8 46.1 all-gather.8
  109.6 50.2 all-gather.10
  218.6 37.4 all-gather.16
  257.8 69.0 all-gather.12
  328.5 43.9 all-gather.14
  374.3 70.1 all-gather.18
  446.3 70.1 all-gather.20
  518.3 43.9 all-gather.22
  702.8 69.5 reduce-scatter.12
  806.2 69.6 reduce-scatter.24
  878.8 43.9 reduce-scatter.14
  953.9 69.4 reduce-scatter.16
  1025.7 45.6 reduce-scatter.26
  1082.4 51.2 reduce-scatter.20
  1148.0 51.8 reduce-scatter.18
  1202.7 43.9 reduce-scatter.22

commit v4 on v3

--- a/solution.py
+++ b/solution.py
@@ -234,7 +234,7 @@
 
 def scan_backward_kernel(
     heads, proj_ref, step_ref, col_ref, row_ref, conv_ref, chan_ref, head_ref, grad_ref, extra_ref,
-    dproj_ref, dstep_ref, dconv_ref, dchan_ref, dhead_ref, flat_ref,
+    dproj_ref, dconv_ref, dchan_ref, dhead_ref, flat_ref,
 ):
     @pl.when(pl.program_id(0) == 0)
     def _():
@@ -301,8 +301,7 @@
     for k in range(1, CK):
         back = d_sum * s["masks"][k] * taps[k : k + 1]
         d_in = d_in + pltpu.roll(back, length - k, 0)
-    dproj_ref[...] = jnp.concatenate([d_z, d_in], axis=1).astype(bf16)
-    dstep_ref[...] = d_pre.astype(bf16)
+    dproj_ref[...] = jnp.concatenate([d_z, d_in, d_pre], axis=1).astype(bf16)
     for k in range(CK):
         dconv_ref[k : k + 1] += jnp.sum(d_sum * s["shifted"][k], axis=0, keepdims=True)
     dconv_ref[CK : CK + 1] += jnp.sum(d_sum, axis=0, keepdims=True)
@@ -347,10 +346,9 @@
         functools.partial(scan_backward_kernel, heads),
         grid=(total // length,),
         in_specs=specs + [rows(chan), rows(128)],
-        out_specs=[rows(width), rows(lanes_), whole((8, width - chan)), whole((8, chan)), whole((8, lanes_))],
+        out_specs=[rows(width + lanes_), whole((8, width - chan)), whole((8, chan)), whole((8, lanes_))],
         out_shape=[
-            jax.ShapeDtypeStruct((total, width), bf16),
-            jax.ShapeDtypeStruct((total, lanes_), bf16),
+            jax.ShapeDtypeStruct((total, width + lanes_), bf16),
             jax.ShapeDtypeStruct((8, width - chan), f32),
             jax.ShapeDtypeStruct((8, chan), f32),
             jax.ShapeDtypeStruct((8, lanes_), f32),
@@ -379,59 +377,60 @@
     return ex / jnp.sum(ex, axis=-1, keepdims=True)
 
 
+def unit_gates(local, units):
+    count = local.shape[1]
+    inner = EXP_FF // lax.axis_size("dp")
+    owner = lax.broadcasted_iota(jnp.int32, (1, units), 1) // inner % count
+    spread = local[:, count - 1 :]
+    for e in range(count - 1):
+        spread = jnp.where(owner == e, local[:, e : e + 1], spread)
+    return spread, owner
+
+
 def moe_forward(own_in, mask, w):
     rows = own_in.shape[0]
     base_in = gather_rows(own_in)
     moe_in = wide(base_in)
     gates = gate_table(moe_in, mask, w["router"])
-    count = w["expert_in"].shape[0]
+    units = w["expert_down"].shape[0]
+    count = units // EXP_FF
     first = lax.axis_index(EX) * count
     local = lax.dynamic_slice(gates, (0, first), (gates.shape[0], count))
-    pre = [nn(moe_in, w["expert_in"][e], bf16) for e in range(count)]
+    pre = nn(moe_in, w["expert_in"], bf16)
     pre_s = nn(base_in, w["shared_in"], bf16)
-    if lax.axis_size("w") > 1:
-        pre, pre_s = lax.optimization_barrier((pre, pre_s))
-    total = None
-    for e in range(count):
-        p = pre[e].astype(f32)
-        act = swiglu(p[:, :EXP_FF], p[:, EXP_FF:])
-        hid = (act * local[:, e : e + 1]).astype(bf16)
-        part = nn(hid, w["expert_down"][e])
-        total = part if total is None else total + part
+    pre, pre_s = lax.optimization_barrier((pre, pre_s))
+    p = pre.astype(f32)
+    spread, _ = unit_gates(local, units)
+    hid = (swiglu(p[:, :units], p[:, units:]) * spread).astype(bf16)
     half = pre_s.shape[1] // 2
     p = pre_s.astype(f32)
     hid_s = swiglu(p[:, :half], p[:, half:]).astype(bf16)
-    total = add_first(total, nt(hid_s, w["shared_down_t"]))
-    branch = return_rows(narrow(total))
-    kept = (moe_in, base_in, gates[:rows], local, pre, pre_s)
-    return branch, kept
+    total = add_first(nn(hid, w["expert_down"]), nt(hid_s, w["shared_down_t"]))
+    return total, (moe_in, base_in, gates[:rows], local, pre, pre_s)
 
 
 def moe_backward(base_z, kept, w, experts_total):
     moe_in, base_in, own_gates, local, pre, pre_s = kept
     pre, pre_s, _ = lax.optimization_barrier((pre, pre_s, base_z))
     grad_z = wide(base_z)
-    rows = own_gates.shape[0]
-    count = len(pre)
-    total = None
+    units = w["expert_down"].shape[0]
+    count = units // EXP_FF
     first = lax.axis_index(EX) * count
+    spread, owner = unit_gates(local, units)
+    p = pre.astype(f32)
+    gate, up = p[:, :units], p[:, units:]
+    grad_hid = nt(grad_z, w["expert_down"])
+    act = swiglu(gate, up)
+    hidden = (act * spread).astype(bf16)
+    product = grad_hid * act
     lane = lax.broadcasted_iota(jnp.int32, (1, experts_total), 1)
     table = jnp.zeros((grad_z.shape[0], experts_total), f32)
-    pre_grads, hidden = [], []
     for e in range(count):
-        p = pre[e].astype(f32)
-        gate, up = p[:, :EXP_FF], p[:, EXP_FF:]
-        grad_hid = nt(grad_z, w["expert_down"][e])
-        share = local[:, e : e + 1]
-        act = swiglu(gate, up)
-        hidden.append((act * share).astype(bf16))
-        weighted = share * jnp.sum(grad_hid * act, axis=-1, keepdims=True)
-        table = table + weighted * (lane == first + e).astype(f32)
-        g_gate, g_up = swiglu_back(grad_hid * share, gate, up)
-        g_pre = jnp.concatenate([g_gate, g_up], axis=1)
-        pre_grads.append(g_pre)
-        part = nt(g_pre, w["expert_in"][e])
-        total = part if total is None else total + part
+        mine = jnp.sum(jnp.where(owner == e, product, 0.0), axis=-1, keepdims=True)
+        table = table + local[:, e : e + 1] * mine * (lane == first + e).astype(f32)
+    g_gate, g_up = swiglu_back(grad_hid * spread, gate, up)
+    g_pre = jnp.concatenate([g_gate, g_up], axis=1)
+    total = nt(g_pre, w["expert_in"])
     half = pre_s.shape[1] // 2
     p = pre_s.astype(f32)
     grad_hid = nn(base_z, w["shared_down_t"])
@@ -442,7 +441,7 @@
     extra = -(-experts_total // 128) * 128
     table = jnp.pad(table, ((0, 0), (0, extra - experts_total)))
     back = return_rows(narrow(jnp.concatenate([total, table], axis=1)))
-    side = (moe_in, grad_z, hidden, hid_s, pre_grads, g_pre_s, base_in, base_z)
+    side = (moe_in, grad_z, hidden, hid_s, g_pre, g_pre_s, base_in, base_z)
     return back, side
 
 
@@ -465,9 +464,8 @@
 
 
 def moe_weight_grads(sides):
-    count = len(sides[0][2])
-    g_down = jnp.stack([tn_sum([(s[2][e], s[1]) for s in sides]) for e in range(count)])
-    g_in = jnp.stack([tn_sum([(s[0], s[4][e]) for s in sides]) for e in range(count)])
+    g_down = tn_sum([(s[2], s[1]) for s in sides])
+    g_in = tn_sum([(s[0], s[4]) for s in sides])
     g_sin = tn_sum([(s[6], s[5]) for s in sides])
     g_sdown_t = tn_sum([(s[7], s[3]) for s in sides])
     return g_in, g_down, g_sin, g_sdown_t
@@ -610,7 +608,10 @@
             by_owner(w_dt, n_tp),
             for_all(little),
             blank,
+            by_owner(w_mix_out.T, n_tp),
         ]
+        + shared_pack(shared_in_m, shared_down_m)
+        + shared_pack(shared_in, shared_down)
     )
     w_m = whole_rows(moved_m)
 
@@ -625,16 +626,10 @@
         info = lanes(hot + [segments[m, 0][:, None].astype(bf16)], info_width)
         x_info, _ = fence(jnp.concatenate([tokens[m], info], axis=1), moved_m)
         rows_in.append(gather_rows(x_info))
-    moved_s = moved_columns(
-        [by_owner(w_mix_out.T, n_tp)]
-        + shared_pack(shared_in_m, shared_down_m)
-        + shared_pack(shared_in, shared_down),
-        rows_in[0],
-    )
-    w_s = whole_rows(moved_s)
     in_width = 2 * chan + 2 * STATE
     w_in_here = w_m[:, :in_width]
-    w_step = w_m[:, in_width:]
+    at = in_width + step_width
+    w_step = w_m[:, in_width:at]
     w_dt_here = w_step[:, :128]
     small_all = w_step[:, heads : heads + small_cols]
     gain_mamba, gain_moe_m, gain_attn, gain_moe = [small_all[:, i].astype(f32) for i in range(4)]
@@ -657,28 +652,41 @@
     log_here = lax.dynamic_slice_in_dim(a_log, slot * heads, heads)
     skip_here = lax.dynamic_slice_in_dim(skip_scale, slot * heads, heads)
 
-    w_mix_t = w_s[:, :chan]
-    expert_in_m, expert_down_m, _ = fence(expert_in_m, expert_down_m, moved_s)
-    at = chan
-
+    w_scan = w_m[:, : in_width + 128]
+    w_mix_t = w_m[:, at : at + chan]
+    at += chan
+
+    n_dp = lax.axis_size("dp")
+
+    def expert_weights(w_up, w_low):
+        count, depth, width = w_up.shape
+        cols = w_up.reshape(count, depth, 2, n_dp, EXP_FF // n_dp).transpose(1, 2, 3, 0, 4)
+        return (
+            by_rows(lax.all_gather(by_rows(cols.reshape(depth, -1)), "dp", axis=0, tiled=True)),
+            lax.all_gather(w_low.reshape(-1, D), "dp", axis=0, tiled=True),
+        )
+
+    expert_in_m, expert_down_m, _ = fence(expert_in_m, expert_down_m, moved_m)
+    up_m, low_m = expert_weights(expert_in_m, expert_down_m)
     moe_m = {
         "router": router_m_full,
-        "shared_in": w_s[:, at : at + 2 * ff],
-        "shared_down_t": w_s[:, at + 2 * ff : at + 3 * ff],
-        "expert_in": lax.all_gather(expert_in_m, "dp", axis=1, tiled=True),
-        "expert_down": lax.all_gather(expert_down_m, "dp", axis=1, tiled=True),
+        "shared_in": w_m[:, at : at + 2 * ff],
+        "shared_down_t": w_m[:, at + 2 * ff : at + 3 * ff],
+        "expert_in": up_m,
+        "expert_down": low_m,
     }
 
     kv = KVH // 2
     q_width = QH // 2 * HEAD
     kv_width = kv * HEAD
     q_all, kv_all = QH * HEAD, KVH * HEAD
+    up_a, low_a = expert_weights(expert_in, expert_down)
     moe_a = {
         "router": router_full,
-        "shared_in": w_s[:, at + 3 * ff : at + 5 * ff],
-        "shared_down_t": w_s[:, at + 5 * ff :],
-        "expert_in": lax.all_gather(expert_in, "dp", axis=1, tiled=True),
-        "expert_down": lax.all_gather(expert_down, "dp", axis=1, tiled=True),
+        "shared_in": w_m[:, at + 3 * ff : at + 5 * ff],
+        "shared_down_t": w_m[:, at + 5 * ff :],
+        "expert_in": up_a,
+        "expert_down": low_a,
     }
 
     def eight(parts):
@@ -701,6 +709,7 @@
         seg = seg_row[:, 0].astype(jnp.int32)
         allowed.append(attn_mask(jnp.stack([seg[0], seg[n_tp // 2]])))
 
+        x_all, _ = fence(x_all, w_m)
         _, scale_x, mamba_in = rms_forward(x_all, gain_mamba)
         total_rows = mamba_in.shape[0]
         proj = nn(mamba_in, w_in_here, bf16)
@@ -730,9 +739,14 @@
         ],
         axis=2,
     ).transpose(1, 0, 2)
-    attn_pack, _ = fence(attn_pack, hidden_one[0])
+    attn_pack, _ = fence(attn_pack, rows_in)
     attn_pack = lax.all_to_all(attn_pack, "core", split_axis=0, concat_axis=0, tiled=True)
-    attn_w = lax.all_gather(attn_pack.reshape(2 * rows, -1), "z", axis=0, tiled=True)
+    own = attn_pack.reshape(2 * rows, -1)
+    n_z = lax.axis_size("z")
+    parts = [send(own, "z", ring(s)) for s in range(n_z - 1, 0, -1)] + [own]
+    twice = jnp.concatenate(parts + parts, axis=0)
+    start = (n_z - 1 - lax.axis_index("z")) * 2 * rows
+    attn_w = lax.dynamic_slice(twice, (start, 0), (n_z * 2 * rows, own.shape[1]))
     attn_w = lax.all_gather(attn_w, FS, axis=0, tiled=True)
     w_qkv_here = attn_w[:, : q_width + 2 * kv_width]
     w_out_t = attn_w[:, q_width + 2 * kv_width :]
@@ -741,8 +755,8 @@
     one_kept, layer_one = [], []
     for m in each:
         normed, scale, own = rms_forward(hidden_one[m], gain_moe_m)
-        branch, kept = moe_forward(own, masks[m][0], moe_m)
-        layer_one.append(hidden_one[m] + branch)
+        total, kept = moe_forward(own, masks[m][0], moe_m)
+        layer_one.append(hidden_one[m] + return_rows(narrow(total)))
         one_kept.append((normed, scale, kept))
     attn_kept, hidden_two = [], []
     for m in each:
@@ -753,14 +767,20 @@
     two_kept, results = [], []
     for m in each:
         normed, scale, own = rms_forward(hidden_two[m], gain_moe)
-        branch, kept = moe_forward(own, masks[m][1], moe_a)
-        results.append((hidden_two[m] + branch).astype(bf16))
+        total, kept = moe_forward(own, masks[m][1], moe_a)
+        results.append(total)
         two_kept.append((normed, scale, kept))
 
     gains = [0.0, 0.0, 0.0, 0.0]
 
     def over_dp(g):
-        return lax.psum_scatter(g, "dp", scatter_dimension=1, tiled=True)
+        return lax.psum_scatter(g, "dp", scatter_dimension=0, tiled=True)
+
+    def expert_out(g_up, g_low):
+        depth = g_up.shape[0]
+        cols = g_up.reshape(depth, 2, n_dp, local_experts, EXP_FF // n_dp)
+        cols = cols.transpose(3, 0, 1, 2, 4).reshape(local_experts, depth, 2 * EXP_FF)
+        return cols.astype(f32), g_low.reshape(local_experts, -1, D).astype(f32)
 
     saving = lax.axis_size("w") > 1
 
@@ -799,6 +819,9 @@
     sum_in_a = over_dp(g_in_a)
     sum_down_a = over_dp(g_down_a)
     grad_two = [cotangent[m].astype(f32) + values[m] for m in each]
+    for m in each:
+        total, _ = fence(results[m], grad_two[m])
+        results[m] = (hidden_two[m] + return_rows(narrow(total))).astype(bf16)
 
     grad_layer, sides = [], []
     attn_back = []
@@ -860,12 +883,12 @@
             g_mix = tn_sum([(x, k[4]) for x, k in zip(mixes, mamba_kept)])
             mix_all, g_mix = fence(mix_all, g_mix)
         grad_gated = nn(mix_all, w_mix_t, bf16)
-        grad_proj, grad_step, *grads = scan_backward(
+        grad_scan, *grads = scan_backward(
             heads, length, *scan_args, grad_gated, extra_all
         )
-        mamba_sides.append((mamba_in, grad_proj, grad_step))
+        mamba_sides.append((mamba_in, grad_scan))
         small = grads if small is None else [a + b for a, b in zip(small, grads)]
-        total = nt(grad_proj, w_in_here) + nt(grad_step, w_dt_here)
+        total = nt(grad_scan, w_scan)
         gains[0] = gains[0] + jnp.sum(total * normed_x, axis=0)
         mamba_back.append(return_rows(total))
 
@@ -881,41 +904,37 @@
     g_s = rows_back(
         jnp.concatenate([g_mix, g_sin_m, g_sdown_m, g_sin_a, g_sdown_a], axis=1)
     )
-    out_mix = owned(g_s[:, :, :chan]).T
-
-    g_proj = tn_sum([(s[0], s[1]) for s in mamba_sides])
-    g_step = tn_sum([(s[0], s[2]) for s in mamba_sides])[:, :heads]
-    g_proj, sum_in_m = fence(g_proj, sum_in_m)
-    out_expert_in = sum_in_a.astype(f32)
-    out_expert_down = sum_down_a.astype(f32)
-    out_expert_in_m = sum_in_m.astype(f32)
-    out_expert_down_m = sum_down_m.astype(f32)
-
+
+    g_scan = tn_sum(mamba_sides, f32)
+    g_scan, sum_in_m, sum_down_m = fence(g_scan, sum_in_m, sum_down_m)
+    out_expert_in, out_expert_down = expert_out(sum_in_a, sum_down_a)
+    out_expert_in_m, out_expert_down_m = expert_out(sum_in_m, sum_down_m)
+
+    conv_sums, chan_sums, head_sums = small
+    g_gate = chan_sums[0]
+    g_skip = jnp.sum(chan_sums[1].reshape(heads, HP), axis=1)
+    head_grad = jnp.stack([head_sums[0, :heads], head_sums[1, :heads], g_skip])
+
+    def spread(part, width):
+        zeros = jnp.zeros(part.shape[:-1] + (width,), f32)
+        return lax.dynamic_update_slice_in_dim(zeros, part[..., :chan], slot * chan, axis=-1)
+
+    conv_grad = jnp.concatenate([conv_sums[CK : CK + 1], conv_sums[:CK]], axis=0)
+    conv_grad = spread(conv_grad, conv_total) + jnp.pad(conv_grad[:, chan:], ((0, 0), (DI, 0)))
+    conv_grad = conv_grad.reshape(CK + 1, n_all, conv_here).transpose(1, 0, 2).reshape(n_all, -1)
+    vec_grad = jnp.concatenate([spread(g_gate, DI).reshape(n_all, gate_here), conv_grad], axis=1)
+    vec_grad = jnp.pad(vec_grad, ((0, 0), (0, rows * vec_cols - vec_len))).reshape(D, vec_cols)
+    little = jnp.concatenate([g[:, None] for g in gains] + [g_router_m, g_router, vec_grad], axis=1)
+    after = step_width - heads - small_cols
+    g_scan = jnp.pad(g_scan, ((0, 0), (0, step_width - 128)))
+    g_m = rows_back((g_scan + jnp.pad(little, ((0, 0), (in_width + heads, after)))).astype(bf16))
+    mamba_back[-1], g_s = fence(mamba_back[-1], g_s)
     grads_in = []
     for m in each:
         scale_x = mamba_kept[m][1]
         grad_values, _ = rms_backward(mamba_back[m], own_normed[m], scale_x, gain_mamba)
         grads_in.append(grad_one[m] + grad_values)
 
-    conv_sums, chan_sums, head_sums = small
-    g_gate = chan_sums[0]
-    g_skip = jnp.sum(chan_sums[1].reshape(heads, HP), axis=1)
-    head_grad = jnp.stack([head_sums[0, :heads], head_sums[1, :heads], g_skip])
-
-    def spread(part, width):
-        zeros = jnp.zeros(part.shape[:-1] + (width,), f32)
-        return lax.dynamic_update_slice_in_dim(zeros, part[..., :chan], slot * chan, axis=-1)
-
-    conv_grad = jnp.concatenate([conv_sums[CK : CK + 1], conv_sums[:CK]], axis=0)
-    conv_grad = spread(conv_grad, conv_total) + jnp.pad(conv_grad[:, chan:], ((0, 0), (DI, 0)))
-    conv_grad = conv_grad.reshape(CK + 1, n_all, conv_here).transpose(1, 0, 2).reshape(n_all, -1)
-    vec_grad = jnp.concatenate([spread(g_gate, DI).reshape(n_all, gate_here), conv_grad], axis=1)
-    vec_grad = jnp.pad(vec_grad, ((0, 0), (0, rows * vec_cols - vec_len))).reshape(D, vec_cols)
-    little = jnp.concatenate(
-        [g[:, None] for g in gains] + [g_router_m, g_router, vec_grad], axis=1
-    ).astype(bf16)
-    blank = jnp.zeros((D, step_width - heads - small_cols), bf16)
-    g_m = rows_back(jnp.concatenate([g_proj, g_step, little, blank], axis=1))
     out_w_in = jnp.concatenate(
         [
             owned(g_m[:, :, :chan]),
@@ -924,6 +943,7 @@
         ],
         axis=1,
     )
+    out_mix = owned(g_s[:, :, :chan]).T
     out_w_dt = owned(g_m[:, :, in_width : in_width + heads])
     little = jnp.sum(g_m[:, :, in_width + heads : in_width + heads + small_cols], axis=0)
     vec = little[:, 4 + 2 * experts_total :].reshape(-1)

time: 1290 us -> 1230 us (0.953)
  waiting for transfers between devices: 466 us -> 343 us
  starting transfers between devices: 227 us -> 157 us
  local copies, waits for them, and re-layouts: 142 us -> 207 us
  blocking collectives: 9.88 us -> 59.1 us
    all_gather x5 -> x4, waiting for transfers between devices: 99.7 us -> 0.01 us  [the longest x2 0.01 us: expert_weights(): lax.all_gather(by_rows(cols.reshape(depth, -1)), 'dp', axis=0, tiled=True)]
    ppermute x145 -> x148, starting transfers between devices: 207 us -> 147 us  [send(): return by_rows(lax.ppermute(by_rows(x), axis, pairs))]
    all_to_all x0 -> x1, blocking collectives: none -> 48.4 us  [moved_columns(): moved = lax.all_to_all(packed, TP, split_axis=0, concat_axis=0, tiled=True)]
    reduce_scatter x4, waiting for transfers between devices: 0.04 us -> 27.8 us  [over_dp(): return lax.psum_scatter(g, 'dp', scatter_dimension=0, tiled=True)]
    convert_element_type x0 -> x6, local copies, waits for them, and re-layouts: none -> 23.5 us  [expert_out(): return (cols.astype(f32), g_low.reshape(local_experts, -1, D).astype(f32))]
    all_to_all x2 -> x0, waiting for transfers between devices: 22.9 us -> none  [moved_columns(): moved = lax.all_to_all(packed, TP, split_axis=0, concat_axis=0, tiled=True)]
    unnamed x742 -> x736, local copies, waits for them, and re-layouts: 76.3 us -> 95.9 us
    another operation x24 -> x15, other arithmetic: 34.3 us -> 15.1 us
  transfers between devices with their start and end apart: 165 -> 164, of which waited for: 60 -> 57; matrix products, arithmetic and copies ran while one was open for 37% -> 40% of each run, Pallas kernels for 2% -> 2%
where the time goes in v4:
time: 1230 us; the launch traced here: 1220 us
  waiting for transfers between devices  343 us (28%)
  matrix products  286 us (23%)
  local copies, waits for them, and re-layouts  207 us (17%)
  starting transfers between devices  157 us (13%)
  other arithmetic  121 us (10%)
  blocking collectives  59.1 us (5%)
  Pallas kernels  28 us (2%)
  between operations  20.2 us (2%)
    ppermute x148, waiting for transfers between devices, send(): return by_rows(lax.ppermute(by_rows(x), axis, pairs))  297 us
    dot_general x86, matrix products, dot(): r = lax.dot_general(a, b, (dims, ((), ())), preferred_element_type=f32)  271 us
    ppermute x148, starting transfers between devices, send(): return by_rows(lax.ppermute(by_rows(x), axis, pairs))  147 us
    unnamed x736, local copies, waits for them, and re-layouts  95.9 us
    all_to_all x1, blocking collectives, moved_columns(): moved = lax.all_to_all(packed, TP, split_axis=0, concat_axis=0, tiled=True)  48.4 us
    reduce_scatter x4, waiting for transfers between devices, over_dp(): return lax.psum_scatter(g, 'dp', scatter_dimension=0, tiled=True)  27.8 us
  transfers between devices with their start and end apart: 164, of which 57 were waited for; matrix products, arithmetic and copies ran while one was open for 40% of the time, Pallas kernels for 2%

profile of v4, /device:TPU:0, one launch (start us, length us, event | category | flops | bytes accessed | tf_op | source)
XLA Modules:
  0.0 1221.1 jit_solution(4777000100787843151)
XLA Ops:
  20.2 48.4 %all_to_all.25 = bf16[8,48,2304]{2,1,0:T(8,128)(2,1)} all-to-all(bf16[8,48,2304]{2,1,0:T(8,128)(2,1)S(1)} %copy.1080), channel_id=1, replica_groups=mesh['dp'=4,'w'=1,'z'=4,'core'=2] {'z','core'}, dimensions={0} | all-to-all | bytes 3538944 | tf_op jit(solution)/shard_map/all_to_all | solution.py:589
  85.3 9.6 collective-permute-done
  94.9 10.4 collective-permute-start.24
  108.4 6.3 collective-permute-done.23
  123.9 4.8 all_to_all.26
  130.8 10.7 collective-permute-done.30
  142.5 21.3 %collective-permute-done.31 = bf16[96,2048]{1,0:T(8,128)(2,1)} collective-permute-done((bf16[96,2048]{1,0:T(8,128)(2,1)}, bf16[96,2048]{1,0:T(8,128)(2,1)}, u32[]{:S(2)}, u32[]{:S(2)}) %collective-permute-start.31) | collective-permute-done | bytes 393248 | tf_op jit(solution)/shard_map/ppermute | solution.py:93
  215.1 4.8 scan_forward.2
  222.4 4.8 scan_forward.3
  235.7 9.0 collective-permute-done.53
  275.4 8.0 collective-permute-done.43
  284.4 4.8 collective-permute-done.10
  289.2 11.4 collective-permute-done.9
  311.9 19.2 %collective-permute-done.12 = bf16[64,1536]{1,0:T(8,128)(2,1)S(1)} collective-permute-done((bf16[64,1536]{1,0:T(8,128)(2,1)S(1)}, bf16[64,1536]{1,0:T(8,128)(2,1)S(1)}, u32[]{:S(2)}, u32[]{:S(2)}) %collective-permute-start.12) | collective-permute-done | bytes 196640 | tf_op jit(solution)/shard_map/ppermute | solution.py:93
  346.8 6.7 convolution_convert_fusion.3
  357.9 5.2 fusion.125
  371.3 6.4 convolution_convert_fusion.1
  386.3 4.7 collective-permute-done.21
  391.0 7.5 collective-permute-done.20
  414.9 4.7 fusion.121
  429.2 10.2 collective-permute-done.35
  444.8 6.7 convolution_convert_fusion.2
  458.0 7.8 select_reduce_fusion.6
  469.4 4.8 multiply_convert_fusion.11
  476.4 6.2 fusion.71
  507.2 7.9 collective-permute-done.61
  520.2 10.9 collective-permute-done.76
  580.8 14.5 %collective-permute-done.81 = bf16[64,1536]{1,0:T(8,128)(2,1)S(1)} collective-permute-done((bf16[64,1536]{1,0:T(8,128)(2,1)S(1)}, bf16[64,1536]{1,0:T(8,128)(2,1)S(1)}, u32[]{:S(2)}, u32[]{:S(2)}) %collective-permute-start.81) | collective-permute-done | bytes 196640 | tf_op jit(solution)/shard_map/ppermute | solution.py:93
  613.6 6.2 multiply_convert_fusion.7
  633.7 6.7 fusion.69
  650.6 4.6 fusion.105
  655.2 8.3 add_convert_fusion.1
  666.7 7.0 add_convert_fusion.4
  679.3 9.6 collective-permute-done.88
  689.0 5.8 collective-permute-done.89
  729.5 8.7 copy.1224
  740.1 27.8 %reduce-scatter.15.cloned.1.call-done = bf16[384,2048]{1,0:T(8,128)(2,1)} async-done(((bf16[1536,2048]{1,0:T(8,128)(2,1)}), bf16[384,2048]{1,0:T(8,128)(2,1)}) %reduce-scatter.15.cloned.1.call-update) | async-done | bytes 1572880 | tf_op jit(solution)/shard_map/reduce_scatter | solution.py:777
  779.5 8.4 collective-permute-done.122
  797.2 4.7 multiply_convert_fusion.5
  805.2 5.9 fusion.67
  818.7 4.7 fusion.107
  826.8 7.8 add_convert_fusion
  837.7 7.0 add_convert_fusion.3
  856.2 8.8 collective-permute-done.131
  865.0 6.5 collective-permute-done.130
  906.0 5.9 collective-permute-done.105
  911.9 6.0 collective-permute-done.106
  938.3 10.4 collective-permute-done.132
  948.7 10.5 collective-permute-start.109
  963.5 5.2 collective-permute-done.108
  1005.0 9.2 scan_backward.3
  1016.9 9.2 scan_backward.2
  1027.7 7.6 multiply_reduce_fusion.1
  1035.3 6.9 multiply_reduce_fusion
  1046.5 5.2 convolution_add_fusion.1
  1051.7 5.3 add_convert_fusion.2
  1057.0 5.8 copy.1226
  1094.3 6.7 collective-permute-done.93
  1108.6 5.2 reshape.798
  1125.6 5.9 all_to_all.27
  1131.5 5.1 all-to-all-start.2
  1145.5 15.2 %all-to-all-done.2 = bf16[8,48,1152]{2,1,0:T(8,128)(2,1)S(1)} async-done(((bf16[8,48,1152]{2,1,0:T(8,128)(2,1)}), bf16[8,48,1152]{2,1,0:T(8,128)(2,1)S(1)}, u32[]{:S(2)}, u32[]{:S(2)}) %all-to-all-start.2) | async-done | bytes 884768 | tf_op jit(solution)/shard_map/all_to_all | solution.py:897
  1164.9 11.8 collective-permute-done.117
  1199.6 5.0 reshape.796
  (1519 shorter events, 642.7 us)
Async XLA Ops:
  7.2 184.5 %all-gather.7.cloned.1.call-start = ((), (), s32[]{:S(2)}) async-start(), calls=%async_computation.13 | async-start | bytes 8847360 | tf_op jit(solution)/shard_map/all_gather | solution.py:593
  68.6 278.2 %all-gather.9.cloned.1.call-start = ((), (), s32[]{:S(2)}) async-start(), calls=%async_computation.14 | async-start | bytes 7864320 | tf_op jit(solution)/shard_map/all_gather | solution.py:665
  74.7 283.2 %all-gather.11.cloned.1.call-start = ((), (), s32[]{:S(2)}) async-start(), calls=%async_computation.15 | async-start | bytes 3932160 | tf_op jit(solution)/shard_map/all_gather | solution.py:666
  78.1 29.3 %collective-permute-start.2 = (bf16[64,1664]{1,0:T(8,128)(2,1)}, bf16[64,1664]{1,0:T(8,128)(2,1)}, u32[]{:S(2)}, u32[]{:S(2)}) collective-permute-start(bf16[64,1664]{1,0:T(8,128)(2,1)} %concatenate.167), channel_id=1, source_target_pairs={{0,6},{2,0},{4,2},{6,4},{1,7},{3,1},{5,3},{7,5},{8,14},{10,8},{12,... | collective-permute-start | bytes 638984 | tf_op jit(solution)/shard_map/ppermute | solution.py:93
  79.4 27.0 %collective-permute-start.1 = (bf16[64,1664]{1,0:T(8,128)(2,1)}, bf16[64,1664]{1,0:T(8,128)(2,1)}, u32[]{:S(2)}, u32[]{:S(2)}) collective-permute-start(bf16[64,1664]{1,0:T(8,128)(2,1)} %concatenate.167), channel_id=1, source_target_pairs={{0,4},{2,6},{4,0},{6,2},{1,5},{3,7},{5,1},{7,3},{8,12},{10,14},{12... | collective-permute-start | bytes 638984 | tf_op jit(solution)/shard_map/ppermute | solution.py:93
  80.1 40.5 %collective-permute-start.3 = (bf16[64,1664]{1,0:T(8,128)(2,1)}, bf16[64,1664]{1,0:T(8,128)(2,1)}, u32[]{:S(2)}, u32[]{:S(2)}) collective-permute-start(bf16[64,1664]{1,0:T(8,128)(2,1)} %concatenate.167), channel_id=1, source_target_pairs={{0,1},{1,0},{2,3},{3,2},{4,5},{5,4},{6,7},{7,6},{8,9},{9,8},{10,11... | collective-permute-start | bytes 638984 | tf_op jit(solution)/shard_map/ppermute | solution.py:93
  80.1 39.0 %collective-permute-start.25 = (bf16[64,1664]{1,0:T(8,128)(2,1)}, bf16[64,1664]{1,0:T(8,128)(2,1)}, u32[]{:S(2)}, u32[]{:S(2)}) collective-permute-start(bf16[64,1664]{1,0:T(8,128)(2,1)} %concatenate.181), channel_id=1, source_target_pairs={{0,6},{2,0},{4,2},{6,4},{1,7},{3,1},{5,3},{7,5},{8,14},{10,8},{12,... | collective-permute-start | bytes 638984 | tf_op jit(solution)/shard_map/ppermute | solution.py:93
  84.3 317.3 %all-gather.13.cloned.1.call-start = ((), (), s32[]{:S(2)}) async-start(), calls=%async_computation.16 | async-start | bytes 7864320 | tf_op jit(solution)/shard_map/all_gather | solution.py:750
  94.9 24.1 %collective-permute-start.24 = (bf16[64,1664]{1,0:T(8,128)(2,1)}, bf16[64,1664]{1,0:T(8,128)(2,1)S(1)}, u32[]{:S(2)}, u32[]{:S(2)}) collective-permute-start(bf16[64,1664]{1,0:T(8,128)(2,1)} %concatenate.181), channel_id=1, source_target_pairs={{0,4},{2,6},{4,0},{6,2},{1,5},{3,7},{5,1},{7,3},{8,12},{10,14},{12... | collective-permute-start | bytes 638984 | tf_op jit(solution)/shard_map/ppermute | solution.py:93
  128.7 35.1 %collective-permute-start.31 = (bf16[96,2048]{1,0:T(8,128)(2,1)}, bf16[96,2048]{1,0:T(8,128)(2,1)}, u32[]{:S(2)}, u32[]{:S(2)}) collective-permute-start(bf16[96,2048]{1,0:T(8,128)(2,1)} %bitcast.25), channel_id=1, source_target_pairs={{0,4},{2,6},{4,0},{6,2},{1,5},{3,7},{5,1},{7,3},{8,12},{10,14},{12... | collective-permute-start | bytes 1179656 | tf_op jit(solution)/shard_map/ppermute | solution.py:93
  128.8 36.0 %collective-permute-start.32 = (bf16[96,2048]{1,0:T(8,128)(2,1)}, bf16[96,2048]{1,0:T(8,128)(2,1)S(1)}, u32[]{:S(2)}, u32[]{:S(2)}) collective-permute-start(bf16[96,2048]{1,0:T(8,128)(2,1)} %bitcast.25), channel_id=1, source_target_pairs={{0,2},{2,4},{4,6},{6,0},{1,3},{3,5},{5,7},{7,1},{8,10},{10,12},{12... | collective-permute-start | bytes 1179656 | tf_op jit(solution)/shard_map/ppermute | solution.py:93
  170.4 274.5 %all-gather.15.cloned.1.call-start = ((), (), s32[]{:S(2)}) async-start(), calls=%async_computation.17 | async-start | bytes 7864320 | tf_op jit(solution)/shard_map/all_gather | solution.py:665
  179.6 278.5 %all-gather.17.cloned.1.call-start = ((), (), s32[]{:S(2)}) async-start(), calls=%async_computation.18 | async-start | bytes 3932160 | tf_op jit(solution)/shard_map/all_gather | solution.py:666
  180.2 587.8 %reduce-scatter.15.cloned.1.call-start = ((), (), s32[]{:S(2)}) async-start(), calls=%async_computation.19 | async-start | bytes 7864320 | tf_op jit(solution)/shard_map/reduce_scatter | solution.py:777
  206.2 44.1 %collective-permute-start.47 = (bf16[64,1536]{1,0:T(8,128)(2,1)S(1)}, bf16[64,1536]{1,0:T(8,128)(2,1)S(1)}, u32[]{:S(2)}, u32[]{:S(2)}) collective-permute-start(bf16[64,1536]{1,0:T(8,128)(2,1)S(1)} %get-tuple-element.109), channel_id=1, source_target_pairs={{0,6},{2,0},{4,2},{6,4},{1,7},{3,1},{5,3},{7,5},{8,14},{10,8},{12,... | collective-permute-start | bytes 589832 | tf_op jit(solution)/shard_map/ppermute | solution.py:93
  206.2 42.5 %collective-permute-start.46 = (bf16[64,1536]{1,0:T(8,128)(2,1)S(1)}, bf16[64,1536]{1,0:T(8,128)(2,1)}, u32[]{:S(2)}, u32[]{:S(2)}) collective-permute-start(bf16[64,1536]{1,0:T(8,128)(2,1)S(1)} %get-tuple-element.109), channel_id=1, source_target_pairs={{0,4},{2,6},{4,0},{6,2},{1,5},{3,7},{5,1},{7,3},{8,12},{10,14},{12... | collective-permute-start | bytes 589832 | tf_op jit(solution)/shard_map/ppermute | solution.py:93
  208.1 39.6 %collective-permute-start.45 = (bf16[64,1536]{1,0:T(8,128)(2,1)S(1)}, bf16[64,1536]{1,0:T(8,128)(2,1)}, u32[]{:S(2)}, u32[]{:S(2)}) collective-permute-start(bf16[64,1536]{1,0:T(8,128)(2,1)S(1)} %get-tuple-element.109), channel_id=1, source_target_pairs={{0,2},{2,4},{4,6},{6,0},{1,3},{3,5},{5,7},{7,1},{8,10},{10,12},{12... | collective-permute-start | bytes 589832 | tf_op jit(solution)/shard_map/ppermute | solution.py:93
  210.1 42.6 %collective-permute-start.48 = (bf16[64,1536]{1,0:T(8,128)(2,1)S(1)}, bf16[64,1536]{1,0:T(8,128)(2,1)}, u32[]{:S(2)}, u32[]{:S(2)}) collective-permute-start(bf16[64,1536]{1,0:T(8,128)(2,1)S(1)} %get-tuple-element.109), channel_id=1, source_target_pairs={{0,1},{1,0},{2,3},{3,2},{4,5},{5,4},{6,7},{7,6},{8,9},{9,8},{10,11... | collective-permute-start | bytes 589832 | tf_op jit(solution)/shard_map/ppermute | solution.py:93
  211.9 20.3 %collective-permute-start.52 = (bf16[64,1536]{1,0:T(8,128)(2,1)S(1)}, bf16[64,1536]{1,0:T(8,128)(2,1)}, u32[]{:S(2)}, u32[]{:S(2)}) collective-permute-start(bf16[64,1536]{1,0:T(8,128)(2,1)S(1)} %get-tuple-element.110), channel_id=1, source_target_pairs={{0,2},{2,4},{4,6},{6,0},{1,3},{3,5},{5,7},{7,1},{8,10},{10,12},{12... | collective-permute-start | bytes 589832 | tf_op jit(solution)/shard_map/ppermute | solution.py:93
  265.1 18.3 %collective-permute-start.43 = (bf16[64,1664]{1,0:T(8,128)(2,1)S(1)}, bf16[64,1664]{1,0:T(8,128)(2,1)S(1)}, u32[]{:S(2)}, u32[]{:S(2)}) collective-permute-start(bf16[64,1664]{1,0:T(8,128)(2,1)S(1)} %get-tuple-element.601), channel_id=1, source_target_pairs={{0,4},{2,6},{4,0},{6,2},{1,5},{3,7},{5,1},{7,3},{8,12},{10,14},{12... | collective-permute-start | bytes 638984 | tf_op jit(solution)/shard_map/ppermute | solution.py:93
  266.1 18.3 %collective-permute-start.8 = (bf16[64,1664]{1,0:T(8,128)(2,1)S(1)}, bf16[64,1664]{1,0:T(8,128)(2,1)S(1)}, u32[]{:S(2)}, u32[]{:S(2)}) collective-permute-start(bf16[64,1664]{1,0:T(8,128)(2,1)S(1)} %get-tuple-element.596), channel_id=1, source_target_pairs={{0,6},{2,0},{4,2},{6,4},{1,7},{3,1},{5,3},{7,5},{8,14},{10,8},{12,... | collective-permute-start | bytes 638984 | tf_op jit(solution)/shard_map/ppermute | solution.py:93
  269.3 19.9 %collective-permute-start.10 = (bf16[64,1664]{1,0:T(8,128)(2,1)S(1)}, bf16[64,1664]{1,0:T(8,128)(2,1)S(1)}, u32[]{:S(2)}, u32[]{:S(2)}) collective-permute-start(bf16[64,1664]{1,0:T(8,128)(2,1)S(1)} %get-tuple-element.597), channel_id=1, source_target_pairs={{0,2},{2,4},{4,6},{6,0},{1,3},{3,5},{5,7},{7,1},{8,10},{10,12},{12... | collective-permute-start | bytes 638984 | tf_op jit(solution)/shard_map/ppermute | solution.py:93
  270.3 30.3 %collective-permute-start.9 = (bf16[64,1664]{1,0:T(8,128)(2,1)S(1)}, bf16[64,1664]{1,0:T(8,128)(2,1)S(1)}, u32[]{:S(2)}, u32[]{:S(2)}) collective-permute-start(bf16[64,1664]{1,0:T(8,128)(2,1)S(1)} %get-tuple-element.598), channel_id=1, source_target_pairs={{0,4},{2,6},{4,0},{6,2},{1,5},{3,7},{5,1},{7,3},{8,12},{10,14},{12... | collective-permute-start | bytes 638984 | tf_op jit(solution)/shard_map/ppermute | solution.py:93
  303.0 28.1 %collective-permute-start.13 = (bf16[64,1536]{1,0:T(8,128)(2,1)S(1)}, bf16[64,1536]{1,0:T(8,128)(2,1)S(1)}, u32[]{:S(2)}, u32[]{:S(2)}) collective-permute-start(bf16[64,1536]{1,0:T(8,128)(2,1)S(1)} %get-tuple-element.534), channel_id=1, source_target_pairs={{0,6},{2,0},{4,2},{6,4},{1,7},{3,1},{5,3},{7,5},{8,14},{10,8},{12,... | collective-permute-start | bytes 589832 | tf_op jit(solution)/shard_map/ppermute | solution.py:93
  306.8 24.3 %collective-permute-start.12 = (bf16[64,1536]{1,0:T(8,128)(2,1)S(1)}, bf16[64,1536]{1,0:T(8,128)(2,1)S(1)}, u32[]{:S(2)}, u32[]{:S(2)}) collective-permute-start(bf16[64,1536]{1,0:T(8,128)(2,1)S(1)} %get-tuple-element.534), channel_id=1, source_target_pairs={{0,4},{2,6},{4,0},{6,2},{1,5},{3,7},{5,1},{7,3},{8,12},{10,14},{12... | collective-permute-start | bytes 589832 | tf_op jit(solution)/shard_map/ppermute | solution.py:93
  306.8 24.4 %collective-permute-start.14 = (bf16[64,1536]{1,0:T(8,128)(2,1)S(1)}, bf16[64,1536]{1,0:T(8,128)(2,1)S(1)}, u32[]{:S(2)}, u32[]{:S(2)}) collective-permute-start(bf16[64,1536]{1,0:T(8,128)(2,1)S(1)} %get-tuple-element.534), channel_id=1, source_target_pairs={{0,1},{1,0},{2,3},{3,2},{4,5},{5,4},{6,7},{7,6},{8,9},{9,8},{10,11... | collective-permute-start | bytes 589832 | tf_op jit(solution)/shard_map/ppermute | solution.py:93
  306.8 28.6 %collective-permute-start.68 = (bf16[64,1536]{1,0:T(8,128)(2,1)S(1)}, bf16[64,1536]{1,0:T(8,128)(2,1)}, u32[]{:S(2)}, u32[]{:S(2)}) collective-permute-start(bf16[64,1536]{1,0:T(8,128)(2,1)S(1)} %get-tuple-element.665), channel_id=1, source_target_pairs={{0,4},{2,6},{4,0},{6,2},{1,5},{3,7},{5,1},{7,3},{8,12},{10,14},{12... | collective-permute-start | bytes 589832 | tf_op jit(solution)/shard_map/ppermute | solution.py:93
  311.9 20.0 %collective-permute-start.67 = (bf16[64,1536]{1,0:T(8,128)(2,1)S(1)}, bf16[64,1536]{1,0:T(8,128)(2,1)}, u32[]{:S(2)}, u32[]{:S(2)}) collective-permute-start(bf16[64,1536]{1,0:T(8,128)(2,1)S(1)} %get-tuple-element.665), channel_id=1, source_target_pairs={{0,2},{2,4},{4,6},{6,0},{1,3},{3,5},{5,7},{7,1},{8,10},{10,12},{12... | collective-permute-start | bytes 589832 | tf_op jit(solution)/shard_map/ppermute | solution.py:93
  339.2 27.2 %collective-permute-start.72 = (bf16[64,1536]{1,0:T(8,128)(2,1)}, bf16[64,1536]{1,0:T(8,128)(2,1)}, u32[]{:S(2)}, u32[]{:S(2)}) collective-permute-start(bf16[64,1536]{1,0:T(8,128)(2,1)} %collective-permute-done.68), channel_id=1, source_target_pairs={{0,1},{1,0},{2,3},{3,2},{4,5},{5,4},{6,7},{7,6},{8,9},{9,8},{10,11... | collective-permute-start | bytes 589832 | tf_op jit(solution)/shard_map/ppermute | solution.py:93
  340.2 25.3 %collective-permute-start.71 = (bf16[64,1536]{1,0:T(8,128)(2,1)}, bf16[64,1536]{1,0:T(8,128)(2,1)}, u32[]{:S(2)}, u32[]{:S(2)}) collective-permute-start(bf16[64,1536]{1,0:T(8,128)(2,1)} %collective-permute-done.67), channel_id=1, source_target_pairs={{0,1},{1,0},{2,3},{3,2},{4,5},{5,4},{6,7},{7,6},{8,9},{9,8},{10,11... | collective-permute-start | bytes 589832 | tf_op jit(solution)/shard_map/ppermute | solution.py:93
  340.8 26.6 %collective-permute-start.73 = (bf16[64,1536]{1,0:T(8,128)(2,1)}, bf16[64,1536]{1,0:T(8,128)(2,1)}, u32[]{:S(2)}, u32[]{:S(2)}) collective-permute-start(bf16[64,1536]{1,0:T(8,128)(2,1)} %collective-permute-done.69), channel_id=1, source_target_pairs={{0,1},{1,0},{2,3},{3,2},{4,5},{5,4},{6,7},{7,6},{8,9},{9,8},{10,11... | collective-permute-start | bytes 589832 | tf_op jit(solution)/shard_map/ppermute | solution.py:93
  426.7 63.2 %collective-permute-start.74 = (bf16[256,1536]{1,0:T(8,128)(2,1)}, bf16[256,1536]{1,0:T(8,128)(2,1)}, u32[]{:S(2)}, u32[]{:S(2)}) collective-permute-start(bf16[256,1536]{1,0:T(8,128)(2,1)} %slice.1886), channel_id=1, source_target_pairs={{0,1},{1,0},{2,3},{3,2},{4,5},{5,4},{6,7},{7,6},{8,9},{9,8},{10,11... | collective-permute-start | bytes 2359304 | tf_op jit(solution)/shard_map/ppermute | solution.py:93
  493.8 21.4 %collective-permute-start.61 = (bf16[64,1664]{1,0:T(8,128)(2,1)S(1)}, bf16[64,1664]{1,0:T(8,128)(2,1)S(1)}, u32[]{:S(2)}, u32[]{:S(2)}) collective-permute-start(bf16[64,1664]{1,0:T(8,128)(2,1)S(1)} %get-tuple-element.595), channel_id=1, source_target_pairs={{0,4},{2,6},{4,0},{6,2},{1,5},{3,7},{5,1},{7,3},{8,12},{10,14},{12... | collective-permute-start | bytes 638984 | tf_op jit(solution)/shard_map/ppermute | solution.py:93
  497.1 21.2 %collective-permute-start.75 = (bf16[64,1536]{1,0:T(8,128)(2,1)S(1)}, bf16[64,1536]{1,0:T(8,128)(2,1)S(1)}, u32[]{:S(2)}, u32[]{:S(2)}) collective-permute-start(bf16[64,1536]{1,0:T(8,128)(2,1)S(1)} %get-tuple-element.629), channel_id=1, source_target_pairs={{0,6},{2,0},{4,2},{6,4},{1,7},{3,1},{5,3},{7,5},{8,14},{10,8},{12,... | collective-permute-start | bytes 589832 | tf_op jit(solution)/shard_map/ppermute | solution.py:93
  498.1 22.1 %collective-permute-start.77 = (bf16[64,1536]{1,0:T(8,128)(2,1)S(1)}, bf16[64,1536]{1,0:T(8,128)(2,1)S(1)}, u32[]{:S(2)}, u32[]{:S(2)}) collective-permute-start(bf16[64,1536]{1,0:T(8,128)(2,1)S(1)} %get-tuple-element.630), channel_id=1, source_target_pairs={{0,2},{2,4},{4,6},{6,0},{1,3},{3,5},{5,7},{7,1},{8,10},{10,12},{12... | collective-permute-start | bytes 589832 | tf_op jit(solution)/shard_map/ppermute | solution.py:93
  499.2 31.9 %collective-permute-start.76 = (bf16[64,1536]{1,0:T(8,128)(2,1)S(1)}, bf16[64,1536]{1,0:T(8,128)(2,1)S(1)}, u32[]{:S(2)}, u32[]{:S(2)}) collective-permute-start(bf16[64,1536]{1,0:T(8,128)(2,1)S(1)} %get-tuple-element.631), channel_id=1, source_target_pairs={{0,4},{2,6},{4,0},{6,2},{1,5},{3,7},{5,1},{7,3},{8,12},{10,14},{12... | collective-permute-start | bytes 589832 | tf_op jit(solution)/shard_map/ppermute | solution.py:93
  574.4 20.9 %collective-permute-start.81 = (bf16[64,1536]{1,0:T(8,128)(2,1)S(1)}, bf16[64,1536]{1,0:T(8,128)(2,1)S(1)}, u32[]{:S(2)}, u32[]{:S(2)}) collective-permute-start(bf16[64,1536]{1,0:T(8,128)(2,1)S(1)} %get-tuple-element.540), channel_id=1, source_target_pairs={{0,4},{2,6},{4,0},{6,2},{1,5},{3,7},{5,1},{7,3},{8,12},{10,14},{12... | collective-permute-start | bytes 589832 | tf_op jit(solution)/shard_map/ppermute | solution.py:93
  649.7 24.0 %collective-permute-start.87 = (bf16[256,1664]{1,0:T(8,128)(2,1)}, bf16[256,1664]{1,0:T(8,128)(2,1)}, u32[]{:S(2)}, u32[]{:S(2)}) collective-permute-start(bf16[256,1664]{1,0:T(8,128)(2,1)} %slice.1881), channel_id=1, source_target_pairs={{0,1},{1,0},{2,3},{3,2},{4,5},{5,4},{6,7},{7,6},{8,9},{9,8},{10,11... | collective-permute-start | bytes 2555912 | tf_op jit(solution)/shard_map/ppermute | solution.py:93
  695.7 225.7 %reduce-scatter.25.cloned.1.call-start = ((), (), s32[]{:S(2)}) async-start(), calls=%async_computation.24 | async-start | bytes 7864320
  738.3 183.2 %reduce-scatter.17.cloned.1.call-start = ((), (), s32[]{:S(2)}) async-start(), calls=%async_computation.20 | async-start | bytes 3932160 | tf_op jit(solution)/shard_map/reduce_scatter | solution.py:777
  776.9 274.8 %reduce-scatter.23.cloned.1.call-start = ((), (), s32[]{:S(2)}) async-start(), calls=%async_computation.23 | async-start | bytes 3932160 | tf_op jit(solution)/shard_map/reduce_scatter | solution.py:777
  814.0 30.7 %collective-permute-start.128 = (bf16[256,1664]{1,0:T(8,128)(2,1)}, bf16[256,1664]{1,0:T(8,128)(2,1)S(1)}, u32[]{:S(2)}, u32[]{:S(2)}) collective-permute-start(bf16[256,1664]{1,0:T(8,128)(2,1)} %slice.1879), channel_id=1, source_target_pairs={{0,1},{1,0},{2,3},{3,2},{4,5},{5,4},{6,7},{7,6},{8,9},{9,8},{10,11... | collective-permute-start | bytes 2555912 | tf_op jit(solution)/shard_map/ppermute | solution.py:93
  846.8 18.2 %collective-permute-start.131 = (bf16[64,1664]{1,0:T(8,128)(2,1)S(1)}, bf16[64,1664]{1,0:T(8,128)(2,1)S(1)}, u32[]{:S(2)}, u32[]{:S(2)}) collective-permute-start(bf16[64,1664]{1,0:T(8,128)(2,1)S(1)} %get-tuple-element.588), channel_id=1, source_target_pairs={{0,2},{2,4},{4,6},{6,0},{1,3},{3,5},{5,7},{7,1},{8,10},{10,12},{12... | collective-permute-start | bytes 638984 | tf_op jit(solution)/shard_map/ppermute | solution.py:93
  850.3 21.2 %collective-permute-start.130 = (bf16[64,1664]{1,0:T(8,128)(2,1)S(1)}, bf16[64,1664]{1,0:T(8,128)(2,1)S(1)}, u32[]{:S(2)}, u32[]{:S(2)}) collective-permute-start(bf16[64,1664]{1,0:T(8,128)(2,1)S(1)} %get-tuple-element.589), channel_id=1, source_target_pairs={{0,4},{2,6},{4,0},{6,2},{1,5},{3,7},{5,1},{7,3},{8,12},{10,14},{12... | collective-permute-start | bytes 638984 | tf_op jit(solution)/shard_map/ppermute | solution.py:93
  872.4 179.3 %reduce-scatter.21.cloned.1.call-start = ((), (), s32[]{:S(2)}) async-start(), calls=%async_computation.22 | async-start | bytes 7864320 | tf_op jit(solution)/shard_map/reduce_scatter | solution.py:777
  873.2 252.4 %reduce-scatter.29.cloned.1.call-start = ((), (), s32[]{:S(2)}) async-start(), calls=%async_computation.26 | async-start | bytes 1966080 | tf_op jit(solution)/shard_map/reduce_scatter | solution.py:841
  921.5 210.1 %reduce-scatter.19.cloned.1.call-start = ((), (), s32[]{:S(2)}) async-start(), calls=%async_computation.21 | async-start | bytes 4423680 | tf_op jit(solution)/shard_map/reduce_scatter | solution.py:896
  928.8 34.0 %collective-permute-start.134 = (bf16[64,1664]{1,0:T(8,128)(2,1)S(1)}, bf16[64,1664]{1,0:T(8,128)(2,1)S(1)}, u32[]{:S(2)}, u32[]{:S(2)}) collective-permute-start(bf16[64,1664]{1,0:T(8,128)(2,1)S(1)} %concatenate.212), channel_id=1, source_target_pairs={{0,6},{2,0},{4,2},{6,4},{1,7},{3,1},{5,3},{7,5},{8,14},{10,8},{12,... | collective-permute-start | bytes 638984 | tf_op jit(solution)/shard_map/ppermute | solution.py:93
  933.3 27.6 %collective-permute-start.133 = (bf16[64,1664]{1,0:T(8,128)(2,1)S(1)}, bf16[64,1664]{1,0:T(8,128)(2,1)}, u32[]{:S(2)}, u32[]{:S(2)}) collective-permute-start(bf16[64,1664]{1,0:T(8,128)(2,1)S(1)} %concatenate.212), channel_id=1, source_target_pairs={{0,4},{2,6},{4,0},{6,2},{1,5},{3,7},{5,1},{7,3},{8,12},{10,14},{12... | collective-permute-start | bytes 638984 | tf_op jit(solution)/shard_map/ppermute | solution.py:93
  933.9 39.4 %collective-permute-start.135 = (bf16[64,1664]{1,0:T(8,128)(2,1)S(1)}, bf16[64,1664]{1,0:T(8,128)(2,1)}, u32[]{:S(2)}, u32[]{:S(2)}) collective-permute-start(bf16[64,1664]{1,0:T(8,128)(2,1)S(1)} %concatenate.212), channel_id=1, source_target_pairs={{0,1},{1,0},{2,3},{3,2},{4,5},{5,4},{6,7},{7,6},{8,9},{9,8},{10,11... | collective-permute-start | bytes 638984 | tf_op jit(solution)/shard_map/ppermute | solution.py:93
  935.1 37.6 %collective-permute-start.110 = (bf16[64,1664]{1,0:T(8,128)(2,1)S(1)}, bf16[64,1664]{1,0:T(8,128)(2,1)S(1)}, u32[]{:S(2)}, u32[]{:S(2)}) collective-permute-start(bf16[64,1664]{1,0:T(8,128)(2,1)S(1)} %concatenate.203), channel_id=1, source_target_pairs={{0,6},{2,0},{4,2},{6,4},{1,7},{3,1},{5,3},{7,5},{8,14},{10,8},{12,... | collective-permute-start | bytes 638984 | tf_op jit(solution)/shard_map/ppermute | solution.py:93
  948.7 23.9 %collective-permute-start.109 = (bf16[64,1664]{1,0:T(8,128)(2,1)S(1)}, bf16[64,1664]{1,0:T(8,128)(2,1)S(1)}, u32[]{:S(2)}, u32[]{:S(2)}) collective-permute-start(bf16[64,1664]{1,0:T(8,128)(2,1)S(1)} %concatenate.203), channel_id=1, source_target_pairs={{0,4},{2,6},{4,0},{6,2},{1,5},{3,7},{5,1},{7,3},{8,12},{10,14},{12... | collective-permute-start | bytes 638984 | tf_op jit(solution)/shard_map/ppermute | solution.py:93
  988.9 190.2 %reduce-scatter.27.cloned.1.call-start = ((), (), s32[]{:S(2)}) async-start(), calls=%async_computation.25 | async-start | bytes 4423680 | tf_op jit(solution)/shard_map/reduce_scatter | solution.py:896
  993.1 76.1 %collective-permute-start.91 = (bf16[256,1536]{1,0:T(8,128)(2,1)}, bf16[256,1536]{1,0:T(8,128)(2,1)}, u32[]{:S(2)}, u32[]{:S(2)}) collective-permute-start(bf16[256,1536]{1,0:T(8,128)(2,1)} %slice.1885), channel_id=1, source_target_pairs={{0,1},{1,0},{2,3},{3,2},{4,5},{5,4},{6,7},{7,6},{8,9},{9,8},{10,11... | collective-permute-start | bytes 2359304 | tf_op jit(solution)/shard_map/ppermute | solution.py:93
  1066.9 18.2 %collective-permute-start.65 = (bf16[64,1536]{1,0:T(8,128)(2,1)S(1)}, bf16[64,1536]{1,0:T(8,128)(2,1)S(1)}, u32[]{:S(2)}, u32[]{:S(2)}) collective-permute-start(bf16[64,1536]{1,0:T(8,128)(2,1)S(1)} %get-tuple-element.618), channel_id=1, source_target_pairs={{0,4},{2,6},{4,0},{6,2},{1,5},{3,7},{5,1},{7,3},{8,12},{10,14},{12... | collective-permute-start | bytes 589832 | tf_op jit(solution)/shard_map/ppermute | solution.py:93
  1073.3 21.0 %collective-permute-start.92 = (bf16[64,1536]{1,0:T(8,128)(2,1)S(1)}, bf16[64,1536]{1,0:T(8,128)(2,1)S(1)}, u32[]{:S(2)}, u32[]{:S(2)}) collective-permute-start(bf16[64,1536]{1,0:T(8,128)(2,1)S(1)} %get-tuple-element.619), channel_id=1, source_target_pairs={{0,6},{2,0},{4,2},{6,4},{1,7},{3,1},{5,3},{7,5},{8,14},{10,8},{12,... | collective-permute-start | bytes 589832 | tf_op jit(solution)/shard_map/ppermute | solution.py:93
  1078.3 22.6 %collective-permute-start.93 = (bf16[64,1536]{1,0:T(8,128)(2,1)S(1)}, bf16[64,1536]{1,0:T(8,128)(2,1)S(1)}, u32[]{:S(2)}, u32[]{:S(2)}) collective-permute-start(bf16[64,1536]{1,0:T(8,128)(2,1)S(1)} %get-tuple-element.621), channel_id=1, source_target_pairs={{0,4},{2,6},{4,0},{6,2},{1,5},{3,7},{5,1},{7,3},{8,12},{10,14},{12... | collective-permute-start | bytes 589832 | tf_op jit(solution)/shard_map/ppermute | solution.py:93
  1088.6 29.4 %collective-permute-start.139 = (bf16[256,1536]{1,0:T(8,128)(2,1)}, bf16[256,1536]{1,0:T(8,128)(2,1)}, u32[]{:S(2)}, u32[]{:S(2)}) collective-permute-start(bf16[256,1536]{1,0:T(8,128)(2,1)} %slice.1883), channel_id=1, source_target_pairs={{0,1},{1,0},{2,3},{3,2},{4,5},{5,4},{6,7},{7,6},{8,9},{9,8},{10,11... | collective-permute-start | bytes 2359304 | tf_op jit(solution)/shard_map/ppermute | solution.py:93
  1121.5 19.8 %collective-permute-start.140 = (bf16[64,1536]{1,0:T(8,128)(2,1)S(1)}, bf16[64,1536]{1,0:T(8,128)(2,1)}, u32[]{:S(2)}, u32[]{:S(2)}) collective-permute-start(bf16[64,1536]{1,0:T(8,128)(2,1)S(1)} %get-tuple-element.609), channel_id=1, source_target_pairs={{0,6},{2,0},{4,2},{6,4},{1,7},{3,1},{5,3},{7,5},{8,14},{10,8},{12,... | collective-permute-start | bytes 589832 | tf_op jit(solution)/shard_map/ppermute | solution.py:93
  1131.5 29.1 %all-to-all-start.2 = ((bf16[8,48,1152]{2,1,0:T(8,128)(2,1)}), bf16[8,48,1152]{2,1,0:T(8,128)(2,1)S(1)}, u32[]{:S(2)}, u32[]{:S(2)}) async-start(bf16[8,48,1152]{2,1,0:T(8,128)(2,1)} %bitcast.440), calls=%async_computation.5 | async-start | bytes 1769472 | tf_op jit(solution)/shard_map/all_to_all | solution.py:897
  1137.5 23.3 %collective-permute-start.116 = (bf16[64,1536]{1,0:T(8,128)(2,1)}, bf16[64,1536]{1,0:T(8,128)(2,1)S(1)}, u32[]{:S(2)}, u32[]{:S(2)}) collective-permute-start(bf16[64,1536]{1,0:T(8,128)(2,1)} %get-tuple-element.606), channel_id=1, source_target_pairs={{0,6},{2,0},{4,2},{6,4},{1,7},{3,1},{5,3},{7,5},{8,14},{10,8},{12,... | collective-permute-start | bytes 589832 | tf_op jit(solution)/shard_map/ppermute | solution.py:93
  1141.3 23.7 %collective-permute-start.118 = (bf16[64,1536]{1,0:T(8,128)(2,1)}, bf16[64,1536]{1,0:T(8,128)(2,1)S(1)}, u32[]{:S(2)}, u32[]{:S(2)}) collective-permute-start(bf16[64,1536]{1,0:T(8,128)(2,1)} %get-tuple-element.607), channel_id=1, source_target_pairs={{0,2},{2,4},{4,6},{6,0},{1,3},{3,5},{5,7},{7,1},{8,10},{10,12},{12... | collective-permute-start | bytes 589832 | tf_op jit(solution)/shard_map/ppermute | solution.py:93
  1141.3 35.4 %collective-permute-start.117 = (bf16[64,1536]{1,0:T(8,128)(2,1)}, bf16[64,1536]{1,0:T(8,128)(2,1)S(1)}, u32[]{:S(2)}, u32[]{:S(2)}) collective-permute-start(bf16[64,1536]{1,0:T(8,128)(2,1)} %get-tuple-element.608), channel_id=1, source_target_pairs={{0,4},{2,6},{4,0},{6,2},{1,5},{3,7},{5,1},{7,3},{8,12},{10,14},{12... | collective-permute-start | bytes 589832 | tf_op jit(solution)/shard_map/ppermute | solution.py:93
  1179.1 27.3 %all-to-all-start.3 = ((bf16[8,48,1152]{2,1,0:T(8,128)(2,1)}), bf16[8,48,1152]{2,1,0:T(8,128)(2,1)}, u32[]{:S(2)}, u32[]{:S(2)}) async-start(bf16[8,48,1152]{2,1,0:T(8,128)(2,1)} %bitcast.441), calls=%async_computation.8 | async-start | bytes 1769472 | tf_op jit(solution)/shard_map/all_to_all | solution.py:897
  (418 other events, 4391.0 us)
Sparse Core Ops, SparseCore 0:
  68.7 75.6 all-gather.6
  146.3 70.1 all-gather.8
  218.3 43.9 all-gather.10
  264.0 70.1 all-gather.12
  335.9 70.1 all-gather.14
  407.8 43.9 all-gather.16
  695.8 72.0 reduce-scatter.14
  770.9 70.2 reduce-scatter.24
  844.7 43.9 reduce-scatter.16
  891.5 43.9 reduce-scatter.22
  938.5 70.1 reduce-scatter.20
  1010.9 35.2 reduce-scatter.28
  1049.3 46.2 reduce-scatter.18
  1098.6 47.2 reduce-scatter.26

commit v5 on v4

--- a/solution.py
+++ b/solution.py
@@ -610,8 +610,6 @@
             blank,
             by_owner(w_mix_out.T, n_tp),
         ]
-        + shared_pack(shared_in_m, shared_down_m)
-        + shared_pack(shared_in, shared_down)
     )
     w_m = whole_rows(moved_m)
 
@@ -628,6 +626,10 @@
         rows_in.append(gather_rows(x_info))
     in_width = 2 * chan + 2 * STATE
     w_in_here = w_m[:, :in_width]
+    moved_s = moved_columns(
+        shared_pack(shared_in_m, shared_down_m) + shared_pack(shared_in, shared_down), rows_in
+    )
+    w_s = whole_rows(moved_s)
     at = in_width + step_width
     w_step = w_m[:, in_width:at]
     w_dt_here = w_step[:, :128]
@@ -653,8 +655,7 @@
     skip_here = lax.dynamic_slice_in_dim(skip_scale, slot * heads, heads)
 
     w_scan = w_m[:, : in_width + 128]
-    w_mix_t = w_m[:, at : at + chan]
-    at += chan
+    w_mix_t = w_m[:, at:]
 
     n_dp = lax.axis_size("dp")
 
@@ -670,8 +671,8 @@
     up_m, low_m = expert_weights(expert_in_m, expert_down_m)
     moe_m = {
         "router": router_m_full,
-        "shared_in": w_m[:, at : at + 2 * ff],
-        "shared_down_t": w_m[:, at + 2 * ff : at + 3 * ff],
+        "shared_in": w_s[:, : 2 * ff],
+        "shared_down_t": w_s[:, 2 * ff : 3 * ff],
         "expert_in": up_m,
         "expert_down": low_m,
     }
@@ -683,8 +684,8 @@
     up_a, low_a = expert_weights(expert_in, expert_down)
     moe_a = {
         "router": router_full,
-        "shared_in": w_m[:, at + 3 * ff : at + 5 * ff],
-        "shared_down_t": w_m[:, at + 5 * ff :],
+        "shared_in": w_s[:, 3 * ff : 5 * ff],
+        "shared_down_t": w_s[:, 5 * ff :],
         "expert_in": up_a,
         "expert_down": low_a,
     }
@@ -715,8 +716,6 @@
         proj = nn(mamba_in, w_in_here, bf16)
         dt_raw = nn(mamba_in, w_dt_here)
         proj_all.append(proj)
-        cot, _ = fence(cotangent[m], proj)
-        cot_all.append(gather_rows(cot))
         pars = (seg_col, seg_row, conv_par, chan_par, head_par)
         gained, square = scan_forward(heads, length, proj, dt_raw, *pars)
         partial = nt(gained, w_mix_t)
@@ -739,7 +738,7 @@
         ],
         axis=2,
     ).transpose(1, 0, 2)
-    attn_pack, _ = fence(attn_pack, rows_in)
+    attn_pack, _ = fence(attn_pack, moved_s)
     attn_pack = lax.all_to_all(attn_pack, "core", split_axis=0, concat_axis=0, tiled=True)
     own = attn_pack.reshape(2 * rows, -1)
     n_z = lax.axis_size("z")
@@ -747,11 +746,11 @@
     twice = jnp.concatenate(parts + parts, axis=0)
     start = (n_z - 1 - lax.axis_index("z")) * 2 * rows
     attn_w = lax.dynamic_slice(twice, (start, 0), (n_z * 2 * rows, own.shape[1]))
+    attn_w, _ = fence(attn_w, mamba_kept[-1][-1])
     attn_w = lax.all_gather(attn_w, FS, axis=0, tiled=True)
     w_qkv_here = attn_w[:, : q_width + 2 * kv_width]
     w_out_t = attn_w[:, q_width + 2 * kv_width :]
 
-    hidden_one[-1], cot_all = fence(hidden_one[-1], cot_all)
     one_kept, layer_one = [], []
     for m in each:
         normed, scale, own = rms_forward(hidden_one[m], gain_moe_m)
@@ -760,12 +759,15 @@
         one_kept.append((normed, scale, kept))
     attn_kept, hidden_two = [], []
     for m in each:
+        cot, _ = fence(cotangent[m], layer_one[m])
+        cot_all.append(gather_rows(cot))
         normed, scale, own = rms_forward(layer_one[m], gain_attn)
         branch, kept = attn_forward(own, allowed[m], w_qkv_here, w_out_t)
         hidden_two.append(layer_one[m] + branch)
         attn_kept.append((normed, scale, kept))
     two_kept, results = [], []
     for m in each:
+        hidden_two[m], cot_all[m] = fence(hidden_two[m], cot_all[m])
         normed, scale, own = rms_forward(hidden_two[m], gain_moe)
         total, kept = moe_forward(own, masks[m][1], moe_a)
         results.append(total)
@@ -831,22 +833,24 @@
         )
         attn_back.append(grad_in)
         sides.append(side)
-    g_attn = jnp.concatenate(
-        [tn_sum([(s[0], s[1]) for s in sides]), tn_sum([(s[3], s[2]) for s in sides])], axis=1
+    g_attn = by_rows(
+        jnp.concatenate(
+            [
+                by_rows(tn_sum([(s[0], s[1]) for s in sides])),
+                by_rows(tn_sum([(s[3], s[2]) for s in sides])),
+            ],
+            axis=1,
+        )
     )
     attn_back[-1], g_attn = lax.optimization_barrier((attn_back[-1], g_attn))
-    attn_back[-1], sum_in_a = fence(attn_back[-1], sum_in_a)
     g_attn = lax.psum_scatter(g_attn, FS, scatter_dimension=0, tiled=True)
     g_part = g_attn
-    g_attn = lax.psum_scatter(g_attn, "z", scatter_dimension=0, tiled=True)
-    g_attn = lax.all_to_all(
-        g_attn.reshape(2, rows, -1), "core", split_axis=0, concat_axis=0, tiled=True
-    ).astype(f32)
     for m in each:
         normed, scale, _ = attn_kept[m]
         grad_values, part = rms_backward(attn_back[m], normed, scale, gain_attn)
         gains[2] = gains[2] + part
         grad_layer.append(grad_two[m] + grad_values)
+    grad_layer[-1], sum_in_a = fence(grad_layer[-1], sum_in_a)
 
     values, (g_in_m, g_down_m, g_sin_m, g_sdown_m), gains[1], g_router_m, before = moe_stage(
         [gather_rows(g.astype(bf16)) for g in grad_layer],
@@ -856,7 +860,8 @@
         sum_down_a,
         g_part,
     )
-    sum_down_a = before[0]
+    sum_down_a, g_part = before
+    out_expert_in, out_expert_down = expert_out(sum_in_a, sum_down_a)
     sum_in_m = over_dp(g_in_m)
     sum_down_m = over_dp(g_down_m)
     grad_one = [grad_layer[m] + values[m] for m in each]
@@ -874,6 +879,10 @@
         mean_term = jnp.sum(grad_mix.astype(f32) * mix_branch, axis=-1, keepdims=True) / DI
         extra = lanes(split_two(gate_scale) + split_two(mean_term), 128)
         rows_all = gather_rows(jnp.concatenate([grad_mix, extra], axis=1))
+        if m == micro - 1:
+            rows_all, out_expert_in, out_expert_down = fence(
+                rows_all, out_expert_in, out_expert_down
+            )
         mix_all = rows_all[:, :D]
         extra_all = rows_all[:, D:]
         scale_all = extra_all[:, 0:1].astype(f32) + extra_all[:, 1:2].astype(f32)
@@ -881,7 +890,7 @@
         mixes.append(scaled_mix)
         if m == micro - 1:
             g_mix = tn_sum([(x, k[4]) for x, k in zip(mixes, mamba_kept)])
-            mix_all, g_mix = fence(mix_all, g_mix)
+            mix_all, g_mix = fence(mix_all, by_rows(g_mix))
         grad_gated = nn(mix_all, w_mix_t, bf16)
         grad_scan, *grads = scan_backward(
             heads, length, *scan_args, grad_gated, extra_all
@@ -892,6 +901,17 @@
         gains[0] = gains[0] + jnp.sum(total * normed_x, axis=0)
         mamba_back.append(return_rows(total))
 
+    g_part, _ = fence(g_part, mixes)
+    blocks = g_part.reshape(n_z, 2 * rows, -1)
+    here = lax.axis_index("z")
+    g_attn = lax.dynamic_index_in_dim(blocks, here, 0, keepdims=False).astype(f32)
+    for shift in range(1, n_z):
+        block = lax.dynamic_index_in_dim(blocks, (here + shift) % n_z, 0, keepdims=False)
+        g_attn = g_attn + send(block, "z", ring(shift)).astype(f32)
+    g_attn = lax.all_to_all(
+        g_attn.astype(bf16).reshape(2, rows, -1), "core", split_axis=0, concat_axis=0, tiled=True
+    ).astype(f32)
+
     def rows_back(packed):
         packed = lax.psum_scatter(packed, FS, scatter_dimension=0, tiled=True)
         return lax.all_to_all(
@@ -905,9 +925,8 @@
         jnp.concatenate([g_mix, g_sin_m, g_sdown_m, g_sin_a, g_sdown_a], axis=1)
     )
 
-    g_scan = tn_sum(mamba_sides, f32)
+    g_scan = by_rows(tn_sum(mamba_sides, f32))
     g_scan, sum_in_m, sum_down_m = fence(g_scan, sum_in_m, sum_down_m)
-    out_expert_in, out_expert_down = expert_out(sum_in_a, sum_down_a)
     out_expert_in_m, out_expert_down_m = expert_out(sum_in_m, sum_down_m)
 
     conv_sums, chan_sums, head_sums = small

time: 1230 us -> 1290 us (1.049)
  waiting for transfers between devices: 343 us -> 465 us
  blocking collectives: 59.1 us -> 27.9 us
  local copies, waits for them, and re-layouts: 207 us -> 180 us
  matrix products: 286 us -> 265 us
    ppermute x148 -> x151, waiting for transfers between devices: 297 us -> 367 us  [send(): return by_rows(lax.ppermute(by_rows(x), axis, pairs))]
    unnamed x736 -> x729, local copies, waits for them, and re-layouts: 95.9 us -> 55.5 us
    all_to_all x0 -> x1, waiting for transfers between devices: none -> 29.3 us  [moved_columns(): moved = lax.all_to_all(packed, TP, split_axis=0, concat_axis=0, tiled=True)]
    all_to_all x1, blocking collectives: 48.4 us -> 19.9 us  [moved_columns(): moved = lax.all_to_all(packed, TP, split_axis=0, concat_axis=0, tiled=True)]
    reduce_scatter x4, waiting for transfers between devices: 27.8 us -> 45.6 us  [over_dp(): return lax.psum_scatter(g, 'dp', scatter_dimension=0, tiled=True)]
    dot_general x86, matrix products: 271 us -> 255 us  [dot(): r = lax.dot_general(a, b, (dims, ((), ())), preferred_element_type=f32)]
    ppermute x148 -> x151, starting transfers between devices: 147 us -> 150 us  [send(): return by_rows(lax.ppermute(by_rows(x), axis, pairs))]
  transfers between devices with their start and end apart: 164 -> 168, of which waited for: 57 -> 76; matrix products, arithmetic and copies ran while one was open for 40% -> 38% of each run, Pallas kernels for 2% -> 2%
where the time goes in v5:
time: 1290 us; the launch traced here: 1280 us
  waiting for transfers between devices  465 us (36%)
  matrix products  265 us (21%)
  local copies, waits for them, and re-layouts  180 us (14%)
  starting transfers between devices  168 us (13%)
  other arithmetic  125 us (10%)
  Pallas kernels  28.2 us (2%)
  blocking collectives  27.9 us (2%)
  between operations  20.1 us (2%)
    ppermute x151, waiting for transfers between devices, send(): return by_rows(lax.ppermute(by_rows(x), axis, pairs))  367 us
    dot_general x86, matrix products, dot(): r = lax.dot_general(a, b, (dims, ((), ())), preferred_element_type=f32)  255 us
    ppermute x151, starting transfers between devices, send(): return by_rows(lax.ppermute(by_rows(x), axis, pairs))  150 us
    unnamed x729, local copies, waits for them, and re-layouts  55.5 us
    reduce_scatter x4, waiting for transfers between devices, over_dp(): return lax.psum_scatter(g, 'dp', scatter_dimension=0, tiled=True)  45.6 us
    all_to_all x1, waiting for transfers between devices, moved_columns(): moved = lax.all_to_all(packed, TP, split_axis=0, concat_axis=0, tiled=True)  29.3 us
    convert_element_type x6, local copies, waits for them, and re-layouts, expert_out(): return (cols.astype(f32), g_low.reshape(local_experts, -1, D).astype(f32))  27.1 us
  transfers between devices with their start and end apart: 168, of which 76 were waited for; matrix products, arithmetic and copies ran while one was open for 38% of the time, Pallas kernels for 2%

profile of v5, /device:TPU:0, one launch (start us, length us, event | category | flops | bytes accessed | tf_op | source)
XLA Modules:
  0.0 1279.9 jit_solution(5251399549583635346)
XLA Ops:
  16.5 6.5 all-to-all-start
  23.1 29.3 %all-to-all-done = bf16[8,48,1536]{2,1,0:T(8,128)(2,1)S(1)} async-done(((bf16[8,48,1536]{2,1,0:T(8,128)(2,1)}), bf16[8,48,1536]{2,1,0:T(8,128)(2,1)S(1)}, u32[]{:S(2)}, u32[]{:S(2)}) %all-to-all-start) | async-done | bytes 1179680 | tf_op jit(solution)/shard_map/all_to_all | solution.py:589
  60.1 11.4 collective-permute-done
  71.5 10.6 collective-permute-start.19
  82.4 8.8 collective-permute-done.18
  99.0 19.9 %all_to_all.30 = bf16[8,48,768]{2,1,0:T(8,128)(2,1)} all-to-all(bf16[8,48,768]{2,1,0:T(8,128)(2,1)S(1)} %copy.871), channel_id=1, replica_groups=mesh['dp'=4,'w'=1,'z'=4,'core'=2] {'z','core'}, dimensions={0} | all-to-all | bytes 1179648 | tf_op jit(solution)/shard_map/all_to_all | solution.py:589
  143.4 6.5 collective-permute-done.30
  149.9 24.8 %collective-permute-done.31 = bf16[96,2048]{1,0:T(8,128)(2,1)S(1)} collective-permute-done((bf16[96,2048]{1,0:T(8,128)(2,1)S(1)}, bf16[96,2048]{1,0:T(8,128)(2,1)S(1)}, u32[]{:S(2)}, u32[]{:S(2)}) %collective-permute-start.31) | collective-permute-done | bytes 393248 | tf_op jit(solution)/shard_map/ppermute | solution.py:93
  245.9 7.6 collective-permute-done.58
  254.6 5.1 collective-permute-done.10
  259.7 11.5 collective-permute-done.9
  282.6 19.7 %collective-permute-done.12 = bf16[64,1536]{1,0:T(8,128)(2,1)S(1)} collective-permute-done((bf16[64,1536]{1,0:T(8,128)(2,1)S(1)}, bf16[64,1536]{1,0:T(8,128)(2,1)S(1)}, u32[]{:S(2)}, u32[]{:S(2)}) %collective-permute-start.12) | collective-permute-done | bytes 196640 | tf_op jit(solution)/shard_map/ppermute | solution.py:93
  322.1 6.8 convolution_convert_fusion.1
  337.7 5.2 fusion.121
  357.4 5.9 collective-permute-done.26
  366.1 13.5 %collective-permute-done.27 = bf16[64,1536]{1,0:T(8,128)(2,1)S(1)} collective-permute-done((bf16[64,1536]{1,0:T(8,128)(2,1)S(1)}, bf16[64,1536]{1,0:T(8,128)(2,1)S(1)}, u32[]{:S(2)}, u32[]{:S(2)}) %collective-permute-start.27) | collective-permute-done | bytes 196640 | tf_op jit(solution)/shard_map/ppermute | solution.py:93
  380.7 12.1 collective-permute-start.34
  401.3 9.0 collective-permute-start.74
  431.9 7.5 collective-permute-done.41
  439.4 10.3 collective-permute-done.42
  465.4 6.7 convolution_convert_fusion.2
  478.0 8.4 select_reduce_fusion.6
  498.8 6.2 fusion.67
  520.1 5.1 collective-permute-done.51
  525.2 6.5 collective-permute-done.50
  588.5 12.3 collective-permute-done.81
  615.7 6.2 multiply_convert_fusion.7
  635.6 6.7 fusion.65
  657.2 8.4 add_convert_fusion.1
  668.3 7.0 add_convert_fusion.4
  682.2 8.2 collective-permute-done.88
  690.4 5.9 collective-permute-done.89
  723.8 45.6 %reduce-scatter.8.cloned.1.call-done = bf16[384,2048]{1,0:T(8,128)(2,1)} async-done(((bf16[1536,2048]{1,0:T(8,128)(2,1)}), bf16[384,2048]{1,0:T(8,128)(2,1)}) %reduce-scatter.8.cloned.1.call-update) | async-done | bytes 1572880 | tf_op jit(solution)/shard_map/reduce_scatter | solution.py:779
  778.2 8.4 collective-permute-done.122
  791.5 5.4 multiply_convert_fusion.5
  804.6 5.8 fusion.63
  825.1 8.3 add_convert_fusion
  836.8 7.4 add_convert_fusion.3
  854.7 8.1 collective-permute-done.131
  862.9 6.8 collective-permute-done.130
  891.7 5.8 fusion.64
  902.1 5.3 fusion.115
  927.9 11.6 collective-permute-done.106
  955.0 5.2 reshape.806
  970.5 5.1 collective-permute-done.132
  975.6 9.0 collective-permute-done.133
  993.1 9.4 collective-permute-done.108
  1002.6 11.1 collective-permute-done.109
  1051.4 9.4 scan_backward.2
  1063.3 9.2 scan_backward.3
  1074.8 8.0 multiply_reduce_fusion
  1082.9 6.9 multiply_reduce_fusion.1
  1099.5 5.2 convolution_add_fusion.1
  1104.6 5.4 add_convert_fusion.2
  1127.2 6.1 collective-permute-done.93
  1143.5 5.3 collective-permute-done.148
  1148.8 7.1 collective-permute-done.150
  1155.9 16.4 %collective-permute-done.149 = bf16[96,2048]{1,0:T(8,128)(2,1)S(1)} collective-permute-done((bf16[96,2048]{1,0:T(8,128)(2,1)S(1)}, bf16[96,2048]{1,0:T(8,128)(2,1)S(1)}, u32[]{:S(2)}, u32[]{:S(2)}) %collective-permute-start.149) | collective-permute-done | bytes 393248 | tf_op jit(solution)/shard_map/ppermute | solution.py:93
  1182.6 5.1 all-to-all-start.3
  1195.5 7.9 collective-permute-done.141
  1204.7 22.4 %all-to-all-done.3 = bf16[8,48,1152]{2,1,0:T(8,128)(2,1)S(1)} async-done(((bf16[8,48,1152]{2,1,0:T(8,128)(2,1)}), bf16[8,48,1152]{2,1,0:T(8,128)(2,1)S(1)}, u32[]{:S(2)}, u32[]{:S(2)}) %all-to-all-start.3) | async-done | bytes 884768 | tf_op jit(solution)/shard_map/all_to_all | solution.py:917
  1227.2 7.3 collective-permute-done.117
  1237.8 5.1 all-to-all-start.4
  1261.3 5.0 reshape.808
  (1527 shorter events, 649.8 us)
Async XLA Ops:
  16.5 35.9 %all-to-all-start = ((bf16[8,48,1536]{2,1,0:T(8,128)(2,1)}), bf16[8,48,1536]{2,1,0:T(8,128)(2,1)S(1)}, u32[]{:S(2)}, u32[]{:S(2)}) async-start(bf16[8,48,1536]{2,1,0:T(8,128)(2,1)} %copy.862), calls=%async_computation | async-start | bytes 2359296 | tf_op jit(solution)/shard_map/all_to_all | solution.py:589
  22.9 153.3 %all-gather.8.cloned.1.call-start = ((), (), s32[]{:S(2)}) async-start(), calls=%async_computation.13 | async-start | bytes 5898240 | tf_op jit(solution)/shard_map/all_gather | solution.py:593
  53.4 263.7 %all-gather.12.cloned.1.call-start = ((), (), s32[]{:S(2)}) async-start(), calls=%async_computation.15 | async-start | bytes 2949120 | tf_op jit(solution)/shard_map/all_gather | solution.py:593
  54.9 27.4 %collective-permute-start.2 = (bf16[64,1664]{1,0:T(8,128)(2,1)S(1)}, bf16[64,1664]{1,0:T(8,128)(2,1)S(1)}, u32[]{:S(2)}, u32[]{:S(2)}) collective-permute-start(bf16[64,1664]{1,0:T(8,128)(2,1)S(1)} %concatenate.170), channel_id=1, source_target_pairs={{0,6},{2,0},{4,2},{6,4},{1,7},{3,1},{5,3},{7,5},{8,14},{10,8},{12,... | collective-permute-start | bytes 638984 | tf_op jit(solution)/shard_map/ppermute | solution.py:93
  56.2 26.0 %collective-permute-start.1 = (bf16[64,1664]{1,0:T(8,128)(2,1)S(1)}, bf16[64,1664]{1,0:T(8,128)(2,1)S(1)}, u32[]{:S(2)}, u32[]{:S(2)}) collective-permute-start(bf16[64,1664]{1,0:T(8,128)(2,1)S(1)} %concatenate.170), channel_id=1, source_target_pairs={{0,4},{2,6},{4,0},{6,2},{1,5},{3,7},{5,1},{7,3},{8,12},{10,14},{12... | collective-permute-start | bytes 638984 | tf_op jit(solution)/shard_map/ppermute | solution.py:93
  57.0 39.2 %collective-permute-start.3 = (bf16[64,1664]{1,0:T(8,128)(2,1)S(1)}, bf16[64,1664]{1,0:T(8,128)(2,1)S(1)}, u32[]{:S(2)}, u32[]{:S(2)}) collective-permute-start(bf16[64,1664]{1,0:T(8,128)(2,1)S(1)} %concatenate.170), channel_id=1, source_target_pairs={{0,1},{1,0},{2,3},{3,2},{4,5},{5,4},{6,7},{7,6},{8,9},{9,8},{10,11... | collective-permute-start | bytes 638984 | tf_op jit(solution)/shard_map/ppermute | solution.py:93
  57.0 38.6 %collective-permute-start.20 = (bf16[64,1664]{1,0:T(8,128)(2,1)S(1)}, bf16[64,1664]{1,0:T(8,128)(2,1)S(1)}, u32[]{:S(2)}, u32[]{:S(2)}) collective-permute-start(bf16[64,1664]{1,0:T(8,128)(2,1)S(1)} %concatenate.183), channel_id=1, source_target_pairs={{0,6},{2,0},{4,2},{6,4},{1,7},{3,1},{5,3},{7,5},{8,14},{10,8},{12,... | collective-permute-start | bytes 638984 | tf_op jit(solution)/shard_map/ppermute | solution.py:93
  71.5 24.0 %collective-permute-start.19 = (bf16[64,1664]{1,0:T(8,128)(2,1)S(1)}, bf16[64,1664]{1,0:T(8,128)(2,1)S(1)}, u32[]{:S(2)}, u32[]{:S(2)}) collective-permute-start(bf16[64,1664]{1,0:T(8,128)(2,1)S(1)} %concatenate.183), channel_id=1, source_target_pairs={{0,4},{2,6},{4,0},{6,2},{1,5},{3,7},{5,1},{7,3},{8,12},{10,14},{12... | collective-permute-start | bytes 638984 | tf_op jit(solution)/shard_map/ppermute | solution.py:93
  118.9 203.2 %all-gather.10.cloned.1.call-start = ((), (), s32[]{:S(2)}) async-start(), calls=%async_computation.14 | async-start | bytes 7864320 | tf_op jit(solution)/shard_map/all_gather | solution.py:666
  131.7 205.9 %all-gather.14.cloned.1.call-start = ((), (), s32[]{:S(2)}) async-start(), calls=%async_computation.16 | async-start | bytes 3932160 | tf_op jit(solution)/shard_map/all_gather | solution.py:667
  132.3 285.9 %all-gather.16.cloned.1.call-start = ((), (), s32[]{:S(2)}) async-start(), calls=%async_computation.17 | async-start | bytes 7864320 | tf_op jit(solution)/shard_map/all_gather | solution.py:750
  142.1 32.6 %collective-permute-start.31 = (bf16[96,2048]{1,0:T(8,128)(2,1)S(1)}, bf16[96,2048]{1,0:T(8,128)(2,1)S(1)}, u32[]{:S(2)}, u32[]{:S(2)}) collective-permute-start(bf16[96,2048]{1,0:T(8,128)(2,1)S(1)} %bitcast.449), channel_id=1, source_target_pairs={{0,4},{2,6},{4,0},{6,2},{1,5},{3,7},{5,1},{7,3},{8,12},{10,14},{12... | collective-permute-start | bytes 1179656 | tf_op jit(solution)/shard_map/ppermute | solution.py:93
  142.8 32.0 %collective-permute-start.32 = (bf16[96,2048]{1,0:T(8,128)(2,1)S(1)}, bf16[96,2048]{1,0:T(8,128)(2,1)S(1)}, u32[]{:S(2)}, u32[]{:S(2)}) collective-permute-start(bf16[96,2048]{1,0:T(8,128)(2,1)S(1)} %bitcast.450), channel_id=1, source_target_pairs={{0,2},{2,4},{4,6},{6,0},{1,3},{3,5},{5,7},{7,1},{8,10},{10,12},{12... | collective-permute-start | bytes 1179656 | tf_op jit(solution)/shard_map/ppermute | solution.py:93
  195.3 270.1 %all-gather.18.cloned.1.call-start = ((), (), s32[]{:S(2)}) async-start(), calls=%async_computation.18 | async-start | bytes 7864320 | tf_op jit(solution)/shard_map/all_gather | solution.py:666
  208.1 269.9 %all-gather.20.cloned.1.call-start = ((), (), s32[]{:S(2)}) async-start(), calls=%async_computation.19 | async-start | bytes 3932160 | tf_op jit(solution)/shard_map/all_gather | solution.py:667
  208.9 560.6 %reduce-scatter.8.cloned.1.call-start = ((), (), s32[]{:S(2)}) async-start(), calls=%async_computation.20 | async-start | bytes 7864320 | tf_op jit(solution)/shard_map/reduce_scatter | solution.py:779
  233.4 20.1 %collective-permute-start.58 = (bf16[64,1664]{1,0:T(8,128)(2,1)S(1)}, bf16[64,1664]{1,0:T(8,128)(2,1)S(1)}, u32[]{:S(2)}, u32[]{:S(2)}) collective-permute-start(bf16[64,1664]{1,0:T(8,128)(2,1)S(1)} %get-tuple-element.563), channel_id=1, source_target_pairs={{0,4},{2,6},{4,0},{6,2},{1,5},{3,7},{5,1},{7,3},{8,12},{10,14},{12... | collective-permute-start | bytes 638984 | tf_op jit(solution)/shard_map/ppermute | solution.py:93
  236.1 18.5 %collective-permute-start.8 = (bf16[64,1664]{1,0:T(8,128)(2,1)S(1)}, bf16[64,1664]{1,0:T(8,128)(2,1)S(1)}, u32[]{:S(2)}, u32[]{:S(2)}) collective-permute-start(bf16[64,1664]{1,0:T(8,128)(2,1)S(1)} %get-tuple-element.558), channel_id=1, source_target_pairs={{0,6},{2,0},{4,2},{6,4},{1,7},{3,1},{5,3},{7,5},{8,14},{10,8},{12,... | collective-permute-start | bytes 638984 | tf_op jit(solution)/shard_map/ppermute | solution.py:93
  237.1 22.6 %collective-permute-start.10 = (bf16[64,1664]{1,0:T(8,128)(2,1)S(1)}, bf16[64,1664]{1,0:T(8,128)(2,1)S(1)}, u32[]{:S(2)}, u32[]{:S(2)}) collective-permute-start(bf16[64,1664]{1,0:T(8,128)(2,1)S(1)} %get-tuple-element.559), channel_id=1, source_target_pairs={{0,2},{2,4},{4,6},{6,0},{1,3},{3,5},{5,7},{7,1},{8,10},{10,12},{12... | collective-permute-start | bytes 638984 | tf_op jit(solution)/shard_map/ppermute | solution.py:93
  239.4 31.8 %collective-permute-start.9 = (bf16[64,1664]{1,0:T(8,128)(2,1)S(1)}, bf16[64,1664]{1,0:T(8,128)(2,1)S(1)}, u32[]{:S(2)}, u32[]{:S(2)}) collective-permute-start(bf16[64,1664]{1,0:T(8,128)(2,1)S(1)} %get-tuple-element.560), channel_id=1, source_target_pairs={{0,4},{2,6},{4,0},{6,2},{1,5},{3,7},{5,1},{7,3},{8,12},{10,14},{12... | collective-permute-start | bytes 638984 | tf_op jit(solution)/shard_map/ppermute | solution.py:93
  273.7 28.7 %collective-permute-start.13 = (bf16[64,1536]{1,0:T(8,128)(2,1)S(1)}, bf16[64,1536]{1,0:T(8,128)(2,1)S(1)}, u32[]{:S(2)}, u32[]{:S(2)}) collective-permute-start(bf16[64,1536]{1,0:T(8,128)(2,1)S(1)} %get-tuple-element.493), channel_id=1, source_target_pairs={{0,6},{2,0},{4,2},{6,4},{1,7},{3,1},{5,3},{7,5},{8,14},{10,8},{12,... | collective-permute-start | bytes 589832 | tf_op jit(solution)/shard_map/ppermute | solution.py:93
  277.5 24.8 %collective-permute-start.12 = (bf16[64,1536]{1,0:T(8,128)(2,1)S(1)}, bf16[64,1536]{1,0:T(8,128)(2,1)S(1)}, u32[]{:S(2)}, u32[]{:S(2)}) collective-permute-start(bf16[64,1536]{1,0:T(8,128)(2,1)S(1)} %get-tuple-element.493), channel_id=1, source_target_pairs={{0,4},{2,6},{4,0},{6,2},{1,5},{3,7},{5,1},{7,3},{8,12},{10,14},{12... | collective-permute-start | bytes 589832 | tf_op jit(solution)/shard_map/ppermute | solution.py:93
  277.5 25.0 %collective-permute-start.14 = (bf16[64,1536]{1,0:T(8,128)(2,1)S(1)}, bf16[64,1536]{1,0:T(8,128)(2,1)S(1)}, u32[]{:S(2)}, u32[]{:S(2)}) collective-permute-start(bf16[64,1536]{1,0:T(8,128)(2,1)S(1)} %get-tuple-element.493), channel_id=1, source_target_pairs={{0,1},{1,0},{2,3},{3,2},{4,5},{5,4},{6,7},{7,6},{8,9},{9,8},{10,11... | collective-permute-start | bytes 589832 | tf_op jit(solution)/shard_map/ppermute | solution.py:93
  277.5 29.0 %collective-permute-start.61 = (bf16[64,1536]{1,0:T(8,128)(2,1)S(1)}, bf16[64,1536]{1,0:T(8,128)(2,1)S(1)}, u32[]{:S(2)}, u32[]{:S(2)}) collective-permute-start(bf16[64,1536]{1,0:T(8,128)(2,1)S(1)} %get-tuple-element.628), channel_id=1, source_target_pairs={{0,4},{2,6},{4,0},{6,2},{1,5},{3,7},{5,1},{7,3},{8,12},{10,14},{12... | collective-permute-start | bytes 589832 | tf_op jit(solution)/shard_map/ppermute | solution.py:93
  282.6 20.5 %collective-permute-start.60 = (bf16[64,1536]{1,0:T(8,128)(2,1)S(1)}, bf16[64,1536]{1,0:T(8,128)(2,1)S(1)}, u32[]{:S(2)}, u32[]{:S(2)}) collective-permute-start(bf16[64,1536]{1,0:T(8,128)(2,1)S(1)} %get-tuple-element.628), channel_id=1, source_target_pairs={{0,2},{2,4},{4,6},{6,0},{1,3},{3,5},{5,7},{7,1},{8,10},{10,12},{12... | collective-permute-start | bytes 589832 | tf_op jit(solution)/shard_map/ppermute | solution.py:93
  353.0 26.5 %collective-permute-start.27 = (bf16[64,1536]{1,0:T(8,128)(2,1)S(1)}, bf16[64,1536]{1,0:T(8,128)(2,1)S(1)}, u32[]{:S(2)}, u32[]{:S(2)}) collective-permute-start(bf16[64,1536]{1,0:T(8,128)(2,1)S(1)} %get-tuple-element.590), channel_id=1, source_target_pairs={{0,4},{2,6},{4,0},{6,2},{1,5},{3,7},{5,1},{7,3},{8,12},{10,14},{12... | collective-permute-start | bytes 589832 | tf_op jit(solution)/shard_map/ppermute | solution.py:93
  353.6 27.1 %collective-permute-start.68 = (bf16[64,1536]{1,0:T(8,128)(2,1)S(1)}, bf16[64,1536]{1,0:T(8,128)(2,1)S(1)}, u32[]{:S(2)}, u32[]{:S(2)}) collective-permute-start(bf16[64,1536]{1,0:T(8,128)(2,1)S(1)} %get-tuple-element.591), channel_id=1, source_target_pairs={{0,6},{2,0},{4,2},{6,4},{1,7},{3,1},{5,3},{7,5},{8,14},{10,8},{12,... | collective-permute-start | bytes 589832 | tf_op jit(solution)/shard_map/ppermute | solution.py:93
  356.8 36.0 %collective-permute-start.70 = (bf16[64,1536]{1,0:T(8,128)(2,1)S(1)}, bf16[64,1536]{1,0:T(8,128)(2,1)S(1)}, u32[]{:S(2)}, u32[]{:S(2)}) collective-permute-start(bf16[64,1536]{1,0:T(8,128)(2,1)S(1)} %get-tuple-element.592), channel_id=1, source_target_pairs={{0,2},{2,4},{4,6},{6,0},{1,3},{3,5},{5,7},{7,1},{8,10},{10,12},{12... | collective-permute-start | bytes 589832 | tf_op jit(solution)/shard_map/ppermute | solution.py:93
  363.4 33.1 %collective-permute-start.69 = (bf16[64,1536]{1,0:T(8,128)(2,1)S(1)}, bf16[64,1536]{1,0:T(8,128)(2,1)S(1)}, u32[]{:S(2)}, u32[]{:S(2)}) collective-permute-start(bf16[64,1536]{1,0:T(8,128)(2,1)S(1)} %get-tuple-element.593), channel_id=1, source_target_pairs={{0,4},{2,6},{4,0},{6,2},{1,5},{3,7},{5,1},{7,3},{8,12},{10,14},{12... | collective-permute-start | bytes 589832 | tf_op jit(solution)/shard_map/ppermute | solution.py:93
  379.8 31.9 %collective-permute-start.36 = (bf16[64,1536]{1,0:T(8,128)(2,1)S(1)}, bf16[64,1536]{1,0:T(8,128)(2,1)}, u32[]{:S(2)}, u32[]{:S(2)}) collective-permute-start(bf16[64,1536]{1,0:T(8,128)(2,1)S(1)} %copy-done.146), channel_id=1, source_target_pairs={{0,6},{2,0},{4,2},{6,4},{1,7},{3,1},{5,3},{7,5},{8,14},{10,8},{12,... | collective-permute-start | bytes 589832 | tf_op jit(solution)/shard_map/ppermute | solution.py:93
  379.9 31.2 %collective-permute-start.35 = (bf16[64,1536]{1,0:T(8,128)(2,1)S(1)}, bf16[64,1536]{1,0:T(8,128)(2,1)S(1)}, u32[]{:S(2)}, u32[]{:S(2)}) collective-permute-start(bf16[64,1536]{1,0:T(8,128)(2,1)S(1)} %copy-done.146), channel_id=1, source_target_pairs={{0,4},{2,6},{4,0},{6,2},{1,5},{3,7},{5,1},{7,3},{8,12},{10,14},{12... | collective-permute-start | bytes 589832 | tf_op jit(solution)/shard_map/ppermute | solution.py:93
  380.7 20.6 %collective-permute-start.34 = (bf16[64,1536]{1,0:T(8,128)(2,1)S(1)}, bf16[64,1536]{1,0:T(8,128)(2,1)S(1)}, u32[]{:S(2)}, u32[]{:S(2)}) collective-permute-start(bf16[64,1536]{1,0:T(8,128)(2,1)S(1)} %copy-done.146), channel_id=1, source_target_pairs={{0,2},{2,4},{4,6},{6,0},{1,3},{3,5},{5,7},{7,1},{8,10},{10,12},{12... | collective-permute-start | bytes 589832 | tf_op jit(solution)/shard_map/ppermute | solution.py:93
  392.8 20.6 %collective-permute-start.37 = (bf16[64,1536]{1,0:T(8,128)(2,1)S(1)}, bf16[64,1536]{1,0:T(8,128)(2,1)S(1)}, u32[]{:S(2)}, u32[]{:S(2)}) collective-permute-start(bf16[64,1536]{1,0:T(8,128)(2,1)S(1)} %copy-done.146), channel_id=1, source_target_pairs={{0,1},{1,0},{2,3},{3,2},{4,5},{5,4},{6,7},{7,6},{8,9},{9,8},{10,11... | collective-permute-start | bytes 589832 | tf_op jit(solution)/shard_map/ppermute | solution.py:93
  397.2 34.1 %collective-permute-start.75 = (bf16[64,1536]{1,0:T(8,128)(2,1)}, bf16[64,1536]{1,0:T(8,128)(2,1)}, u32[]{:S(2)}, u32[]{:S(2)}) collective-permute-start(bf16[64,1536]{1,0:T(8,128)(2,1)} %get-tuple-element.127), channel_id=1, source_target_pairs={{0,6},{2,0},{4,2},{6,4},{1,7},{3,1},{5,3},{7,5},{8,14},{10,8},{12,... | collective-permute-start | bytes 589832 | tf_op jit(solution)/shard_map/ppermute | solution.py:93
  401.3 30.0 %collective-permute-start.74 = (bf16[64,1536]{1,0:T(8,128)(2,1)}, bf16[64,1536]{1,0:T(8,128)(2,1)}, u32[]{:S(2)}, u32[]{:S(2)}) collective-permute-start(bf16[64,1536]{1,0:T(8,128)(2,1)} %get-tuple-element.127), channel_id=1, source_target_pairs={{0,4},{2,6},{4,0},{6,2},{1,5},{3,7},{5,1},{7,3},{8,12},{10,14},{12... | collective-permute-start | bytes 589832 | tf_op jit(solution)/shard_map/ppermute | solution.py:93
  411.0 20.8 %collective-permute-start.73 = (bf16[64,1536]{1,0:T(8,128)(2,1)}, bf16[64,1536]{1,0:T(8,128)(2,1)}, u32[]{:S(2)}, u32[]{:S(2)}) collective-permute-start(bf16[64,1536]{1,0:T(8,128)(2,1)} %get-tuple-element.127), channel_id=1, source_target_pairs={{0,2},{2,4},{4,6},{6,0},{1,3},{3,5},{5,7},{7,1},{8,10},{10,12},{12... | collective-permute-start | bytes 589832 | tf_op jit(solution)/shard_map/ppermute | solution.py:93
  411.7 97.2 %collective-permute-start.76 = (bf16[64,1536]{1,0:T(8,128)(2,1)}, bf16[64,1536]{1,0:T(8,128)(2,1)}, u32[]{:S(2)}, u32[]{:S(2)}) collective-permute-start(bf16[64,1536]{1,0:T(8,128)(2,1)} %get-tuple-element.127), channel_id=1, source_target_pairs={{0,1},{1,0},{2,3},{3,2},{4,5},{5,4},{6,7},{7,6},{8,9},{9,8},{10,11... | collective-permute-start | bytes 589832 | tf_op jit(solution)/shard_map/ppermute | solution.py:93
  431.3 119.5 %collective-permute-start.79 = (bf16[64,1536]{1,0:T(8,128)(2,1)}, bf16[64,1536]{1,0:T(8,128)(2,1)}, u32[]{:S(2)}, u32[]{:S(2)}) collective-permute-start(bf16[64,1536]{1,0:T(8,128)(2,1)} %collective-permute-done.75), channel_id=1, source_target_pairs={{0,1},{1,0},{2,3},{3,2},{4,5},{5,4},{6,7},{7,6},{8,9},{9,8},{10,11... | collective-permute-start | bytes 589832 | tf_op jit(solution)/shard_map/ppermute | solution.py:93
  431.3 103.5 %collective-permute-start.78 = (bf16[64,1536]{1,0:T(8,128)(2,1)}, bf16[64,1536]{1,0:T(8,128)(2,1)}, u32[]{:S(2)}, u32[]{:S(2)}) collective-permute-start(bf16[64,1536]{1,0:T(8,128)(2,1)} %collective-permute-done.74), channel_id=1, source_target_pairs={{0,1},{1,0},{2,3},{3,2},{4,5},{5,4},{6,7},{7,6},{8,9},{9,8},{10,11... | collective-permute-start | bytes 589832 | tf_op jit(solution)/shard_map/ppermute | solution.py:93
  431.8 82.6 %collective-permute-start.77 = (bf16[64,1536]{1,0:T(8,128)(2,1)}, bf16[64,1536]{1,0:T(8,128)(2,1)}, u32[]{:S(2)}, u32[]{:S(2)}) collective-permute-start(bf16[64,1536]{1,0:T(8,128)(2,1)} %collective-permute-done.73), channel_id=1, source_target_pairs={{0,1},{1,0},{2,3},{3,2},{4,5},{5,4},{6,7},{7,6},{8,9},{9,8},{10,11... | collective-permute-start | bytes 589832 | tf_op jit(solution)/shard_map/ppermute | solution.py:93
  579.8 20.9 %collective-permute-start.81 = (bf16[64,1536]{1,0:T(8,128)(2,1)S(1)}, bf16[64,1536]{1,0:T(8,128)(2,1)S(1)}, u32[]{:S(2)}, u32[]{:S(2)}) collective-permute-start(bf16[64,1536]{1,0:T(8,128)(2,1)S(1)} %get-tuple-element.499), channel_id=1, source_target_pairs={{0,4},{2,6},{4,0},{6,2},{1,5},{3,7},{5,1},{7,3},{8,12},{10,14},{12... | collective-permute-start | bytes 589832 | tf_op jit(solution)/shard_map/ppermute | solution.py:93
  651.7 23.6 %collective-permute-start.87 = (bf16[256,1664]{1,0:T(8,128)(2,1)}, bf16[256,1664]{1,0:T(8,128)(2,1)}, u32[]{:S(2)}, u32[]{:S(2)}) collective-permute-start(bf16[256,1664]{1,0:T(8,128)(2,1)} %slice.1871), channel_id=1, source_target_pairs={{0,1},{1,0},{2,3},{3,2},{4,5},{5,4},{6,7},{7,6},{8,9},{9,8},{10,11... | collective-permute-start | bytes 2555912 | tf_op jit(solution)/shard_map/ppermute | solution.py:93
  697.2 263.0 %reduce-scatter.10.cloned.1.call-start = ((), (), s32[]{:S(2)}) async-start(), calls=%async_computation.21 | async-start | bytes 3932160 | tf_op jit(solution)/shard_map/reduce_scatter | solution.py:779
  698.2 262.0 %reduce-scatter.12.cloned.1.call-start = ((), (), s32[]{:S(2)}) async-start(), calls=%async_computation.22 | async-start | bytes 7864320 | tf_op jit(solution)/shard_map/reduce_scatter | solution.py:846
  720.2 384.4 %reduce-scatter.18.cloned.1.call-start = ((), (), s32[]{:S(2)}) async-start(), calls=%async_computation.25 | async-start | bytes 3932160 | tf_op jit(solution)/shard_map/reduce_scatter | solution.py:779
  812.3 31.8 %collective-permute-start.128 = (bf16[256,1664]{1,0:T(8,128)(2,1)}, bf16[256,1664]{1,0:T(8,128)(2,1)}, u32[]{:S(2)}, u32[]{:S(2)}) collective-permute-start(bf16[256,1664]{1,0:T(8,128)(2,1)} %slice.1869), channel_id=1, source_target_pairs={{0,1},{1,0},{2,3},{3,2},{4,5},{5,4},{6,7},{7,6},{8,9},{9,8},{10,11... | collective-permute-start | bytes 2555912 | tf_op jit(solution)/shard_map/ppermute | solution.py:93
  849.1 20.6 %collective-permute-start.130 = (bf16[64,1664]{1,0:T(8,128)(2,1)S(1)}, bf16[64,1664]{1,0:T(8,128)(2,1)S(1)}, u32[]{:S(2)}, u32[]{:S(2)}) collective-permute-start(bf16[64,1664]{1,0:T(8,128)(2,1)S(1)} %get-tuple-element.551), channel_id=1, source_target_pairs={{0,4},{2,6},{4,0},{6,2},{1,5},{3,7},{5,1},{7,3},{8,12},{10,14},{12... | collective-permute-start | bytes 638984 | tf_op jit(solution)/shard_map/ppermute | solution.py:93
  870.6 234.0 %reduce-scatter.16.cloned.1.call-start = ((), (), s32[]{:S(2)}) async-start(), calls=%async_computation.24 | async-start | bytes 7864320 | tf_op jit(solution)/shard_map/reduce_scatter | solution.py:779
  886.2 231.1 %collective-permute-start.53 = (bf16[64,1536]{1,0:T(8,128)(2,1)}, bf16[64,1536]{1,0:T(8,128)(2,1)}, u32[]{:S(2)}, u32[]{:S(2)}) collective-permute-start(bf16[64,1536]{1,0:T(8,128)(2,1)} %get-tuple-element.578), channel_id=1, source_target_pairs={{0,6},{2,0},{4,2},{6,4},{1,7},{3,1},{5,3},{7,5},{8,14},{10,8},{12,... | collective-permute-start | bytes 589832 | tf_op jit(solution)/shard_map/ppermute | solution.py:93
  887.2 232.3 %collective-permute-start.55 = (bf16[64,1536]{1,0:T(8,128)(2,1)}, bf16[64,1536]{1,0:T(8,128)(2,1)}, u32[]{:S(2)}, u32[]{:S(2)}) collective-permute-start(bf16[64,1536]{1,0:T(8,128)(2,1)} %get-tuple-element.579), channel_id=1, source_target_pairs={{0,2},{2,4},{4,6},{6,0},{1,3},{3,5},{5,7},{7,1},{8,10},{10,12},{12... | collective-permute-start | bytes 589832 | tf_op jit(solution)/shard_map/ppermute | solution.py:93
  901.5 281.2 %reduce-scatter.14.cloned.1.call-start = ((), (), s32[]{:S(2)}) async-start(), calls=%async_computation.23 | async-start | bytes 4423680 | tf_op jit(solution)/shard_map/reduce_scatter | solution.py:916
  916.7 22.8 %collective-permute-start.106 = (bf16[64,1664]{1,0:T(8,128)(2,1)}, bf16[64,1664]{1,0:T(8,128)(2,1)}, u32[]{:S(2)}, u32[]{:S(2)}) collective-permute-start(bf16[64,1664]{1,0:T(8,128)(2,1)} %get-tuple-element.548), channel_id=1, source_target_pairs={{0,4},{2,6},{4,0},{6,2},{1,5},{3,7},{5,1},{7,3},{8,12},{10,14},{12... | collective-permute-start | bytes 638984 | tf_op jit(solution)/shard_map/ppermute | solution.py:93
  927.9 193.1 %collective-permute-start.54 = (bf16[64,1536]{1,0:T(8,128)(2,1)}, bf16[64,1536]{1,0:T(8,128)(2,1)}, u32[]{:S(2)}, u32[]{:S(2)}) collective-permute-start(bf16[64,1536]{1,0:T(8,128)(2,1)} %get-tuple-element.580), channel_id=1, source_target_pairs={{0,4},{2,6},{4,0},{6,2},{1,5},{3,7},{5,1},{7,3},{8,12},{10,14},{12... | collective-permute-start | bytes 589832 | tf_op jit(solution)/shard_map/ppermute | solution.py:93
  927.9 112.2 %collective-permute-start.91 = (bf16[256,1536]{1,0:T(8,128)(2,1)}, bf16[256,1536]{1,0:T(8,128)(2,1)}, u32[]{:S(2)}, u32[]{:S(2)}) collective-permute-start(bf16[256,1536]{1,0:T(8,128)(2,1)} %slice.1875), channel_id=1, source_target_pairs={{0,1},{1,0},{2,3},{3,2},{4,5},{5,4},{6,7},{7,6},{8,9},{9,8},{10,11... | collective-permute-start | bytes 2359304 | tf_op jit(solution)/shard_map/ppermute | solution.py:93
  1040.0 197.8 %reduce-scatter.20.cloned.1.call-start = ((), (), s32[]{:S(2)}) async-start(), calls=%async_computation.26 | async-start | bytes 4423680 | tf_op jit(solution)/shard_map/reduce_scatter | solution.py:916
  1138.7 33.5 %collective-permute-start.149 = (bf16[96,2048]{1,0:T(8,128)(2,1)S(1)}, bf16[96,2048]{1,0:T(8,128)(2,1)S(1)}, u32[]{:S(2)}, u32[]{:S(2)}) collective-permute-start(bf16[96,2048]{1,0:T(8,128)(2,1)S(1)} %get-tuple-element.545), channel_id=1, source_target_pairs={{0,4},{2,6},{4,0},{6,2},{1,5},{3,7},{5,1},{7,3},{8,12},{10,14},{12... | collective-permute-start | bytes 1179656 | tf_op jit(solution)/shard_map/ppermute | solution.py:93
  1142.3 45.4 %collective-permute-start.115 = (bf16[256,1536]{1,0:T(8,128)(2,1)S(1)}, bf16[256,1536]{1,0:T(8,128)(2,1)}, u32[]{:S(2)}, u32[]{:S(2)}) collective-permute-start(bf16[256,1536]{1,0:T(8,128)(2,1)S(1)} %slice.1874), channel_id=1, source_target_pairs={{0,1},{1,0},{2,3},{3,2},{4,5},{5,4},{6,7},{7,6},{8,9},{9,8},{10,11... | collective-permute-start | bytes 2359304 | tf_op jit(solution)/shard_map/ppermute | solution.py:93
  1142.9 35.4 %collective-permute-start.139 = (bf16[256,1536]{1,0:T(8,128)(2,1)S(1)}, bf16[256,1536]{1,0:T(8,128)(2,1)S(1)}, u32[]{:S(2)}, u32[]{:S(2)}) collective-permute-start(bf16[256,1536]{1,0:T(8,128)(2,1)S(1)} %slice.1873), channel_id=1, source_target_pairs={{0,1},{1,0},{2,3},{3,2},{4,5},{5,4},{6,7},{7,6},{8,9},{9,8},{10,11... | collective-permute-start | bytes 2359304 | tf_op jit(solution)/shard_map/ppermute | solution.py:93
  1182.4 21.0 %collective-permute-start.141 = (bf16[64,1536]{1,0:T(8,128)(2,1)S(1)}, bf16[64,1536]{1,0:T(8,128)(2,1)}, u32[]{:S(2)}, u32[]{:S(2)}) collective-permute-start(bf16[64,1536]{1,0:T(8,128)(2,1)S(1)} %get-tuple-element.573), channel_id=1, source_target_pairs={{0,4},{2,6},{4,0},{6,2},{1,5},{3,7},{5,1},{7,3},{8,12},{10,14},{12... | collective-permute-start | bytes 589832 | tf_op jit(solution)/shard_map/ppermute | solution.py:93
  1182.6 44.4 %all-to-all-start.3 = ((bf16[8,48,1152]{2,1,0:T(8,128)(2,1)}), bf16[8,48,1152]{2,1,0:T(8,128)(2,1)S(1)}, u32[]{:S(2)}, u32[]{:S(2)}) async-start(bf16[8,48,1152]{2,1,0:T(8,128)(2,1)} %bitcast.465), calls=%async_computation.7 | async-start | bytes 1769472 | tf_op jit(solution)/shard_map/all_to_all | solution.py:917
  1190.5 36.7 %collective-permute-start.116 = (bf16[64,1536]{1,0:T(8,128)(2,1)}, bf16[64,1536]{1,0:T(8,128)(2,1)S(1)}, u32[]{:S(2)}, u32[]{:S(2)}) collective-permute-start(bf16[64,1536]{1,0:T(8,128)(2,1)} %get-tuple-element.568), channel_id=1, source_target_pairs={{0,6},{2,0},{4,2},{6,4},{1,7},{3,1},{5,3},{7,5},{8,14},{10,8},{12,... | collective-permute-start | bytes 589832 | tf_op jit(solution)/shard_map/ppermute | solution.py:93
  1194.3 32.9 %collective-permute-start.118 = (bf16[64,1536]{1,0:T(8,128)(2,1)}, bf16[64,1536]{1,0:T(8,128)(2,1)S(1)}, u32[]{:S(2)}, u32[]{:S(2)}) collective-permute-start(bf16[64,1536]{1,0:T(8,128)(2,1)} %get-tuple-element.569), channel_id=1, source_target_pairs={{0,2},{2,4},{4,6},{6,0},{1,3},{3,5},{5,7},{7,1},{8,10},{10,12},{12... | collective-permute-start | bytes 589832 | tf_op jit(solution)/shard_map/ppermute | solution.py:93
  1194.3 40.2 %collective-permute-start.117 = (bf16[64,1536]{1,0:T(8,128)(2,1)}, bf16[64,1536]{1,0:T(8,128)(2,1)}, u32[]{:S(2)}, u32[]{:S(2)}) collective-permute-start(bf16[64,1536]{1,0:T(8,128)(2,1)} %get-tuple-element.570), channel_id=1, source_target_pairs={{0,4},{2,6},{4,0},{6,2},{1,5},{3,7},{5,1},{7,3},{8,12},{10,14},{12... | collective-permute-start | bytes 589832 | tf_op jit(solution)/shard_map/ppermute | solution.py:93
  1237.8 28.5 %all-to-all-start.4 = ((bf16[8,48,1152]{2,1,0:T(8,128)(2,1)}), bf16[8,48,1152]{2,1,0:T(8,128)(2,1)S(1)}, u32[]{:S(2)}, u32[]{:S(2)}) async-start(bf16[8,48,1152]{2,1,0:T(8,128)(2,1)} %bitcast.466), calls=%async_computation.11 | async-start | bytes 1769472 | tf_op jit(solution)/shard_map/all_to_all | solution.py:917
  (414 other events, 4298.5 us)
Sparse Core Ops, SparseCore 0:
  53.5 55.9 all-gather.7
  119.0 36.3 all-gather.11
  157.3 70.2 all-gather.9
  229.3 43.9 all-gather.13
  275.5 70.1 all-gather.15
  348.0 70.1 all-gather.17
  420.0 43.9 all-gather.19
  697.3 72.0 reduce-scatter.7
  772.4 43.9 reduce-scatter.9
  819.3 70.1 reduce-scatter.11
  892.5 43.9 reduce-scatter.17
  939.3 70.2 reduce-scatter.15
  1040.1 48.6 reduce-scatter.13
  1110.1 48.4 reduce-scatter.19

commit v6 on v5

--- a/solution.py
+++ b/solution.py
@@ -96,8 +96,8 @@
 def gather_rows(x):
     n = lax.axis_size("z")
     parts = [x] + [send(x, "z", ring(s)) for s in range(1, n)]
-    other = [send(p, "core", SWAP) for p in parts]
-    return by_rows(jnp.concatenate(parts + other, axis=0))
+    mine = by_rows(jnp.concatenate(parts, axis=0))
+    return by_rows(jnp.concatenate([mine, send(mine, "core", SWAP)], axis=0))
 
 
 def return_rows(total):
@@ -379,8 +379,7 @@
 
 def unit_gates(local, units):
     count = local.shape[1]
-    inner = EXP_FF // lax.axis_size("dp")
-    owner = lax.broadcasted_iota(jnp.int32, (1, units), 1) // inner % count
+    owner = lax.broadcasted_iota(jnp.int32, (1, units), 1) // EXP_FF
     spread = local[:, count - 1 :]
     for e in range(count - 1):
         spread = jnp.where(owner == e, local[:, e : e + 1], spread)
@@ -556,7 +555,14 @@
     expert_down,
     cotangent,
 ):
-    micro, length, _ = tokens.shape
+    batches, length, _ = tokens.shape
+    micro = batches if lax.axis_size("w") > 1 else 1
+    seqs = batches // micro
+    own_rows = seqs * length
+    tokens = tokens.reshape(micro, own_rows, D)
+    cotangent = cotangent.reshape(micro, own_rows, D)
+    routes = routes.reshape(2, micro, own_rows, TOP)
+    segments = segments.reshape(micro, own_rows)
     n_tp = lax.axis_size("z") * lax.axis_size("core")
     n_ex = lax.axis_size("w") * n_tp
     n_all = lax.axis_size("dp") * n_ex
@@ -621,7 +627,7 @@
         hot = [
             jnp.any(routes[b, m][:, :, None] == expert_ids, axis=1).astype(bf16) for b in range(2)
         ]
-        info = lanes(hot + [segments[m, 0][:, None].astype(bf16)], info_width)
+        info = lanes(hot + [segments[m][:, None].astype(bf16)], info_width)
         x_info, _ = fence(jnp.concatenate([tokens[m], info], axis=1), moved_m)
         rows_in.append(gather_rows(x_info))
     in_width = 2 * chan + 2 * STATE
@@ -657,14 +663,13 @@
     w_scan = w_m[:, : in_width + 128]
     w_mix_t = w_m[:, at:]
 
-    n_dp = lax.axis_size("dp")
-
     def expert_weights(w_up, w_low):
-        count, depth, width = w_up.shape
-        cols = w_up.reshape(count, depth, 2, n_dp, EXP_FF // n_dp).transpose(1, 2, 3, 0, 4)
+        count = w_up.shape[0]
+        cols = [w_up[e, :, :EXP_FF] for e in range(count)] + [w_up[e, :, EXP_FF:] for e in range(count)]
+        cols = by_rows(jnp.concatenate(cols, axis=1))
         return (
-            by_rows(lax.all_gather(by_rows(cols.reshape(depth, -1)), "dp", axis=0, tiled=True)),
-            lax.all_gather(w_low.reshape(-1, D), "dp", axis=0, tiled=True),
+            by_rows(lax.all_gather(cols, "dp", axis=0, tiled=True)),
+            lax.all_gather(w_low, "dp", axis=1, tiled=True).reshape(-1, D),
         )
 
     expert_in_m, expert_down_m, _ = fence(expert_in_m, expert_down_m, moved_m)
@@ -706,9 +711,11 @@
         marks = wide(rows_all[:, D : D + 2 * experts_total]) > 0.5
         masks.append([marks[:, :experts_total], marks[:, experts_total:]])
         seg_col = rows_all[:, D + 2 * experts_total :][:, :1].astype(f32)
-        seg_row = seg_col.reshape(n_tp, 1, length)
+        seg_row = seg_col.reshape(n_tp * seqs, 1, length)
         seg = seg_row[:, 0].astype(jnp.int32)
-        allowed.append(attn_mask(jnp.stack([seg[0], seg[n_tp // 2]])))
+        middle = n_tp * seqs // 2
+        pair = jnp.concatenate([seg[:seqs], seg[middle : middle + seqs]], axis=0)
+        allowed.append(attn_mask(pair))
 
         x_all, _ = fence(x_all, w_m)
         _, scale_x, mamba_in = rms_forward(x_all, gain_mamba)
@@ -726,7 +733,7 @@
         gate_scale = lax.rsqrt((back[:, D : D + 1] + back[:, D + 1 : D + 2]) / DI + epsilon)
         mix_branch = back[:, :D] * gate_scale
         hidden_one.append(x_own[m] + mix_branch)
-        mamba_kept.append((rows_all, scale_x[:length], mamba_in, (proj, dt_raw, *pars), gained))
+        mamba_kept.append((rows_all, scale_x[:own_rows], mamba_in, (proj, dt_raw, *pars), gained))
         mix_kept.append((mix_branch, gate_scale))
 
     attn_pack = jnp.concatenate(
@@ -743,10 +750,10 @@
     own = attn_pack.reshape(2 * rows, -1)
     n_z = lax.axis_size("z")
     parts = [send(own, "z", ring(s)) for s in range(n_z - 1, 0, -1)] + [own]
+    parts, _ = fence(parts, mamba_kept[-1][-1])
     twice = jnp.concatenate(parts + parts, axis=0)
     start = (n_z - 1 - lax.axis_index("z")) * 2 * rows
     attn_w = lax.dynamic_slice(twice, (start, 0), (n_z * 2 * rows, own.shape[1]))
-    attn_w, _ = fence(attn_w, mamba_kept[-1][-1])
     attn_w = lax.all_gather(attn_w, FS, axis=0, tiled=True)
     w_qkv_here = attn_w[:, : q_width + 2 * kv_width]
     w_out_t = attn_w[:, q_width + 2 * kv_width :]
@@ -775,25 +782,32 @@
 
     gains = [0.0, 0.0, 0.0, 0.0]
 
-    def over_dp(g):
+    def up_over_dp(g):
         return lax.psum_scatter(g, "dp", scatter_dimension=0, tiled=True)
 
+    def low_over_dp(g):
+        g = g.reshape(local_experts, EXP_FF, D)
+        return lax.psum_scatter(g, "dp", scatter_dimension=1, tiled=True)
+
     def expert_out(g_up, g_low):
-        depth = g_up.shape[0]
-        cols = g_up.reshape(depth, 2, n_dp, local_experts, EXP_FF // n_dp)
-        cols = cols.transpose(3, 0, 1, 2, 4).reshape(local_experts, depth, 2 * EXP_FF)
-        return cols.astype(f32), g_low.reshape(local_experts, -1, D).astype(f32)
+        units = local_experts * EXP_FF
+        cols = []
+        for e in range(local_experts):
+            low, high = e * EXP_FF, (e + 1) * EXP_FF
+            pair = [g_up[:, low:high], g_up[:, units + low : units + high]]
+            cols.append(jnp.concatenate(pair, axis=1).astype(f32))
+        return jnp.stack(cols), g_low.astype(f32)
 
     saving = lax.axis_size("w") > 1
 
     def moe_stage(grads, kept_all, w, gain, *before):
         grads = list(grads)
-        backs, sides, own_rows = [], [], []
+        backs, sides, first_rows = [], [], []
         for m in each:
             back, side = moe_backward(grads[m], kept_all[m][2], w, experts_total)
             backs.append(back)
             sides.append(side)
-            own_rows.append(side[6][:length])
+            first_rows.append(side[6][:own_rows])
             if saving:
                 newer = moe_weight_grads(sides[-1:])
                 hold = (back, newer, grads[m + 1 :])
@@ -812,14 +826,14 @@
             grad_values, part = rms_backward(grad_in, normed, scale, gain)
             grad_gain = grad_gain + part
             values.append(grad_values)
-        g_router = tn_sum(list(zip(own_rows, logits)), f32)
+        g_router = tn_sum(list(zip(first_rows, logits)), f32)
         return values, weights, grad_gain, g_router, before
 
     values, (g_in_a, g_down_a, g_sin_a, g_sdown_a), gains[3], g_router, _ = moe_stage(
         cot_all, two_kept, moe_a, gain_moe
     )
-    sum_in_a = over_dp(g_in_a)
-    sum_down_a = over_dp(g_down_a)
+    sum_in_a = up_over_dp(g_in_a)
+    sum_down_a = low_over_dp(g_down_a)
     grad_two = [cotangent[m].astype(f32) + values[m] for m in each]
     for m in each:
         total, _ = fence(results[m], grad_two[m])
@@ -850,21 +864,39 @@
         grad_values, part = rms_backward(attn_back[m], normed, scale, gain_attn)
         gains[2] = gains[2] + part
         grad_layer.append(grad_two[m] + grad_values)
-    grad_layer[-1], sum_in_a = fence(grad_layer[-1], sum_in_a)
 
     values, (g_in_m, g_down_m, g_sin_m, g_sdown_m), gains[1], g_router_m, before = moe_stage(
         [gather_rows(g.astype(bf16)) for g in grad_layer],
         one_kept,
         moe_m,
         gain_moe_m,
+        sum_in_a,
         sum_down_a,
         g_part,
     )
-    sum_down_a, g_part = before
+    sum_in_a, sum_down_a, g_part = before
     out_expert_in, out_expert_down = expert_out(sum_in_a, sum_down_a)
-    sum_in_m = over_dp(g_in_m)
-    sum_down_m = over_dp(g_down_m)
+    sum_in_m = up_over_dp(g_in_m)
+    sum_down_m = low_over_dp(g_down_m)
     grad_one = [grad_layer[m] + values[m] for m in each]
+
+    def attn_owner(g_part, *after):
+        blocks = fence(g_part, *after)[0].reshape(n_z, 2 * rows, -1)
+        here = lax.axis_index("z")
+        own = lax.dynamic_index_in_dim(blocks, here, 0, keepdims=False)
+        sent = []
+        for shift in range(1, n_z):
+            block = lax.dynamic_index_in_dim(blocks, (here + shift) % n_z, 0, keepdims=False)
+            sent.append(send(block, "z", ring(shift)))
+        return own, sent
+
+    def attn_total(own, sent):
+        total = own.astype(f32)
+        for block in sent:
+            total = total + block.astype(f32)
+        return lax.all_to_all(
+            total.astype(bf16).reshape(2, rows, -1), "core", split_axis=0, concat_axis=0, tiled=True
+        ).astype(f32)
 
     small = None
     mamba_sides, mamba_back, mixes, own_normed = [], [], [], []
@@ -874,7 +906,7 @@
         x_rows, _ = fence(x_rows, grad_one[m])
         x_rows = x_rows[:, :D].astype(f32)
         normed_x = x_rows * row_scale(x_rows)
-        own_normed.append(normed_x[:length])
+        own_normed.append(normed_x[:own_rows])
         grad_mix = grad_one[m].astype(bf16)
         mean_term = jnp.sum(grad_mix.astype(f32) * mix_branch, axis=-1, keepdims=True) / DI
         extra = lanes(split_two(gate_scale) + split_two(mean_term), 128)
@@ -891,26 +923,21 @@
         if m == micro - 1:
             g_mix = tn_sum([(x, k[4]) for x, k in zip(mixes, mamba_kept)])
             mix_all, g_mix = fence(mix_all, by_rows(g_mix))
+        if m == micro - 1:
+            attn_sent = attn_owner(g_part, mix_all)
         grad_gated = nn(mix_all, w_mix_t, bf16)
         grad_scan, *grads = scan_backward(
             heads, length, *scan_args, grad_gated, extra_all
         )
+        if m == micro - 1:
+            grad_scan, attn_sent = fence(grad_scan, attn_sent)
         mamba_sides.append((mamba_in, grad_scan))
         small = grads if small is None else [a + b for a, b in zip(small, grads)]
         total = nt(grad_scan, w_scan)
         gains[0] = gains[0] + jnp.sum(total * normed_x, axis=0)
         mamba_back.append(return_rows(total))
 
-    g_part, _ = fence(g_part, mixes)
-    blocks = g_part.reshape(n_z, 2 * rows, -1)
-    here = lax.axis_index("z")
-    g_attn = lax.dynamic_index_in_dim(blocks, here, 0, keepdims=False).astype(f32)
-    for shift in range(1, n_z):
-        block = lax.dynamic_index_in_dim(blocks, (here + shift) % n_z, 0, keepdims=False)
-        g_attn = g_attn + send(block, "z", ring(shift)).astype(f32)
-    g_attn = lax.all_to_all(
-        g_attn.astype(bf16).reshape(2, rows, -1), "core", split_axis=0, concat_axis=0, tiled=True
-    ).astype(f32)
+    g_attn = attn_total(*attn_sent)
 
     def rows_back(packed):
         packed = lax.psum_scatter(packed, FS, scatter_dimension=0, tiled=True)
@@ -999,8 +1026,8 @@
     out_sin, out_sdown = shared_out(g_s[:, :, chan + 3 * ff :])
 
     return (
-        jnp.stack(results),
-        jnp.stack(grads_in),
+        jnp.stack(results).reshape(batches, length, D),
+        jnp.stack(grads_in).reshape(batches, length, D),
         little[:, 0],
         out_w_in,
         out_w_dt,

time: 1290 us -> 1130 us (0.88)
  local copies, waits for them, and re-layouts: 180 us -> 98.3 us
  matrix products: 265 us -> 197 us
  starting transfers between devices: 168 us -> 109 us
  blocking collectives: 27.9 us -> 70.4 us
  other arithmetic: 125 us -> 152 us
    dot_general x86 -> x43, matrix products: 255 us -> 189 us  [dot(): r = lax.dot_general(a, b, (dims, ((), ())), preferred_element_type=f32)]
    ppermute x151 -> x63, starting transfers between devices: 150 us -> 99.1 us  [send(): return by_rows(lax.ppermute(by_rows(x), axis, pairs))]
    reduce_scatter x4, waiting for transfers between devices: 45.6 us -> 0.04 us  [the longest x2 0.02 us: low_over_dp(): return lax.psum_scatter(g, 'dp', scatter_dimension=1, tiled=True)]
    all_to_all x1 -> x2, blocking collectives: 19.9 us -> 62.3 us  [moved_columns(): moved = lax.all_to_all(packed, TP, split_axis=0, concat_axis=0, tiled=True)]
    all_to_all x1 -> x0, waiting for transfers between devices: 29.3 us -> none  [moved_columns(): moved = lax.all_to_all(packed, TP, split_axis=0, concat_axis=0, tiled=True)]
    convert_element_type x9 -> x1, local copies, waits for them, and re-layouts: 27.3 us -> 0.16 us  [body(): info = lanes(hot + [segments[m][:, None].astype(bf16)], info_width)]
    ppermute x151 -> x63, waiting for transfers between devices: 367 us -> 394 us  [send(): return by_rows(lax.ppermute(by_rows(x), axis, pairs))]
    reshape x8 -> x1, local copies, waits for them, and re-layouts: 25.6 us -> 0.07 us  [body(): seg_row = seg_col.reshape(n_tp * seqs, 1, length)]
  transfers between devices with their start and end apart: 168 -> 79, of which waited for: 76 -> 37; matrix products, arithmetic and copies ran while one was open for 38% -> 33% of each run, Pallas kernels for 2% -> 2%
where the time goes in v6:
time: 1130 us
  waiting for transfers between devices  456 us (40%)
  matrix products  197 us (17%)
  other arithmetic  152 us (13%)
  starting transfers between devices  109 us (10%)
  local copies, waits for them, and re-layouts  98.3 us (9%)
  blocking collectives  70.4 us (6%)
  Pallas kernels  27.9 us (2%)
  between operations  17.3 us (2%)
    ppermute x63, waiting for transfers between devices, send(): return by_rows(lax.ppermute(by_rows(x), axis, pairs))  394 us
    dot_general x43, matrix products, dot(): r = lax.dot_general(a, b, (dims, ((), ())), preferred_element_type=f32)  189 us
    ppermute x63, starting transfers between devices, send(): return by_rows(lax.ppermute(by_rows(x), axis, pairs))  99.1 us
    all_to_all x2, blocking collectives, moved_columns(): moved = lax.all_to_all(packed, TP, split_axis=0, concat_axis=0, tiled=True)  62.3 us
    unnamed x349, local copies, waits for them, and re-layouts  39.8 us
    another operation x7, other arithmetic  23.5 us
    all_gather x2, waiting for transfers between devices, expert_weights(): lax.all_gather(w_low, 'dp', axis=1, tiled=True).reshape(-1, D)  23 us
  transfers between devices with their start and end apart: 79, of which 37 were waited for; matrix products, arithmetic and copies ran while one was open for 33% of the time, Pallas kernels for 2%

profile of v6, /device:TPU:0, one launch (start us, length us, event | category | flops | bytes accessed | tf_op | source)
XLA Modules:
  0.0 1127.9 jit_solution(2382593102926477709)
XLA Ops:
  15.5 35.6 %all_to_all.30 = bf16[8,48,1536]{2,1,0:T(8,128)(2,1)} all-to-all(bf16[8,48,1536]{2,1,0:T(8,128)(2,1)S(1)} %copy.586), channel_id=1, replica_groups=mesh['dp'=4,'w'=1,'z'=4,'core'=2] {'z','core'}, dimensions={0} | all-to-all | bytes 2359296 | tf_op jit(solution)/shard_map/all_to_all | solution.py:595
  56.0 10.8 collective-permute-done
  66.8 16.9 %collective-permute-done.1 = bf16[128,1664]{1,0:T(8,128)(2,1)S(1)} collective-permute-done((bf16[128,1664]{1,0:T(8,128)(2,1)S(1)}, bf16[128,1664]{1,0:T(8,128)(2,1)S(1)}, u32[]{:S(2)}, u32[]{:S(2)}) %collective-permute-start.1) | collective-permute-done | bytes 426016 | tf_op jit(solution)/shard_map/ppermute | solution.py:93
  90.4 26.7 %all_to_all.31 = bf16[8,48,768]{2,1,0:T(8,128)(2,1)} all-to-all(bf16[8,48,768]{2,1,0:T(8,128)(2,1)S(1)} %copy.589), channel_id=1, replica_groups=mesh['dp'=4,'w'=1,'z'=4,'core'=2] {'z','core'}, dimensions={0} | all-to-all | bytes 1179648 | tf_op jit(solution)/shard_map/all_to_all | solution.py:595
  124.2 5.0 fusion.16
  154.9 9.6 scan_forward.1
  175.8 4.6 fusion.207
  187.7 7.8 collective-permute-done.5
  195.4 28.0 %collective-permute-done.6 = bf16[128,1664]{1,0:T(8,128)(2,1)} collective-permute-done((bf16[128,1664]{1,0:T(8,128)(2,1)}, bf16[128,1664]{1,0:T(8,128)(2,1)}, u32[]{:S(2)}, u32[]{:S(2)}) %collective-permute-start.6) | collective-permute-done | bytes 426016 | tf_op jit(solution)/shard_map/ppermute | solution.py:93
  231.9 8.1 collective-permute-done.10
  240.0 9.4 collective-permute-done.8
  249.4 14.2 %collective-permute-done.9 = bf16[128,1536]{1,0:T(8,128)(2,1)S(1)} collective-permute-done((bf16[128,1536]{1,0:T(8,128)(2,1)S(1)}, bf16[128,1536]{1,0:T(8,128)(2,1)S(1)}, u32[]{:S(2)}, u32[]{:S(2)}) %collective-permute-start.9) | collective-permute-done | bytes 393248 | tf_op jit(solution)/shard_map/ppermute | solution.py:93
  274.7 9.9 convolution_convert_fusion.4
  284.6 4.4 convert_element_type.558
  294.0 7.2 fusion.35
  319.8 8.0 collective-permute-done.13
  327.8 23.2 %collective-permute-done.14 = bf16[128,1536]{1,0:T(8,128)(2,1)} collective-permute-done((bf16[128,1536]{1,0:T(8,128)(2,1)S(1)}, bf16[128,1536]{1,0:T(8,128)(2,1)}, u32[]{:S(2)}, u32[]{:S(2)}) %collective-permute-start.14) | collective-permute-done | bytes 393248 | tf_op jit(solution)/shard_map/ppermute | solution.py:93
  360.7 6.2 collective-permute-done.21
  367.7 14.4 %collective-permute-done.22 = bf16[128,1536]{1,0:T(8,128)(2,1)S(1)} collective-permute-done((bf16[128,1536]{1,0:T(8,128)(2,1)S(1)}, bf16[128,1536]{1,0:T(8,128)(2,1)S(1)}, u32[]{:S(2)}, u32[]{:S(2)}) %collective-permute-start.22) | collective-permute-done | bytes 393248 | tf_op jit(solution)/shard_map/ppermute | solution.py:93
  400.6 8.0 collective-permute-start.25
  411.6 9.5 collective-permute-done.25
  421.1 16.2 %collective-permute-done.26 = bf16[128,1536]{1,0:T(8,128)(2,1)S(1)} collective-permute-done((bf16[128,1536]{1,0:T(8,128)(2,1)S(1)}, bf16[128,1536]{1,0:T(8,128)(2,1)S(1)}, u32[]{:S(2)}, u32[]{:S(2)}) %collective-permute-start.26) | collective-permute-done | bytes 393248 | tf_op jit(solution)/shard_map/ppermute | solution.py:93
  448.5 9.9 convolution_convert_fusion.3
  459.5 4.5 convert_element_type.586
  467.1 23.0 %all-gather.20.cloned.1.call-done = bf16[2,512,1536]{2,1,0:T(8,128)(2,1)} async-done(((bf16[2,128,1536]{2,1,0:T(8,128)(2,1)}), bf16[2,512,1536]{2,1,0:T(8,128)(2,1)}) %all-gather.20.cloned.1.call-update) | async-done | bytes 3145744 | tf_op jit(solution)/shard_map/all_gather | solution.py:672
  490.1 12.5 %select_reduce_fusion.2 = (f32[1024]{0:T(1024)S(1)}, f32[1024]{0:T(1024)S(1)}, f32[1024,1024]{1,0:T(8,128)}, f32[1024,1024]{1,0:T(8,128)}) fusion(pred[1024]{0:T(1024)(128)(4,1)S(1)} %copy-done.147, pred[1024]{0:T(1024)(128)(4,1)S(1)} %fusion.143, f32[1024,2048]{1,0:T(8,128)} %convert_element_type.586, bf16[1024,1536]{1,0:T(8,128)(2,1)} %pad_maximum_fusion.7, ...), kind=kOutput, calls=%fused_computation.49 | convolution fusion | flops 3231709184 | bytes 23078912 | tf_op jit(solution)/shard_map/dot_general | solution.py:37
  505.9 6.9 multiply_convert_fusion.5
  514.2 9.0 fusion.23
  526.2 9.3 convolution_convert_fusion.6
  535.6 8.8 convolution_convert_fusion.1
  556.1 5.0 collective-permute-done.30
  561.1 26.2 %collective-permute-done.31 = bf16[128,1664]{1,0:T(8,128)(2,1)S(1)} collective-permute-done((bf16[128,1664]{1,0:T(8,128)(2,1)S(1)}, bf16[128,1664]{1,0:T(8,128)(2,1)S(1)}, u32[]{:S(2)}, u32[]{:S(2)}) %collective-permute-start.31) | collective-permute-done | bytes 426016 | tf_op jit(solution)/shard_map/ppermute | solution.py:93
  628.8 8.1 collective-permute-done.39
  636.9 16.0 %collective-permute-done.40 = bf16[128,1536]{1,0:T(8,128)(2,1)S(1)} collective-permute-done((bf16[128,1536]{1,0:T(8,128)(2,1)S(1)}, bf16[128,1536]{1,0:T(8,128)(2,1)S(1)}, u32[]{:S(2)}, u32[]{:S(2)}) %collective-permute-start.40) | collective-permute-done | bytes 393248 | tf_op jit(solution)/shard_map/ppermute | solution.py:93
  660.4 8.1 multiply_convert_fusion.3
  673.7 8.9 fusion.22
  691.1 5.1 convolution_convert_fusion.5
  696.2 9.0 convolution_convert_fusion
  708.3 10.0 collective-permute-start.44
  722.6 5.9 collective-permute-done.44
  728.5 26.9 %collective-permute-done.45 = bf16[128,1664]{1,0:T(8,128)(2,1)S(1)} collective-permute-done((bf16[128,1664]{1,0:T(8,128)(2,1)S(1)}, bf16[128,1664]{1,0:T(8,128)(2,1)S(1)}, u32[]{:S(2)}, u32[]{:S(2)}) %collective-permute-start.45) | collective-permute-done | bytes 426016 | tf_op jit(solution)/shard_map/ppermute | solution.py:93
  757.3 20.9 %reduce-scatter.12.cloned.1.call-done = bf16[384,2048]{1,0:T(8,128)(2,1)} async-done(((bf16[1536,2048]{1,0:T(8,128)(2,1)}), bf16[384,2048]{1,0:T(8,128)(2,1)}) %reduce-scatter.12.cloned.1.call-update) | async-done | bytes 1572880 | tf_op jit(solution)/shard_map/reduce_scatter | solution.py:860
  790.4 9.3 collective-permute-done.47
  799.7 17.1 %collective-permute-done.48 = bf16[128,1664]{1,0:T(8,128)(2,1)S(1)} collective-permute-done((bf16[128,1664]{1,0:T(8,128)(2,1)S(1)}, bf16[128,1664]{1,0:T(8,128)(2,1)S(1)}, u32[]{:S(2)}, u32[]{:S(2)}) %collective-permute-start.48) | collective-permute-done | bytes 426016 | tf_op jit(solution)/shard_map/ppermute | solution.py:93
  818.9 6.7 convert_element_type.581
  829.8 5.9 pad_maximum_fusion.5
  844.4 7.6 fusion.33
  869.3 18.2 %scan_backward.1 = (bf16[1024,1152]{1,0:T(8,128)(2,1)S(1)}, f32[8,640]{1,0:T(8,128)S(1)}, f32[8,384]{1,0:T(8,128)S(1)}, f32[8,128]{1,0:T(8,128)S(1)}) custom-call(bf16[1024,1024]{1,0:T(8,128)(2,1)S(1)} %copy-done.1, f32[1024,128]{1,0:T(8,128)S(1)} %copy-done.3, f32[1024,1]{1,0:T(8,128)S(1)} %get-tuple-element.415.col_ref, f32[16,1,64]{2,1,0:T(1,128)S(1)} %bitcast.313, ...), custom_call_target="tpu_custom_call" | custom-call | tf_op jit(solution)/shard_map/scan_backward/pallas_call | solution.py:345
  888.7 9.6 collective-permute-start.51
  902.8 6.2 collective-permute-done.51
  909.0 16.9 %collective-permute-done.52 = bf16[96,2048]{1,0:T(8,128)(2,1)} collective-permute-done((bf16[96,2048]{1,0:T(8,128)(2,1)}, bf16[96,2048]{1,0:T(8,128)(2,1)}, u32[]{:S(2)}, u32[]{:S(2)}) %collective-permute-start.52) | collective-permute-done | bytes 393248 | tf_op jit(solution)/shard_map/ppermute | solution.py:93
  925.9 9.6 multiply_reduce_fusion
  936.6 4.7 concatenate.246
  941.3 9.1 fusion.233
  950.4 5.6 add_convert_fusion
  956.1 4.6 fusion.201
  961.7 10.3 collective-permute-start.34
  984.2 13.6 %collective-permute-done.60 = f32[8,128]{1,0:T(8,128)S(1)} collective-permute-done((f32[8,128]{1,0:T(8,128)S(1)}, f32[8,128]{1,0:T(8,128)S(1)}, u32[]{:S(2)}, u32[]{:S(2)}) %collective-permute-start.60) | collective-permute-done | bytes 4128 | tf_op jit(solution)/shard_map/ppermute | solution.py:93
  999.0 7.9 collective-permute-done.61
  1020.6 4.2 all-to-all-start.3
  1036.1 14.5 %collective-permute-done.55 = bf16[128,1536]{1,0:T(8,128)(2,1)S(1)} collective-permute-done((bf16[128,1536]{1,0:T(8,128)(2,1)S(1)}, bf16[128,1536]{1,0:T(8,128)(2,1)S(1)}, u32[]{:S(2)}, u32[]{:S(2)}) %collective-permute-start.55) | collective-permute-done | bytes 393248 | tf_op jit(solution)/shard_map/ppermute | solution.py:93
  1050.6 31.0 %collective-permute-done.56 = bf16[128,1536]{1,0:T(8,128)(2,1)S(1)} collective-permute-done((bf16[128,1536]{1,0:T(8,128)(2,1)S(1)}, bf16[128,1536]{1,0:T(8,128)(2,1)S(1)}, u32[]{:S(2)}, u32[]{:S(2)}) %collective-permute-start.56) | collective-permute-done | bytes 393248 | tf_op jit(solution)/shard_map/ppermute | solution.py:93
  1085.9 4.4 all-to-all-start.4
  1096.4 17.0 %all-to-all-done.4 = bf16[8,48,1152]{2,1,0:T(8,128)(2,1)} async-done(((bf16[8,48,1152]{2,1,0:T(8,128)(2,1)}), bf16[8,48,1152]{2,1,0:T(8,128)(2,1)}, u32[]{:S(2)}, u32[]{:S(2)}) %all-to-all-start.4) | async-done | bytes 884768 | tf_op jit(solution)/shard_map/all_to_all | solution.py:944
  (791 shorter events, 359.1 us)
Async XLA Ops:
  7.2 128.4 %all-gather.8.cloned.1.call-start = ((), (), s32[]{:S(2)}) async-start(), calls=%async_computation.13 | async-start | bytes 5898240 | tf_op jit(solution)/shard_map/all_gather | solution.py:599
  51.2 220.4 %all-gather.12.cloned.1.call-start = ((), (), s32[]{:S(2)}) async-start(), calls=%async_computation.15 | async-start | bytes 2949120 | tf_op jit(solution)/shard_map/all_gather | solution.py:599
  52.0 14.7 %collective-permute-start = (bf16[128,1664]{1,0:T(8,128)(2,1)S(1)}, bf16[128,1664]{1,0:T(8,128)(2,1)S(1)}, u32[]{:S(2)}, u32[]{:S(2)}) collective-permute-start(bf16[128,1664]{1,0:T(8,128)(2,1)S(1)} %concatenate.198), channel_id=1, source_target_pairs={{0,2},{2,4},{4,6},{6,0},{1,3},{3,5},{5,7},{7,1},{8,10},{10,12},{12... | collective-permute-start | bytes 1277960 | tf_op jit(solution)/shard_map/ppermute | solution.py:93
  52.3 31.4 %collective-permute-start.1 = (bf16[128,1664]{1,0:T(8,128)(2,1)S(1)}, bf16[128,1664]{1,0:T(8,128)(2,1)S(1)}, u32[]{:S(2)}, u32[]{:S(2)}) collective-permute-start(bf16[128,1664]{1,0:T(8,128)(2,1)S(1)} %concatenate.198), channel_id=1, source_target_pairs={{0,4},{2,6},{4,0},{6,2},{1,5},{3,7},{5,1},{7,3},{8,12},{10,14},{12... | collective-permute-start | bytes 1277960 | tf_op jit(solution)/shard_map/ppermute | solution.py:93
  53.9 29.8 %collective-permute-start.2 = (bf16[128,1664]{1,0:T(8,128)(2,1)S(1)}, bf16[128,1664]{1,0:T(8,128)(2,1)S(1)}, u32[]{:S(2)}, u32[]{:S(2)}) collective-permute-start(bf16[128,1664]{1,0:T(8,128)(2,1)S(1)} %concatenate.198), channel_id=1, source_target_pairs={{0,6},{2,0},{4,2},{6,4},{1,7},{3,1},{5,3},{7,5},{8,14},{10,8},{12,... | collective-permute-start | bytes 1277960 | tf_op jit(solution)/shard_map/ppermute | solution.py:93
  117.1 157.6 %all-gather.10.cloned.1.call-start = ((), (), s32[]{:S(2)}) async-start(), calls=%async_computation.14 | async-start | bytes 7864320 | tf_op jit(solution)/shard_map/all_gather | solution.py:671
  120.0 174.0 %all-gather.14.cloned.1.call-start = ((), (), s32[]{:S(2)}) async-start(), calls=%async_computation.16 | async-start | bytes 3932160 | tf_op jit(solution)/shard_map/all_gather | solution.py:672
  122.0 262.4 %all-gather.16.cloned.1.call-start = ((), (), s32[]{:S(2)}) async-start(), calls=%async_computation.17 | async-start | bytes 7864320 | tf_op jit(solution)/shard_map/all_gather | solution.py:757
  133.2 36.4 %collective-permute-start.17 = (bf16[96,2048]{1,0:T(8,128)(2,1)S(1)}, bf16[96,2048]{1,0:T(8,128)(2,1)}, u32[]{:S(2)}, u32[]{:S(2)}) collective-permute-start(bf16[96,2048]{1,0:T(8,128)(2,1)S(1)} %bitcast.318), channel_id=1, source_target_pairs={{0,6},{2,0},{4,2},{6,4},{1,7},{3,1},{5,3},{7,5},{8,14},{10,8},{12,... | collective-permute-start | bytes 1179656 | tf_op jit(solution)/shard_map/ppermute | solution.py:93
  134.4 35.2 %collective-permute-start.18 = (bf16[96,2048]{1,0:T(8,128)(2,1)S(1)}, bf16[96,2048]{1,0:T(8,128)(2,1)}, u32[]{:S(2)}, u32[]{:S(2)}) collective-permute-start(bf16[96,2048]{1,0:T(8,128)(2,1)S(1)} %bitcast.319), channel_id=1, source_target_pairs={{0,4},{2,6},{4,0},{6,2},{1,5},{3,7},{5,1},{7,3},{8,12},{10,14},{12... | collective-permute-start | bytes 1179656 | tf_op jit(solution)/shard_map/ppermute | solution.py:93
  135.1 34.5 %collective-permute-start.19 = (bf16[96,2048]{1,0:T(8,128)(2,1)S(1)}, bf16[96,2048]{1,0:T(8,128)(2,1)}, u32[]{:S(2)}, u32[]{:S(2)}) collective-permute-start(bf16[96,2048]{1,0:T(8,128)(2,1)S(1)} %bitcast.320), channel_id=1, source_target_pairs={{0,2},{2,4},{4,6},{6,0},{1,3},{3,5},{5,7},{7,1},{8,10},{10,12},{12... | collective-permute-start | bytes 1179656 | tf_op jit(solution)/shard_map/ppermute | solution.py:93
  181.4 14.0 %collective-permute-start.5 = (bf16[128,1664]{1,0:T(8,128)(2,1)}, bf16[128,1664]{1,0:T(8,128)(2,1)}, u32[]{:S(2)}, u32[]{:S(2)}) collective-permute-start(bf16[128,1664]{1,0:T(8,128)(2,1)} %get-tuple-element.447), channel_id=1, source_target_pairs={{0,6},{2,0},{4,2},{6,4},{1,7},{3,1},{5,3},{7,5},{8,14},{10,8},{12,... | collective-permute-start | bytes 1277960 | tf_op jit(solution)/shard_map/ppermute | solution.py:93
  184.9 38.5 %collective-permute-start.6 = (bf16[128,1664]{1,0:T(8,128)(2,1)}, bf16[128,1664]{1,0:T(8,128)(2,1)}, u32[]{:S(2)}, u32[]{:S(2)}) collective-permute-start(bf16[128,1664]{1,0:T(8,128)(2,1)} %get-tuple-element.449), channel_id=1, source_target_pairs={{0,4},{2,6},{4,0},{6,2},{1,5},{3,7},{5,1},{7,3},{8,12},{10,14},{12... | collective-permute-start | bytes 1277960 | tf_op jit(solution)/shard_map/ppermute | solution.py:93
  185.5 37.9 %collective-permute-start.7 = (bf16[128,1664]{1,0:T(8,128)(2,1)S(1)}, bf16[128,1664]{1,0:T(8,128)(2,1)}, u32[]{:S(2)}, u32[]{:S(2)}) collective-permute-start(bf16[128,1664]{1,0:T(8,128)(2,1)S(1)} %get-tuple-element.448), channel_id=1, source_target_pairs={{0,2},{2,4},{4,6},{6,0},{1,3},{3,5},{5,7},{7,1},{8,10},{10,12},{12... | collective-permute-start | bytes 1277960 | tf_op jit(solution)/shard_map/ppermute | solution.py:93
  187.6 260.9 %all-gather.18.cloned.1.call-start = ((), (), s32[]{:S(2)}) async-start(), calls=%async_computation.18 | async-start | bytes 7864320 | tf_op jit(solution)/shard_map/all_gather | solution.py:671
  227.4 12.6 %collective-permute-start.10 = (bf16[128,1536]{1,0:T(8,128)(2,1)S(1)}, bf16[128,1536]{1,0:T(8,128)(2,1)S(1)}, u32[]{:S(2)}, u32[]{:S(2)}) collective-permute-start(bf16[128,1536]{1,0:T(8,128)(2,1)S(1)} %multiply_convert_fusion.12), channel_id=1, source_target_pairs={{0,6},{2,0},{4,2},{6,4},{1,7},{3,1},{5,3},{7,5},{8,14},{10,8},{12,... | collective-permute-start | bytes 1179656 | tf_op jit(solution)/shard_map/ppermute | solution.py:93
  227.5 21.9 %collective-permute-start.8 = (bf16[128,1536]{1,0:T(8,128)(2,1)S(1)}, bf16[128,1536]{1,0:T(8,128)(2,1)S(1)}, u32[]{:S(2)}, u32[]{:S(2)}) collective-permute-start(bf16[128,1536]{1,0:T(8,128)(2,1)S(1)} %multiply_convert_fusion.12), channel_id=1, source_target_pairs={{0,2},{2,4},{4,6},{6,0},{1,3},{3,5},{5,7},{7,1},{8,10},{10,12},{12... | collective-permute-start | bytes 1179656 | tf_op jit(solution)/shard_map/ppermute | solution.py:93
  230.0 33.6 %collective-permute-start.9 = (bf16[128,1536]{1,0:T(8,128)(2,1)S(1)}, bf16[128,1536]{1,0:T(8,128)(2,1)S(1)}, u32[]{:S(2)}, u32[]{:S(2)}) collective-permute-start(bf16[128,1536]{1,0:T(8,128)(2,1)S(1)} %multiply_convert_fusion.12), channel_id=1, source_target_pairs={{0,4},{2,6},{4,0},{6,2},{1,5},{3,7},{5,1},{7,3},{8,12},{10,14},{12... | collective-permute-start | bytes 1179656 | tf_op jit(solution)/shard_map/ppermute | solution.py:93
  309.5 180.6 %all-gather.20.cloned.1.call-start = ((), (), s32[]{:S(2)}) async-start(), calls=%async_computation.19 | async-start | bytes 3932160 | tf_op jit(solution)/shard_map/all_gather | solution.py:672
  315.3 12.5 %collective-permute-start.13 = (bf16[128,1536]{1,0:T(8,128)(2,1)S(1)}, bf16[128,1536]{1,0:T(8,128)(2,1)S(1)}, u32[]{:S(2)}, u32[]{:S(2)}) collective-permute-start(bf16[128,1536]{1,0:T(8,128)(2,1)S(1)} %get-tuple-element.476), channel_id=1, source_target_pairs={{0,6},{2,0},{4,2},{6,4},{1,7},{3,1},{5,3},{7,5},{8,14},{10,8},{12,... | collective-permute-start | bytes 1179656 | tf_op jit(solution)/shard_map/ppermute | solution.py:93
  317.4 33.6 %collective-permute-start.14 = (bf16[128,1536]{1,0:T(8,128)(2,1)S(1)}, bf16[128,1536]{1,0:T(8,128)(2,1)}, u32[]{:S(2)}, u32[]{:S(2)}) collective-permute-start(bf16[128,1536]{1,0:T(8,128)(2,1)S(1)} %get-tuple-element.478), channel_id=1, source_target_pairs={{0,4},{2,6},{4,0},{6,2},{1,5},{3,7},{5,1},{7,3},{8,12},{10,14},{12... | collective-permute-start | bytes 1179656 | tf_op jit(solution)/shard_map/ppermute | solution.py:93
  317.4 33.6 %collective-permute-start.15 = (bf16[128,1536]{1,0:T(8,128)(2,1)S(1)}, bf16[128,1536]{1,0:T(8,128)(2,1)}, u32[]{:S(2)}, u32[]{:S(2)}) collective-permute-start(bf16[128,1536]{1,0:T(8,128)(2,1)S(1)} %get-tuple-element.477), channel_id=1, source_target_pairs={{0,2},{2,4},{4,6},{6,0},{1,3},{3,5},{5,7},{7,1},{8,10},{10,12},{12... | collective-permute-start | bytes 1179656 | tf_op jit(solution)/shard_map/ppermute | solution.py:93
  352.9 14.0 %collective-permute-start.21 = (bf16[128,1536]{1,0:T(8,128)(2,1)S(1)}, bf16[128,1536]{1,0:T(8,128)(2,1)S(1)}, u32[]{:S(2)}, u32[]{:S(2)}) collective-permute-start(bf16[128,1536]{1,0:T(8,128)(2,1)S(1)} %bitcast.330), channel_id=1, source_target_pairs={{0,2},{2,4},{4,6},{6,0},{1,3},{3,5},{5,7},{7,1},{8,10},{10,12},{12... | collective-permute-start | bytes 1179656 | tf_op jit(solution)/shard_map/ppermute | solution.py:93
  353.9 28.2 %collective-permute-start.22 = (bf16[128,1536]{1,0:T(8,128)(2,1)S(1)}, bf16[128,1536]{1,0:T(8,128)(2,1)S(1)}, u32[]{:S(2)}, u32[]{:S(2)}) collective-permute-start(bf16[128,1536]{1,0:T(8,128)(2,1)S(1)} %bitcast.331), channel_id=1, source_target_pairs={{0,4},{2,6},{4,0},{6,2},{1,5},{3,7},{5,1},{7,3},{8,12},{10,14},{12... | collective-permute-start | bytes 1179656 | tf_op jit(solution)/shard_map/ppermute | solution.py:93
  356.1 26.7 %collective-permute-start.23 = (bf16[128,1536]{1,0:T(8,128)(2,1)S(1)}, bf16[128,1536]{1,0:T(8,128)(2,1)S(1)}, u32[]{:S(2)}, u32[]{:S(2)}) collective-permute-start(bf16[128,1536]{1,0:T(8,128)(2,1)S(1)} %bitcast.332), channel_id=1, source_target_pairs={{0,6},{2,0},{4,2},{6,4},{1,7},{3,1},{5,3},{7,5},{8,14},{10,8},{12,... | collective-permute-start | bytes 1179656 | tf_op jit(solution)/shard_map/ppermute | solution.py:93
  359.8 24.5 %collective-permute-start.16 = (bf16[128,1536]{1,0:T(8,128)(2,1)S(1)}, bf16[128,1536]{1,0:T(8,128)(2,1)S(1)}, u32[]{:S(2)}, u32[]{:S(2)}) collective-permute-start(bf16[128,1536]{1,0:T(8,128)(2,1)S(1)} %multiply_convert_fusion.11), channel_id=1, source_target_pairs={{0,1},{1,0},{2,3},{3,2},{4,5},{5,4},{6,7},{7,6},{8,9},{9,8},{10,11... | collective-permute-start | bytes 1179656 | tf_op jit(solution)/shard_map/ppermute | solution.py:93
  400.6 20.5 %collective-permute-start.25 = (bf16[128,1536]{1,0:T(8,128)(2,1)S(1)}, bf16[128,1536]{1,0:T(8,128)(2,1)S(1)}, u32[]{:S(2)}, u32[]{:S(2)}) collective-permute-start(bf16[128,1536]{1,0:T(8,128)(2,1)S(1)} %multiply_convert_fusion.10), channel_id=1, source_target_pairs={{0,2},{2,4},{4,6},{6,0},{1,3},{3,5},{5,7},{7,1},{8,10},{10,12},{12... | collective-permute-start | bytes 1179656 | tf_op jit(solution)/shard_map/ppermute | solution.py:93
  408.5 28.8 %collective-permute-start.26 = (bf16[128,1536]{1,0:T(8,128)(2,1)S(1)}, bf16[128,1536]{1,0:T(8,128)(2,1)S(1)}, u32[]{:S(2)}, u32[]{:S(2)}) collective-permute-start(bf16[128,1536]{1,0:T(8,128)(2,1)S(1)} %multiply_convert_fusion.10), channel_id=1, source_target_pairs={{0,4},{2,6},{4,0},{6,2},{1,5},{3,7},{5,1},{7,3},{8,12},{10,14},{12... | collective-permute-start | bytes 1179656 | tf_op jit(solution)/shard_map/ppermute | solution.py:93
  411.6 25.7 %collective-permute-start.27 = (bf16[128,1536]{1,0:T(8,128)(2,1)S(1)}, bf16[128,1536]{1,0:T(8,128)(2,1)S(1)}, u32[]{:S(2)}, u32[]{:S(2)}) collective-permute-start(bf16[128,1536]{1,0:T(8,128)(2,1)S(1)} %multiply_convert_fusion.10), channel_id=1, source_target_pairs={{0,6},{2,0},{4,2},{6,4},{1,7},{3,1},{5,3},{7,5},{8,14},{10,8},{12,... | collective-permute-start | bytes 1179656 | tf_op jit(solution)/shard_map/ppermute | solution.py:93
  439.3 317.9 %reduce-scatter.10.cloned.1.call-start = ((), (), s32[]{:S(2)}) async-start(), calls=%async_computation.21 | async-start | bytes 3932160 | tf_op jit(solution)/shard_map/reduce_scatter | solution.py:790
  526.2 18.1 %collective-permute-start.29 = (bf16[512,1664]{1,0:T(8,128)(2,1)}, bf16[512,1664]{1,0:T(8,128)(2,1)}, u32[]{:S(2)}, u32[]{:S(2)}) collective-permute-start(bf16[512,1664]{1,0:T(8,128)(2,1)} %slice.1190), channel_id=1, source_target_pairs={{0,1},{1,0},{2,3},{3,2},{4,5},{5,4},{6,7},{7,6},{8,9},{9,8},{10,11... | collective-permute-start | bytes 5111816 | tf_op jit(solution)/shard_map/ppermute | solution.py:93
  547.5 13.7 %collective-permute-start.30 = (bf16[128,1664]{1,0:T(8,128)(2,1)S(1)}, bf16[128,1664]{1,0:T(8,128)(2,1)S(1)}, u32[]{:S(2)}, u32[]{:S(2)}) collective-permute-start(bf16[128,1664]{1,0:T(8,128)(2,1)S(1)} %get-tuple-element.444), channel_id=1, source_target_pairs={{0,6},{2,0},{4,2},{6,4},{1,7},{3,1},{5,3},{7,5},{8,14},{10,8},{12,... | collective-permute-start | bytes 1277960 | tf_op jit(solution)/shard_map/ppermute | solution.py:93
  550.8 36.5 %collective-permute-start.31 = (bf16[128,1664]{1,0:T(8,128)(2,1)S(1)}, bf16[128,1664]{1,0:T(8,128)(2,1)S(1)}, u32[]{:S(2)}, u32[]{:S(2)}) collective-permute-start(bf16[128,1664]{1,0:T(8,128)(2,1)S(1)} %get-tuple-element.446), channel_id=1, source_target_pairs={{0,4},{2,6},{4,0},{6,2},{1,5},{3,7},{5,1},{7,3},{8,12},{10,14},{12... | collective-permute-start | bytes 1277960 | tf_op jit(solution)/shard_map/ppermute | solution.py:93
  550.9 36.5 %collective-permute-start.32 = (bf16[128,1664]{1,0:T(8,128)(2,1)S(1)}, bf16[128,1664]{1,0:T(8,128)(2,1)S(1)}, u32[]{:S(2)}, u32[]{:S(2)}) collective-permute-start(bf16[128,1664]{1,0:T(8,128)(2,1)S(1)} %get-tuple-element.445), channel_id=1, source_target_pairs={{0,2},{2,4},{4,6},{6,0},{1,3},{3,5},{5,7},{7,1},{8,10},{10,12},{12... | collective-permute-start | bytes 1277960 | tf_op jit(solution)/shard_map/ppermute | solution.py:93
  588.4 168.8 %reduce-scatter.8.cloned.1.call-start = ((), (), s32[]{:S(2)}) async-start(), calls=%async_computation.20 | async-start | bytes 7864320 | tf_op jit(solution)/shard_map/reduce_scatter | solution.py:786
  589.2 189.0 %reduce-scatter.12.cloned.1.call-start = ((), (), s32[]{:S(2)}) async-start(), calls=%async_computation.22 | async-start | bytes 7864320 | tf_op jit(solution)/shard_map/reduce_scatter | solution.py:860
  623.0 13.9 %collective-permute-start.39 = (bf16[128,1536]{1,0:T(8,128)(2,1)S(1)}, bf16[128,1536]{1,0:T(8,128)(2,1)S(1)}, u32[]{:S(2)}, u32[]{:S(2)}) collective-permute-start(bf16[128,1536]{1,0:T(8,128)(2,1)S(1)} %get-tuple-element.405), channel_id=1, source_target_pairs={{0,2},{2,4},{4,6},{6,0},{1,3},{3,5},{5,7},{7,1},{8,10},{10,12},{12... | collective-permute-start | bytes 1179656 | tf_op jit(solution)/shard_map/ppermute | solution.py:93
  624.2 28.7 %collective-permute-start.40 = (bf16[128,1536]{1,0:T(8,128)(2,1)S(1)}, bf16[128,1536]{1,0:T(8,128)(2,1)S(1)}, u32[]{:S(2)}, u32[]{:S(2)}) collective-permute-start(bf16[128,1536]{1,0:T(8,128)(2,1)S(1)} %get-tuple-element.405), channel_id=1, source_target_pairs={{0,4},{2,6},{4,0},{6,2},{1,5},{3,7},{5,1},{7,3},{8,12},{10,14},{12... | collective-permute-start | bytes 1179656 | tf_op jit(solution)/shard_map/ppermute | solution.py:93
  625.7 27.2 %collective-permute-start.41 = (bf16[128,1536]{1,0:T(8,128)(2,1)S(1)}, bf16[128,1536]{1,0:T(8,128)(2,1)S(1)}, u32[]{:S(2)}, u32[]{:S(2)}) collective-permute-start(bf16[128,1536]{1,0:T(8,128)(2,1)S(1)} %get-tuple-element.405), channel_id=1, source_target_pairs={{0,6},{2,0},{4,2},{6,4},{1,7},{3,1},{5,3},{7,5},{8,14},{10,8},{12,... | collective-permute-start | bytes 1179656 | tf_op jit(solution)/shard_map/ppermute | solution.py:93
  628.6 321.8 %reduce-scatter.18.cloned.1.call-start = ((), (), s32[]{:S(2)}) async-start(), calls=%async_computation.25 | async-start | bytes 3932160 | tf_op jit(solution)/shard_map/reduce_scatter | solution.py:790
  686.8 18.4 %collective-permute-start.43 = (bf16[512,1664]{1,0:T(8,128)(2,1)}, bf16[512,1664]{1,0:T(8,128)(2,1)}, u32[]{:S(2)}, u32[]{:S(2)}) collective-permute-start(bf16[512,1664]{1,0:T(8,128)(2,1)} %slice.1189), channel_id=1, source_target_pairs={{0,1},{1,0},{2,3},{3,2},{4,5},{5,4},{6,7},{7,6},{8,9},{9,8},{10,11... | collective-permute-start | bytes 5111816 | tf_op jit(solution)/shard_map/ppermute | solution.py:93
  708.3 20.2 %collective-permute-start.44 = (bf16[128,1664]{1,0:T(8,128)(2,1)S(1)}, bf16[128,1664]{1,0:T(8,128)(2,1)S(1)}, u32[]{:S(2)}, u32[]{:S(2)}) collective-permute-start(bf16[128,1664]{1,0:T(8,128)(2,1)S(1)} %get-tuple-element.441), channel_id=1, source_target_pairs={{0,6},{2,0},{4,2},{6,4},{1,7},{3,1},{5,3},{7,5},{8,14},{10,8},{12,... | collective-permute-start | bytes 1277960 | tf_op jit(solution)/shard_map/ppermute | solution.py:93
  718.2 37.2 %collective-permute-start.45 = (bf16[128,1664]{1,0:T(8,128)(2,1)S(1)}, bf16[128,1664]{1,0:T(8,128)(2,1)S(1)}, u32[]{:S(2)}, u32[]{:S(2)}) collective-permute-start(bf16[128,1664]{1,0:T(8,128)(2,1)S(1)} %get-tuple-element.443), channel_id=1, source_target_pairs={{0,4},{2,6},{4,0},{6,2},{1,5},{3,7},{5,1},{7,3},{8,12},{10,14},{12... | collective-permute-start | bytes 1277960 | tf_op jit(solution)/shard_map/ppermute | solution.py:93
  718.4 37.1 %collective-permute-start.46 = (bf16[128,1664]{1,0:T(8,128)(2,1)S(1)}, bf16[128,1664]{1,0:T(8,128)(2,1)S(1)}, u32[]{:S(2)}, u32[]{:S(2)}) collective-permute-start(bf16[128,1664]{1,0:T(8,128)(2,1)S(1)} %get-tuple-element.442), channel_id=1, source_target_pairs={{0,2},{2,4},{4,6},{6,0},{1,3},{3,5},{5,7},{7,1},{8,10},{10,12},{12... | collective-permute-start | bytes 1277960 | tf_op jit(solution)/shard_map/ppermute | solution.py:93
  756.6 193.8 %reduce-scatter.16.cloned.1.call-start = ((), (), s32[]{:S(2)}) async-start(), calls=%async_computation.24 | async-start | bytes 7864320 | tf_op jit(solution)/shard_map/reduce_scatter | solution.py:786
  757.2 263.4 %reduce-scatter.14.cloned.1.call-start = ((), (), s32[]{:S(2)}) async-start(), calls=%async_computation.23 | async-start | bytes 4423680 | tf_op jit(solution)/shard_map/reduce_scatter | solution.py:943
  785.0 14.7 %collective-permute-start.47 = (bf16[128,1664]{1,0:T(8,128)(2,1)S(1)}, bf16[128,1664]{1,0:T(8,128)(2,1)S(1)}, u32[]{:S(2)}, u32[]{:S(2)}) collective-permute-start(bf16[128,1664]{1,0:T(8,128)(2,1)S(1)} %concatenate.234), channel_id=1, source_target_pairs={{0,2},{2,4},{4,6},{6,0},{1,3},{3,5},{5,7},{7,1},{8,10},{10,12},{12... | collective-permute-start | bytes 1277960 | tf_op jit(solution)/shard_map/ppermute | solution.py:93
  786.6 30.3 %collective-permute-start.48 = (bf16[128,1664]{1,0:T(8,128)(2,1)S(1)}, bf16[128,1664]{1,0:T(8,128)(2,1)S(1)}, u32[]{:S(2)}, u32[]{:S(2)}) collective-permute-start(bf16[128,1664]{1,0:T(8,128)(2,1)S(1)} %concatenate.234), channel_id=1, source_target_pairs={{0,4},{2,6},{4,0},{6,2},{1,5},{3,7},{5,1},{7,3},{8,12},{10,14},{12... | collective-permute-start | bytes 1277960 | tf_op jit(solution)/shard_map/ppermute | solution.py:93
  789.0 27.9 %collective-permute-start.49 = (bf16[128,1664]{1,0:T(8,128)(2,1)S(1)}, bf16[128,1664]{1,0:T(8,128)(2,1)S(1)}, u32[]{:S(2)}, u32[]{:S(2)}) collective-permute-start(bf16[128,1664]{1,0:T(8,128)(2,1)S(1)} %concatenate.234), channel_id=1, source_target_pairs={{0,6},{2,0},{4,2},{6,4},{1,7},{3,1},{5,3},{7,5},{8,14},{10,8},{12,... | collective-permute-start | bytes 1277960 | tf_op jit(solution)/shard_map/ppermute | solution.py:93
  844.4 241.5 %reduce-scatter.20.cloned.1.call-start = ((), (), s32[]{:S(2)}) async-start(), calls=%async_computation.26 | async-start | bytes 4423680 | tf_op jit(solution)/shard_map/reduce_scatter | solution.py:943
  856.7 99.3 %collective-permute-start.33 = (bf16[512,1536]{1,0:T(8,128)(2,1)}, bf16[512,1536]{1,0:T(8,128)(2,1)}, u32[]{:S(2)}, u32[]{:S(2)}) collective-permute-start(bf16[512,1536]{1,0:T(8,128)(2,1)} %slice.1192), channel_id=1, source_target_pairs={{0,1},{1,0},{2,3},{3,2},{4,5},{5,4},{6,7},{7,6},{8,9},{9,8},{10,11... | collective-permute-start | bytes 4718600 | tf_op jit(solution)/shard_map/ppermute | solution.py:93
  888.7 20.3 %collective-permute-start.51 = (bf16[96,2048]{1,0:T(8,128)(2,1)}, bf16[96,2048]{1,0:T(8,128)(2,1)S(1)}, u32[]{:S(2)}, u32[]{:S(2)}) collective-permute-start(bf16[96,2048]{1,0:T(8,128)(2,1)} %get-tuple-element.459), channel_id=1, source_target_pairs={{0,2},{2,4},{4,6},{6,0},{1,3},{3,5},{5,7},{7,1},{8,10},{10,12},{12... | collective-permute-start | bytes 1179656 | tf_op jit(solution)/shard_map/ppermute | solution.py:93
  898.3 27.6 %collective-permute-start.52 = (bf16[96,2048]{1,0:T(8,128)(2,1)}, bf16[96,2048]{1,0:T(8,128)(2,1)}, u32[]{:S(2)}, u32[]{:S(2)}) collective-permute-start(bf16[96,2048]{1,0:T(8,128)(2,1)} %get-tuple-element.458), channel_id=1, source_target_pairs={{0,4},{2,6},{4,0},{6,2},{1,5},{3,7},{5,1},{7,3},{8,12},{10,14},{12... | collective-permute-start | bytes 1179656 | tf_op jit(solution)/shard_map/ppermute | solution.py:93
  899.2 26.7 %collective-permute-start.53 = (bf16[96,2048]{1,0:T(8,128)(2,1)}, bf16[96,2048]{1,0:T(8,128)(2,1)}, u32[]{:S(2)}, u32[]{:S(2)}) collective-permute-start(bf16[96,2048]{1,0:T(8,128)(2,1)} %get-tuple-element.457), channel_id=1, source_target_pairs={{0,6},{2,0},{4,2},{6,4},{1,7},{3,1},{5,3},{7,5},{8,14},{10,8},{12,... | collective-permute-start | bytes 1179656 | tf_op jit(solution)/shard_map/ppermute | solution.py:93
  961.7 48.9 %collective-permute-start.34 = (bf16[128,1536]{1,0:T(8,128)(2,1)}, bf16[128,1536]{1,0:T(8,128)(2,1)S(1)}, u32[]{:S(2)}, u32[]{:S(2)}) collective-permute-start(bf16[128,1536]{1,0:T(8,128)(2,1)} %get-tuple-element.467), channel_id=1, source_target_pairs={{0,6},{2,0},{4,2},{6,4},{1,7},{3,1},{5,3},{7,5},{8,14},{10,8},{12,... | collective-permute-start | bytes 1179656 | tf_op jit(solution)/shard_map/ppermute | solution.py:93
  972.0 38.6 %collective-permute-start.35 = (bf16[128,1536]{1,0:T(8,128)(2,1)}, bf16[128,1536]{1,0:T(8,128)(2,1)}, u32[]{:S(2)}, u32[]{:S(2)}) collective-permute-start(bf16[128,1536]{1,0:T(8,128)(2,1)} %get-tuple-element.469), channel_id=1, source_target_pairs={{0,4},{2,6},{4,0},{6,2},{1,5},{3,7},{5,1},{7,3},{8,12},{10,14},{12... | collective-permute-start | bytes 1179656 | tf_op jit(solution)/shard_map/ppermute | solution.py:93
  972.1 38.6 %collective-permute-start.36 = (bf16[128,1536]{1,0:T(8,128)(2,1)}, bf16[128,1536]{1,0:T(8,128)(2,1)}, u32[]{:S(2)}, u32[]{:S(2)}) collective-permute-start(bf16[128,1536]{1,0:T(8,128)(2,1)} %get-tuple-element.468), channel_id=1, source_target_pairs={{0,2},{2,4},{4,6},{6,0},{1,3},{3,5},{5,7},{7,1},{8,10},{10,12},{12... | collective-permute-start | bytes 1179656 | tf_op jit(solution)/shard_map/ppermute | solution.py:93
  980.9 16.9 %collective-permute-start.60 = (f32[8,128]{1,0:T(8,128)S(1)}, f32[8,128]{1,0:T(8,128)S(1)}, u32[]{:S(2)}, u32[]{:S(2)}) collective-permute-start(f32[8,128]{1,0:T(8,128)S(1)} %add.449), channel_id=1, source_target_pairs={{0,2},{2,0},{4,6},{6,4},{1,3},{3,1},{5,7},{7,5},{8,10},{10,8},{12,... | collective-permute-start | bytes 12296 | tf_op jit(solution)/shard_map/ppermute | solution.py:93
  1010.2 14.7 %collective-permute-start.54 = (bf16[512,1536]{1,0:T(8,128)(2,1)}, bf16[512,1536]{1,0:T(8,128)(2,1)S(1)}, u32[]{:S(2)}, u32[]{:S(2)}) collective-permute-start(bf16[512,1536]{1,0:T(8,128)(2,1)} %slice.1191), channel_id=1, source_target_pairs={{0,1},{1,0},{2,3},{3,2},{4,5},{5,4},{6,7},{7,6},{8,9},{9,8},{10,11... | collective-permute-start | bytes 4718600 | tf_op jit(solution)/shard_map/ppermute | solution.py:93
  1020.6 61.1 %all-to-all-start.3 = ((bf16[8,48,1152]{2,1,0:T(8,128)(2,1)}), bf16[8,48,1152]{2,1,0:T(8,128)(2,1)}, u32[]{:S(2)}, u32[]{:S(2)}) async-start(bf16[8,48,1152]{2,1,0:T(8,128)(2,1)} %bitcast.341), calls=%async_computation.7 | async-start | bytes 1769472 | tf_op jit(solution)/shard_map/all_to_all | solution.py:944
  1027.5 23.1 %collective-permute-start.55 = (bf16[128,1536]{1,0:T(8,128)(2,1)S(1)}, bf16[128,1536]{1,0:T(8,128)(2,1)S(1)}, u32[]{:S(2)}, u32[]{:S(2)}) collective-permute-start(bf16[128,1536]{1,0:T(8,128)(2,1)S(1)} %get-tuple-element.454), channel_id=1, source_target_pairs={{0,6},{2,0},{4,2},{6,4},{1,7},{3,1},{5,3},{7,5},{8,14},{10,8},{12,... | collective-permute-start | bytes 1179656 | tf_op jit(solution)/shard_map/ppermute | solution.py:93
  1031.2 50.3 %collective-permute-start.56 = (bf16[128,1536]{1,0:T(8,128)(2,1)S(1)}, bf16[128,1536]{1,0:T(8,128)(2,1)S(1)}, u32[]{:S(2)}, u32[]{:S(2)}) collective-permute-start(bf16[128,1536]{1,0:T(8,128)(2,1)S(1)} %get-tuple-element.456), channel_id=1, source_target_pairs={{0,4},{2,6},{4,0},{6,2},{1,5},{3,7},{5,1},{7,3},{8,12},{10,14},{12... | collective-permute-start | bytes 1179656 | tf_op jit(solution)/shard_map/ppermute | solution.py:93
  1031.2 50.3 %collective-permute-start.57 = (bf16[128,1536]{1,0:T(8,128)(2,1)S(1)}, bf16[128,1536]{1,0:T(8,128)(2,1)S(1)}, u32[]{:S(2)}, u32[]{:S(2)}) collective-permute-start(bf16[128,1536]{1,0:T(8,128)(2,1)S(1)} %get-tuple-element.455), channel_id=1, source_target_pairs={{0,2},{2,4},{4,6},{6,0},{1,3},{3,5},{5,7},{7,1},{8,10},{10,12},{12... | collective-permute-start | bytes 1179656 | tf_op jit(solution)/shard_map/ppermute | solution.py:93
  1085.9 27.5 %all-to-all-start.4 = ((bf16[8,48,1152]{2,1,0:T(8,128)(2,1)}), bf16[8,48,1152]{2,1,0:T(8,128)(2,1)}, u32[]{:S(2)}, u32[]{:S(2)}) async-start(bf16[8,48,1152]{2,1,0:T(8,128)(2,1)} %bitcast.342), calls=%async_computation.11 | async-start | bytes 1769472 | tf_op jit(solution)/shard_map/all_to_all | solution.py:944
  (173 other events, 1912.8 us)
Sparse Core Ops, SparseCore 0:
  51.3 55.9 all-gather.7
  117.2 36.3 all-gather.11
  156.1 70.2 all-gather.9
  228.0 43.9 all-gather.13
  273.7 70.1 all-gather.15
  346.2 70.1 all-gather.17
  439.4 50.6 all-gather.19
  588.5 43.3 reduce-scatter.9
  634.9 70.1 reduce-scatter.7
  707.9 70.1 reduce-scatter.11
  781.1 43.9 reduce-scatter.17
  828.0 70.1 reduce-scatter.15
  901.3 47.2 reduce-scatter.13
  956.2 54.0 reduce-scatter.19

commit v7 on v6

--- a/solution.py
+++ b/solution.py
@@ -93,24 +93,39 @@
     return by_rows(lax.ppermute(by_rows(x), axis, pairs))
 
 
-def gather_rows(x):
-    n = lax.axis_size("z")
-    parts = [x] + [send(x, "z", ring(s)) for s in range(1, n)]
+def gather_start(x):
+    return [x] + [send(x, "z", ring(s)) for s in range(1, lax.axis_size("z"))]
+
+
+def gather_finish(parts):
     mine = by_rows(jnp.concatenate(parts, axis=0))
     return by_rows(jnp.concatenate([mine, send(mine, "core", SWAP)], axis=0))
 
 
-def return_rows(total):
+def gather_rows(x):
+    return gather_finish(gather_start(x))
+
+
+def return_start(total):
     n = lax.axis_size("z")
     half = total.shape[0] // 2
     rows = half // n
     recv = send(total[half:].astype(bf16), "core", SWAP)
     mine = total[:half] + recv.astype(f32)
-    out = mine[:rows]
-    for s in range(1, n):
-        part = mine[s * rows : (s + 1) * rows].astype(bf16)
-        out = out + send(part, "z", ring(-s)).astype(f32)
-    return out
+    sent = [
+        send(mine[s * rows : (s + 1) * rows].astype(bf16), "z", ring(-s)) for s in range(1, n)
+    ]
+    return mine[:rows], sent
+
+
+def return_finish(own, sent):
+    for part in sent:
+        own = own + part.astype(f32)
+    return own
+
+
+def return_rows(total):
+    return return_finish(*return_start(total))
 
 
 def pair_gather(x):
@@ -386,7 +401,7 @@
     return spread, owner
 
 
-def moe_forward(own_in, mask, w):
+def moe_forward(own_in, mask, w, riders=None):
     rows = own_in.shape[0]
     base_in = gather_rows(own_in)
     moe_in = wide(base_in)
@@ -397,6 +412,9 @@
     local = lax.dynamic_slice(gates, (0, first), (gates.shape[0], count))
     pre = nn(moe_in, w["expert_in"], bf16)
     pre_s = nn(base_in, w["shared_in"], bf16)
+    if riders is not None:
+        riders = gather_start(riders)
+        riders[1], pre = fence(riders[1], pre)
     pre, pre_s = lax.optimization_barrier((pre, pre_s))
     p = pre.astype(f32)
     spread, _ = unit_gates(local, units)
@@ -404,8 +422,12 @@
     half = pre_s.shape[1] // 2
     p = pre_s.astype(f32)
     hid_s = swiglu(p[:, :half], p[:, half:]).astype(bf16)
-    total = add_first(nn(hid, w["expert_down"]), nt(hid_s, w["shared_down_t"]))
-    return total, (moe_in, base_in, gates[:rows], local, pre, pre_s)
+    low = nn(hid, w["expert_down"])
+    if riders is not None:
+        riders[2:], low = fence(riders[2:], low)
+    total = add_first(low, nt(hid_s, w["shared_down_t"]))
+    kept = (moe_in, base_in, gates[:rows], local, pre, pre_s)
+    return (total, kept) if riders is None else (total, kept, riders)
 
 
 def moe_backward(base_z, kept, w, experts_total):
@@ -439,9 +461,9 @@
     total = add_first(total, nt(g_pre_s, w["shared_in"]))
     extra = -(-experts_total // 128) * 128
     table = jnp.pad(table, ((0, 0), (0, extra - experts_total)))
-    back = return_rows(narrow(jnp.concatenate([total, table], axis=1)))
+    total = jnp.concatenate([total, table], axis=1)
     side = (moe_in, grad_z, hidden, hid_s, g_pre, g_pre_s, base_in, base_z)
-    return back, side
+    return total, side
 
 
 def moe_finish(back, kept, w, experts_total):
@@ -589,9 +611,10 @@
     def for_all(x):
         return jnp.broadcast_to(x[:, None], (rows, n_tp, x.shape[1]))
 
-    def moved_columns(parts, *after):
-        packed = jnp.concatenate(parts, axis=2).transpose(1, 0, 2)
-        packed = fence(packed, *after)[0]
+    def packed_columns(parts):
+        return jnp.concatenate(parts, axis=2).transpose(1, 0, 2)
+
+    def moved_columns(packed):
         moved = lax.all_to_all(packed, TP, split_axis=0, concat_axis=0, tiled=True)
         return moved.reshape(n_tp * rows, -1)
 
@@ -606,7 +629,7 @@
         ]
 
     blank = jnp.zeros((rows, n_tp, step_width - heads - small_cols), bf16)
-    moved_m = moved_columns(
+    packed_m = packed_columns(
         [
             by_owner(w_in[:, :DI], n_tp),
             by_owner(w_in[:, DI : 2 * DI], n_tp),
@@ -617,7 +640,7 @@
             by_owner(w_mix_out.T, n_tp),
         ]
     )
-    w_m = whole_rows(moved_m)
+    moved_m = moved_columns(packed_m)
 
     expert_ids = jnp.arange(experts_total, dtype=jnp.int32)
     info_width = -(-(2 * experts_total + 1) // 128) * 128
@@ -628,19 +651,18 @@
             jnp.any(routes[b, m][:, :, None] == expert_ids, axis=1).astype(bf16) for b in range(2)
         ]
         info = lanes(hot + [segments[m][:, None].astype(bf16)], info_width)
-        x_info, _ = fence(jnp.concatenate([tokens[m], info], axis=1), moved_m)
+        x_info, moved_m = fence(jnp.concatenate([tokens[m], info], axis=1), moved_m)
         rows_in.append(gather_rows(x_info))
+    w_m = whole_rows(moved_m)
     in_width = 2 * chan + 2 * STATE
     w_in_here = w_m[:, :in_width]
-    moved_s = moved_columns(
-        shared_pack(shared_in_m, shared_down_m) + shared_pack(shared_in, shared_down), rows_in
-    )
-    w_s = whole_rows(moved_s)
     at = in_width + step_width
     w_step = w_m[:, in_width:at]
     w_dt_here = w_step[:, :128]
     small_all = w_step[:, heads : heads + small_cols]
-    gain_mamba, gain_moe_m, gain_attn, gain_moe = [small_all[:, i].astype(f32) for i in range(4)]
+    pick = (jnp.arange(128)[None, :] == heads + jnp.arange(8)[:, None]).astype(bf16)
+    gain_rows = nt(pick, w_dt_here)
+    gain_mamba, gain_moe_m, gain_attn, gain_moe = [gain_rows[i] for i in range(4)]
     router_m_full = small_all[:, 4 : 4 + experts_total]
     router_full = small_all[:, 4 + experts_total : 4 + 2 * experts_total]
     vec_all = small_all[:, 4 + 2 * experts_total :].reshape(n_all, rows * vec_cols).astype(f32)
@@ -672,29 +694,28 @@
             lax.all_gather(w_low, "dp", axis=1, tiled=True).reshape(-1, D),
         )
 
-    expert_in_m, expert_down_m, _ = fence(expert_in_m, expert_down_m, moved_m)
     up_m, low_m = expert_weights(expert_in_m, expert_down_m)
-    moe_m = {
-        "router": router_m_full,
-        "shared_in": w_s[:, : 2 * ff],
-        "shared_down_t": w_s[:, 2 * ff : 3 * ff],
-        "expert_in": up_m,
-        "expert_down": low_m,
-    }
-
     kv = KVH // 2
     q_width = QH // 2 * HEAD
     kv_width = kv * HEAD
     q_all, kv_all = QH * HEAD, KVH * HEAD
-    up_a, low_a = expert_weights(expert_in, expert_down)
-    moe_a = {
-        "router": router_full,
-        "shared_in": w_s[:, 3 * ff : 5 * ff],
-        "shared_down_t": w_s[:, 5 * ff :],
-        "expert_in": up_a,
-        "expert_down": low_a,
-    }
-
+    attn_pack = jnp.concatenate(
+        [
+            by_owner(w_qkv[:, :q_all], 2),
+            by_owner(w_qkv[:, q_all : q_all + kv_all], 2),
+            by_owner(w_qkv[:, q_all + kv_all :], 2),
+            by_owner(w_out.T, 2),
+        ],
+        axis=2,
+    ).transpose(1, 0, 2)
+    packed_s = shared_pack(shared_in_m, shared_down_m) + shared_pack(shared_in, shared_down)
+    packed_s, rows_in = fence(packed_columns(packed_s), rows_in)
+    moved_s = moved_columns(packed_s)
+    attn_pack, moved_s = fence(attn_pack, moved_s)
+    attn_pack = lax.all_to_all(attn_pack, "core", split_axis=0, concat_axis=0, tiled=True)
+    own = attn_pack.reshape(2 * rows, -1)
+    n_z = lax.axis_size("z")
+    attn_parts = [send(own, "z", ring(s)) for s in range(n_z - 1, 0, -1)] + [own]
     def eight(parts):
         block = jnp.concatenate([p.reshape(-1, p.shape[-1]) for p in parts], axis=0)
         return jnp.pad(block, ((0, 8 - block.shape[0]), (0, 0)))
@@ -717,7 +738,6 @@
         pair = jnp.concatenate([seg[:seqs], seg[middle : middle + seqs]], axis=0)
         allowed.append(attn_mask(pair))
 
-        x_all, _ = fence(x_all, w_m)
         _, scale_x, mamba_in = rms_forward(x_all, gain_mamba)
         total_rows = mamba_in.shape[0]
         proj = nn(mamba_in, w_in_here, bf16)
@@ -725,56 +745,61 @@
         proj_all.append(proj)
         pars = (seg_col, seg_row, conv_par, chan_par, head_par)
         gained, square = scan_forward(heads, length, proj, dt_raw, *pars)
+        if m == micro - 1:
+            attn_parts, gained = fence(attn_parts, gained)
         partial = nt(gained, w_mix_t)
         high = square.astype(bf16).astype(f32)
         lane = lax.broadcasted_iota(jnp.int32, square.shape, 1)
         extra = jnp.where(lane == 0, high, jnp.where(lane == 1, square - high, 0.0))
-        back = return_rows(jnp.concatenate([partial, extra], axis=1))
+        own, sent = return_start(jnp.concatenate([partial, extra], axis=1))
+        back = return_finish(own, sent)
         gate_scale = lax.rsqrt((back[:, D : D + 1] + back[:, D + 1 : D + 2]) / DI + epsilon)
         mix_branch = back[:, :D] * gate_scale
         hidden_one.append(x_own[m] + mix_branch)
         mamba_kept.append((rows_all, scale_x[:own_rows], mamba_in, (proj, dt_raw, *pars), gained))
         mix_kept.append((mix_branch, gate_scale))
 
-    attn_pack = jnp.concatenate(
-        [
-            by_owner(w_qkv[:, :q_all], 2),
-            by_owner(w_qkv[:, q_all : q_all + kv_all], 2),
-            by_owner(w_qkv[:, q_all + kv_all :], 2),
-            by_owner(w_out.T, 2),
-        ],
-        axis=2,
-    ).transpose(1, 0, 2)
-    attn_pack, _ = fence(attn_pack, moved_s)
-    attn_pack = lax.all_to_all(attn_pack, "core", split_axis=0, concat_axis=0, tiled=True)
-    own = attn_pack.reshape(2 * rows, -1)
-    n_z = lax.axis_size("z")
-    parts = [send(own, "z", ring(s)) for s in range(n_z - 1, 0, -1)] + [own]
-    parts, _ = fence(parts, mamba_kept[-1][-1])
-    twice = jnp.concatenate(parts + parts, axis=0)
+    twice = jnp.concatenate(attn_parts + attn_parts, axis=0)
     start = (n_z - 1 - lax.axis_index("z")) * 2 * rows
-    attn_w = lax.dynamic_slice(twice, (start, 0), (n_z * 2 * rows, own.shape[1]))
+    attn_w = lax.dynamic_slice(twice, (start, 0), (n_z * 2 * rows, twice.shape[1]))
     attn_w = lax.all_gather(attn_w, FS, axis=0, tiled=True)
     w_qkv_here = attn_w[:, : q_width + 2 * kv_width]
     w_out_t = attn_w[:, q_width + 2 * kv_width :]
 
+    w_s = whole_rows(moved_s)
+    moe_m = {
+        "router": router_m_full,
+        "shared_in": w_s[:, : 2 * ff],
+        "shared_down_t": w_s[:, 2 * ff : 3 * ff],
+        "expert_in": up_m,
+        "expert_down": low_m,
+    }
+
+    up_a, low_a = fence(*expert_weights(expert_in, expert_down))
+    moe_a = {
+        "router": router_full,
+        "shared_in": w_s[:, 3 * ff : 5 * ff],
+        "shared_down_t": w_s[:, 5 * ff :],
+        "expert_in": up_a,
+        "expert_down": low_a,
+    }
+
     one_kept, layer_one = [], []
     for m in each:
         normed, scale, own = rms_forward(hidden_one[m], gain_moe_m)
-        total, kept = moe_forward(own, masks[m][0], moe_m)
+        total, kept, riders = moe_forward(own, masks[m][0], moe_m, cotangent[m])
+        cot_all.append(riders)
         layer_one.append(hidden_one[m] + return_rows(narrow(total)))
         one_kept.append((normed, scale, kept))
     attn_kept, hidden_two = [], []
     for m in each:
-        cot, _ = fence(cotangent[m], layer_one[m])
-        cot_all.append(gather_rows(cot))
         normed, scale, own = rms_forward(layer_one[m], gain_attn)
         branch, kept = attn_forward(own, allowed[m], w_qkv_here, w_out_t)
         hidden_two.append(layer_one[m] + branch)
         attn_kept.append((normed, scale, kept))
     two_kept, results = [], []
     for m in each:
-        hidden_two[m], cot_all[m] = fence(hidden_two[m], cot_all[m])
+        cot_all[m] = gather_finish(cot_all[m])
         normed, scale, own = rms_forward(hidden_two[m], gain_moe)
         total, kept = moe_forward(own, masks[m][1], moe_a)
         results.append(total)
@@ -802,20 +827,22 @@
 
     def moe_stage(grads, kept_all, w, gain, *before):
         grads = list(grads)
-        backs, sides, first_rows = [], [], []
+        backs, first_rows = [], []
         for m in each:
-            back, side = moe_backward(grads[m], kept_all[m][2], w, experts_total)
-            backs.append(back)
-            sides.append(side)
+            total, side = moe_backward(grads[m], kept_all[m][2], w, experts_total)
+            own, sent = return_start(narrow(total))
             first_rows.append(side[6][:own_rows])
             if saving:
-                newer = moe_weight_grads(sides[-1:])
-                hold = (back, newer, grads[m + 1 :])
-                backs[-1], newer, grads[m + 1 :] = lax.optimization_barrier(hold)
+                back = return_finish(own, sent)
+                hold = (back, moe_weight_grads([side]), grads[m + 1 :])
+                back, newer, grads[m + 1 :] = lax.optimization_barrier(hold)
                 weights = newer if m == 0 else [a + b for a, b in zip(weights, newer)]
-        if not saving:
-            weights = moe_weight_grads(sides)
-            backs[-1], weights = lax.optimization_barrier((backs[-1], weights))
+            else:
+                hidden, g_pre, own = fence(side[2], side[4], own)
+                weights = moe_weight_grads([(*side[:2], hidden, side[3], g_pre, *side[5:])])
+                sent, weights = fence(sent, weights)
+                back = return_finish(own, sent)
+            backs.append(back)
         backs[-1], before = fence(backs[-1], before)
         grad_gain = 0.0
         values, logits = [], []
@@ -836,7 +863,7 @@
     sum_down_a = low_over_dp(g_down_a)
     grad_two = [cotangent[m].astype(f32) + values[m] for m in each]
     for m in each:
-        total, _ = fence(results[m], grad_two[m])
+        total, grad_two[m] = fence(results[m], grad_two[m])
         results[m] = (hidden_two[m] + return_rows(narrow(total))).astype(bf16)
 
     grad_layer, sides = [], []
@@ -872,16 +899,15 @@
         gain_moe_m,
         sum_in_a,
         sum_down_a,
-        g_part,
-    )
-    sum_in_a, sum_down_a, g_part = before
+    )
+    sum_in_a, sum_down_a = before
     out_expert_in, out_expert_down = expert_out(sum_in_a, sum_down_a)
     sum_in_m = up_over_dp(g_in_m)
     sum_down_m = low_over_dp(g_down_m)
     grad_one = [grad_layer[m] + values[m] for m in each]
 
-    def attn_owner(g_part, *after):
-        blocks = fence(g_part, *after)[0].reshape(n_z, 2 * rows, -1)
+    def attn_owner(g_part):
+        blocks = g_part.reshape(n_z, 2 * rows, -1)
         here = lax.axis_index("z")
         own = lax.dynamic_index_in_dim(blocks, here, 0, keepdims=False)
         sent = []
@@ -924,23 +950,24 @@
             g_mix = tn_sum([(x, k[4]) for x, k in zip(mixes, mamba_kept)])
             mix_all, g_mix = fence(mix_all, by_rows(g_mix))
         if m == micro - 1:
-            attn_sent = attn_owner(g_part, mix_all)
+            g_part, mix_all = fence(g_part, mix_all)
+            attn_sent = attn_owner(g_part)
         grad_gated = nn(mix_all, w_mix_t, bf16)
         grad_scan, *grads = scan_backward(
             heads, length, *scan_args, grad_gated, extra_all
         )
-        if m == micro - 1:
-            grad_scan, attn_sent = fence(grad_scan, attn_sent)
-        mamba_sides.append((mamba_in, grad_scan))
         small = grads if small is None else [a + b for a, b in zip(small, grads)]
         total = nt(grad_scan, w_scan)
         gains[0] = gains[0] + jnp.sum(total * normed_x, axis=0)
-        mamba_back.append(return_rows(total))
-
-    g_attn = attn_total(*attn_sent)
+        own, sent = return_start(total)
+        grad_scan, own = fence(grad_scan, own)
+        mamba_sides.append((mamba_in, grad_scan))
+        mamba_back.append((own, sent))
+
+    def rows_sum(packed):
+        return lax.psum_scatter(packed, FS, scatter_dimension=0, tiled=True)
 
     def rows_back(packed):
-        packed = lax.psum_scatter(packed, FS, scatter_dimension=0, tiled=True)
         return lax.all_to_all(
             packed.reshape(n_tp, rows, -1), TP, split_axis=0, concat_axis=0, tiled=True
         ).astype(f32)
@@ -948,12 +975,16 @@
     def owned(block):
         return block.transpose(1, 0, 2).reshape(rows, -1)
 
-    g_s = rows_back(
+    g_s = rows_sum(
         jnp.concatenate([g_mix, g_sin_m, g_sdown_m, g_sin_a, g_sdown_a], axis=1)
     )
 
     g_scan = by_rows(tn_sum(mamba_sides, f32))
-    g_scan, sum_in_m, sum_down_m = fence(g_scan, sum_in_m, sum_down_m)
+    mamba_back, g_scan, attn_sent = fence(mamba_back, g_scan, attn_sent)
+    mamba_back = [return_finish(*pair) for pair in mamba_back]
+    g_attn = attn_total(*attn_sent)
+    g_s, mamba_back[-1] = fence(g_s, mamba_back[-1])
+    g_s = rows_back(g_s)
     out_expert_in_m, out_expert_down_m = expert_out(sum_in_m, sum_down_m)
 
     conv_sums, chan_sums, head_sums = small
@@ -971,10 +1002,11 @@
     vec_grad = jnp.concatenate([spread(g_gate, DI).reshape(n_all, gate_here), conv_grad], axis=1)
     vec_grad = jnp.pad(vec_grad, ((0, 0), (0, rows * vec_cols - vec_len))).reshape(D, vec_cols)
     little = jnp.concatenate([g[:, None] for g in gains] + [g_router_m, g_router, vec_grad], axis=1)
-    after = step_width - heads - small_cols
+    spare = step_width - heads - small_cols
     g_scan = jnp.pad(g_scan, ((0, 0), (0, step_width - 128)))
-    g_m = rows_back((g_scan + jnp.pad(little, ((0, 0), (in_width + heads, after)))).astype(bf16))
-    mamba_back[-1], g_s = fence(mamba_back[-1], g_s)
+    g_m = rows_sum((g_scan + jnp.pad(little, ((0, 0), (in_width + heads, spare)))).astype(bf16))
+    g_m, g_s = fence(g_m, g_s)
+    g_m = rows_back(g_m)
     grads_in = []
     for m in each:
         scale_x = mamba_kept[m][1]
@@ -998,6 +1030,7 @@
     out_conv_w = vec[gate_here + conv_here : vec_len].reshape(CK, conv_here)
 
     head_grad = lax.dynamic_update_slice(jnp.zeros((8, 128), f32), head_grad, (0, slot * heads))
+    head_grad, mamba_back[-1] = fence(head_grad, mamba_back[-1])
     for axis in ALL:
         size = lax.axis_size(axis)
         step = 1

time: 1130 us -> 1070 us (0.947); the launches traced: 1130 us -> 1060 us
  blocking collectives: 70.4 us -> 9.15 us
  other arithmetic: 152 us -> 121 us
  starting transfers between devices: 109 us -> 125 us
    all_to_all x2 -> x0, blocking collectives: 62.3 us -> none  [moved_columns(): moved = lax.all_to_all(packed, TP, split_axis=0, concat_axis=0, tiled=True)]
    all_to_all x0 -> x2, waiting for transfers between devices: none -> 41.8 us  [moved_columns(): moved = lax.all_to_all(packed, TP, split_axis=0, concat_axis=0, tiled=True)]
    all_gather x2, waiting for transfers between devices: 0.04 us -> 38.5 us  [expert_weights(): lax.all_gather(cols, 'dp', axis=0, tiled=True)]
    ppermute x63, waiting for transfers between devices: 394 us -> 365 us  [send(): return by_rows(lax.ppermute(by_rows(x), axis, pairs))]
    all_gather x2, waiting for transfers between devices: 23 us -> 0.04 us  [expert_weights(): lax.all_gather(w_low, 'dp', axis=1, tiled=True).reshape(-1, D)]
    reduce_scatter x1, waiting for transfers between devices: 20.9 us -> 0.02 us  [body(): g_attn = lax.psum_scatter(g_attn, FS, scatter_dimension=0, tiled=True)]
    all_to_all x0 -> x2, starting transfers between devices: none -> 16.3 us  [moved_columns(): moved = lax.all_to_all(packed, TP, split_axis=0, concat_axis=0, tiled=True)]
    convert_element_type x3 -> x1, other arithmetic: 14.1 us -> 2.28 us  [body(): (g_scan + jnp.pad(little, ((0, 0), (in_width + heads, spare)))).astype(bf16)]
  transfers between devices with their start and end apart: 79 -> 81, of which waited for: 37 -> 37; matrix products, arithmetic and copies ran while one was open for 33% -> 29% of each run, Pallas kernels for 2% -> 3%
where the time goes in v7:
time: 1070 us; the launch traced here: 1060 us
  waiting for transfers between devices  463 us (43%)
  matrix products  194 us (18%)
  starting transfers between devices  125 us (12%)
  other arithmetic  121 us (11%)
  local copies, waits for them, and re-layouts  97 us (9%)
  Pallas kernels  27.9 us (3%)
  between operations  17.8 us (2%)
    ppermute x63, waiting for transfers between devices, send(): return by_rows(lax.ppermute(by_rows(x), axis, pairs))  365 us
    dot_general x44, matrix products, dot(): r = lax.dot_general(a, b, (dims, ((), ())), preferred_element_type=f32)  186 us
    ppermute x63, starting transfers between devices, send(): return by_rows(lax.ppermute(by_rows(x), axis, pairs))  87.5 us
    all_to_all x2, waiting for transfers between devices, moved_columns(): moved = lax.all_to_all(packed, TP, split_axis=0, concat_axis=0, tiled=True)  41.8 us
    all_gather x2, waiting for transfers between devices, expert_weights(): lax.all_gather(cols, 'dp', axis=0, tiled=True)  38.5 us
    unnamed x370, local copies, waits for them, and re-layouts  34.3 us
  transfers between devices with their start and end apart: 81, of which 37 were waited for; matrix products, arithmetic and copies ran while one was open for 29% of the time, Pallas kernels for 3%

profile of v7, /device:TPU:0, one launch (start us, length us, event | category | flops | bytes accessed | tf_op | source)
XLA Modules:
  0.0 1055.9 jit_solution(15306947879803369717)
XLA Ops:
  16.5 6.3 all-to-all-start
  24.6 27.6 %all-to-all-done = bf16[8,48,1536]{2,1,0:T(8,128)(2,1)S(1)} async-done(((bf16[8,48,1536]{2,1,0:T(8,128)(2,1)}), bf16[8,48,1536]{2,1,0:T(8,128)(2,1)S(1)}, u32[]{:S(2)}, u32[]{:S(2)}) %all-to-all-start) | async-done | bytes 1179680 | tf_op jit(solution)/shard_map/all_to_all | solution.py:618
  58.7 10.8 %collective-permute-done = bf16[128,1664]{1,0:T(8,128)(2,1)S(1)} collective-permute-done((bf16[128,1664]{1,0:T(8,128)(2,1)S(1)}, bf16[128,1664]{1,0:T(8,128)(2,1)S(1)}, u32[]{:S(2)}, u32[]{:S(2)}) %collective-permute-start) | collective-permute-done | bytes 426016 | tf_op jit(solution)/shard_map/ppermute | solution.py:93
  69.5 16.9 %collective-permute-done.1 = bf16[128,1664]{1,0:T(8,128)(2,1)S(1)} collective-permute-done((bf16[128,1664]{1,0:T(8,128)(2,1)S(1)}, bf16[128,1664]{1,0:T(8,128)(2,1)S(1)}, u32[]{:S(2)}, u32[]{:S(2)}) %collective-permute-start.1) | collective-permute-done | bytes 426016 | tf_op jit(solution)/shard_map/ppermute | solution.py:93
  91.4 10.0 all-to-all-start.1
  104.0 14.3 %all-to-all-done.1 = bf16[8,48,768]{2,1,0:T(8,128)(2,1)} async-done(((bf16[8,48,768]{2,1,0:T(8,128)(2,1)}), bf16[8,48,768]{2,1,0:T(8,128)(2,1)}, u32[]{:S(2)}, u32[]{:S(2)}) %all-to-all-start.1) | async-done | bytes 589856 | tf_op jit(solution)/shard_map/all_to_all | solution.py:618
  124.7 5.1 all_to_all.30
  135.5 6.5 fusion.36.proj_ref
  144.4 9.6 scan_forward.1
  154.1 10.2 collective-permute-done.5
  173.6 3.6 collective-permute-done.7
  183.4 8.9 collective-permute-done.10
  192.3 8.3 collective-permute-done.8
  200.6 18.3 %collective-permute-done.9 = bf16[128,1664]{1,0:T(8,128)(2,1)S(1)} collective-permute-done((bf16[128,1664]{1,0:T(8,128)(2,1)S(1)}, bf16[128,1664]{1,0:T(8,128)(2,1)S(1)}, u32[]{:S(2)}, u32[]{:S(2)}) %collective-permute-start.9) | collective-permute-done | bytes 426016 | tf_op jit(solution)/shard_map/ppermute | solution.py:93
  224.3 10.1 collective-permute-done.14
  234.4 15.9 %collective-permute-done.15 = bf16[128,1536]{1,0:T(8,128)(2,1)S(1)} collective-permute-done((bf16[128,1536]{1,0:T(8,128)(2,1)S(1)}, bf16[128,1536]{1,0:T(8,128)(2,1)S(1)}, u32[]{:S(2)}, u32[]{:S(2)}) %collective-permute-start.15) | collective-permute-done | bytes 393248 | tf_op jit(solution)/shard_map/ppermute | solution.py:93
  251.7 8.0 collective-permute-start.13
  269.4 11.0 %convolution_convert_fusion.4 = bf16[1024,2048]{1,0:T(8,128)(2,1)} fusion(bf16[1024,1536]{1,0:T(8,128)(2,1)} %pad_maximum_fusion.6, bf16[1536,2048]{1,0:T(8,128)(2,1)} %all-gather.10.cloned.1.call-done), kind=kOutput, calls=%fused_computation.51 | convolution fusion | flops 6444548096 | bytes 13631488 | tf_op jit(solution)/shard_map/dot_general | solution.py:37
  283.8 4.4 convert_element_type.515
  292.6 10.6 %fusion.28 = f32[1024,1536]{1,0:T(8,128)} fusion(bf16[1024,1536]{1,0:T(8,128)(2,1)} %bitcast.388, f32[1024,2048]{1,0:T(8,128)} %convert_element_type.515, f32[1024]{0:T(1024)S(1)} %get-tuple-element.428, f32[1024]{0:T(1024)S(1)} %get-tuple-element.427, pred[1024]{0:T(1024)(128)(4,1)S(1)} %copy-done.153), kind=kOutput, calls=%fused_computation.94 | convolution fusion | flops 3229614080 | bytes 17835008 | tf_op jit(solution)/shard_map/dot_general | solution.py:37
  305.6 4.2 add.390
  315.8 11.8 %reduce-scatter.10.cloned.1.call-start = ((), (), s32[]{:S(2)}) async-start(), calls=%async_computation.21 | async-start | bytes 3932160 | tf_op jit(solution)/shard_map/reduce_scatter | solution.py:815
  334.1 8.7 collective-permute-done.19
  342.8 24.2 %collective-permute-done.20 = bf16[128,1536]{1,0:T(8,128)(2,1)S(1)} collective-permute-done((bf16[128,1536]{1,0:T(8,128)(2,1)S(1)}, bf16[128,1536]{1,0:T(8,128)(2,1)S(1)}, u32[]{:S(2)}, u32[]{:S(2)}) %collective-permute-start.20) | collective-permute-done | bytes 393248 | tf_op jit(solution)/shard_map/ppermute | solution.py:93
  394.5 7.0 collective-permute-done.24
  401.5 16.3 %collective-permute-done.25 = bf16[128,1536]{1,0:T(8,128)(2,1)S(1)} collective-permute-done((bf16[128,1536]{1,0:T(8,128)(2,1)S(1)}, bf16[128,1536]{1,0:T(8,128)(2,1)S(1)}, u32[]{:S(2)}, u32[]{:S(2)}) %collective-permute-start.25) | collective-permute-done | bytes 393248 | tf_op jit(solution)/shard_map/ppermute | solution.py:93
  419.3 38.5 %all-gather.18.cloned.1.call-done = bf16[1536,2048]{1,0:T(8,128)(2,1)} async-done(((bf16[384,2048]{1,0:T(8,128)(2,1)}), bf16[1536,2048]{1,0:T(8,128)(2,1)}) %all-gather.18.cloned.1.call-update) | async-done | bytes 6291472 | tf_op jit(solution)/shard_map/all_gather | solution.py:693
  464.0 6.9 convolution_convert_fusion.3
  480.0 6.8 select_reduce_fusion.2
  491.1 9.2 multiply_convert_fusion.4
  500.4 6.7 fusion.177
  520.8 9.0 convolution_convert_fusion.1
  535.7 7.6 convolution_convert_fusion.6
  544.9 26.3 %collective-permute-done.31 = bf16[128,1664]{1,0:T(8,128)(2,1)S(1)} collective-permute-done((bf16[128,1664]{1,0:T(8,128)(2,1)S(1)}, bf16[128,1664]{1,0:T(8,128)(2,1)S(1)}, u32[]{:S(2)}, u32[]{:S(2)}) %collective-permute-start.31) | collective-permute-done | bytes 426016 | tf_op jit(solution)/shard_map/ppermute | solution.py:93
  577.2 3.8 fusion.26
  581.1 4.8 convolution_add_fusion
  622.5 8.7 collective-permute-done.39
  631.3 16.1 %collective-permute-done.40 = bf16[128,1536]{1,0:T(8,128)(2,1)S(1)} collective-permute-done((bf16[128,1536]{1,0:T(8,128)(2,1)S(1)}, bf16[128,1536]{1,0:T(8,128)(2,1)S(1)}, u32[]{:S(2)}, u32[]{:S(2)}) %collective-permute-start.40) | collective-permute-done | bytes 393248 | tf_op jit(solution)/shard_map/ppermute | solution.py:93
  648.7 3.7 collective-permute-done.42
  655.9 9.5 multiply_convert_fusion.2
  673.4 9.3 fusion.176
  691.9 9.6 collective-permute-start.44
  702.2 8.8 convolution_convert_fusion
  711.0 7.6 convolution_convert_fusion.5
  718.6 20.4 %collective-permute-done.45 = bf16[128,1664]{1,0:T(8,128)(2,1)} collective-permute-done((bf16[128,1664]{1,0:T(8,128)(2,1)S(1)}, bf16[128,1664]{1,0:T(8,128)(2,1)}, u32[]{:S(2)}, u32[]{:S(2)}) %collective-permute-start.45) | collective-permute-done | bytes 426016 | tf_op jit(solution)/shard_map/ppermute | solution.py:93
  752.4 9.7 collective-permute-done.47
  762.1 16.8 %collective-permute-done.48 = bf16[128,1664]{1,0:T(8,128)(2,1)S(1)} collective-permute-done((bf16[128,1664]{1,0:T(8,128)(2,1)S(1)}, bf16[128,1664]{1,0:T(8,128)(2,1)S(1)}, u32[]{:S(2)}, u32[]{:S(2)}) %collective-permute-start.48) | collective-permute-done | bytes 426016 | tf_op jit(solution)/shard_map/ppermute | solution.py:93
  782.7 6.2 pad_maximum_fusion.5
  800.7 4.2 convolution_convert_fusion.12.grad_ref
  805.0 18.3 %scan_backward.1 = (bf16[1024,1152]{1,0:T(8,128)(2,1)S(1)}, f32[8,640]{1,0:T(8,128)S(1)}, f32[8,384]{1,0:T(8,128)S(1)}, f32[8,128]{1,0:T(8,128)S(1)}) custom-call(bf16[1024,1024]{1,0:T(8,128)(2,1)S(1)} %copy-done.1, f32[1024,128]{1,0:T(8,128)S(1)} %copy-done.5, f32[1024,1]{1,0:T(8,128)S(1)} %copy-done.3, f32[16,1,64]{2,1,0:T(1,128)S(1)} %bitcast.313, ...), custom_call_target="tpu_custom_call" | custom-call | tf_op jit(solution)/shard_map/scan_backward/pallas_call | solution.py:360
  823.3 9.0 multiply_reduce_fusion
  848.1 8.2 collective-permute-start.55
  868.8 4.4 fusion.178
  873.2 11.2 %collective-permute-done.56 = bf16[96,2048]{1,0:T(8,128)(2,1)} collective-permute-done((bf16[96,2048]{1,0:T(8,128)(2,1)}, bf16[96,2048]{1,0:T(8,128)(2,1)}, u32[]{:S(2)}, u32[]{:S(2)}) %collective-permute-start.56) | collective-permute-done | bytes 393248 | tf_op jit(solution)/shard_map/ppermute | solution.py:93
  884.5 8.1 collective-permute-done.52
  892.6 33.8 %collective-permute-done.53 = bf16[128,1536]{1,0:T(8,128)(2,1)S(1)} collective-permute-done((bf16[128,1536]{1,0:T(8,128)(2,1)S(1)}, bf16[128,1536]{1,0:T(8,128)(2,1)S(1)}, u32[]{:S(2)}, u32[]{:S(2)}) %collective-permute-start.53) | collective-permute-done | bytes 393248 | tf_op jit(solution)/shard_map/ppermute | solution.py:93
  935.8 4.1 fusion.186
  942.8 10.6 %collective-permute-done.34 = bf16[128,1536]{1,0:T(8,128)(2,1)S(1)} collective-permute-done((bf16[128,1536]{1,0:T(8,128)(2,1)}, bf16[128,1536]{1,0:T(8,128)(2,1)S(1)}, u32[]{:S(2)}, u32[]{:S(2)}) %collective-permute-start.34) | collective-permute-done | bytes 393248 | tf_op jit(solution)/shard_map/ppermute | solution.py:93
  953.4 21.8 %collective-permute-done.35 = bf16[128,1536]{1,0:T(8,128)(2,1)S(1)} collective-permute-done((bf16[128,1536]{1,0:T(8,128)(2,1)S(1)}, bf16[128,1536]{1,0:T(8,128)(2,1)S(1)}, u32[]{:S(2)}, u32[]{:S(2)}) %collective-permute-start.35) | collective-permute-done | bytes 393248 | tf_op jit(solution)/shard_map/ppermute | solution.py:93
  982.0 4.0 all_to_all.31
  987.4 5.0 all-to-all-start.3
  1007.9 4.5 collective-permute-start.61
  1015.8 3.6 all-to-all-start.4
  1026.4 16.0 %all-to-all-done.4 = bf16[8,48,1152]{2,1,0:T(8,128)(2,1)S(1)} async-done(((bf16[8,48,1152]{2,1,0:T(8,128)(2,1)}), bf16[8,48,1152]{2,1,0:T(8,128)(2,1)S(1)}, u32[]{:S(2)}, u32[]{:S(2)}) %all-to-all-start.4) | async-done | bytes 884768 | tf_op jit(solution)/shard_map/all_to_all | solution.py:971
  (818 shorter events, 336.9 us)
Async XLA Ops:
  16.5 35.7 %all-to-all-start = ((bf16[8,48,1536]{2,1,0:T(8,128)(2,1)}), bf16[8,48,1536]{2,1,0:T(8,128)(2,1)S(1)}, u32[]{:S(2)}, u32[]{:S(2)}) async-start(bf16[8,48,1536]{2,1,0:T(8,128)(2,1)} %copy.590), calls=%async_computation | async-start | bytes 2359296 | tf_op jit(solution)/shard_map/all_to_all | solution.py:618
  22.8 109.0 %all-gather.8.cloned.1.call-start = ((), (), s32[]{:S(2)}) async-start(), calls=%async_computation.13 | async-start | bytes 5898240 | tf_op jit(solution)/shard_map/all_gather | solution.py:622
  53.2 216.1 %all-gather.10.cloned.1.call-start = ((), (), s32[]{:S(2)}) async-start(), calls=%async_computation.14 | async-start | bytes 7864320 | tf_op jit(solution)/shard_map/all_gather | solution.py:693
  54.8 14.7 %collective-permute-start = (bf16[128,1664]{1,0:T(8,128)(2,1)S(1)}, bf16[128,1664]{1,0:T(8,128)(2,1)S(1)}, u32[]{:S(2)}, u32[]{:S(2)}) collective-permute-start(bf16[128,1664]{1,0:T(8,128)(2,1)S(1)} %concatenate.200), channel_id=1, source_target_pairs={{0,2},{2,4},{4,6},{6,0},{1,3},{3,5},{5,7},{7,1},{8,10},{10,12},{12... | collective-permute-start | bytes 1277960 | tf_op jit(solution)/shard_map/ppermute | solution.py:93
  54.9 31.6 %collective-permute-start.1 = (bf16[128,1664]{1,0:T(8,128)(2,1)S(1)}, bf16[128,1664]{1,0:T(8,128)(2,1)S(1)}, u32[]{:S(2)}, u32[]{:S(2)}) collective-permute-start(bf16[128,1664]{1,0:T(8,128)(2,1)S(1)} %concatenate.200), channel_id=1, source_target_pairs={{0,4},{2,6},{4,0},{6,2},{1,5},{3,7},{5,1},{7,3},{8,12},{10,14},{12... | collective-permute-start | bytes 1277960 | tf_op jit(solution)/shard_map/ppermute | solution.py:93
  56.7 29.8 %collective-permute-start.2 = (bf16[128,1664]{1,0:T(8,128)(2,1)S(1)}, bf16[128,1664]{1,0:T(8,128)(2,1)S(1)}, u32[]{:S(2)}, u32[]{:S(2)}) collective-permute-start(bf16[128,1664]{1,0:T(8,128)(2,1)S(1)} %concatenate.200), channel_id=1, source_target_pairs={{0,6},{2,0},{4,2},{6,4},{1,7},{3,1},{5,3},{7,5},{8,14},{10,8},{12,... | collective-permute-start | bytes 1277960 | tf_op jit(solution)/shard_map/ppermute | solution.py:93
  91.4 26.8 %all-to-all-start.1 = ((bf16[8,48,768]{2,1,0:T(8,128)(2,1)}), bf16[8,48,768]{2,1,0:T(8,128)(2,1)}, u32[]{:S(2)}, u32[]{:S(2)}) async-start(bf16[8,48,768]{2,1,0:T(8,128)(2,1)} %copy.591), calls=%async_computation.1 | async-start | bytes 1179648 | tf_op jit(solution)/shard_map/all_to_all | solution.py:618
  101.4 179.1 %all-gather.12.cloned.1.call-start = ((), (), s32[]{:S(2)}) async-start(), calls=%async_computation.15 | async-start | bytes 2949120 | tf_op jit(solution)/shard_map/all_gather | solution.py:622
  118.2 174.4 %all-gather.14.cloned.1.call-start = ((), (), s32[]{:S(2)}) async-start(), calls=%async_computation.16 | async-start | bytes 3932160 | tf_op jit(solution)/shard_map/all_gather | solution.py:694
  118.8 250.7 %all-gather.16.cloned.1.call-start = ((), (), s32[]{:S(2)}) async-start(), calls=%async_computation.17 | async-start | bytes 7864320 | tf_op jit(solution)/shard_map/all_gather | solution.py:765
  129.8 24.2 %collective-permute-start.4 = (bf16[96,2048]{1,0:T(8,128)(2,1)S(1)}, bf16[96,2048]{1,0:T(8,128)(2,1)S(1)}, u32[]{:S(2)}, u32[]{:S(2)}) collective-permute-start(bf16[96,2048]{1,0:T(8,128)(2,1)S(1)} %bitcast.321), channel_id=1, source_target_pairs={{0,6},{2,0},{4,2},{6,4},{1,7},{3,1},{5,3},{7,5},{8,14},{10,8},{12,... | collective-permute-start | bytes 1179656 | tf_op jit(solution)/shard_map/ppermute | solution.py:93
  131.1 33.2 %collective-permute-start.5 = (bf16[96,2048]{1,0:T(8,128)(2,1)S(1)}, bf16[96,2048]{1,0:T(8,128)(2,1)}, u32[]{:S(2)}, u32[]{:S(2)}) collective-permute-start(bf16[96,2048]{1,0:T(8,128)(2,1)S(1)} %bitcast.322), channel_id=1, source_target_pairs={{0,4},{2,6},{4,0},{6,2},{1,5},{3,7},{5,1},{7,3},{8,12},{10,14},{12... | collective-permute-start | bytes 1179656 | tf_op jit(solution)/shard_map/ppermute | solution.py:93
  131.1 33.2 %collective-permute-start.6 = (bf16[96,2048]{1,0:T(8,128)(2,1)S(1)}, bf16[96,2048]{1,0:T(8,128)(2,1)}, u32[]{:S(2)}, u32[]{:S(2)}) collective-permute-start(bf16[96,2048]{1,0:T(8,128)(2,1)S(1)} %bitcast.323), channel_id=1, source_target_pairs={{0,2},{2,4},{4,6},{6,0},{1,3},{3,5},{5,7},{7,1},{8,10},{10,12},{12... | collective-permute-start | bytes 1179656 | tf_op jit(solution)/shard_map/ppermute | solution.py:93
  169.8 249.5 %all-gather.20.cloned.1.call-start = ((), (), s32[]{:S(2)}) async-start(), calls=%async_computation.19 | async-start | bytes 3932160 | tf_op jit(solution)/shard_map/all_gather | solution.py:694
  177.8 14.6 %collective-permute-start.10 = (bf16[128,1664]{1,0:T(8,128)(2,1)S(1)}, bf16[128,1664]{1,0:T(8,128)(2,1)S(1)}, u32[]{:S(2)}, u32[]{:S(2)}) collective-permute-start(bf16[128,1664]{1,0:T(8,128)(2,1)S(1)} %get-tuple-element.492), channel_id=1, source_target_pairs={{0,2},{2,4},{4,6},{6,0},{1,3},{3,5},{5,7},{7,1},{8,10},{10,12},{12... | collective-permute-start | bytes 1277960 | tf_op jit(solution)/shard_map/ppermute | solution.py:93
  179.4 21.2 %collective-permute-start.8 = (bf16[128,1664]{1,0:T(8,128)(2,1)S(1)}, bf16[128,1664]{1,0:T(8,128)(2,1)S(1)}, u32[]{:S(2)}, u32[]{:S(2)}) collective-permute-start(bf16[128,1664]{1,0:T(8,128)(2,1)S(1)} %get-tuple-element.491), channel_id=1, source_target_pairs={{0,6},{2,0},{4,2},{6,4},{1,7},{3,1},{5,3},{7,5},{8,14},{10,8},{12,... | collective-permute-start | bytes 1277960 | tf_op jit(solution)/shard_map/ppermute | solution.py:93
  181.6 37.2 %collective-permute-start.9 = (bf16[128,1664]{1,0:T(8,128)(2,1)S(1)}, bf16[128,1664]{1,0:T(8,128)(2,1)S(1)}, u32[]{:S(2)}, u32[]{:S(2)}) collective-permute-start(bf16[128,1664]{1,0:T(8,128)(2,1)S(1)} %get-tuple-element.493), channel_id=1, source_target_pairs={{0,4},{2,6},{4,0},{6,2},{1,5},{3,7},{5,1},{7,3},{8,12},{10,14},{12... | collective-permute-start | bytes 1277960 | tf_op jit(solution)/shard_map/ppermute | solution.py:93
  220.5 14.0 %collective-permute-start.14 = (bf16[128,1536]{1,0:T(8,128)(2,1)S(1)}, bf16[128,1536]{1,0:T(8,128)(2,1)S(1)}, u32[]{:S(2)}, u32[]{:S(2)}) collective-permute-start(bf16[128,1536]{1,0:T(8,128)(2,1)S(1)} %multiply_convert_fusion.11), channel_id=1, source_target_pairs={{0,2},{2,4},{4,6},{6,0},{1,3},{3,5},{5,7},{7,1},{8,10},{10,12},{12... | collective-permute-start | bytes 1179656 | tf_op jit(solution)/shard_map/ppermute | solution.py:93
  220.5 29.8 %collective-permute-start.15 = (bf16[128,1536]{1,0:T(8,128)(2,1)S(1)}, bf16[128,1536]{1,0:T(8,128)(2,1)S(1)}, u32[]{:S(2)}, u32[]{:S(2)}) collective-permute-start(bf16[128,1536]{1,0:T(8,128)(2,1)S(1)} %multiply_convert_fusion.11), channel_id=1, source_target_pairs={{0,4},{2,6},{4,0},{6,2},{1,5},{3,7},{5,1},{7,3},{8,12},{10,14},{12... | collective-permute-start | bytes 1179656 | tf_op jit(solution)/shard_map/ppermute | solution.py:93
  223.8 26.6 %collective-permute-start.16 = (bf16[128,1536]{1,0:T(8,128)(2,1)S(1)}, bf16[128,1536]{1,0:T(8,128)(2,1)S(1)}, u32[]{:S(2)}, u32[]{:S(2)}) collective-permute-start(bf16[128,1536]{1,0:T(8,128)(2,1)S(1)} %multiply_convert_fusion.11), channel_id=1, source_target_pairs={{0,6},{2,0},{4,2},{6,4},{1,7},{3,1},{5,3},{7,5},{8,14},{10,8},{12,... | collective-permute-start | bytes 1179656 | tf_op jit(solution)/shard_map/ppermute | solution.py:93
  251.7 14.7 %collective-permute-start.17 = (bf16[512,1536]{1,0:T(8,128)(2,1)}, bf16[512,1536]{1,0:T(8,128)(2,1)}, u32[]{:S(2)}, u32[]{:S(2)}) collective-permute-start(bf16[512,1536]{1,0:T(8,128)(2,1)} %pad_maximum_fusion.11), channel_id=1, source_target_pairs={{0,1},{1,0},{2,3},{3,2},{4,5},{5,4},{6,7},{7,6},{8,9},{9,8},{10,11... | collective-permute-start | bytes 4718600 | tf_op jit(solution)/shard_map/ppermute | solution.py:93
  251.7 28.7 %collective-permute-start.13 = (bf16[128,1536]{1,0:T(8,128)(2,1)S(1)}, bf16[128,1536]{1,0:T(8,128)(2,1)S(1)}, u32[]{:S(2)}, u32[]{:S(2)}) collective-permute-start(bf16[128,1536]{1,0:T(8,128)(2,1)S(1)} %bitcast.316), channel_id=1, source_target_pairs={{0,2},{2,4},{4,6},{6,0},{1,3},{3,5},{5,7},{7,1},{8,10},{10,12},{12... | collective-permute-start | bytes 1179656 | tf_op jit(solution)/shard_map/ppermute | solution.py:93
  259.8 43.5 %collective-permute-start.11 = (bf16[128,1536]{1,0:T(8,128)(2,1)S(1)}, bf16[128,1536]{1,0:T(8,128)(2,1)S(1)}, u32[]{:S(2)}, u32[]{:S(2)}) collective-permute-start(bf16[128,1536]{1,0:T(8,128)(2,1)S(1)} %bitcast.317), channel_id=1, source_target_pairs={{0,4},{2,6},{4,0},{6,2},{1,5},{3,7},{5,1},{7,3},{8,12},{10,14},{12... | collective-permute-start | bytes 1179656 | tf_op jit(solution)/shard_map/ppermute | solution.py:93
  259.8 43.5 %collective-permute-start.12 = (bf16[128,1536]{1,0:T(8,128)(2,1)S(1)}, bf16[128,1536]{1,0:T(8,128)(2,1)S(1)}, u32[]{:S(2)}, u32[]{:S(2)}) collective-permute-start(bf16[128,1536]{1,0:T(8,128)(2,1)S(1)} %bitcast.318), channel_id=1, source_target_pairs={{0,6},{2,0},{4,2},{6,4},{1,7},{3,1},{5,3},{7,5},{8,14},{10,8},{12,... | collective-permute-start | bytes 1179656 | tf_op jit(solution)/shard_map/ppermute | solution.py:93
  262.2 195.6 %all-gather.18.cloned.1.call-start = ((), (), s32[]{:S(2)}) async-start(), calls=%async_computation.18 | async-start | bytes 7864320 | tf_op jit(solution)/shard_map/all_gather | solution.py:693
  313.8 13.8 %collective-permute-start.18 = (bf16[512,1536]{1,0:T(8,128)(2,1)}, bf16[512,1536]{1,0:T(8,128)(2,1)}, u32[]{:S(2)}, u32[]{:S(2)}) collective-permute-start(bf16[512,1536]{1,0:T(8,128)(2,1)} %slice.1155), channel_id=1, source_target_pairs={{0,1},{1,0},{2,3},{3,2},{4,5},{5,4},{6,7},{7,6},{8,9},{9,8},{10,11... | collective-permute-start | bytes 4718600 | tf_op jit(solution)/shard_map/ppermute | solution.py:93
  315.8 425.9 %reduce-scatter.10.cloned.1.call-start = ((), (), s32[]{:S(2)}) async-start(), calls=%async_computation.21 | async-start | bytes 3932160 | tf_op jit(solution)/shard_map/reduce_scatter | solution.py:815
  333.2 33.7 %collective-permute-start.20 = (bf16[128,1536]{1,0:T(8,128)(2,1)S(1)}, bf16[128,1536]{1,0:T(8,128)(2,1)S(1)}, u32[]{:S(2)}, u32[]{:S(2)}) collective-permute-start(bf16[128,1536]{1,0:T(8,128)(2,1)S(1)} %get-tuple-element.522), channel_id=1, source_target_pairs={{0,4},{2,6},{4,0},{6,2},{1,5},{3,7},{5,1},{7,3},{8,12},{10,14},{12... | collective-permute-start | bytes 1179656 | tf_op jit(solution)/shard_map/ppermute | solution.py:93
  333.2 33.7 %collective-permute-start.21 = (bf16[128,1536]{1,0:T(8,128)(2,1)S(1)}, bf16[128,1536]{1,0:T(8,128)(2,1)S(1)}, u32[]{:S(2)}, u32[]{:S(2)}) collective-permute-start(bf16[128,1536]{1,0:T(8,128)(2,1)S(1)} %get-tuple-element.521), channel_id=1, source_target_pairs={{0,2},{2,4},{4,6},{6,0},{1,3},{3,5},{5,7},{7,1},{8,10},{10,12},{12... | collective-permute-start | bytes 1179656 | tf_op jit(solution)/shard_map/ppermute | solution.py:93
  387.6 13.9 %collective-permute-start.24 = (bf16[128,1536]{1,0:T(8,128)(2,1)S(1)}, bf16[128,1536]{1,0:T(8,128)(2,1)S(1)}, u32[]{:S(2)}, u32[]{:S(2)}) collective-permute-start(bf16[128,1536]{1,0:T(8,128)(2,1)S(1)} %multiply_convert_fusion.9), channel_id=1, source_target_pairs={{0,2},{2,4},{4,6},{6,0},{1,3},{3,5},{5,7},{7,1},{8,10},{10,12},{12... | collective-permute-start | bytes 1179656 | tf_op jit(solution)/shard_map/ppermute | solution.py:93
  388.4 29.4 %collective-permute-start.25 = (bf16[128,1536]{1,0:T(8,128)(2,1)S(1)}, bf16[128,1536]{1,0:T(8,128)(2,1)S(1)}, u32[]{:S(2)}, u32[]{:S(2)}) collective-permute-start(bf16[128,1536]{1,0:T(8,128)(2,1)S(1)} %multiply_convert_fusion.9), channel_id=1, source_target_pairs={{0,4},{2,6},{4,0},{6,2},{1,5},{3,7},{5,1},{7,3},{8,12},{10,14},{12... | collective-permute-start | bytes 1179656 | tf_op jit(solution)/shard_map/ppermute | solution.py:93
  390.4 27.4 %collective-permute-start.26 = (bf16[128,1536]{1,0:T(8,128)(2,1)S(1)}, bf16[128,1536]{1,0:T(8,128)(2,1)S(1)}, u32[]{:S(2)}, u32[]{:S(2)}) collective-permute-start(bf16[128,1536]{1,0:T(8,128)(2,1)S(1)} %multiply_convert_fusion.9), channel_id=1, source_target_pairs={{0,6},{2,0},{4,2},{6,4},{1,7},{3,1},{5,3},{7,5},{8,14},{10,8},{12,... | collective-permute-start | bytes 1179656 | tf_op jit(solution)/shard_map/ppermute | solution.py:93
  394.5 63.4 %collective-permute-start.28 = (bf16[512,1536]{1,0:T(8,128)(2,1)}, bf16[512,1536]{1,0:T(8,128)(2,1)}, u32[]{:S(2)}, u32[]{:S(2)}) collective-permute-start(bf16[512,1536]{1,0:T(8,128)(2,1)} %pad_maximum_fusion.15), channel_id=1, source_target_pairs={{0,1},{1,0},{2,3},{3,2},{4,5},{5,4},{6,7},{7,6},{8,9},{9,8},{10,11... | collective-permute-start | bytes 4718600 | tf_op jit(solution)/shard_map/ppermute | solution.py:93
  419.2 40.4 %collective-permute-start.27 = (bf16[512,1536]{1,0:T(8,128)(2,1)}, bf16[512,1536]{1,0:T(8,128)(2,1)}, u32[]{:S(2)}, u32[]{:S(2)}) collective-permute-start(bf16[512,1536]{1,0:T(8,128)(2,1)} %pad_maximum_fusion.13), channel_id=1, source_target_pairs={{0,1},{1,0},{2,3},{3,2},{4,5},{5,4},{6,7},{7,6},{8,9},{9,8},{10,11... | collective-permute-start | bytes 4718600 | tf_op jit(solution)/shard_map/ppermute | solution.py:93
  531.2 13.6 %collective-permute-start.30 = (bf16[128,1664]{1,0:T(8,128)(2,1)S(1)}, bf16[128,1664]{1,0:T(8,128)(2,1)S(1)}, u32[]{:S(2)}, u32[]{:S(2)}) collective-permute-start(bf16[128,1664]{1,0:T(8,128)(2,1)S(1)} %get-tuple-element.490), channel_id=1, source_target_pairs={{0,6},{2,0},{4,2},{6,4},{1,7},{3,1},{5,3},{7,5},{8,14},{10,8},{12,... | collective-permute-start | bytes 1277960 | tf_op jit(solution)/shard_map/ppermute | solution.py:93
  534.6 36.5 %collective-permute-start.31 = (bf16[128,1664]{1,0:T(8,128)(2,1)S(1)}, bf16[128,1664]{1,0:T(8,128)(2,1)S(1)}, u32[]{:S(2)}, u32[]{:S(2)}) collective-permute-start(bf16[128,1664]{1,0:T(8,128)(2,1)S(1)} %get-tuple-element.489), channel_id=1, source_target_pairs={{0,4},{2,6},{4,0},{6,2},{1,5},{3,7},{5,1},{7,3},{8,12},{10,14},{12... | collective-permute-start | bytes 1277960 | tf_op jit(solution)/shard_map/ppermute | solution.py:93
  534.6 36.5 %collective-permute-start.32 = (bf16[128,1664]{1,0:T(8,128)(2,1)S(1)}, bf16[128,1664]{1,0:T(8,128)(2,1)S(1)}, u32[]{:S(2)}, u32[]{:S(2)}) collective-permute-start(bf16[128,1664]{1,0:T(8,128)(2,1)S(1)} %get-tuple-element.488), channel_id=1, source_target_pairs={{0,2},{2,4},{4,6},{6,0},{1,3},{3,5},{5,7},{7,1},{8,10},{10,12},{12... | collective-permute-start | bytes 1277960 | tf_op jit(solution)/shard_map/ppermute | solution.py:93
  572.7 169.0 %reduce-scatter.8.cloned.1.call-start = ((), (), s32[]{:S(2)}) async-start(), calls=%async_computation.20 | async-start | bytes 7864320 | tf_op jit(solution)/shard_map/reduce_scatter | solution.py:811
  573.4 227.3 %reduce-scatter.14.cloned.1.call-start = ((), (), s32[]{:S(2)}) async-start(), calls=%async_computation.23 | async-start | bytes 7864320 | tf_op jit(solution)/shard_map/reduce_scatter | solution.py:887
  617.4 13.9 %collective-permute-start.39 = (bf16[128,1536]{1,0:T(8,128)(2,1)S(1)}, bf16[128,1536]{1,0:T(8,128)(2,1)S(1)}, u32[]{:S(2)}, u32[]{:S(2)}) collective-permute-start(bf16[128,1536]{1,0:T(8,128)(2,1)S(1)} %get-tuple-element.450), channel_id=1, source_target_pairs={{0,2},{2,4},{4,6},{6,0},{1,3},{3,5},{5,7},{7,1},{8,10},{10,12},{12... | collective-permute-start | bytes 1179656 | tf_op jit(solution)/shard_map/ppermute | solution.py:93
  618.0 29.4 %collective-permute-start.40 = (bf16[128,1536]{1,0:T(8,128)(2,1)S(1)}, bf16[128,1536]{1,0:T(8,128)(2,1)S(1)}, u32[]{:S(2)}, u32[]{:S(2)}) collective-permute-start(bf16[128,1536]{1,0:T(8,128)(2,1)S(1)} %get-tuple-element.450), channel_id=1, source_target_pairs={{0,4},{2,6},{4,0},{6,2},{1,5},{3,7},{5,1},{7,3},{8,12},{10,14},{12... | collective-permute-start | bytes 1179656 | tf_op jit(solution)/shard_map/ppermute | solution.py:93
  619.6 27.7 %collective-permute-start.41 = (bf16[128,1536]{1,0:T(8,128)(2,1)S(1)}, bf16[128,1536]{1,0:T(8,128)(2,1)S(1)}, u32[]{:S(2)}, u32[]{:S(2)}) collective-permute-start(bf16[128,1536]{1,0:T(8,128)(2,1)S(1)} %get-tuple-element.450), channel_id=1, source_target_pairs={{0,6},{2,0},{4,2},{6,4},{1,7},{3,1},{5,3},{7,5},{8,14},{10,8},{12,... | collective-permute-start | bytes 1179656 | tf_op jit(solution)/shard_map/ppermute | solution.py:93
  648.6 328.8 %reduce-scatter.20.cloned.1.call-start = ((), (), s32[]{:S(2)}) async-start(), calls=%async_computation.26 | async-start | bytes 3932160 | tf_op jit(solution)/shard_map/reduce_scatter | solution.py:815
  691.9 26.7 %collective-permute-start.44 = (bf16[128,1664]{1,0:T(8,128)(2,1)S(1)}, bf16[128,1664]{1,0:T(8,128)(2,1)}, u32[]{:S(2)}, u32[]{:S(2)}) collective-permute-start(bf16[128,1664]{1,0:T(8,128)(2,1)S(1)} %get-tuple-element.487), channel_id=1, source_target_pairs={{0,6},{2,0},{4,2},{6,4},{1,7},{3,1},{5,3},{7,5},{8,14},{10,8},{12,... | collective-permute-start | bytes 1277960 | tf_op jit(solution)/shard_map/ppermute | solution.py:93
  701.5 37.4 %collective-permute-start.45 = (bf16[128,1664]{1,0:T(8,128)(2,1)S(1)}, bf16[128,1664]{1,0:T(8,128)(2,1)}, u32[]{:S(2)}, u32[]{:S(2)}) collective-permute-start(bf16[128,1664]{1,0:T(8,128)(2,1)S(1)} %get-tuple-element.486), channel_id=1, source_target_pairs={{0,4},{2,6},{4,0},{6,2},{1,5},{3,7},{5,1},{7,3},{8,12},{10,14},{12... | collective-permute-start | bytes 1277960 | tf_op jit(solution)/shard_map/ppermute | solution.py:93
  701.6 37.4 %collective-permute-start.46 = (bf16[128,1664]{1,0:T(8,128)(2,1)S(1)}, bf16[128,1664]{1,0:T(8,128)(2,1)}, u32[]{:S(2)}, u32[]{:S(2)}) collective-permute-start(bf16[128,1664]{1,0:T(8,128)(2,1)S(1)} %get-tuple-element.485), channel_id=1, source_target_pairs={{0,2},{2,4},{4,6},{6,0},{1,3},{3,5},{5,7},{7,1},{8,10},{10,12},{12... | collective-permute-start | bytes 1277960 | tf_op jit(solution)/shard_map/ppermute | solution.py:93
  739.0 248.4 %reduce-scatter.12.cloned.1.call-start = ((), (), s32[]{:S(2)}) async-start(), calls=%async_computation.22 | async-start | bytes 4423680 | tf_op jit(solution)/shard_map/reduce_scatter | solution.py:968
  747.4 14.7 %collective-permute-start.47 = (bf16[128,1664]{1,0:T(8,128)(2,1)S(1)}, bf16[128,1664]{1,0:T(8,128)(2,1)S(1)}, u32[]{:S(2)}, u32[]{:S(2)}) collective-permute-start(bf16[128,1664]{1,0:T(8,128)(2,1)S(1)} %concatenate.234), channel_id=1, source_target_pairs={{0,2},{2,4},{4,6},{6,0},{1,3},{3,5},{5,7},{7,1},{8,10},{10,12},{12... | collective-permute-start | bytes 1277960 | tf_op jit(solution)/shard_map/ppermute | solution.py:93
  747.8 31.1 %collective-permute-start.48 = (bf16[128,1664]{1,0:T(8,128)(2,1)S(1)}, bf16[128,1664]{1,0:T(8,128)(2,1)S(1)}, u32[]{:S(2)}, u32[]{:S(2)}) collective-permute-start(bf16[128,1664]{1,0:T(8,128)(2,1)S(1)} %concatenate.234), channel_id=1, source_target_pairs={{0,4},{2,6},{4,0},{6,2},{1,5},{3,7},{5,1},{7,3},{8,12},{10,14},{12... | collective-permute-start | bytes 1277960 | tf_op jit(solution)/shard_map/ppermute | solution.py:93
  749.5 29.4 %collective-permute-start.49 = (bf16[128,1664]{1,0:T(8,128)(2,1)S(1)}, bf16[128,1664]{1,0:T(8,128)(2,1)S(1)}, u32[]{:S(2)}, u32[]{:S(2)}) collective-permute-start(bf16[128,1664]{1,0:T(8,128)(2,1)S(1)} %concatenate.234), channel_id=1, source_target_pairs={{0,6},{2,0},{4,2},{6,4},{1,7},{3,1},{5,3},{7,5},{8,14},{10,8},{12,... | collective-permute-start | bytes 1277960 | tf_op jit(solution)/shard_map/ppermute | solution.py:93
  797.0 198.5 %reduce-scatter.18.cloned.1.call-start = ((), (), s32[]{:S(2)}) async-start(), calls=%async_computation.25 | async-start | bytes 7864320 | tf_op jit(solution)/shard_map/reduce_scatter | solution.py:811
  797.7 218.0 %reduce-scatter.16.cloned.1.call-start = ((), (), s32[]{:S(2)}) async-start(), calls=%async_computation.24 | async-start | bytes 4423680 | tf_op jit(solution)/shard_map/reduce_scatter | solution.py:968
  836.3 25.7 %collective-permute-start.51 = (bf16[512,1536]{1,0:T(8,128)(2,1)}, bf16[512,1536]{1,0:T(8,128)(2,1)}, u32[]{:S(2)}, u32[]{:S(2)}) collective-permute-start(bf16[512,1536]{1,0:T(8,128)(2,1)} %slice.1153), channel_id=1, source_target_pairs={{0,1},{1,0},{2,3},{3,2},{4,5},{5,4},{6,7},{7,6},{8,9},{9,8},{10,11... | collective-permute-start | bytes 4718600 | tf_op jit(solution)/shard_map/ppermute | solution.py:93
  848.1 20.3 %collective-permute-start.55 = (bf16[96,2048]{1,0:T(8,128)(2,1)}, bf16[96,2048]{1,0:T(8,128)(2,1)}, u32[]{:S(2)}, u32[]{:S(2)}) collective-permute-start(bf16[96,2048]{1,0:T(8,128)(2,1)} %get-tuple-element.500), channel_id=1, source_target_pairs={{0,2},{2,4},{4,6},{6,0},{1,3},{3,5},{5,7},{7,1},{8,10},{10,12},{12... | collective-permute-start | bytes 1179656 | tf_op jit(solution)/shard_map/ppermute | solution.py:93
  856.3 28.2 %collective-permute-start.56 = (bf16[96,2048]{1,0:T(8,128)(2,1)}, bf16[96,2048]{1,0:T(8,128)(2,1)}, u32[]{:S(2)}, u32[]{:S(2)}) collective-permute-start(bf16[96,2048]{1,0:T(8,128)(2,1)} %get-tuple-element.499), channel_id=1, source_target_pairs={{0,4},{2,6},{4,0},{6,2},{1,5},{3,7},{5,1},{7,3},{8,12},{10,14},{12... | collective-permute-start | bytes 1179656 | tf_op jit(solution)/shard_map/ppermute | solution.py:93
  858.1 26.3 %collective-permute-start.57 = (bf16[96,2048]{1,0:T(8,128)(2,1)}, bf16[96,2048]{1,0:T(8,128)(2,1)}, u32[]{:S(2)}, u32[]{:S(2)}) collective-permute-start(bf16[96,2048]{1,0:T(8,128)(2,1)} %get-tuple-element.498), channel_id=1, source_target_pairs={{0,6},{2,0},{4,2},{6,4},{1,7},{3,1},{5,3},{7,5},{8,14},{10,8},{12,... | collective-permute-start | bytes 1179656 | tf_op jit(solution)/shard_map/ppermute | solution.py:93
  865.4 27.2 %collective-permute-start.52 = (bf16[128,1536]{1,0:T(8,128)(2,1)S(1)}, bf16[128,1536]{1,0:T(8,128)(2,1)S(1)}, u32[]{:S(2)}, u32[]{:S(2)}) collective-permute-start(bf16[128,1536]{1,0:T(8,128)(2,1)S(1)} %get-tuple-element.504), channel_id=1, source_target_pairs={{0,6},{2,0},{4,2},{6,4},{1,7},{3,1},{5,3},{7,5},{8,14},{10,8},{12,... | collective-permute-start | bytes 1179656 | tf_op jit(solution)/shard_map/ppermute | solution.py:93
  867.5 58.9 %collective-permute-start.53 = (bf16[128,1536]{1,0:T(8,128)(2,1)S(1)}, bf16[128,1536]{1,0:T(8,128)(2,1)S(1)}, u32[]{:S(2)}, u32[]{:S(2)}) collective-permute-start(bf16[128,1536]{1,0:T(8,128)(2,1)S(1)} %get-tuple-element.503), channel_id=1, source_target_pairs={{0,4},{2,6},{4,0},{6,2},{1,5},{3,7},{5,1},{7,3},{8,12},{10,14},{12... | collective-permute-start | bytes 1179656 | tf_op jit(solution)/shard_map/ppermute | solution.py:93
  868.4 58.0 %collective-permute-start.54 = (bf16[128,1536]{1,0:T(8,128)(2,1)S(1)}, bf16[128,1536]{1,0:T(8,128)(2,1)S(1)}, u32[]{:S(2)}, u32[]{:S(2)}) collective-permute-start(bf16[128,1536]{1,0:T(8,128)(2,1)S(1)} %get-tuple-element.502), channel_id=1, source_target_pairs={{0,2},{2,4},{4,6},{6,0},{1,3},{3,5},{5,7},{7,1},{8,10},{10,12},{12... | collective-permute-start | bytes 1179656 | tf_op jit(solution)/shard_map/ppermute | solution.py:93
  940.7 12.6 %collective-permute-start.34 = (bf16[128,1536]{1,0:T(8,128)(2,1)}, bf16[128,1536]{1,0:T(8,128)(2,1)S(1)}, u32[]{:S(2)}, u32[]{:S(2)}) collective-permute-start(bf16[128,1536]{1,0:T(8,128)(2,1)} %get-tuple-element.511), channel_id=1, source_target_pairs={{0,6},{2,0},{4,2},{6,4},{1,7},{3,1},{5,3},{7,5},{8,14},{10,8},{12,... | collective-permute-start | bytes 1179656 | tf_op jit(solution)/shard_map/ppermute | solution.py:93
  940.7 34.5 %collective-permute-start.35 = (bf16[128,1536]{1,0:T(8,128)(2,1)S(1)}, bf16[128,1536]{1,0:T(8,128)(2,1)S(1)}, u32[]{:S(2)}, u32[]{:S(2)}) collective-permute-start(bf16[128,1536]{1,0:T(8,128)(2,1)S(1)} %get-tuple-element.513), channel_id=1, source_target_pairs={{0,4},{2,6},{4,0},{6,2},{1,5},{3,7},{5,1},{7,3},{8,12},{10,14},{12... | collective-permute-start | bytes 1179656 | tf_op jit(solution)/shard_map/ppermute | solution.py:93
  940.7 34.5 %collective-permute-start.36 = (bf16[128,1536]{1,0:T(8,128)(2,1)S(1)}, bf16[128,1536]{1,0:T(8,128)(2,1)}, u32[]{:S(2)}, u32[]{:S(2)}) collective-permute-start(bf16[128,1536]{1,0:T(8,128)(2,1)S(1)} %get-tuple-element.512), channel_id=1, source_target_pairs={{0,2},{2,4},{4,6},{6,0},{1,3},{3,5},{5,7},{7,1},{8,10},{10,12},{12... | collective-permute-start | bytes 1179656 | tf_op jit(solution)/shard_map/ppermute | solution.py:93
  987.4 28.2 %all-to-all-start.3 = ((bf16[8,48,1152]{2,1,0:T(8,128)(2,1)}), bf16[8,48,1152]{2,1,0:T(8,128)(2,1)S(1)}, u32[]{:S(2)}, u32[]{:S(2)}) async-start(bf16[8,48,1152]{2,1,0:T(8,128)(2,1)} %bitcast.339), calls=%async_computation.8 | async-start | bytes 1769472 | tf_op jit(solution)/shard_map/all_to_all | solution.py:971
  1015.8 26.6 %all-to-all-start.4 = ((bf16[8,48,1152]{2,1,0:T(8,128)(2,1)}), bf16[8,48,1152]{2,1,0:T(8,128)(2,1)S(1)}, u32[]{:S(2)}, u32[]{:S(2)}) async-start(bf16[8,48,1152]{2,1,0:T(8,128)(2,1)} %bitcast.340), calls=%async_computation.9 | async-start | bytes 1769472 | tf_op jit(solution)/shard_map/all_to_all | solution.py:971
  (185 other events, 2623.4 us)
Sparse Core Ops, SparseCore 0:
  53.4 55.9 all-gather.7
  111.8 70.2 all-gather.9
  183.9 37.4 all-gather.11
  223.1 43.9 all-gather.13
  269.4 70.1 all-gather.15
  341.2 43.9 all-gather.19
  387.7 70.1 all-gather.17
  572.8 42.5 reduce-scatter.9
  618.4 70.1 reduce-scatter.7
  691.4 70.2 reduce-scatter.13
  764.7 43.9 reduce-scatter.19
  811.6 47.1 reduce-scatter.11
  861.8 70.2 reduce-scatter.17
  935.0 47.2 reduce-scatter.15

commit v8 on v7

--- a/solution.py
+++ b/solution.py
@@ -430,7 +430,7 @@
     return (total, kept) if riders is None else (total, kept, riders)
 
 
-def moe_backward(base_z, kept, w, experts_total):
+def moe_backward(base_z, kept, w, experts_total, riders=None):
     moe_in, base_in, own_gates, local, pre, pre_s = kept
     pre, pre_s, _ = lax.optimization_barrier((pre, pre_s, base_z))
     grad_z = wide(base_z)
@@ -441,6 +441,8 @@
     p = pre.astype(f32)
     gate, up = p[:, :units], p[:, units:]
     grad_hid = nt(grad_z, w["expert_down"])
+    if riders is not None:
+        riders[:1], grad_hid = fence(riders[:1], grad_hid)
     act = swiglu(gate, up)
     hidden = (act * spread).astype(bf16)
     product = grad_hid * act
@@ -452,6 +454,8 @@
     g_gate, g_up = swiglu_back(grad_hid * spread, gate, up)
     g_pre = jnp.concatenate([g_gate, g_up], axis=1)
     total = nt(g_pre, w["expert_in"])
+    if riders is not None:
+        riders[1:], total = fence(riders[1:], total)
     half = pre_s.shape[1] // 2
     p = pre_s.astype(f32)
     grad_hid = nn(base_z, w["shared_down_t"])
@@ -653,6 +657,11 @@
         info = lanes(hot + [segments[m][:, None].astype(bf16)], info_width)
         x_info, moved_m = fence(jnp.concatenate([tokens[m], info], axis=1), moved_m)
         rows_in.append(gather_rows(x_info))
+    def low_weights(w_low):
+        return lax.all_gather(w_low, "dp", axis=1, tiled=True).reshape(-1, D)
+
+    low_m = low_weights(expert_down_m)
+    moved_m, low_m = fence(moved_m, low_m)
     w_m = whole_rows(moved_m)
     in_width = 2 * chan + 2 * STATE
     w_in_here = w_m[:, :in_width]
@@ -685,16 +694,13 @@
     w_scan = w_m[:, : in_width + 128]
     w_mix_t = w_m[:, at:]
 
-    def expert_weights(w_up, w_low):
+    def up_weights(w_up):
         count = w_up.shape[0]
         cols = [w_up[e, :, :EXP_FF] for e in range(count)] + [w_up[e, :, EXP_FF:] for e in range(count)]
         cols = by_rows(jnp.concatenate(cols, axis=1))
-        return (
-            by_rows(lax.all_gather(cols, "dp", axis=0, tiled=True)),
-            lax.all_gather(w_low, "dp", axis=1, tiled=True).reshape(-1, D),
-        )
-
-    up_m, low_m = expert_weights(expert_in_m, expert_down_m)
+        return by_rows(lax.all_gather(cols, "dp", axis=0, tiled=True))
+
+    up_m = up_weights(expert_in_m)
     kv = KVH // 2
     q_width = QH // 2 * HEAD
     kv_width = kv * HEAD
@@ -775,7 +781,7 @@
         "expert_down": low_m,
     }
 
-    up_a, low_a = fence(*expert_weights(expert_in, expert_down))
+    up_a, low_a = fence(up_weights(expert_in), low_weights(expert_down))
     moe_a = {
         "router": router_full,
         "shared_in": w_s[:, 3 * ff : 5 * ff],
@@ -825,11 +831,12 @@
 
     saving = lax.axis_size("w") > 1
 
-    def moe_stage(grads, kept_all, w, gain, *before):
+    def moe_stage(grads, kept_all, w, gain, *before, riders=None):
         grads = list(grads)
         backs, first_rows = [], []
         for m in each:
-            total, side = moe_backward(grads[m], kept_all[m][2], w, experts_total)
+            rider = None if riders is None else riders[m][1]
+            total, side = moe_backward(grads[m], kept_all[m][2], w, experts_total, rider)
             own, sent = return_start(narrow(total))
             first_rows.append(side[6][:own_rows])
             if saving:
@@ -839,8 +846,12 @@
                 weights = newer if m == 0 else [a + b for a, b in zip(weights, newer)]
             else:
                 hidden, g_pre, own = fence(side[2], side[4], own)
-                weights = moe_weight_grads([(*side[:2], hidden, side[3], g_pre, *side[5:])])
-                sent, weights = fence(sent, weights)
+                g_low = tn_sum([(hidden, side[1])])
+                g_up = tn_sum([(side[0], g_pre)])
+                g_pre_s, g_low, g_up = fence(side[5], g_low, g_up)
+                g_sin = tn_sum([(side[6], g_pre_s)])
+                sent, g_sin = fence(sent, g_sin)
+                weights = (g_up, g_low, g_sin, tn_sum([(side[7], side[3])]))
                 back = return_finish(own, sent)
             backs.append(back)
         backs[-1], before = fence(backs[-1], before)
@@ -864,7 +875,7 @@
     grad_two = [cotangent[m].astype(f32) + values[m] for m in each]
     for m in each:
         total, grad_two[m] = fence(results[m], grad_two[m])
-        results[m] = (hidden_two[m] + return_rows(narrow(total))).astype(bf16)
+        results[m] = return_start(narrow(total))
 
     grad_layer, sides = [], []
     attn_back = []
@@ -899,8 +910,11 @@
         gain_moe_m,
         sum_in_a,
         sum_down_a,
+        riders=results,
     )
     sum_in_a, sum_down_a = before
+    for m in each:
+        results[m] = (hidden_two[m] + return_finish(*results[m])).astype(bf16)
     out_expert_in, out_expert_down = expert_out(sum_in_a, sum_down_a)
     sum_in_m = up_over_dp(g_in_m)
     sum_down_m = low_over_dp(g_down_m)
@@ -957,7 +971,14 @@
             heads, length, *scan_args, grad_gated, extra_all
         )
         small = grads if small is None else [a + b for a, b in zip(small, grads)]
+        own_part, sent_part = attn_sent if m == micro - 1 else (None, [])
+        if m == micro - 1:
+            sent_part[:2], grad_scan = fence(sent_part[:2], grad_scan)
         total = nt(grad_scan, w_scan)
+        if m == micro - 1:
+            sent_part[2:], total = fence(sent_part[2:], total)
+            total, sum_in_m = fence(total, sum_in_m)
+            attn_sent = (own_part, sent_part)
         gains[0] = gains[0] + jnp.sum(total * normed_x, axis=0)
         own, sent = return_start(total)
         grad_scan, own = fence(grad_scan, own)
@@ -980,7 +1001,7 @@
     )
 
     g_scan = by_rows(tn_sum(mamba_sides, f32))
-    mamba_back, g_scan, attn_sent = fence(mamba_back, g_scan, attn_sent)
+    mamba_back, g_scan = fence(mamba_back, g_scan)
     mamba_back = [return_finish(*pair) for pair in mamba_back]
     g_attn = attn_total(*attn_sent)
     g_s, mamba_back[-1] = fence(g_s, mamba_back[-1])

time: 1070 us -> 1020 us (0.953)
  waiting for transfers between devices: 463 us -> 419 us
  other arithmetic: 121 us -> 144 us
  matrix products: 194 us -> 180 us
    ppermute x63, waiting for transfers between devices: 365 us -> 326 us  [send(): return by_rows(lax.ppermute(by_rows(x), axis, pairs))]
    dot_general x44, matrix products: 186 us -> 172 us  [dot(): r = lax.dot_general(a, b, (dims, ((), ())), preferred_element_type=f32)]
    reduce_scatter x2, starting transfers between devices: 11.8 us -> 0.08 us  [low_over_dp(): return lax.psum_scatter(g, 'dp', scatter_dimension=1, tiled=True)]
    unnamed x370 -> x429, local copies, waits for them, and re-layouts: 34.3 us -> 25 us
  transfers between devices with their start and end apart: 81 -> 81, of which waited for: 37 -> 40; matrix products, arithmetic and copies ran while one was open for 29% -> 32% of each run, Pallas kernels for 3% -> 3%
where the time goes in v8:
time: 1020 us; the launch traced here: 1010 us
  waiting for transfers between devices  419 us (41%)
  matrix products  180 us (18%)
  other arithmetic  144 us (14%)
  starting transfers between devices  126 us (12%)
  local copies, waits for them, and re-layouts  88.3 us (9%)
  Pallas kernels  27.9 us (3%)
  between operations  17.8 us (2%)
    ppermute x63, waiting for transfers between devices, send(): return by_rows(lax.ppermute(by_rows(x), axis, pairs))  326 us
    dot_general x44, matrix products, dot(): r = lax.dot_general(a, b, (dims, ((), ())), preferred_element_type=f32)  172 us
    ppermute x63, starting transfers between devices, send(): return by_rows(lax.ppermute(by_rows(x), axis, pairs))  98 us
    all_to_all x2, waiting for transfers between devices, moved_columns(): moved = lax.all_to_all(packed, TP, split_axis=0, concat_axis=0, tiled=True)  38.5 us
    unnamed x429, local copies, waits for them, and re-layouts  25 us
    all_gather x2, waiting for transfers between devices, up_weights(): return by_rows(lax.all_gather(cols, 'dp', axis=0, tiled=True))  22.8 us
  transfers between devices with their start and end apart: 81, of which 40 were waited for; matrix products, arithmetic and copies ran while one was open for 32% of the time, Pallas kernels for 3%

profile of v8, /device:TPU:0, one launch (start us, length us, event | category | flops | bytes accessed | tf_op | source)
XLA Modules:
  0.0 1011.8 jit_solution(5923563395882357415)
XLA Ops:
  12.3 6.3 all-to-all-start
  20.6 27.5 %all-to-all-done = bf16[8,48,1536]{2,1,0:T(8,128)(2,1)S(1)} async-done(((bf16[8,48,1536]{2,1,0:T(8,128)(2,1)}), bf16[8,48,1536]{2,1,0:T(8,128)(2,1)S(1)}, u32[]{:S(2)}, u32[]{:S(2)}) %all-to-all-start) | async-done | bytes 1179680 | tf_op jit(solution)/shard_map/all_to_all | solution.py:622
  48.1 8.6 all-gather.8.cloned.1.call-done
  64.4 8.7 collective-permute-done
  73.1 17.1 %collective-permute-done.1 = bf16[128,1664]{1,0:T(8,128)(2,1)S(1)} collective-permute-done((bf16[128,1664]{1,0:T(8,128)(2,1)S(1)}, bf16[128,1664]{1,0:T(8,128)(2,1)S(1)}, u32[]{:S(2)}, u32[]{:S(2)}) %collective-permute-start.1) | collective-permute-done | bytes 426016 | tf_op jit(solution)/shard_map/ppermute | solution.py:93
  98.4 11.8 %all-to-all-start.1 = ((bf16[8,48,768]{2,1,0:T(8,128)(2,1)}), bf16[8,48,768]{2,1,0:T(8,128)(2,1)S(1)}, u32[]{:S(2)}, u32[]{:S(2)}) async-start(bf16[8,48,768]{2,1,0:T(8,128)(2,1)} %copy.591), calls=%async_computation.1 | async-start | bytes 1179648 | tf_op jit(solution)/shard_map/all_to_all | solution.py:622
  116.0 11.0 %all-to-all-done.1 = bf16[8,48,768]{2,1,0:T(8,128)(2,1)S(1)} async-done(((bf16[8,48,768]{2,1,0:T(8,128)(2,1)}), bf16[8,48,768]{2,1,0:T(8,128)(2,1)S(1)}, u32[]{:S(2)}, u32[]{:S(2)}) %all-to-all-start.1) | async-done | bytes 589856 | tf_op jit(solution)/shard_map/all_to_all | solution.py:622
  127.0 4.0 all_to_all.30
  137.4 6.5 fusion.38.proj_ref
  146.3 9.6 scan_forward.1
  155.9 9.5 collective-permute-done.5
  180.8 9.0 collective-permute-done.10
  189.7 8.3 collective-permute-done.8
  198.0 18.3 %collective-permute-done.9 = bf16[128,1664]{1,0:T(8,128)(2,1)S(1)} collective-permute-done((bf16[128,1664]{1,0:T(8,128)(2,1)S(1)}, bf16[128,1664]{1,0:T(8,128)(2,1)S(1)}, u32[]{:S(2)}, u32[]{:S(2)}) %collective-permute-start.9) | collective-permute-done | bytes 426016 | tf_op jit(solution)/shard_map/ppermute | solution.py:93
  222.2 10.1 collective-permute-done.14
  232.3 15.9 %collective-permute-done.15 = bf16[128,1536]{1,0:T(8,128)(2,1)S(1)} collective-permute-done((bf16[128,1536]{1,0:T(8,128)(2,1)S(1)}, bf16[128,1536]{1,0:T(8,128)(2,1)S(1)}, u32[]{:S(2)}, u32[]{:S(2)}) %collective-permute-start.15) | collective-permute-done | bytes 393248 | tf_op jit(solution)/shard_map/ppermute | solution.py:93
  249.7 7.9 collective-permute-start.13
  266.7 11.0 %convolution_convert_fusion.4 = bf16[1024,2048]{1,0:T(8,128)(2,1)} fusion(bf16[1024,1536]{1,0:T(8,128)(2,1)} %pad_maximum_fusion.6, bf16[1536,2048]{1,0:T(8,128)(2,1)} %all-gather.12.cloned.1.call-done), kind=kOutput, calls=%fused_computation.50 | convolution fusion | flops 6444548096 | bytes 13631488 | tf_op jit(solution)/shard_map/dot_general | solution.py:37
  287.9 6.1 fusion.30
  314.4 8.6 collective-permute-done.19
  322.9 24.2 %collective-permute-done.20 = bf16[128,1536]{1,0:T(8,128)(2,1)S(1)} collective-permute-done((bf16[128,1536]{1,0:T(8,128)(2,1)S(1)}, bf16[128,1536]{1,0:T(8,128)(2,1)S(1)}, u32[]{:S(2)}, u32[]{:S(2)}) %collective-permute-start.20) | collective-permute-done | bytes 393248 | tf_op jit(solution)/shard_map/ppermute | solution.py:93
  371.8 5.9 collective-permute-done.24
  377.8 16.3 %collective-permute-done.25 = bf16[128,1536]{1,0:T(8,128)(2,1)S(1)} collective-permute-done((bf16[128,1536]{1,0:T(8,128)(2,1)S(1)}, bf16[128,1536]{1,0:T(8,128)(2,1)S(1)}, u32[]{:S(2)}, u32[]{:S(2)}) %collective-permute-start.25) | collective-permute-done | bytes 393248 | tf_op jit(solution)/shard_map/ppermute | solution.py:93
  396.6 22.8 %all-gather.18.cloned.1.call-done = bf16[1536,2048]{1,0:T(8,128)(2,1)} async-done(((bf16[384,2048]{1,0:T(8,128)(2,1)}), bf16[1536,2048]{1,0:T(8,128)(2,1)}) %all-gather.18.cloned.1.call-update) | async-done | bytes 6291472 | tf_op jit(solution)/shard_map/all_gather | solution.py:701
  428.1 6.9 convolution_convert_fusion.3
  439.7 6.9 select_reduce_fusion.2
  451.3 9.4 multiply_convert_fusion.4
  460.8 6.7 fusion.179
  476.8 8.9 convolution_convert_fusion.1
  485.6 7.7 convolution_convert_fusion.6
  497.6 3.9 fusion.28
  510.7 4.5 collective-permute-done.30
  515.3 26.6 %collective-permute-done.31 = bf16[128,1664]{1,0:T(8,128)(2,1)S(1)} collective-permute-done((bf16[128,1664]{1,0:T(8,128)(2,1)S(1)}, bf16[128,1664]{1,0:T(8,128)(2,1)S(1)}, u32[]{:S(2)}, u32[]{:S(2)}) %collective-permute-start.31) | collective-permute-done | bytes 426016 | tf_op jit(solution)/shard_map/ppermute | solution.py:93
  546.7 3.7 fusion.46
  582.8 8.2 collective-permute-done.37
  591.0 16.3 %collective-permute-done.38 = bf16[128,1536]{1,0:T(8,128)(2,1)S(1)} collective-permute-done((bf16[128,1536]{1,0:T(8,128)(2,1)S(1)}, bf16[128,1536]{1,0:T(8,128)(2,1)S(1)}, u32[]{:S(2)}, u32[]{:S(2)}) %collective-permute-start.38) | collective-permute-done | bytes 393248 | tf_op jit(solution)/shard_map/ppermute | solution.py:93
  608.6 4.7 fusion.188
  613.5 10.1 collective-permute-start.34
  634.2 7.8 fusion.6
  642.1 8.8 fusion.178
  652.0 6.2 collective-permute-done.41
  665.9 3.7 add.428
  677.6 5.1 convolution_convert_fusion.5
  682.7 8.8 convolution_convert_fusion
  698.5 3.9 convolution_convert_fusion.8
  706.1 27.9 %collective-permute-done.45 = bf16[128,1664]{1,0:T(8,128)(2,1)} collective-permute-done((bf16[128,1664]{1,0:T(8,128)(2,1)}, bf16[128,1664]{1,0:T(8,128)(2,1)}, u32[]{:S(2)}, u32[]{:S(2)}) %collective-permute-start.45) | collective-permute-done | bytes 426016 | tf_op jit(solution)/shard_map/ppermute | solution.py:93
  747.4 10.8 %collective-permute-done.47 = bf16[128,1664]{1,0:T(8,128)(2,1)S(1)} collective-permute-done((bf16[128,1664]{1,0:T(8,128)(2,1)S(1)}, bf16[128,1664]{1,0:T(8,128)(2,1)S(1)}, u32[]{:S(2)}, u32[]{:S(2)}) %collective-permute-start.47) | collective-permute-done | bytes 426016 | tf_op jit(solution)/shard_map/ppermute | solution.py:93
  758.2 16.8 %collective-permute-done.48 = bf16[128,1664]{1,0:T(8,128)(2,1)S(1)} collective-permute-done((bf16[128,1664]{1,0:T(8,128)(2,1)S(1)}, bf16[128,1664]{1,0:T(8,128)(2,1)S(1)}, u32[]{:S(2)}, u32[]{:S(2)}) %collective-permute-start.48) | collective-permute-done | bytes 426016 | tf_op jit(solution)/shard_map/ppermute | solution.py:93
  788.1 5.5 pad_maximum_fusion.5
  811.2 7.9 collective-permute-start.51
  821.9 4.0 convolution_convert_fusion.12.grad_ref
  826.0 18.3 %scan_backward.1 = (bf16[1024,1152]{1,0:T(8,128)(2,1)S(1)}, f32[8,640]{1,0:T(8,128)S(1)}, f32[8,384]{1,0:T(8,128)S(1)}, f32[8,128]{1,0:T(8,128)S(1)}) custom-call(bf16[1024,1024]{1,0:T(8,128)(2,1)S(1)} %copy-done.1, f32[1024,128]{1,0:T(8,128)S(1)} %copy-done.3, f32[1024,1]{1,0:T(8,128)S(1)} %get-tuple-element.496.col_ref, f32[16,1,64]{2,1,0:T(1,128)S(1)} %bitcast.316, ...), custom_call_target="tpu_custom_call" | custom-call | tf_op jit(solution)/shard_map/scan_backward/pallas_call | solution.py:360
  846.9 8.3 fusion.9
  860.7 7.4 multiply_reduce_fusion
  876.1 9.4 collective-permute-start.55
  886.4 4.6 fusion.180
  891.0 4.1 collective-permute-done.55
  895.1 23.9 %collective-permute-done.56 = bf16[128,1536]{1,0:T(8,128)(2,1)S(1)} collective-permute-done((bf16[128,1536]{1,0:T(8,128)(2,1)S(1)}, bf16[128,1536]{1,0:T(8,128)(2,1)S(1)}, u32[]{:S(2)}, u32[]{:S(2)}) %collective-permute-start.56) | collective-permute-done | bytes 393248 | tf_op jit(solution)/shard_map/ppermute | solution.py:93
  930.1 4.0 all_to_all.31
  935.8 4.2 all-to-all-start.3
  955.5 4.5 collective-permute-start.61
  964.6 4.9 reduce-scatter.18.cloned.1.call-done
  969.5 4.6 all-to-all-start.4
  981.2 16.2 %all-to-all-done.4 = bf16[8,48,1152]{2,1,0:T(8,128)(2,1)} async-done(((bf16[8,48,1152]{2,1,0:T(8,128)(2,1)}), bf16[8,48,1152]{2,1,0:T(8,128)(2,1)}, u32[]{:S(2)}, u32[]{:S(2)}) %all-to-all-start.4) | async-done | bytes 884768 | tf_op jit(solution)/shard_map/all_to_all | solution.py:992
  (883 shorter events, 352.9 us)
Async XLA Ops:
  7.3 49.4 %all-gather.8.cloned.1.call-start = ((), (), s32[]{:S(2)}) async-start(), calls=%async_computation.13 | async-start | bytes 3932160 | tf_op jit(solution)/shard_map/all_gather | solution.py:661
  12.3 35.7 %all-to-all-start = ((bf16[8,48,1536]{2,1,0:T(8,128)(2,1)}), bf16[8,48,1536]{2,1,0:T(8,128)(2,1)S(1)}, u32[]{:S(2)}, u32[]{:S(2)}) async-start(bf16[8,48,1536]{2,1,0:T(8,128)(2,1)} %copy.590), calls=%async_computation | async-start | bytes 2359296 | tf_op jit(solution)/shard_map/all_to_all | solution.py:622
  18.7 114.5 %all-gather.10.cloned.1.call-start = ((), (), s32[]{:S(2)}) async-start(), calls=%async_computation.14 | async-start | bytes 5898240 | tf_op jit(solution)/shard_map/all_gather | solution.py:626
  56.7 210.0 %all-gather.12.cloned.1.call-start = ((), (), s32[]{:S(2)}) async-start(), calls=%async_computation.15 | async-start | bytes 7864320 | tf_op jit(solution)/shard_map/all_gather | solution.py:701
  58.4 14.7 %collective-permute-start = (bf16[128,1664]{1,0:T(8,128)(2,1)S(1)}, bf16[128,1664]{1,0:T(8,128)(2,1)S(1)}, u32[]{:S(2)}, u32[]{:S(2)}) collective-permute-start(bf16[128,1664]{1,0:T(8,128)(2,1)S(1)} %concatenate.200), channel_id=1, source_target_pairs={{0,2},{2,4},{4,6},{6,0},{1,3},{3,5},{5,7},{7,1},{8,10},{10,12},{12... | collective-permute-start | bytes 1277960 | tf_op jit(solution)/shard_map/ppermute | solution.py:93
  60.5 29.7 %collective-permute-start.1 = (bf16[128,1664]{1,0:T(8,128)(2,1)S(1)}, bf16[128,1664]{1,0:T(8,128)(2,1)S(1)}, u32[]{:S(2)}, u32[]{:S(2)}) collective-permute-start(bf16[128,1664]{1,0:T(8,128)(2,1)S(1)} %concatenate.200), channel_id=1, source_target_pairs={{0,4},{2,6},{4,0},{6,2},{1,5},{3,7},{5,1},{7,3},{8,12},{10,14},{12... | collective-permute-start | bytes 1277960 | tf_op jit(solution)/shard_map/ppermute | solution.py:93
  62.9 27.3 %collective-permute-start.2 = (bf16[128,1664]{1,0:T(8,128)(2,1)S(1)}, bf16[128,1664]{1,0:T(8,128)(2,1)S(1)}, u32[]{:S(2)}, u32[]{:S(2)}) collective-permute-start(bf16[128,1664]{1,0:T(8,128)(2,1)S(1)} %concatenate.200), channel_id=1, source_target_pairs={{0,6},{2,0},{4,2},{6,4},{1,7},{3,1},{5,3},{7,5},{8,14},{10,8},{12,... | collective-permute-start | bytes 1277960 | tf_op jit(solution)/shard_map/ppermute | solution.py:93
  98.4 28.5 %all-to-all-start.1 = ((bf16[8,48,768]{2,1,0:T(8,128)(2,1)}), bf16[8,48,768]{2,1,0:T(8,128)(2,1)S(1)}, u32[]{:S(2)}, u32[]{:S(2)}) async-start(bf16[8,48,768]{2,1,0:T(8,128)(2,1)} %copy.591), calls=%async_computation.1 | async-start | bytes 1179648 | tf_op jit(solution)/shard_map/all_to_all | solution.py:622
  110.2 167.6 %all-gather.14.cloned.1.call-start = ((), (), s32[]{:S(2)}) async-start(), calls=%async_computation.16 | async-start | bytes 2949120 | tf_op jit(solution)/shard_map/all_gather | solution.py:626
  131.0 24.9 %collective-permute-start.4 = (bf16[96,2048]{1,0:T(8,128)(2,1)S(1)}, bf16[96,2048]{1,0:T(8,128)(2,1)S(1)}, u32[]{:S(2)}, u32[]{:S(2)}) collective-permute-start(bf16[96,2048]{1,0:T(8,128)(2,1)S(1)} %bitcast.324), channel_id=1, source_target_pairs={{0,6},{2,0},{4,2},{6,4},{1,7},{3,1},{5,3},{7,5},{8,14},{10,8},{12,... | collective-permute-start | bytes 1179656 | tf_op jit(solution)/shard_map/ppermute | solution.py:93
  132.3 33.2 %collective-permute-start.5 = (bf16[96,2048]{1,0:T(8,128)(2,1)S(1)}, bf16[96,2048]{1,0:T(8,128)(2,1)S(1)}, u32[]{:S(2)}, u32[]{:S(2)}) collective-permute-start(bf16[96,2048]{1,0:T(8,128)(2,1)S(1)} %bitcast.325), channel_id=1, source_target_pairs={{0,4},{2,6},{4,0},{6,2},{1,5},{3,7},{5,1},{7,3},{8,12},{10,14},{12... | collective-permute-start | bytes 1179656 | tf_op jit(solution)/shard_map/ppermute | solution.py:93
  132.3 33.2 %collective-permute-start.6 = (bf16[96,2048]{1,0:T(8,128)(2,1)S(1)}, bf16[96,2048]{1,0:T(8,128)(2,1)S(1)}, u32[]{:S(2)}, u32[]{:S(2)}) collective-permute-start(bf16[96,2048]{1,0:T(8,128)(2,1)S(1)} %bitcast.326), channel_id=1, source_target_pairs={{0,2},{2,4},{4,6},{6,0},{1,3},{3,5},{5,7},{7,1},{8,10},{10,12},{12... | collective-permute-start | bytes 1179656 | tf_op jit(solution)/shard_map/ppermute | solution.py:93
  133.1 216.7 %all-gather.16.cloned.1.call-start = ((), (), s32[]{:S(2)}) async-start(), calls=%async_computation.17 | async-start | bytes 7864320 | tf_op jit(solution)/shard_map/all_gather | solution.py:771
  167.0 229.6 %all-gather.20.cloned.1.call-start = ((), (), s32[]{:S(2)}) async-start(), calls=%async_computation.19 | async-start | bytes 3932160 | tf_op jit(solution)/shard_map/all_gather | solution.py:661
  175.2 14.6 %collective-permute-start.10 = (bf16[128,1664]{1,0:T(8,128)(2,1)S(1)}, bf16[128,1664]{1,0:T(8,128)(2,1)S(1)}, u32[]{:S(2)}, u32[]{:S(2)}) collective-permute-start(bf16[128,1664]{1,0:T(8,128)(2,1)S(1)} %get-tuple-element.512), channel_id=1, source_target_pairs={{0,2},{2,4},{4,6},{6,0},{1,3},{3,5},{5,7},{7,1},{8,10},{10,12},{12... | collective-permute-start | bytes 1277960 | tf_op jit(solution)/shard_map/ppermute | solution.py:93
  176.8 21.2 %collective-permute-start.8 = (bf16[128,1664]{1,0:T(8,128)(2,1)S(1)}, bf16[128,1664]{1,0:T(8,128)(2,1)S(1)}, u32[]{:S(2)}, u32[]{:S(2)}) collective-permute-start(bf16[128,1664]{1,0:T(8,128)(2,1)S(1)} %get-tuple-element.511), channel_id=1, source_target_pairs={{0,6},{2,0},{4,2},{6,4},{1,7},{3,1},{5,3},{7,5},{8,14},{10,8},{12,... | collective-permute-start | bytes 1277960 | tf_op jit(solution)/shard_map/ppermute | solution.py:93
  179.1 37.2 %collective-permute-start.9 = (bf16[128,1664]{1,0:T(8,128)(2,1)S(1)}, bf16[128,1664]{1,0:T(8,128)(2,1)S(1)}, u32[]{:S(2)}, u32[]{:S(2)}) collective-permute-start(bf16[128,1664]{1,0:T(8,128)(2,1)S(1)} %get-tuple-element.513), channel_id=1, source_target_pairs={{0,4},{2,6},{4,0},{6,2},{1,5},{3,7},{5,1},{7,3},{8,12},{10,14},{12... | collective-permute-start | bytes 1277960 | tf_op jit(solution)/shard_map/ppermute | solution.py:93
  218.4 13.9 %collective-permute-start.14 = (bf16[128,1536]{1,0:T(8,128)(2,1)S(1)}, bf16[128,1536]{1,0:T(8,128)(2,1)S(1)}, u32[]{:S(2)}, u32[]{:S(2)}) collective-permute-start(bf16[128,1536]{1,0:T(8,128)(2,1)S(1)} %multiply_convert_fusion.11), channel_id=1, source_target_pairs={{0,2},{2,4},{4,6},{6,0},{1,3},{3,5},{5,7},{7,1},{8,10},{10,12},{12... | collective-permute-start | bytes 1179656 | tf_op jit(solution)/shard_map/ppermute | solution.py:93
  218.4 29.9 %collective-permute-start.15 = (bf16[128,1536]{1,0:T(8,128)(2,1)S(1)}, bf16[128,1536]{1,0:T(8,128)(2,1)S(1)}, u32[]{:S(2)}, u32[]{:S(2)}) collective-permute-start(bf16[128,1536]{1,0:T(8,128)(2,1)S(1)} %multiply_convert_fusion.11), channel_id=1, source_target_pairs={{0,4},{2,6},{4,0},{6,2},{1,5},{3,7},{5,1},{7,3},{8,12},{10,14},{12... | collective-permute-start | bytes 1179656 | tf_op jit(solution)/shard_map/ppermute | solution.py:93
  221.6 26.7 %collective-permute-start.16 = (bf16[128,1536]{1,0:T(8,128)(2,1)S(1)}, bf16[128,1536]{1,0:T(8,128)(2,1)S(1)}, u32[]{:S(2)}, u32[]{:S(2)}) collective-permute-start(bf16[128,1536]{1,0:T(8,128)(2,1)S(1)} %multiply_convert_fusion.11), channel_id=1, source_target_pairs={{0,6},{2,0},{4,2},{6,4},{1,7},{3,1},{5,3},{7,5},{8,14},{10,8},{12,... | collective-permute-start | bytes 1179656 | tf_op jit(solution)/shard_map/ppermute | solution.py:93
  249.6 14.1 %collective-permute-start.17 = (bf16[512,1536]{1,0:T(8,128)(2,1)}, bf16[512,1536]{1,0:T(8,128)(2,1)}, u32[]{:S(2)}, u32[]{:S(2)}) collective-permute-start(bf16[512,1536]{1,0:T(8,128)(2,1)} %pad_maximum_fusion.11), channel_id=1, source_target_pairs={{0,1},{1,0},{2,3},{3,2},{4,5},{5,4},{6,7},{7,6},{8,9},{9,8},{10,11... | collective-permute-start | bytes 4718600 | tf_op jit(solution)/shard_map/ppermute | solution.py:93
  249.7 28.1 %collective-permute-start.13 = (bf16[128,1536]{1,0:T(8,128)(2,1)S(1)}, bf16[128,1536]{1,0:T(8,128)(2,1)S(1)}, u32[]{:S(2)}, u32[]{:S(2)}) collective-permute-start(bf16[128,1536]{1,0:T(8,128)(2,1)S(1)} %bitcast.319), channel_id=1, source_target_pairs={{0,2},{2,4},{4,6},{6,0},{1,3},{3,5},{5,7},{7,1},{8,10},{10,12},{12... | collective-permute-start | bytes 1179656 | tf_op jit(solution)/shard_map/ppermute | solution.py:93
  257.6 36.6 %collective-permute-start.11 = (bf16[128,1536]{1,0:T(8,128)(2,1)S(1)}, bf16[128,1536]{1,0:T(8,128)(2,1)S(1)}, u32[]{:S(2)}, u32[]{:S(2)}) collective-permute-start(bf16[128,1536]{1,0:T(8,128)(2,1)S(1)} %bitcast.320), channel_id=1, source_target_pairs={{0,4},{2,6},{4,0},{6,2},{1,5},{3,7},{5,1},{7,3},{8,12},{10,14},{12... | collective-permute-start | bytes 1179656 | tf_op jit(solution)/shard_map/ppermute | solution.py:93
  257.6 36.6 %collective-permute-start.12 = (bf16[128,1536]{1,0:T(8,128)(2,1)S(1)}, bf16[128,1536]{1,0:T(8,128)(2,1)}, u32[]{:S(2)}, u32[]{:S(2)}) collective-permute-start(bf16[128,1536]{1,0:T(8,128)(2,1)S(1)} %bitcast.321), channel_id=1, source_target_pairs={{0,6},{2,0},{4,2},{6,4},{1,7},{3,1},{5,3},{7,5},{8,14},{10,8},{12,... | collective-permute-start | bytes 1179656 | tf_op jit(solution)/shard_map/ppermute | solution.py:93
  260.0 159.4 %all-gather.18.cloned.1.call-start = ((), (), s32[]{:S(2)}) async-start(), calls=%async_computation.18 | async-start | bytes 7864320 | tf_op jit(solution)/shard_map/all_gather | solution.py:701
  305.9 430.5 %reduce-scatter.10.cloned.1.call-start = ((), (), s32[]{:S(2)}) async-start(), calls=%async_computation.21 | async-start | bytes 3932160 | tf_op jit(solution)/shard_map/reduce_scatter | solution.py:821
  313.4 33.8 %collective-permute-start.20 = (bf16[128,1536]{1,0:T(8,128)(2,1)S(1)}, bf16[128,1536]{1,0:T(8,128)(2,1)S(1)}, u32[]{:S(2)}, u32[]{:S(2)}) collective-permute-start(bf16[128,1536]{1,0:T(8,128)(2,1)S(1)} %get-tuple-element.541), channel_id=1, source_target_pairs={{0,4},{2,6},{4,0},{6,2},{1,5},{3,7},{5,1},{7,3},{8,12},{10,14},{12... | collective-permute-start | bytes 1179656 | tf_op jit(solution)/shard_map/ppermute | solution.py:93
  313.4 33.8 %collective-permute-start.21 = (bf16[128,1536]{1,0:T(8,128)(2,1)S(1)}, bf16[128,1536]{1,0:T(8,128)(2,1)S(1)}, u32[]{:S(2)}, u32[]{:S(2)}) collective-permute-start(bf16[128,1536]{1,0:T(8,128)(2,1)S(1)} %get-tuple-element.540), channel_id=1, source_target_pairs={{0,2},{2,4},{4,6},{6,0},{1,3},{3,5},{5,7},{7,1},{8,10},{10,12},{12... | collective-permute-start | bytes 1179656 | tf_op jit(solution)/shard_map/ppermute | solution.py:93
  363.9 13.9 %collective-permute-start.24 = (bf16[128,1536]{1,0:T(8,128)(2,1)S(1)}, bf16[128,1536]{1,0:T(8,128)(2,1)S(1)}, u32[]{:S(2)}, u32[]{:S(2)}) collective-permute-start(bf16[128,1536]{1,0:T(8,128)(2,1)S(1)} %multiply_convert_fusion.9), channel_id=1, source_target_pairs={{0,2},{2,4},{4,6},{6,0},{1,3},{3,5},{5,7},{7,1},{8,10},{10,12},{12... | collective-permute-start | bytes 1179656 | tf_op jit(solution)/shard_map/ppermute | solution.py:93
  364.7 29.4 %collective-permute-start.25 = (bf16[128,1536]{1,0:T(8,128)(2,1)S(1)}, bf16[128,1536]{1,0:T(8,128)(2,1)S(1)}, u32[]{:S(2)}, u32[]{:S(2)}) collective-permute-start(bf16[128,1536]{1,0:T(8,128)(2,1)S(1)} %multiply_convert_fusion.9), channel_id=1, source_target_pairs={{0,4},{2,6},{4,0},{6,2},{1,5},{3,7},{5,1},{7,3},{8,12},{10,14},{12... | collective-permute-start | bytes 1179656 | tf_op jit(solution)/shard_map/ppermute | solution.py:93
  366.8 27.3 %collective-permute-start.26 = (bf16[128,1536]{1,0:T(8,128)(2,1)S(1)}, bf16[128,1536]{1,0:T(8,128)(2,1)S(1)}, u32[]{:S(2)}, u32[]{:S(2)}) collective-permute-start(bf16[128,1536]{1,0:T(8,128)(2,1)S(1)} %multiply_convert_fusion.9), channel_id=1, source_target_pairs={{0,6},{2,0},{4,2},{6,4},{1,7},{3,1},{5,3},{7,5},{8,14},{10,8},{12,... | collective-permute-start | bytes 1179656 | tf_op jit(solution)/shard_map/ppermute | solution.py:93
  371.8 47.6 %collective-permute-start.28 = (bf16[512,1536]{1,0:T(8,128)(2,1)}, bf16[512,1536]{1,0:T(8,128)(2,1)}, u32[]{:S(2)}, u32[]{:S(2)}) collective-permute-start(bf16[512,1536]{1,0:T(8,128)(2,1)} %pad_maximum_fusion.15), channel_id=1, source_target_pairs={{0,1},{1,0},{2,3},{3,2},{4,5},{5,4},{6,7},{7,6},{8,9},{9,8},{10,11... | collective-permute-start | bytes 4718600 | tf_op jit(solution)/shard_map/ppermute | solution.py:93
  395.5 25.8 %collective-permute-start.27 = (bf16[512,1536]{1,0:T(8,128)(2,1)}, bf16[512,1536]{1,0:T(8,128)(2,1)}, u32[]{:S(2)}, u32[]{:S(2)}) collective-permute-start(bf16[512,1536]{1,0:T(8,128)(2,1)} %pad_maximum_fusion.13), channel_id=1, source_target_pairs={{0,1},{1,0},{2,3},{3,2},{4,5},{5,4},{6,7},{7,6},{8,9},{9,8},{10,11... | collective-permute-start | bytes 4718600 | tf_op jit(solution)/shard_map/ppermute | solution.py:93
  493.3 243.1 %reduce-scatter.8.cloned.1.call-start = ((), (), s32[]{:S(2)}) async-start(), calls=%async_computation.20 | async-start | bytes 7864320 | tf_op jit(solution)/shard_map/reduce_scatter | solution.py:817
  494.1 315.7 %reduce-scatter.14.cloned.1.call-start = ((), (), s32[]{:S(2)}) async-start(), calls=%async_computation.23 | async-start | bytes 7864320 | tf_op jit(solution)/shard_map/reduce_scatter | solution.py:898
  501.6 13.6 %collective-permute-start.30 = (bf16[128,1664]{1,0:T(8,128)(2,1)S(1)}, bf16[128,1664]{1,0:T(8,128)(2,1)S(1)}, u32[]{:S(2)}, u32[]{:S(2)}) collective-permute-start(bf16[128,1664]{1,0:T(8,128)(2,1)S(1)} %get-tuple-element.510), channel_id=1, source_target_pairs={{0,6},{2,0},{4,2},{6,4},{1,7},{3,1},{5,3},{7,5},{8,14},{10,8},{12,... | collective-permute-start | bytes 1277960 | tf_op jit(solution)/shard_map/ppermute | solution.py:93
  505.0 36.8 %collective-permute-start.31 = (bf16[128,1664]{1,0:T(8,128)(2,1)S(1)}, bf16[128,1664]{1,0:T(8,128)(2,1)S(1)}, u32[]{:S(2)}, u32[]{:S(2)}) collective-permute-start(bf16[128,1664]{1,0:T(8,128)(2,1)S(1)} %get-tuple-element.509), channel_id=1, source_target_pairs={{0,4},{2,6},{4,0},{6,2},{1,5},{3,7},{5,1},{7,3},{8,12},{10,14},{12... | collective-permute-start | bytes 1277960 | tf_op jit(solution)/shard_map/ppermute | solution.py:93
  505.0 36.8 %collective-permute-start.32 = (bf16[128,1664]{1,0:T(8,128)(2,1)S(1)}, bf16[128,1664]{1,0:T(8,128)(2,1)S(1)}, u32[]{:S(2)}, u32[]{:S(2)}) collective-permute-start(bf16[128,1664]{1,0:T(8,128)(2,1)S(1)} %get-tuple-element.508), channel_id=1, source_target_pairs={{0,2},{2,4},{4,6},{6,0},{1,3},{3,5},{5,7},{7,1},{8,10},{10,12},{12... | collective-permute-start | bytes 1277960 | tf_op jit(solution)/shard_map/ppermute | solution.py:93
  546.2 62.4 %collective-permute-start.33 = (bf16[512,1536]{1,0:T(8,128)(2,1)}, bf16[512,1536]{1,0:T(8,128)(2,1)}, u32[]{:S(2)}, u32[]{:S(2)}) collective-permute-start(bf16[512,1536]{1,0:T(8,128)(2,1)} %slice.1149), channel_id=1, source_target_pairs={{0,1},{1,0},{2,3},{3,2},{4,5},{5,4},{6,7},{7,6},{8,9},{9,8},{10,11... | collective-permute-start | bytes 4718600 | tf_op jit(solution)/shard_map/ppermute | solution.py:93
  577.1 13.9 %collective-permute-start.37 = (bf16[128,1536]{1,0:T(8,128)(2,1)S(1)}, bf16[128,1536]{1,0:T(8,128)(2,1)S(1)}, u32[]{:S(2)}, u32[]{:S(2)}) collective-permute-start(bf16[128,1536]{1,0:T(8,128)(2,1)S(1)} %get-tuple-element.470), channel_id=1, source_target_pairs={{0,2},{2,4},{4,6},{6,0},{1,3},{3,5},{5,7},{7,1},{8,10},{10,12},{12... | collective-permute-start | bytes 1179656 | tf_op jit(solution)/shard_map/ppermute | solution.py:93
  578.1 29.1 %collective-permute-start.38 = (bf16[128,1536]{1,0:T(8,128)(2,1)S(1)}, bf16[128,1536]{1,0:T(8,128)(2,1)S(1)}, u32[]{:S(2)}, u32[]{:S(2)}) collective-permute-start(bf16[128,1536]{1,0:T(8,128)(2,1)S(1)} %get-tuple-element.470), channel_id=1, source_target_pairs={{0,4},{2,6},{4,0},{6,2},{1,5},{3,7},{5,1},{7,3},{8,12},{10,14},{12... | collective-permute-start | bytes 1179656 | tf_op jit(solution)/shard_map/ppermute | solution.py:93
  579.9 27.4 %collective-permute-start.39 = (bf16[128,1536]{1,0:T(8,128)(2,1)S(1)}, bf16[128,1536]{1,0:T(8,128)(2,1)S(1)}, u32[]{:S(2)}, u32[]{:S(2)}) collective-permute-start(bf16[128,1536]{1,0:T(8,128)(2,1)S(1)} %get-tuple-element.470), channel_id=1, source_target_pairs={{0,6},{2,0},{4,2},{6,4},{1,7},{3,1},{5,3},{7,5},{8,14},{10,8},{12,... | collective-permute-start | bytes 1179656 | tf_op jit(solution)/shard_map/ppermute | solution.py:93
  608.5 15.6 %collective-permute-start.40 = (bf16[512,1536]{1,0:T(8,128)(2,1)}, bf16[512,1536]{1,0:T(8,128)(2,1)}, u32[]{:S(2)}, u32[]{:S(2)}) collective-permute-start(bf16[512,1536]{1,0:T(8,128)(2,1)} %pad_maximum_fusion.16), channel_id=1, source_target_pairs={{0,1},{1,0},{2,3},{3,2},{4,5},{5,4},{6,7},{7,6},{8,9},{9,8},{10,11... | collective-permute-start | bytes 4718600 | tf_op jit(solution)/shard_map/ppermute | solution.py:93
  608.6 246.7 %reduce-scatter.16.cloned.1.call-start = ((), (), s32[]{:S(2)}) async-start(), calls=%async_computation.24 | async-start | bytes 7864320 | tf_op jit(solution)/shard_map/reduce_scatter | solution.py:817
  613.5 19.6 %collective-permute-start.34 = (bf16[128,1536]{1,0:T(8,128)(2,1)S(1)}, bf16[128,1536]{1,0:T(8,128)(2,1)S(1)}, u32[]{:S(2)}, u32[]{:S(2)}) collective-permute-start(bf16[128,1536]{1,0:T(8,128)(2,1)S(1)} %get-tuple-element.530), channel_id=1, source_target_pairs={{0,6},{2,0},{4,2},{6,4},{1,7},{3,1},{5,3},{7,5},{8,14},{10,8},{12,... | collective-permute-start | bytes 1179656 | tf_op jit(solution)/shard_map/ppermute | solution.py:93
  623.5 34.6 %collective-permute-start.41 = (bf16[128,1536]{1,0:T(8,128)(2,1)S(1)}, bf16[128,1536]{1,0:T(8,128)(2,1)S(1)}, u32[]{:S(2)}, u32[]{:S(2)}) collective-permute-start(bf16[128,1536]{1,0:T(8,128)(2,1)S(1)} %get-tuple-element.532), channel_id=1, source_target_pairs={{0,4},{2,6},{4,0},{6,2},{1,5},{3,7},{5,1},{7,3},{8,12},{10,14},{12... | collective-permute-start | bytes 1179656 | tf_op jit(solution)/shard_map/ppermute | solution.py:93
  623.5 34.6 %collective-permute-start.42 = (bf16[128,1536]{1,0:T(8,128)(2,1)S(1)}, bf16[128,1536]{1,0:T(8,128)(2,1)S(1)}, u32[]{:S(2)}, u32[]{:S(2)}) collective-permute-start(bf16[128,1536]{1,0:T(8,128)(2,1)S(1)} %get-tuple-element.531), channel_id=1, source_target_pairs={{0,2},{2,4},{4,6},{6,0},{1,3},{3,5},{5,7},{7,1},{8,10},{10,12},{12... | collective-permute-start | bytes 1179656 | tf_op jit(solution)/shard_map/ppermute | solution.py:93
  691.5 234.1 %reduce-scatter.20.cloned.1.call-start = ((), (), s32[]{:S(2)}) async-start(), calls=%async_computation.26 | async-start | bytes 3932160 | tf_op jit(solution)/shard_map/reduce_scatter | solution.py:821
  693.9 40.1 %collective-permute-start.45 = (bf16[128,1664]{1,0:T(8,128)(2,1)}, bf16[128,1664]{1,0:T(8,128)(2,1)}, u32[]{:S(2)}, u32[]{:S(2)}) collective-permute-start(bf16[128,1664]{1,0:T(8,128)(2,1)} %get-tuple-element.506), channel_id=1, source_target_pairs={{0,4},{2,6},{4,0},{6,2},{1,5},{3,7},{5,1},{7,3},{8,12},{10,14},{12... | collective-permute-start | bytes 1277960 | tf_op jit(solution)/shard_map/ppermute | solution.py:93
  696.2 37.8 %collective-permute-start.46 = (bf16[128,1664]{1,0:T(8,128)(2,1)}, bf16[128,1664]{1,0:T(8,128)(2,1)}, u32[]{:S(2)}, u32[]{:S(2)}) collective-permute-start(bf16[128,1664]{1,0:T(8,128)(2,1)} %get-tuple-element.505), channel_id=1, source_target_pairs={{0,2},{2,4},{4,6},{6,0},{1,3},{3,5},{5,7},{7,1},{8,10},{10,12},{12... | collective-permute-start | bytes 1277960 | tf_op jit(solution)/shard_map/ppermute | solution.py:93
  698.3 237.6 %reduce-scatter.12.cloned.1.call-start = ((), (), s32[]{:S(2)}) async-start(), calls=%async_computation.22 | async-start | bytes 4423680 | tf_op jit(solution)/shard_map/reduce_scatter | solution.py:989
  743.5 14.7 %collective-permute-start.47 = (bf16[128,1664]{1,0:T(8,128)(2,1)S(1)}, bf16[128,1664]{1,0:T(8,128)(2,1)S(1)}, u32[]{:S(2)}, u32[]{:S(2)}) collective-permute-start(bf16[128,1664]{1,0:T(8,128)(2,1)S(1)} %concatenate.234), channel_id=1, source_target_pairs={{0,2},{2,4},{4,6},{6,0},{1,3},{3,5},{5,7},{7,1},{8,10},{10,12},{12... | collective-permute-start | bytes 1277960 | tf_op jit(solution)/shard_map/ppermute | solution.py:93
  743.5 31.4 %collective-permute-start.48 = (bf16[128,1664]{1,0:T(8,128)(2,1)S(1)}, bf16[128,1664]{1,0:T(8,128)(2,1)S(1)}, u32[]{:S(2)}, u32[]{:S(2)}) collective-permute-start(bf16[128,1664]{1,0:T(8,128)(2,1)S(1)} %concatenate.234), channel_id=1, source_target_pairs={{0,4},{2,6},{4,0},{6,2},{1,5},{3,7},{5,1},{7,3},{8,12},{10,14},{12... | collective-permute-start | bytes 1277960 | tf_op jit(solution)/shard_map/ppermute | solution.py:93
  744.2 30.7 %collective-permute-start.49 = (bf16[128,1664]{1,0:T(8,128)(2,1)S(1)}, bf16[128,1664]{1,0:T(8,128)(2,1)S(1)}, u32[]{:S(2)}, u32[]{:S(2)}) collective-permute-start(bf16[128,1664]{1,0:T(8,128)(2,1)S(1)} %concatenate.234), channel_id=1, source_target_pairs={{0,6},{2,0},{4,2},{6,4},{1,7},{3,1},{5,3},{7,5},{8,14},{10,8},{12,... | collective-permute-start | bytes 1277960 | tf_op jit(solution)/shard_map/ppermute | solution.py:93
  805.7 163.8 %reduce-scatter.18.cloned.1.call-start = ((), (), s32[]{:S(2)}) async-start(), calls=%async_computation.25 | async-start | bytes 4423680 | tf_op jit(solution)/shard_map/reduce_scatter | solution.py:989
  811.2 33.1 %collective-permute-start.51 = (bf16[96,2048]{1,0:T(8,128)(2,1)S(1)}, bf16[96,2048]{1,0:T(8,128)(2,1)S(1)}, u32[]{:S(2)}, u32[]{:S(2)}) collective-permute-start(bf16[96,2048]{1,0:T(8,128)(2,1)S(1)} %get-tuple-element.523), channel_id=1, source_target_pairs={{0,2},{2,4},{4,6},{6,0},{1,3},{3,5},{5,7},{7,1},{8,10},{10,12},{12... | collective-permute-start | bytes 1179656 | tf_op jit(solution)/shard_map/ppermute | solution.py:93
  819.0 27.9 %collective-permute-start.52 = (bf16[96,2048]{1,0:T(8,128)(2,1)S(1)}, bf16[96,2048]{1,0:T(8,128)(2,1)S(1)}, u32[]{:S(2)}, u32[]{:S(2)}) collective-permute-start(bf16[96,2048]{1,0:T(8,128)(2,1)S(1)} %get-tuple-element.522), channel_id=1, source_target_pairs={{0,4},{2,6},{4,0},{6,2},{1,5},{3,7},{5,1},{7,3},{8,12},{10,14},{12... | collective-permute-start | bytes 1179656 | tf_op jit(solution)/shard_map/ppermute | solution.py:93
  820.9 34.4 %collective-permute-start.53 = (bf16[96,2048]{1,0:T(8,128)(2,1)S(1)}, bf16[96,2048]{1,0:T(8,128)(2,1)S(1)}, u32[]{:S(2)}, u32[]{:S(2)}) collective-permute-start(bf16[96,2048]{1,0:T(8,128)(2,1)S(1)} %get-tuple-element.521), channel_id=1, source_target_pairs={{0,6},{2,0},{4,2},{6,4},{1,7},{3,1},{5,3},{7,5},{8,14},{10,8},{12,... | collective-permute-start | bytes 1179656 | tf_op jit(solution)/shard_map/ppermute | solution.py:93
  858.6 14.2 %collective-permute-start.54 = (bf16[512,1536]{1,0:T(8,128)(2,1)}, bf16[512,1536]{1,0:T(8,128)(2,1)}, u32[]{:S(2)}, u32[]{:S(2)}) collective-permute-start(bf16[512,1536]{1,0:T(8,128)(2,1)} %slice.1148), channel_id=1, source_target_pairs={{0,1},{1,0},{2,3},{3,2},{4,5},{5,4},{6,7},{7,6},{8,9},{9,8},{10,11... | collective-permute-start | bytes 4718600 | tf_op jit(solution)/shard_map/ppermute | solution.py:93
  876.1 18.9 %collective-permute-start.55 = (bf16[128,1536]{1,0:T(8,128)(2,1)S(1)}, bf16[128,1536]{1,0:T(8,128)(2,1)S(1)}, u32[]{:S(2)}, u32[]{:S(2)}) collective-permute-start(bf16[128,1536]{1,0:T(8,128)(2,1)S(1)} %get-tuple-element.520), channel_id=1, source_target_pairs={{0,6},{2,0},{4,2},{6,4},{1,7},{3,1},{5,3},{7,5},{8,14},{10,8},{12,... | collective-permute-start | bytes 1179656 | tf_op jit(solution)/shard_map/ppermute | solution.py:93
  885.6 33.4 %collective-permute-start.56 = (bf16[128,1536]{1,0:T(8,128)(2,1)S(1)}, bf16[128,1536]{1,0:T(8,128)(2,1)S(1)}, u32[]{:S(2)}, u32[]{:S(2)}) collective-permute-start(bf16[128,1536]{1,0:T(8,128)(2,1)S(1)} %get-tuple-element.519), channel_id=1, source_target_pairs={{0,4},{2,6},{4,0},{6,2},{1,5},{3,7},{5,1},{7,3},{8,12},{10,14},{12... | collective-permute-start | bytes 1179656 | tf_op jit(solution)/shard_map/ppermute | solution.py:93
  885.6 33.4 %collective-permute-start.57 = (bf16[128,1536]{1,0:T(8,128)(2,1)S(1)}, bf16[128,1536]{1,0:T(8,128)(2,1)}, u32[]{:S(2)}, u32[]{:S(2)}) collective-permute-start(bf16[128,1536]{1,0:T(8,128)(2,1)S(1)} %get-tuple-element.518), channel_id=1, source_target_pairs={{0,2},{2,4},{4,6},{6,0},{1,3},{3,5},{5,7},{7,1},{8,10},{10,12},{12... | collective-permute-start | bytes 1179656 | tf_op jit(solution)/shard_map/ppermute | solution.py:93
  935.8 27.5 %all-to-all-start.3 = ((bf16[8,48,1152]{2,1,0:T(8,128)(2,1)}), bf16[8,48,1152]{2,1,0:T(8,128)(2,1)}, u32[]{:S(2)}, u32[]{:S(2)}) async-start(bf16[8,48,1152]{2,1,0:T(8,128)(2,1)} %bitcast.344), calls=%async_computation.9 | async-start | bytes 1769472 | tf_op jit(solution)/shard_map/all_to_all | solution.py:992
  969.5 27.8 %all-to-all-start.4 = ((bf16[8,48,1152]{2,1,0:T(8,128)(2,1)}), bf16[8,48,1152]{2,1,0:T(8,128)(2,1)}, u32[]{:S(2)}, u32[]{:S(2)}) async-start(bf16[8,48,1152]{2,1,0:T(8,128)(2,1)} %bitcast.345), calls=%async_computation.10 | async-start | bytes 1769472 | tf_op jit(solution)/shard_map/all_to_all | solution.py:992
  (215 other events, 2260.6 us)
Sparse Core Ops, SparseCore 0:
  10.0 46.6 all-gather.7
  59.1 57.0 all-gather.9
  118.7 70.1 all-gather.11
  191.1 37.4 all-gather.13
  230.9 70.1 all-gather.15
  302.8 43.9 all-gather.19
  349.2 70.1 all-gather.17
  493.4 43.9 reduce-scatter.9
  540.4 70.1 reduce-scatter.7
  613.5 72.4 reduce-scatter.13
  691.7 69.4 reduce-scatter.15
  764.0 43.9 reduce-scatter.19
  811.0 48.4 reduce-scatter.11
  922.2 47.2 reduce-scatter.17

commit v9 on v8

--- a/solution.py
+++ b/solution.py
@@ -848,9 +848,9 @@
                 hidden, g_pre, own = fence(side[2], side[4], own)
                 g_low = tn_sum([(hidden, side[1])])
                 g_up = tn_sum([(side[0], g_pre)])
-                g_pre_s, g_low, g_up = fence(side[5], g_low, g_up)
-                g_sin = tn_sum([(side[6], g_pre_s)])
-                sent, g_sin = fence(sent, g_sin)
+                sent[:1], g_low = fence(sent[:1], g_low)
+                sent[1:], g_up = fence(sent[1:], g_up)
+                g_sin = tn_sum([(side[6], side[5])])
                 weights = (g_up, g_low, g_sin, tn_sum([(side[7], side[3])]))
                 back = return_finish(own, sent)
             backs.append(back)
@@ -1001,7 +1001,8 @@
     )
 
     g_scan = by_rows(tn_sum(mamba_sides, f32))
-    mamba_back, g_scan = fence(mamba_back, g_scan)
+    last_own, last_sent = mamba_back[-1]
+    last_sent[:1], g_scan = fence(last_sent[:1], g_scan)
     mamba_back = [return_finish(*pair) for pair in mamba_back]
     g_attn = attn_total(*attn_sent)
     g_s, mamba_back[-1] = fence(g_s, mamba_back[-1])

time: 1020 us -> 1010 us (level)
  waiting for transfers between devices: 419 us -> 376 us
  starting transfers between devices: 126 us -> 140 us
  local copies, waits for them, and re-layouts: 88.3 us -> 101 us
    ppermute x63, waiting for transfers between devices: 326 us -> 295 us  [send(): return by_rows(lax.ppermute(by_rows(x), axis, pairs))]
    ppermute x63, starting transfers between devices: 98 us -> 112 us  [send(): return by_rows(lax.ppermute(by_rows(x), axis, pairs))]
    unnamed x429 -> x453, local copies, waits for them, and re-layouts: 25 us -> 34.4 us
  transfers between devices with their start and end apart: 81 -> 81, of which waited for: 40 -> 40; matrix products, arithmetic and copies ran while one was open for 32% -> 35% of each run, Pallas kernels for 3% -> 3%
where the time goes in v9:
time: 1010 us; the launch traced here: 1000 us
  waiting for transfers between devices  376 us (37%)
  matrix products  189 us (19%)
  other arithmetic  141 us (14%)
  starting transfers between devices  140 us (14%)
  local copies, waits for them, and re-layouts  101 us (10%)
  Pallas kernels  27.9 us (3%)
  between operations  17.8 us (2%)
    ppermute x63, waiting for transfers between devices, send(): return by_rows(lax.ppermute(by_rows(x), axis, pairs))  295 us
    dot_general x44, matrix products, dot(): r = lax.dot_general(a, b, (dims, ((), ())), preferred_element_type=f32)  180 us
    ppermute x63, starting transfers between devices, send(): return by_rows(lax.ppermute(by_rows(x), axis, pairs))  112 us
    all_to_all x2, waiting for transfers between devices, moved_columns(): moved = lax.all_to_all(packed, TP, split_axis=0, concat_axis=0, tiled=True)  38.5 us
    unnamed x453, local copies, waits for them, and re-layouts  34.4 us
  transfers between devices with their start and end apart: 81, of which 40 were waited for; matrix products, arithmetic and copies ran while one was open for 35% of the time, Pallas kernels for 3%

profile of v9, /device:TPU:0, one launch (start us, length us, event | category | flops | bytes accessed | tf_op | source)
XLA Modules:
  0.0 1001.0 jit_solution(5811745420602766567)
XLA Ops:
  12.3 6.3 all-to-all-start
  20.6 27.5 %all-to-all-done = bf16[8,48,1536]{2,1,0:T(8,128)(2,1)S(1)} async-done(((bf16[8,48,1536]{2,1,0:T(8,128)(2,1)}), bf16[8,48,1536]{2,1,0:T(8,128)(2,1)S(1)}, u32[]{:S(2)}, u32[]{:S(2)}) %all-to-all-start) | async-done | bytes 1179680 | tf_op jit(solution)/shard_map/all_to_all | solution.py:622
  48.1 8.6 all-gather.8.cloned.1.call-done
  65.6 7.5 collective-permute-done
  73.1 17.1 %collective-permute-done.1 = bf16[128,1664]{1,0:T(8,128)(2,1)S(1)} collective-permute-done((bf16[128,1664]{1,0:T(8,128)(2,1)S(1)}, bf16[128,1664]{1,0:T(8,128)(2,1)S(1)}, u32[]{:S(2)}, u32[]{:S(2)}) %collective-permute-start.1) | collective-permute-done | bytes 426016 | tf_op jit(solution)/shard_map/ppermute | solution.py:93
  98.4 11.8 %all-to-all-start.1 = ((bf16[8,48,768]{2,1,0:T(8,128)(2,1)}), bf16[8,48,768]{2,1,0:T(8,128)(2,1)S(1)}, u32[]{:S(2)}, u32[]{:S(2)}) async-start(bf16[8,48,768]{2,1,0:T(8,128)(2,1)} %copy.607), calls=%async_computation.1 | async-start | bytes 1179648 | tf_op jit(solution)/shard_map/all_to_all | solution.py:622
  116.0 11.0 %all-to-all-done.1 = bf16[8,48,768]{2,1,0:T(8,128)(2,1)S(1)} async-done(((bf16[8,48,768]{2,1,0:T(8,128)(2,1)}), bf16[8,48,768]{2,1,0:T(8,128)(2,1)S(1)}, u32[]{:S(2)}, u32[]{:S(2)}) %all-to-all-start.1) | async-done | bytes 589856 | tf_op jit(solution)/shard_map/all_to_all | solution.py:622
  127.0 4.0 all_to_all.30
  137.4 6.4 fusion.40.proj_ref
  146.3 9.6 scan_forward.1
  155.9 9.6 collective-permute-done.5
  184.8 9.0 collective-permute-done.10
  193.8 8.3 collective-permute-done.8
  202.1 18.3 %collective-permute-done.9 = bf16[128,1664]{1,0:T(8,128)(2,1)S(1)} collective-permute-done((bf16[128,1664]{1,0:T(8,128)(2,1)S(1)}, bf16[128,1664]{1,0:T(8,128)(2,1)S(1)}, u32[]{:S(2)}, u32[]{:S(2)}) %collective-permute-start.9) | collective-permute-done | bytes 426016 | tf_op jit(solution)/shard_map/ppermute | solution.py:93
  226.2 10.1 %collective-permute-done.14 = bf16[128,1536]{1,0:T(8,128)(2,1)S(1)} collective-permute-done((bf16[128,1536]{1,0:T(8,128)(2,1)S(1)}, bf16[128,1536]{1,0:T(8,128)(2,1)S(1)}, u32[]{:S(2)}, u32[]{:S(2)}) %collective-permute-start.14) | collective-permute-done | bytes 393248 | tf_op jit(solution)/shard_map/ppermute | solution.py:93
  236.3 15.9 %collective-permute-done.15 = bf16[128,1536]{1,0:T(8,128)(2,1)S(1)} collective-permute-done((bf16[128,1536]{1,0:T(8,128)(2,1)S(1)}, bf16[128,1536]{1,0:T(8,128)(2,1)S(1)}, u32[]{:S(2)}, u32[]{:S(2)}) %collective-permute-start.15) | collective-permute-done | bytes 393248 | tf_op jit(solution)/shard_map/ppermute | solution.py:93
  253.6 7.9 collective-permute-start.13
  268.1 10.8 %convolution_convert_fusion.4 = bf16[1024,2048]{1,0:T(8,128)(2,1)} fusion(bf16[1536,2048]{1,0:T(8,128)(2,1)} %all-gather.12.cloned.1.call-done, bf16[512,1536]{1,0:T(8,128)(2,1)} %collective-permute-done.17, bf16[128,1536]{1,0:T(8,128)(2,1)} %copy-done.109, bf16[128,1536]{1,0:T(8,128)(2,1)} %copy-done.105, ...), kind=kOutput, calls=%fused_computation.50 | convolution fusion | flops 6460276736 | bytes 13631488 | tf_op jit(solution)/shard_map/dot_general | solution.py:37
  288.5 6.2 fusion.32
  311.8 4.2 collective-permute-start.19
  316.8 8.8 collective-permute-done.19
  325.6 23.3 %collective-permute-done.20 = bf16[128,1536]{1,0:T(8,128)(2,1)S(1)} collective-permute-done((bf16[128,1536]{1,0:T(8,128)(2,1)S(1)}, bf16[128,1536]{1,0:T(8,128)(2,1)S(1)}, u32[]{:S(2)}, u32[]{:S(2)}) %collective-permute-start.20) | collective-permute-done | bytes 393248 | tf_op jit(solution)/shard_map/ppermute | solution.py:93
  378.5 5.1 collective-permute-done.24
  383.5 16.3 %collective-permute-done.25 = bf16[128,1536]{1,0:T(8,128)(2,1)S(1)} collective-permute-done((bf16[128,1536]{1,0:T(8,128)(2,1)S(1)}, bf16[128,1536]{1,0:T(8,128)(2,1)S(1)}, u32[]{:S(2)}, u32[]{:S(2)}) %collective-permute-start.25) | collective-permute-done | bytes 393248 | tf_op jit(solution)/shard_map/ppermute | solution.py:93
  402.3 17.1 %all-gather.18.cloned.1.call-done = bf16[1536,2048]{1,0:T(8,128)(2,1)} async-done(((bf16[384,2048]{1,0:T(8,128)(2,1)}), bf16[1536,2048]{1,0:T(8,128)(2,1)}) %all-gather.18.cloned.1.call-update) | async-done | bytes 6291472 | tf_op jit(solution)/shard_map/all_gather | solution.py:701
  429.7 8.9 convolution_convert_fusion.3
  442.4 6.8 select_reduce_fusion.2
  454.9 9.4 multiply_convert_fusion.4
  464.4 6.7 fusion.185
  484.3 5.0 convolution_convert_fusion.6
  489.2 4.4 collective-permute-done.30
  499.4 11.5 %convolution_convert_fusion.1 = bf16[1536,2048]{1,0:T(8,128)(2,1)} fusion(bf16[1024,2048]{1,0:T(8,128)(2,1)} %pad_maximum_fusion.1, bf16[512,1536]{1,0:T(8,128)(2,1)} %collective-permute-done.27, bf16[128,1536]{1,0:T(8,128)(2,1)} %copy-done.120, bf16[128,1536]{1,0:T(8,128)(2,1)} %copy-done.117, bf16[128,1536]{1,0:T(8,128)(2,1)S(1)} %copy-done.115, ...), kind=kOutput, calls=%fused_computation.12 | convolution fusion | flops 6461325312 | bytes 13631488 | tf_op jit(solution)/shard_map/dot_general | solution.py:37
  510.9 14.1 %collective-permute-done.31 = bf16[128,1664]{1,0:T(8,128)(2,1)} collective-permute-done((bf16[128,1664]{1,0:T(8,128)(2,1)}, bf16[128,1664]{1,0:T(8,128)(2,1)}, u32[]{:S(2)}, u32[]{:S(2)}) %collective-permute-start.31) | collective-permute-done | bytes 426016 | tf_op jit(solution)/shard_map/ppermute | solution.py:93
  528.9 3.9 fusion.30
  576.2 9.9 collective-permute-done.37
  586.1 15.9 %collective-permute-done.38 = bf16[128,1536]{1,0:T(8,128)(2,1)S(1)} collective-permute-done((bf16[128,1536]{1,0:T(8,128)(2,1)S(1)}, bf16[128,1536]{1,0:T(8,128)(2,1)S(1)}, u32[]{:S(2)}, u32[]{:S(2)}) %collective-permute-start.38) | collective-permute-done | bytes 393248 | tf_op jit(solution)/shard_map/ppermute | solution.py:93
  603.3 4.8 fusion.194
  608.2 8.5 collective-permute-start.34
  627.3 7.8 fusion.6
  635.2 8.8 fusion.184
  645.1 7.3 collective-permute-done.41
  671.6 11.2 %collective-permute-start.45 = (bf16[128,1664]{1,0:T(8,128)(2,1)}, bf16[128,1664]{1,0:T(8,128)(2,1)}, u32[]{:S(2)}, u32[]{:S(2)}) collective-permute-start(bf16[128,1664]{1,0:T(8,128)(2,1)} %get-tuple-element.493), channel_id=1, source_target_pairs={{0,4},{2,6},{4,0},{6,2},{1,5},{3,7},{5,1},{7,3},{8,12},{10,14},{12... | collective-permute-start | bytes 1277960 | tf_op jit(solution)/shard_map/ppermute | solution.py:93
  683.1 10.1 %convolution_convert_fusion = bf16[1536,2048]{1,0:T(8,128)(2,1)} fusion(bf16[1024,2048]{1,0:T(8,128)(2,1)S(1)} %pad_maximum_fusion.2, bf16[512,1536]{1,0:T(8,128)(2,1)} %collective-permute-done.17, bf16[128,1536]{1,0:T(8,128)(2,1)S(1)} %copy-done.111, bf16[128,1536]{1,0:T(8,128)(2,1)S(1)} %copy-done.107, bf16[128,1536]{1,0:T(8,128)(2,1)S(1)} %copy-done.103, ...), kind=kOutput, calls=%fused_computation.11 | convolution fusion | flops 6461325312 | bytes 13631488 | tf_op jit(solution)/shard_map/dot_general | solution.py:37
  693.2 18.4 %collective-permute-done.45 = bf16[128,1664]{1,0:T(8,128)(2,1)} collective-permute-done((bf16[128,1664]{1,0:T(8,128)(2,1)}, bf16[128,1664]{1,0:T(8,128)(2,1)}, u32[]{:S(2)}, u32[]{:S(2)}) %collective-permute-start.45) | collective-permute-done | bytes 426016 | tf_op jit(solution)/shard_map/ppermute | solution.py:93
  711.7 7.6 convolution_convert_fusion.5
  738.5 10.2 %collective-permute-done.47 = bf16[128,1664]{1,0:T(8,128)(2,1)S(1)} collective-permute-done((bf16[128,1664]{1,0:T(8,128)(2,1)S(1)}, bf16[128,1664]{1,0:T(8,128)(2,1)S(1)}, u32[]{:S(2)}, u32[]{:S(2)}) %collective-permute-start.47) | collective-permute-done | bytes 426016 | tf_op jit(solution)/shard_map/ppermute | solution.py:93
  748.7 15.7 %collective-permute-done.48 = bf16[128,1664]{1,0:T(8,128)(2,1)S(1)} collective-permute-done((bf16[128,1664]{1,0:T(8,128)(2,1)S(1)}, bf16[128,1664]{1,0:T(8,128)(2,1)S(1)}, u32[]{:S(2)}, u32[]{:S(2)}) %collective-permute-start.48) | collective-permute-done | bytes 426016 | tf_op jit(solution)/shard_map/ppermute | solution.py:93
  777.5 5.5 pad_maximum_fusion.5
  789.0 3.8 fusion.26
  805.2 8.2 collective-permute-start.51
  815.9 4.3 convolution_convert_fusion.12.grad_ref
  820.2 18.3 %scan_backward.1 = (bf16[1024,1152]{1,0:T(8,128)(2,1)S(1)}, f32[8,640]{1,0:T(8,128)S(1)}, f32[8,384]{1,0:T(8,128)S(1)}, f32[8,128]{1,0:T(8,128)S(1)}) custom-call(bf16[1024,1024]{1,0:T(8,128)(2,1)S(1)} %copy-done.1, f32[1024,128]{1,0:T(8,128)S(1)} %copy-done.3, f32[1024,1]{1,0:T(8,128)S(1)} %get-tuple-element.482.col_ref, f32[16,1,64]{2,1,0:T(1,128)S(1)} %bitcast.304, ...), custom_call_target="tpu_custom_call" | custom-call | tf_op jit(solution)/shard_map/scan_backward/pallas_call | solution.py:360
  841.4 8.5 fusion.9
  855.3 7.5 multiply_reduce_fusion
  863.9 3.8 concatenate.246
  871.8 9.6 collective-permute-start.55
  881.4 4.6 fusion.186
  886.0 4.5 collective-permute-done.55
  906.8 4.0 all_to_all.31
  910.9 18.2 %collective-permute-done.56 = bf16[128,1536]{1,0:T(8,128)(2,1)S(1)} collective-permute-done((bf16[128,1536]{1,0:T(8,128)(2,1)}, bf16[128,1536]{1,0:T(8,128)(2,1)S(1)}, u32[]{:S(2)}, u32[]{:S(2)}) %collective-permute-start.56) | collective-permute-done | bytes 393248 | tf_op jit(solution)/shard_map/ppermute | solution.py:93
  930.4 4.2 all-to-all-start.3
  950.1 4.4 collective-permute-start.61
  959.2 4.2 all-to-all-start.4
  970.4 16.1 %all-to-all-done.4 = bf16[8,48,1152]{2,1,0:T(8,128)(2,1)} async-done(((bf16[8,48,1152]{2,1,0:T(8,128)(2,1)}), bf16[8,48,1152]{2,1,0:T(8,128)(2,1)}, u32[]{:S(2)}, u32[]{:S(2)}) %all-to-all-start.4) | async-done | bytes 884768 | tf_op jit(solution)/shard_map/all_to_all | solution.py:992
  (903 shorter events, 365.9 us)
Async XLA Ops:
  7.3 49.4 %all-gather.8.cloned.1.call-start = ((), (), s32[]{:S(2)}) async-start(), calls=%async_computation.13 | async-start | bytes 3932160 | tf_op jit(solution)/shard_map/all_gather | solution.py:661
  12.3 35.7 %all-to-all-start = ((bf16[8,48,1536]{2,1,0:T(8,128)(2,1)}), bf16[8,48,1536]{2,1,0:T(8,128)(2,1)S(1)}, u32[]{:S(2)}, u32[]{:S(2)}) async-start(bf16[8,48,1536]{2,1,0:T(8,128)(2,1)} %copy.606), calls=%async_computation | async-start | bytes 2359296 | tf_op jit(solution)/shard_map/all_to_all | solution.py:622
  18.7 114.5 %all-gather.10.cloned.1.call-start = ((), (), s32[]{:S(2)}) async-start(), calls=%async_computation.14 | async-start | bytes 5898240 | tf_op jit(solution)/shard_map/all_gather | solution.py:626
  56.7 211.3 %all-gather.12.cloned.1.call-start = ((), (), s32[]{:S(2)}) async-start(), calls=%async_computation.15 | async-start | bytes 7864320 | tf_op jit(solution)/shard_map/all_gather | solution.py:701
  58.4 14.7 %collective-permute-start = (bf16[128,1664]{1,0:T(8,128)(2,1)S(1)}, bf16[128,1664]{1,0:T(8,128)(2,1)S(1)}, u32[]{:S(2)}, u32[]{:S(2)}) collective-permute-start(bf16[128,1664]{1,0:T(8,128)(2,1)S(1)} %concatenate.200), channel_id=1, source_target_pairs={{0,2},{2,4},{4,6},{6,0},{1,3},{3,5},{5,7},{7,1},{8,10},{10,12},{12... | collective-permute-start | bytes 1277960 | tf_op jit(solution)/shard_map/ppermute | solution.py:93
  61.7 28.5 %collective-permute-start.1 = (bf16[128,1664]{1,0:T(8,128)(2,1)S(1)}, bf16[128,1664]{1,0:T(8,128)(2,1)S(1)}, u32[]{:S(2)}, u32[]{:S(2)}) collective-permute-start(bf16[128,1664]{1,0:T(8,128)(2,1)S(1)} %concatenate.200), channel_id=1, source_target_pairs={{0,4},{2,6},{4,0},{6,2},{1,5},{3,7},{5,1},{7,3},{8,12},{10,14},{12... | collective-permute-start | bytes 1277960 | tf_op jit(solution)/shard_map/ppermute | solution.py:93
  64.2 26.1 %collective-permute-start.2 = (bf16[128,1664]{1,0:T(8,128)(2,1)S(1)}, bf16[128,1664]{1,0:T(8,128)(2,1)S(1)}, u32[]{:S(2)}, u32[]{:S(2)}) collective-permute-start(bf16[128,1664]{1,0:T(8,128)(2,1)S(1)} %concatenate.200), channel_id=1, source_target_pairs={{0,6},{2,0},{4,2},{6,4},{1,7},{3,1},{5,3},{7,5},{8,14},{10,8},{12,... | collective-permute-start | bytes 1277960 | tf_op jit(solution)/shard_map/ppermute | solution.py:93
  98.4 28.5 %all-to-all-start.1 = ((bf16[8,48,768]{2,1,0:T(8,128)(2,1)}), bf16[8,48,768]{2,1,0:T(8,128)(2,1)S(1)}, u32[]{:S(2)}, u32[]{:S(2)}) async-start(bf16[8,48,768]{2,1,0:T(8,128)(2,1)} %copy.607), calls=%async_computation.1 | async-start | bytes 1179648 | tf_op jit(solution)/shard_map/all_to_all | solution.py:622
  110.2 168.7 %all-gather.14.cloned.1.call-start = ((), (), s32[]{:S(2)}) async-start(), calls=%async_computation.16 | async-start | bytes 2949120 | tf_op jit(solution)/shard_map/all_gather | solution.py:626
  131.0 24.9 %collective-permute-start.4 = (bf16[96,2048]{1,0:T(8,128)(2,1)S(1)}, bf16[96,2048]{1,0:T(8,128)(2,1)S(1)}, u32[]{:S(2)}, u32[]{:S(2)}) collective-permute-start(bf16[96,2048]{1,0:T(8,128)(2,1)S(1)} %bitcast.312), channel_id=1, source_target_pairs={{0,6},{2,0},{4,2},{6,4},{1,7},{3,1},{5,3},{7,5},{8,14},{10,8},{12,... | collective-permute-start | bytes 1179656 | tf_op jit(solution)/shard_map/ppermute | solution.py:93
  132.3 33.3 %collective-permute-start.5 = (bf16[96,2048]{1,0:T(8,128)(2,1)S(1)}, bf16[96,2048]{1,0:T(8,128)(2,1)}, u32[]{:S(2)}, u32[]{:S(2)}) collective-permute-start(bf16[96,2048]{1,0:T(8,128)(2,1)S(1)} %bitcast.313), channel_id=1, source_target_pairs={{0,4},{2,6},{4,0},{6,2},{1,5},{3,7},{5,1},{7,3},{8,12},{10,14},{12... | collective-permute-start | bytes 1179656 | tf_op jit(solution)/shard_map/ppermute | solution.py:93
  132.3 33.3 %collective-permute-start.6 = (bf16[96,2048]{1,0:T(8,128)(2,1)S(1)}, bf16[96,2048]{1,0:T(8,128)(2,1)}, u32[]{:S(2)}, u32[]{:S(2)}) collective-permute-start(bf16[96,2048]{1,0:T(8,128)(2,1)S(1)} %bitcast.314), channel_id=1, source_target_pairs={{0,2},{2,4},{4,6},{6,0},{1,3},{3,5},{5,7},{7,1},{8,10},{10,12},{12... | collective-permute-start | bytes 1179656 | tf_op jit(solution)/shard_map/ppermute | solution.py:93
  133.1 218.4 %all-gather.16.cloned.1.call-start = ((), (), s32[]{:S(2)}) async-start(), calls=%async_computation.17 | async-start | bytes 7864320 | tf_op jit(solution)/shard_map/all_gather | solution.py:771
  171.1 231.3 %all-gather.20.cloned.1.call-start = ((), (), s32[]{:S(2)}) async-start(), calls=%async_computation.19 | async-start | bytes 3932160 | tf_op jit(solution)/shard_map/all_gather | solution.py:661
  179.2 14.6 %collective-permute-start.10 = (bf16[128,1664]{1,0:T(8,128)(2,1)S(1)}, bf16[128,1664]{1,0:T(8,128)(2,1)S(1)}, u32[]{:S(2)}, u32[]{:S(2)}) collective-permute-start(bf16[128,1664]{1,0:T(8,128)(2,1)S(1)} %get-tuple-element.498), channel_id=1, source_target_pairs={{0,2},{2,4},{4,6},{6,0},{1,3},{3,5},{5,7},{7,1},{8,10},{10,12},{12... | collective-permute-start | bytes 1277960 | tf_op jit(solution)/shard_map/ppermute | solution.py:93
  180.8 21.3 %collective-permute-start.8 = (bf16[128,1664]{1,0:T(8,128)(2,1)S(1)}, bf16[128,1664]{1,0:T(8,128)(2,1)S(1)}, u32[]{:S(2)}, u32[]{:S(2)}) collective-permute-start(bf16[128,1664]{1,0:T(8,128)(2,1)S(1)} %get-tuple-element.497), channel_id=1, source_target_pairs={{0,6},{2,0},{4,2},{6,4},{1,7},{3,1},{5,3},{7,5},{8,14},{10,8},{12,... | collective-permute-start | bytes 1277960 | tf_op jit(solution)/shard_map/ppermute | solution.py:93
  183.1 37.2 %collective-permute-start.9 = (bf16[128,1664]{1,0:T(8,128)(2,1)S(1)}, bf16[128,1664]{1,0:T(8,128)(2,1)S(1)}, u32[]{:S(2)}, u32[]{:S(2)}) collective-permute-start(bf16[128,1664]{1,0:T(8,128)(2,1)S(1)} %get-tuple-element.499), channel_id=1, source_target_pairs={{0,4},{2,6},{4,0},{6,2},{1,5},{3,7},{5,1},{7,3},{8,12},{10,14},{12... | collective-permute-start | bytes 1277960 | tf_op jit(solution)/shard_map/ppermute | solution.py:93
  222.4 13.9 %collective-permute-start.14 = (bf16[128,1536]{1,0:T(8,128)(2,1)S(1)}, bf16[128,1536]{1,0:T(8,128)(2,1)S(1)}, u32[]{:S(2)}, u32[]{:S(2)}) collective-permute-start(bf16[128,1536]{1,0:T(8,128)(2,1)S(1)} %multiply_convert_fusion.11), channel_id=1, source_target_pairs={{0,2},{2,4},{4,6},{6,0},{1,3},{3,5},{5,7},{7,1},{8,10},{10,12},{12... | collective-permute-start | bytes 1179656 | tf_op jit(solution)/shard_map/ppermute | solution.py:93
  222.4 29.9 %collective-permute-start.15 = (bf16[128,1536]{1,0:T(8,128)(2,1)S(1)}, bf16[128,1536]{1,0:T(8,128)(2,1)S(1)}, u32[]{:S(2)}, u32[]{:S(2)}) collective-permute-start(bf16[128,1536]{1,0:T(8,128)(2,1)S(1)} %multiply_convert_fusion.11), channel_id=1, source_target_pairs={{0,4},{2,6},{4,0},{6,2},{1,5},{3,7},{5,1},{7,3},{8,12},{10,14},{12... | collective-permute-start | bytes 1179656 | tf_op jit(solution)/shard_map/ppermute | solution.py:93
  225.6 26.7 %collective-permute-start.16 = (bf16[128,1536]{1,0:T(8,128)(2,1)S(1)}, bf16[128,1536]{1,0:T(8,128)(2,1)S(1)}, u32[]{:S(2)}, u32[]{:S(2)}) collective-permute-start(bf16[128,1536]{1,0:T(8,128)(2,1)S(1)} %multiply_convert_fusion.11), channel_id=1, source_target_pairs={{0,6},{2,0},{4,2},{6,4},{1,7},{3,1},{5,3},{7,5},{8,14},{10,8},{12,... | collective-permute-start | bytes 1179656 | tf_op jit(solution)/shard_map/ppermute | solution.py:93
  253.6 14.4 %collective-permute-start.17 = (bf16[512,1536]{1,0:T(8,128)(2,1)}, bf16[512,1536]{1,0:T(8,128)(2,1)}, u32[]{:S(2)}, u32[]{:S(2)}) collective-permute-start(bf16[512,1536]{1,0:T(8,128)(2,1)} %pad_maximum_fusion.11), channel_id=1, source_target_pairs={{0,1},{1,0},{2,3},{3,2},{4,5},{5,4},{6,7},{7,6},{8,9},{9,8},{10,11... | collective-permute-start | bytes 4718600 | tf_op jit(solution)/shard_map/ppermute | solution.py:93
  253.6 25.3 %collective-permute-start.13 = (bf16[128,1536]{1,0:T(8,128)(2,1)S(1)}, bf16[128,1536]{1,0:T(8,128)(2,1)S(1)}, u32[]{:S(2)}, u32[]{:S(2)}) collective-permute-start(bf16[128,1536]{1,0:T(8,128)(2,1)S(1)} %bitcast.307), channel_id=1, source_target_pairs={{0,2},{2,4},{4,6},{6,0},{1,3},{3,5},{5,7},{7,1},{8,10},{10,12},{12... | collective-permute-start | bytes 1179656 | tf_op jit(solution)/shard_map/ppermute | solution.py:93
  261.6 33.2 %collective-permute-start.11 = (bf16[128,1536]{1,0:T(8,128)(2,1)S(1)}, bf16[128,1536]{1,0:T(8,128)(2,1)S(1)}, u32[]{:S(2)}, u32[]{:S(2)}) collective-permute-start(bf16[128,1536]{1,0:T(8,128)(2,1)S(1)} %bitcast.308), channel_id=1, source_target_pairs={{0,4},{2,6},{4,0},{6,2},{1,5},{3,7},{5,1},{7,3},{8,12},{10,14},{12... | collective-permute-start | bytes 1179656 | tf_op jit(solution)/shard_map/ppermute | solution.py:93
  261.6 33.2 %collective-permute-start.12 = (bf16[128,1536]{1,0:T(8,128)(2,1)S(1)}, bf16[128,1536]{1,0:T(8,128)(2,1)}, u32[]{:S(2)}, u32[]{:S(2)}) collective-permute-start(bf16[128,1536]{1,0:T(8,128)(2,1)S(1)} %bitcast.309), channel_id=1, source_target_pairs={{0,6},{2,0},{4,2},{6,4},{1,7},{3,1},{5,3},{7,5},{8,14},{10,8},{12,... | collective-permute-start | bytes 1179656 | tf_op jit(solution)/shard_map/ppermute | solution.py:93
  264.0 155.4 %all-gather.18.cloned.1.call-start = ((), (), s32[]{:S(2)}) async-start(), calls=%async_computation.18 | async-start | bytes 7864320 | tf_op jit(solution)/shard_map/all_gather | solution.py:701
  306.5 420.4 %reduce-scatter.10.cloned.1.call-start = ((), (), s32[]{:S(2)}) async-start(), calls=%async_computation.21 | async-start | bytes 3932160 | tf_op jit(solution)/shard_map/reduce_scatter | solution.py:821
  311.8 13.7 %collective-permute-start.19 = (bf16[128,1536]{1,0:T(8,128)(2,1)S(1)}, bf16[128,1536]{1,0:T(8,128)(2,1)S(1)}, u32[]{:S(2)}, u32[]{:S(2)}) collective-permute-start(bf16[128,1536]{1,0:T(8,128)(2,1)S(1)} %get-tuple-element.525), channel_id=1, source_target_pairs={{0,6},{2,0},{4,2},{6,4},{1,7},{3,1},{5,3},{7,5},{8,14},{10,8},{12,... | collective-permute-start | bytes 1179656 | tf_op jit(solution)/shard_map/ppermute | solution.py:93
  316.0 32.9 %collective-permute-start.20 = (bf16[128,1536]{1,0:T(8,128)(2,1)S(1)}, bf16[128,1536]{1,0:T(8,128)(2,1)S(1)}, u32[]{:S(2)}, u32[]{:S(2)}) collective-permute-start(bf16[128,1536]{1,0:T(8,128)(2,1)S(1)} %get-tuple-element.527), channel_id=1, source_target_pairs={{0,4},{2,6},{4,0},{6,2},{1,5},{3,7},{5,1},{7,3},{8,12},{10,14},{12... | collective-permute-start | bytes 1179656 | tf_op jit(solution)/shard_map/ppermute | solution.py:93
  316.0 32.9 %collective-permute-start.21 = (bf16[128,1536]{1,0:T(8,128)(2,1)S(1)}, bf16[128,1536]{1,0:T(8,128)(2,1)S(1)}, u32[]{:S(2)}, u32[]{:S(2)}) collective-permute-start(bf16[128,1536]{1,0:T(8,128)(2,1)S(1)} %get-tuple-element.526), channel_id=1, source_target_pairs={{0,2},{2,4},{4,6},{6,0},{1,3},{3,5},{5,7},{7,1},{8,10},{10,12},{12... | collective-permute-start | bytes 1179656 | tf_op jit(solution)/shard_map/ppermute | solution.py:93
  369.6 13.9 %collective-permute-start.24 = (bf16[128,1536]{1,0:T(8,128)(2,1)S(1)}, bf16[128,1536]{1,0:T(8,128)(2,1)S(1)}, u32[]{:S(2)}, u32[]{:S(2)}) collective-permute-start(bf16[128,1536]{1,0:T(8,128)(2,1)S(1)} %multiply_convert_fusion.9), channel_id=1, source_target_pairs={{0,2},{2,4},{4,6},{6,0},{1,3},{3,5},{5,7},{7,1},{8,10},{10,12},{12... | collective-permute-start | bytes 1179656 | tf_op jit(solution)/shard_map/ppermute | solution.py:93
  371.4 28.4 %collective-permute-start.25 = (bf16[128,1536]{1,0:T(8,128)(2,1)S(1)}, bf16[128,1536]{1,0:T(8,128)(2,1)S(1)}, u32[]{:S(2)}, u32[]{:S(2)}) collective-permute-start(bf16[128,1536]{1,0:T(8,128)(2,1)S(1)} %multiply_convert_fusion.9), channel_id=1, source_target_pairs={{0,4},{2,6},{4,0},{6,2},{1,5},{3,7},{5,1},{7,3},{8,12},{10,14},{12... | collective-permute-start | bytes 1179656 | tf_op jit(solution)/shard_map/ppermute | solution.py:93
  373.4 26.4 %collective-permute-start.26 = (bf16[128,1536]{1,0:T(8,128)(2,1)S(1)}, bf16[128,1536]{1,0:T(8,128)(2,1)S(1)}, u32[]{:S(2)}, u32[]{:S(2)}) collective-permute-start(bf16[128,1536]{1,0:T(8,128)(2,1)S(1)} %multiply_convert_fusion.9), channel_id=1, source_target_pairs={{0,6},{2,0},{4,2},{6,4},{1,7},{3,1},{5,3},{7,5},{8,14},{10,8},{12,... | collective-permute-start | bytes 1179656 | tf_op jit(solution)/shard_map/ppermute | solution.py:93
  378.5 41.0 %collective-permute-start.28 = (bf16[512,1536]{1,0:T(8,128)(2,1)}, bf16[512,1536]{1,0:T(8,128)(2,1)}, u32[]{:S(2)}, u32[]{:S(2)}) collective-permute-start(bf16[512,1536]{1,0:T(8,128)(2,1)} %pad_maximum_fusion.15), channel_id=1, source_target_pairs={{0,1},{1,0},{2,3},{3,2},{4,5},{5,4},{6,7},{7,6},{8,9},{9,8},{10,11... | collective-permute-start | bytes 4718600 | tf_op jit(solution)/shard_map/ppermute | solution.py:93
  401.3 20.0 %collective-permute-start.27 = (bf16[512,1536]{1,0:T(8,128)(2,1)}, bf16[512,1536]{1,0:T(8,128)(2,1)}, u32[]{:S(2)}, u32[]{:S(2)}) collective-permute-start(bf16[512,1536]{1,0:T(8,128)(2,1)} %pad_maximum_fusion.13), channel_id=1, source_target_pairs={{0,1},{1,0},{2,3},{3,2},{4,5},{5,4},{6,7},{7,6},{8,9},{9,8},{10,11... | collective-permute-start | bytes 4718600 | tf_op jit(solution)/shard_map/ppermute | solution.py:93
  494.4 232.4 %reduce-scatter.8.cloned.1.call-start = ((), (), s32[]{:S(2)}) async-start(), calls=%async_computation.20 | async-start | bytes 7864320 | tf_op jit(solution)/shard_map/reduce_scatter | solution.py:817
  494.5 30.6 %collective-permute-start.31 = (bf16[128,1664]{1,0:T(8,128)(2,1)}, bf16[128,1664]{1,0:T(8,128)(2,1)}, u32[]{:S(2)}, u32[]{:S(2)}) collective-permute-start(bf16[128,1664]{1,0:T(8,128)(2,1)} %get-tuple-element.496), channel_id=1, source_target_pairs={{0,4},{2,6},{4,0},{6,2},{1,5},{3,7},{5,1},{7,3},{8,12},{10,14},{12... | collective-permute-start | bytes 1277960 | tf_op jit(solution)/shard_map/ppermute | solution.py:93
  496.1 28.9 %collective-permute-start.32 = (bf16[128,1664]{1,0:T(8,128)(2,1)}, bf16[128,1664]{1,0:T(8,128)(2,1)}, u32[]{:S(2)}, u32[]{:S(2)}) collective-permute-start(bf16[128,1664]{1,0:T(8,128)(2,1)} %get-tuple-element.495), channel_id=1, source_target_pairs={{0,2},{2,4},{4,6},{6,0},{1,3},{3,5},{5,7},{7,1},{8,10},{10,12},{12... | collective-permute-start | bytes 1277960 | tf_op jit(solution)/shard_map/ppermute | solution.py:93
  525.1 278.7 %reduce-scatter.14.cloned.1.call-start = ((), (), s32[]{:S(2)}) async-start(), calls=%async_computation.23 | async-start | bytes 7864320 | tf_op jit(solution)/shard_map/reduce_scatter | solution.py:898
  541.4 61.9 %collective-permute-start.33 = (bf16[512,1536]{1,0:T(8,128)(2,1)}, bf16[512,1536]{1,0:T(8,128)(2,1)}, u32[]{:S(2)}, u32[]{:S(2)}) collective-permute-start(bf16[512,1536]{1,0:T(8,128)(2,1)} %slice.1149), channel_id=1, source_target_pairs={{0,1},{1,0},{2,3},{3,2},{4,5},{5,4},{6,7},{7,6},{8,9},{9,8},{10,11... | collective-permute-start | bytes 4718600 | tf_op jit(solution)/shard_map/ppermute | solution.py:93
  572.2 13.9 %collective-permute-start.37 = (bf16[128,1536]{1,0:T(8,128)(2,1)S(1)}, bf16[128,1536]{1,0:T(8,128)(2,1)S(1)}, u32[]{:S(2)}, u32[]{:S(2)}) collective-permute-start(bf16[128,1536]{1,0:T(8,128)(2,1)S(1)} %get-tuple-element.456), channel_id=1, source_target_pairs={{0,2},{2,4},{4,6},{6,0},{1,3},{3,5},{5,7},{7,1},{8,10},{10,12},{12... | collective-permute-start | bytes 1179656 | tf_op jit(solution)/shard_map/ppermute | solution.py:93
  572.2 29.7 %collective-permute-start.38 = (bf16[128,1536]{1,0:T(8,128)(2,1)S(1)}, bf16[128,1536]{1,0:T(8,128)(2,1)S(1)}, u32[]{:S(2)}, u32[]{:S(2)}) collective-permute-start(bf16[128,1536]{1,0:T(8,128)(2,1)S(1)} %get-tuple-element.456), channel_id=1, source_target_pairs={{0,4},{2,6},{4,0},{6,2},{1,5},{3,7},{5,1},{7,3},{8,12},{10,14},{12... | collective-permute-start | bytes 1179656 | tf_op jit(solution)/shard_map/ppermute | solution.py:93
  573.3 28.7 %collective-permute-start.39 = (bf16[128,1536]{1,0:T(8,128)(2,1)S(1)}, bf16[128,1536]{1,0:T(8,128)(2,1)S(1)}, u32[]{:S(2)}, u32[]{:S(2)}) collective-permute-start(bf16[128,1536]{1,0:T(8,128)(2,1)S(1)} %get-tuple-element.456), channel_id=1, source_target_pairs={{0,6},{2,0},{4,2},{6,4},{1,7},{3,1},{5,3},{7,5},{8,14},{10,8},{12,... | collective-permute-start | bytes 1179656 | tf_op jit(solution)/shard_map/ppermute | solution.py:93
  603.2 14.4 %collective-permute-start.40 = (bf16[512,1536]{1,0:T(8,128)(2,1)}, bf16[512,1536]{1,0:T(8,128)(2,1)}, u32[]{:S(2)}, u32[]{:S(2)}) collective-permute-start(bf16[512,1536]{1,0:T(8,128)(2,1)} %pad_maximum_fusion.16), channel_id=1, source_target_pairs={{0,1},{1,0},{2,3},{3,2},{4,5},{5,4},{6,7},{7,6},{8,9},{9,8},{10,11... | collective-permute-start | bytes 4718600 | tf_op jit(solution)/shard_map/ppermute | solution.py:93
  603.3 246.7 %reduce-scatter.16.cloned.1.call-start = ((), (), s32[]{:S(2)}) async-start(), calls=%async_computation.24 | async-start | bytes 7864320 | tf_op jit(solution)/shard_map/reduce_scatter | solution.py:817
  608.2 18.0 %collective-permute-start.34 = (bf16[128,1536]{1,0:T(8,128)(2,1)S(1)}, bf16[128,1536]{1,0:T(8,128)(2,1)S(1)}, u32[]{:S(2)}, u32[]{:S(2)}) collective-permute-start(bf16[128,1536]{1,0:T(8,128)(2,1)S(1)} %get-tuple-element.516), channel_id=1, source_target_pairs={{0,6},{2,0},{4,2},{6,4},{1,7},{3,1},{5,3},{7,5},{8,14},{10,8},{12,... | collective-permute-start | bytes 1179656 | tf_op jit(solution)/shard_map/ppermute | solution.py:93
  616.7 35.7 %collective-permute-start.41 = (bf16[128,1536]{1,0:T(8,128)(2,1)S(1)}, bf16[128,1536]{1,0:T(8,128)(2,1)S(1)}, u32[]{:S(2)}, u32[]{:S(2)}) collective-permute-start(bf16[128,1536]{1,0:T(8,128)(2,1)S(1)} %get-tuple-element.518), channel_id=1, source_target_pairs={{0,4},{2,6},{4,0},{6,2},{1,5},{3,7},{5,1},{7,3},{8,12},{10,14},{12... | collective-permute-start | bytes 1179656 | tf_op jit(solution)/shard_map/ppermute | solution.py:93
  617.6 34.9 %collective-permute-start.42 = (bf16[128,1536]{1,0:T(8,128)(2,1)S(1)}, bf16[128,1536]{1,0:T(8,128)(2,1)S(1)}, u32[]{:S(2)}, u32[]{:S(2)}) collective-permute-start(bf16[128,1536]{1,0:T(8,128)(2,1)S(1)} %get-tuple-element.517), channel_id=1, source_target_pairs={{0,2},{2,4},{4,6},{6,0},{1,3},{3,5},{5,7},{7,1},{8,10},{10,12},{12... | collective-permute-start | bytes 1179656 | tf_op jit(solution)/shard_map/ppermute | solution.py:93
  671.6 39.9 %collective-permute-start.45 = (bf16[128,1664]{1,0:T(8,128)(2,1)}, bf16[128,1664]{1,0:T(8,128)(2,1)}, u32[]{:S(2)}, u32[]{:S(2)}) collective-permute-start(bf16[128,1664]{1,0:T(8,128)(2,1)} %get-tuple-element.493), channel_id=1, source_target_pairs={{0,4},{2,6},{4,0},{6,2},{1,5},{3,7},{5,1},{7,3},{8,12},{10,14},{12... | collective-permute-start | bytes 1277960 | tf_op jit(solution)/shard_map/ppermute | solution.py:93
  682.9 28.7 %collective-permute-start.46 = (bf16[128,1664]{1,0:T(8,128)(2,1)S(1)}, bf16[128,1664]{1,0:T(8,128)(2,1)}, u32[]{:S(2)}, u32[]{:S(2)}) collective-permute-start(bf16[128,1664]{1,0:T(8,128)(2,1)S(1)} %get-tuple-element.492), channel_id=1, source_target_pairs={{0,2},{2,4},{4,6},{6,0},{1,3},{3,5},{5,7},{7,1},{8,10},{10,12},{12... | collective-permute-start | bytes 1277960 | tf_op jit(solution)/shard_map/ppermute | solution.py:93
  711.6 185.6 %reduce-scatter.20.cloned.1.call-start = ((), (), s32[]{:S(2)}) async-start(), calls=%async_computation.26 | async-start | bytes 3932160 | tf_op jit(solution)/shard_map/reduce_scatter | solution.py:821
  723.8 206.5 %reduce-scatter.12.cloned.1.call-start = ((), (), s32[]{:S(2)}) async-start(), calls=%async_computation.22 | async-start | bytes 4423680 | tf_op jit(solution)/shard_map/reduce_scatter | solution.py:989
  734.0 14.7 %collective-permute-start.47 = (bf16[128,1664]{1,0:T(8,128)(2,1)S(1)}, bf16[128,1664]{1,0:T(8,128)(2,1)S(1)}, u32[]{:S(2)}, u32[]{:S(2)}) collective-permute-start(bf16[128,1664]{1,0:T(8,128)(2,1)S(1)} %concatenate.234), channel_id=1, source_target_pairs={{0,2},{2,4},{4,6},{6,0},{1,3},{3,5},{5,7},{7,1},{8,10},{10,12},{12... | collective-permute-start | bytes 1277960 | tf_op jit(solution)/shard_map/ppermute | solution.py:93
  734.2 30.3 %collective-permute-start.48 = (bf16[128,1664]{1,0:T(8,128)(2,1)S(1)}, bf16[128,1664]{1,0:T(8,128)(2,1)S(1)}, u32[]{:S(2)}, u32[]{:S(2)}) collective-permute-start(bf16[128,1664]{1,0:T(8,128)(2,1)S(1)} %concatenate.234), channel_id=1, source_target_pairs={{0,4},{2,6},{4,0},{6,2},{1,5},{3,7},{5,1},{7,3},{8,12},{10,14},{12... | collective-permute-start | bytes 1277960 | tf_op jit(solution)/shard_map/ppermute | solution.py:93
  736.3 28.2 %collective-permute-start.49 = (bf16[128,1664]{1,0:T(8,128)(2,1)S(1)}, bf16[128,1664]{1,0:T(8,128)(2,1)S(1)}, u32[]{:S(2)}, u32[]{:S(2)}) collective-permute-start(bf16[128,1664]{1,0:T(8,128)(2,1)S(1)} %concatenate.234), channel_id=1, source_target_pairs={{0,6},{2,0},{4,2},{6,4},{1,7},{3,1},{5,3},{7,5},{8,14},{10,8},{12,... | collective-permute-start | bytes 1277960 | tf_op jit(solution)/shard_map/ppermute | solution.py:93
  800.3 158.8 %reduce-scatter.18.cloned.1.call-start = ((), (), s32[]{:S(2)}) async-start(), calls=%async_computation.25 | async-start | bytes 4423680 | tf_op jit(solution)/shard_map/reduce_scatter | solution.py:989
  805.2 33.3 %collective-permute-start.51 = (bf16[96,2048]{1,0:T(8,128)(2,1)S(1)}, bf16[96,2048]{1,0:T(8,128)(2,1)S(1)}, u32[]{:S(2)}, u32[]{:S(2)}) collective-permute-start(bf16[96,2048]{1,0:T(8,128)(2,1)S(1)} %get-tuple-element.509), channel_id=1, source_target_pairs={{0,2},{2,4},{4,6},{6,0},{1,3},{3,5},{5,7},{7,1},{8,10},{10,12},{12... | collective-permute-start | bytes 1179656 | tf_op jit(solution)/shard_map/ppermute | solution.py:93
  813.4 28.0 %collective-permute-start.52 = (bf16[96,2048]{1,0:T(8,128)(2,1)S(1)}, bf16[96,2048]{1,0:T(8,128)(2,1)S(1)}, u32[]{:S(2)}, u32[]{:S(2)}) collective-permute-start(bf16[96,2048]{1,0:T(8,128)(2,1)S(1)} %get-tuple-element.507), channel_id=1, source_target_pairs={{0,4},{2,6},{4,0},{6,2},{1,5},{3,7},{5,1},{7,3},{8,12},{10,14},{12... | collective-permute-start | bytes 1179656 | tf_op jit(solution)/shard_map/ppermute | solution.py:93
  815.3 34.6 %collective-permute-start.53 = (bf16[96,2048]{1,0:T(8,128)(2,1)S(1)}, bf16[96,2048]{1,0:T(8,128)(2,1)}, u32[]{:S(2)}, u32[]{:S(2)}) collective-permute-start(bf16[96,2048]{1,0:T(8,128)(2,1)S(1)} %get-tuple-element.508), channel_id=1, source_target_pairs={{0,6},{2,0},{4,2},{6,4},{1,7},{3,1},{5,3},{7,5},{8,14},{10,8},{12,... | collective-permute-start | bytes 1179656 | tf_op jit(solution)/shard_map/ppermute | solution.py:93
  853.2 14.6 %collective-permute-start.54 = (bf16[512,1536]{1,0:T(8,128)(2,1)}, bf16[512,1536]{1,0:T(8,128)(2,1)}, u32[]{:S(2)}, u32[]{:S(2)}) collective-permute-start(bf16[512,1536]{1,0:T(8,128)(2,1)} %slice.1148), channel_id=1, source_target_pairs={{0,1},{1,0},{2,3},{3,2},{4,5},{5,4},{6,7},{7,6},{8,9},{9,8},{10,11... | collective-permute-start | bytes 4718600 | tf_op jit(solution)/shard_map/ppermute | solution.py:93
  871.8 18.7 %collective-permute-start.55 = (bf16[128,1536]{1,0:T(8,128)(2,1)S(1)}, bf16[128,1536]{1,0:T(8,128)(2,1)S(1)}, u32[]{:S(2)}, u32[]{:S(2)}) collective-permute-start(bf16[128,1536]{1,0:T(8,128)(2,1)S(1)} %get-tuple-element.504), channel_id=1, source_target_pairs={{0,6},{2,0},{4,2},{6,4},{1,7},{3,1},{5,3},{7,5},{8,14},{10,8},{12,... | collective-permute-start | bytes 1179656 | tf_op jit(solution)/shard_map/ppermute | solution.py:93
  900.1 29.0 %collective-permute-start.56 = (bf16[128,1536]{1,0:T(8,128)(2,1)}, bf16[128,1536]{1,0:T(8,128)(2,1)S(1)}, u32[]{:S(2)}, u32[]{:S(2)}) collective-permute-start(bf16[128,1536]{1,0:T(8,128)(2,1)} %get-tuple-element.506), channel_id=1, source_target_pairs={{0,4},{2,6},{4,0},{6,2},{1,5},{3,7},{5,1},{7,3},{8,12},{10,14},{12... | collective-permute-start | bytes 1179656 | tf_op jit(solution)/shard_map/ppermute | solution.py:93
  901.7 27.5 %collective-permute-start.57 = (bf16[128,1536]{1,0:T(8,128)(2,1)S(1)}, bf16[128,1536]{1,0:T(8,128)(2,1)S(1)}, u32[]{:S(2)}, u32[]{:S(2)}) collective-permute-start(bf16[128,1536]{1,0:T(8,128)(2,1)S(1)} %get-tuple-element.505), channel_id=1, source_target_pairs={{0,2},{2,4},{4,6},{6,0},{1,3},{3,5},{5,7},{7,1},{8,10},{10,12},{12... | collective-permute-start | bytes 1179656 | tf_op jit(solution)/shard_map/ppermute | solution.py:93
  930.4 27.5 %all-to-all-start.3 = ((bf16[8,48,1152]{2,1,0:T(8,128)(2,1)}), bf16[8,48,1152]{2,1,0:T(8,128)(2,1)}, u32[]{:S(2)}, u32[]{:S(2)}) async-start(bf16[8,48,1152]{2,1,0:T(8,128)(2,1)} %bitcast.332), calls=%async_computation.9 | async-start | bytes 1769472 | tf_op jit(solution)/shard_map/all_to_all | solution.py:992
  959.2 27.3 %all-to-all-start.4 = ((bf16[8,48,1152]{2,1,0:T(8,128)(2,1)}), bf16[8,48,1152]{2,1,0:T(8,128)(2,1)}, u32[]{:S(2)}, u32[]{:S(2)}) async-start(bf16[8,48,1152]{2,1,0:T(8,128)(2,1)} %bitcast.333), calls=%async_computation.10 | async-start | bytes 1769472 | tf_op jit(solution)/shard_map/all_to_all | solution.py:992
  (228 other events, 2108.1 us)
Sparse Core Ops, SparseCore 0:
  10.0 46.6 all-gather.7
  59.1 57.0 all-gather.9
  118.7 70.1 all-gather.11
  191.2 37.4 all-gather.13
  230.9 70.1 all-gather.15
  302.8 43.9 all-gather.19
  349.2 70.1 all-gather.17
  494.6 44.8 reduce-scatter.9
  542.5 70.1 reduce-scatter.7
  615.5 70.2 reduce-scatter.13
  711.7 68.4 reduce-scatter.15
  783.0 43.9 reduce-scatter.19
  830.1 47.2 reduce-scatter.11
  893.7 47.7 reduce-scatter.17

commit v10 on v9

--- a/solution.py
+++ b/solution.py
@@ -1027,7 +1027,7 @@
     spare = step_width - heads - small_cols
     g_scan = jnp.pad(g_scan, ((0, 0), (0, step_width - 128)))
     g_m = rows_sum((g_scan + jnp.pad(little, ((0, 0), (in_width + heads, spare)))).astype(bf16))
-    g_m, g_s = fence(g_m, g_s)
+    g_m, g_s, head_grad = fence(g_m, g_s, head_grad)
     g_m = rows_back(g_m)
     grads_in = []
     for m in each:
@@ -1052,7 +1052,6 @@
     out_conv_w = vec[gate_here + conv_here : vec_len].reshape(CK, conv_here)
 
     head_grad = lax.dynamic_update_slice(jnp.zeros((8, 128), f32), head_grad, (0, slot * heads))
-    head_grad, mamba_back[-1] = fence(head_grad, mamba_back[-1])
     for axis in ALL:
         size = lax.axis_size(axis)
         step = 1

time: 1010 us -> 1020 us (level)
  transfers between devices with their start and end apart: 81 -> 81, of which waited for: 40 -> 39; matrix products, arithmetic and copies ran while one was open for 35% -> 35% of each run, Pallas kernels for 3% -> 3%
where the time goes in v10:
time: 1020 us; the launch traced here: 1010 us
  waiting for transfers between devices  382 us (37%)
  matrix products  189 us (19%)
  other arithmetic  141 us (14%)
  starting transfers between devices  139 us (14%)
  local copies, waits for them, and re-layouts  101 us (10%)
  Pallas kernels  27.9 us (3%)
  between operations  17.8 us (2%)
    ppermute x63, waiting for transfers between devices, send(): return by_rows(lax.ppermute(by_rows(x), axis, pairs))  300 us
    dot_general x44, matrix products, dot(): r = lax.dot_general(a, b, (dims, ((), ())), preferred_element_type=f32)  180 us
    ppermute x63, starting transfers between devices, send(): return by_rows(lax.ppermute(by_rows(x), axis, pairs))  111 us
    all_to_all x2, waiting for transfers between devices, moved_columns(): moved = lax.all_to_all(packed, TP, split_axis=0, concat_axis=0, tiled=True)  38.5 us
    unnamed x453, local copies, waits for them, and re-layouts  34.4 us
  transfers between devices with their start and end apart: 81, of which 39 were waited for; matrix products, arithmetic and copies ran while one was open for 35% of the time, Pallas kernels for 3%

profile of v10, /device:TPU:0, one launch (start us, length us, event | category | flops | bytes accessed | tf_op | source)
XLA Modules:
  0.0 1005.5 jit_solution(7896655850384632571)
XLA Ops:
  12.3 6.3 all-to-all-start
  20.6 27.5 %all-to-all-done = bf16[8,48,1536]{2,1,0:T(8,128)(2,1)S(1)} async-done(((bf16[8,48,1536]{2,1,0:T(8,128)(2,1)}), bf16[8,48,1536]{2,1,0:T(8,128)(2,1)S(1)}, u32[]{:S(2)}, u32[]{:S(2)}) %all-to-all-start) | async-done | bytes 1179680 | tf_op jit(solution)/shard_map/all_to_all | solution.py:622
  48.1 8.6 all-gather.8.cloned.1.call-done
  65.6 7.5 collective-permute-done
  73.1 17.1 %collective-permute-done.1 = bf16[128,1664]{1,0:T(8,128)(2,1)S(1)} collective-permute-done((bf16[128,1664]{1,0:T(8,128)(2,1)S(1)}, bf16[128,1664]{1,0:T(8,128)(2,1)S(1)}, u32[]{:S(2)}, u32[]{:S(2)}) %collective-permute-start.1) | collective-permute-done | bytes 426016 | tf_op jit(solution)/shard_map/ppermute | solution.py:93
  98.4 11.8 %all-to-all-start.1 = ((bf16[8,48,768]{2,1,0:T(8,128)(2,1)}), bf16[8,48,768]{2,1,0:T(8,128)(2,1)S(1)}, u32[]{:S(2)}, u32[]{:S(2)}) async-start(bf16[8,48,768]{2,1,0:T(8,128)(2,1)} %copy.607), calls=%async_computation.1 | async-start | bytes 1179648 | tf_op jit(solution)/shard_map/all_to_all | solution.py:622
  116.0 11.0 %all-to-all-done.1 = bf16[8,48,768]{2,1,0:T(8,128)(2,1)S(1)} async-done(((bf16[8,48,768]{2,1,0:T(8,128)(2,1)}), bf16[8,48,768]{2,1,0:T(8,128)(2,1)S(1)}, u32[]{:S(2)}, u32[]{:S(2)}) %all-to-all-start.1) | async-done | bytes 589856 | tf_op jit(solution)/shard_map/all_to_all | solution.py:622
  127.0 4.0 all_to_all.30
  137.4 6.4 fusion.40.proj_ref
  146.3 9.6 scan_forward.1
  155.9 9.6 collective-permute-done.5
  184.8 9.0 collective-permute-done.10
  193.8 8.3 collective-permute-done.8
  202.1 18.3 %collective-permute-done.9 = bf16[128,1664]{1,0:T(8,128)(2,1)S(1)} collective-permute-done((bf16[128,1664]{1,0:T(8,128)(2,1)S(1)}, bf16[128,1664]{1,0:T(8,128)(2,1)S(1)}, u32[]{:S(2)}, u32[]{:S(2)}) %collective-permute-start.9) | collective-permute-done | bytes 426016 | tf_op jit(solution)/shard_map/ppermute | solution.py:93
  226.2 10.1 %collective-permute-done.14 = bf16[128,1536]{1,0:T(8,128)(2,1)S(1)} collective-permute-done((bf16[128,1536]{1,0:T(8,128)(2,1)S(1)}, bf16[128,1536]{1,0:T(8,128)(2,1)S(1)}, u32[]{:S(2)}, u32[]{:S(2)}) %collective-permute-start.14) | collective-permute-done | bytes 393248 | tf_op jit(solution)/shard_map/ppermute | solution.py:93
  236.3 15.9 %collective-permute-done.15 = bf16[128,1536]{1,0:T(8,128)(2,1)S(1)} collective-permute-done((bf16[128,1536]{1,0:T(8,128)(2,1)S(1)}, bf16[128,1536]{1,0:T(8,128)(2,1)S(1)}, u32[]{:S(2)}, u32[]{:S(2)}) %collective-permute-start.15) | collective-permute-done | bytes 393248 | tf_op jit(solution)/shard_map/ppermute | solution.py:93
  253.6 7.9 collective-permute-start.13
  268.1 10.8 %convolution_convert_fusion.4 = bf16[1024,2048]{1,0:T(8,128)(2,1)} fusion(bf16[1536,2048]{1,0:T(8,128)(2,1)} %all-gather.12.cloned.1.call-done, bf16[512,1536]{1,0:T(8,128)(2,1)} %collective-permute-done.17, bf16[128,1536]{1,0:T(8,128)(2,1)} %copy-done.109, bf16[128,1536]{1,0:T(8,128)(2,1)} %copy-done.105, ...), kind=kOutput, calls=%fused_computation.50 | convolution fusion | flops 6460276736 | bytes 13631488 | tf_op jit(solution)/shard_map/dot_general | solution.py:37
  288.5 6.2 fusion.32
  311.8 4.2 collective-permute-start.19
  316.8 8.8 collective-permute-done.19
  325.6 23.3 %collective-permute-done.20 = bf16[128,1536]{1,0:T(8,128)(2,1)S(1)} collective-permute-done((bf16[128,1536]{1,0:T(8,128)(2,1)S(1)}, bf16[128,1536]{1,0:T(8,128)(2,1)S(1)}, u32[]{:S(2)}, u32[]{:S(2)}) %collective-permute-start.20) | collective-permute-done | bytes 393248 | tf_op jit(solution)/shard_map/ppermute | solution.py:93
  378.5 5.1 collective-permute-done.24
  383.5 16.3 %collective-permute-done.25 = bf16[128,1536]{1,0:T(8,128)(2,1)S(1)} collective-permute-done((bf16[128,1536]{1,0:T(8,128)(2,1)S(1)}, bf16[128,1536]{1,0:T(8,128)(2,1)S(1)}, u32[]{:S(2)}, u32[]{:S(2)}) %collective-permute-start.25) | collective-permute-done | bytes 393248 | tf_op jit(solution)/shard_map/ppermute | solution.py:93
  402.3 17.1 %all-gather.18.cloned.1.call-done = bf16[1536,2048]{1,0:T(8,128)(2,1)} async-done(((bf16[384,2048]{1,0:T(8,128)(2,1)}), bf16[1536,2048]{1,0:T(8,128)(2,1)}) %all-gather.18.cloned.1.call-update) | async-done | bytes 6291472 | tf_op jit(solution)/shard_map/all_gather | solution.py:701
  429.7 8.9 convolution_convert_fusion.3
  442.4 6.8 select_reduce_fusion.2
  454.9 9.4 multiply_convert_fusion.4
  464.4 6.7 fusion.186
  484.3 5.0 convolution_convert_fusion.6
  489.2 4.4 collective-permute-done.30
  499.4 11.5 %convolution_convert_fusion.1 = bf16[1536,2048]{1,0:T(8,128)(2,1)} fusion(bf16[1024,2048]{1,0:T(8,128)(2,1)} %pad_maximum_fusion.1, bf16[512,1536]{1,0:T(8,128)(2,1)} %collective-permute-done.27, bf16[128,1536]{1,0:T(8,128)(2,1)} %copy-done.120, bf16[128,1536]{1,0:T(8,128)(2,1)} %copy-done.117, bf16[128,1536]{1,0:T(8,128)(2,1)S(1)} %copy-done.115, ...), kind=kOutput, calls=%fused_computation.12 | convolution fusion | flops 6461325312 | bytes 13631488 | tf_op jit(solution)/shard_map/dot_general | solution.py:37
  510.9 14.1 %collective-permute-done.31 = bf16[128,1664]{1,0:T(8,128)(2,1)} collective-permute-done((bf16[128,1664]{1,0:T(8,128)(2,1)}, bf16[128,1664]{1,0:T(8,128)(2,1)}, u32[]{:S(2)}, u32[]{:S(2)}) %collective-permute-start.31) | collective-permute-done | bytes 426016 | tf_op jit(solution)/shard_map/ppermute | solution.py:93
  528.9 3.9 fusion.30
  576.2 9.9 collective-permute-done.37
  586.1 15.9 %collective-permute-done.38 = bf16[128,1536]{1,0:T(8,128)(2,1)S(1)} collective-permute-done((bf16[128,1536]{1,0:T(8,128)(2,1)S(1)}, bf16[128,1536]{1,0:T(8,128)(2,1)S(1)}, u32[]{:S(2)}, u32[]{:S(2)}) %collective-permute-start.38) | collective-permute-done | bytes 393248 | tf_op jit(solution)/shard_map/ppermute | solution.py:93
  603.3 4.8 fusion.195
  608.2 8.5 collective-permute-start.34
  627.3 7.8 fusion.6
  635.2 8.8 fusion.185
  645.1 7.3 collective-permute-done.41
  671.6 11.2 %collective-permute-start.45 = (bf16[128,1664]{1,0:T(8,128)(2,1)}, bf16[128,1664]{1,0:T(8,128)(2,1)}, u32[]{:S(2)}, u32[]{:S(2)}) collective-permute-start(bf16[128,1664]{1,0:T(8,128)(2,1)} %get-tuple-element.493), channel_id=1, source_target_pairs={{0,4},{2,6},{4,0},{6,2},{1,5},{3,7},{5,1},{7,3},{8,12},{10,14},{12... | collective-permute-start | bytes 1277960 | tf_op jit(solution)/shard_map/ppermute | solution.py:93
  683.1 10.1 %convolution_convert_fusion = bf16[1536,2048]{1,0:T(8,128)(2,1)} fusion(bf16[1024,2048]{1,0:T(8,128)(2,1)S(1)} %pad_maximum_fusion.2, bf16[512,1536]{1,0:T(8,128)(2,1)} %collective-permute-done.17, bf16[128,1536]{1,0:T(8,128)(2,1)S(1)} %copy-done.111, bf16[128,1536]{1,0:T(8,128)(2,1)S(1)} %copy-done.107, bf16[128,1536]{1,0:T(8,128)(2,1)S(1)} %copy-done.103, ...), kind=kOutput, calls=%fused_computation.11 | convolution fusion | flops 6461325312 | bytes 13631488 | tf_op jit(solution)/shard_map/dot_general | solution.py:37
  693.2 18.4 %collective-permute-done.45 = bf16[128,1664]{1,0:T(8,128)(2,1)} collective-permute-done((bf16[128,1664]{1,0:T(8,128)(2,1)}, bf16[128,1664]{1,0:T(8,128)(2,1)}, u32[]{:S(2)}, u32[]{:S(2)}) %collective-permute-start.45) | collective-permute-done | bytes 426016 | tf_op jit(solution)/shard_map/ppermute | solution.py:93
  711.7 7.6 convolution_convert_fusion.5
  738.5 10.2 %collective-permute-done.47 = bf16[128,1664]{1,0:T(8,128)(2,1)S(1)} collective-permute-done((bf16[128,1664]{1,0:T(8,128)(2,1)S(1)}, bf16[128,1664]{1,0:T(8,128)(2,1)S(1)}, u32[]{:S(2)}, u32[]{:S(2)}) %collective-permute-start.47) | collective-permute-done | bytes 426016 | tf_op jit(solution)/shard_map/ppermute | solution.py:93
  748.7 15.7 %collective-permute-done.48 = bf16[128,1664]{1,0:T(8,128)(2,1)S(1)} collective-permute-done((bf16[128,1664]{1,0:T(8,128)(2,1)S(1)}, bf16[128,1664]{1,0:T(8,128)(2,1)S(1)}, u32[]{:S(2)}, u32[]{:S(2)}) %collective-permute-start.48) | collective-permute-done | bytes 426016 | tf_op jit(solution)/shard_map/ppermute | solution.py:93
  777.5 5.5 pad_maximum_fusion.5
  805.2 8.2 collective-permute-start.51
  815.9 4.3 convolution_convert_fusion.12.grad_ref
  820.2 18.3 %scan_backward.1 = (bf16[1024,1152]{1,0:T(8,128)(2,1)S(1)}, f32[8,640]{1,0:T(8,128)S(1)}, f32[8,384]{1,0:T(8,128)S(1)}, f32[8,128]{1,0:T(8,128)S(1)}) custom-call(bf16[1024,1024]{1,0:T(8,128)(2,1)S(1)} %copy-done.1, f32[1024,128]{1,0:T(8,128)S(1)} %copy-done.3, f32[1024,1]{1,0:T(8,128)S(1)} %get-tuple-element.482.col_ref, f32[16,1,64]{2,1,0:T(1,128)S(1)} %bitcast.304, ...), custom_call_target="tpu_custom_call" | custom-call | tf_op jit(solution)/shard_map/scan_backward/pallas_call | solution.py:360
  841.4 8.5 fusion.9
  855.3 7.5 multiply_reduce_fusion
  863.9 3.8 concatenate.246
  871.8 9.6 collective-permute-start.55
  881.4 4.6 fusion.187
  886.0 4.5 collective-permute-done.55
  906.3 4.0 all_to_all.31
  910.4 18.2 %collective-permute-done.56 = bf16[128,1536]{1,0:T(8,128)(2,1)S(1)} collective-permute-done((bf16[128,1536]{1,0:T(8,128)(2,1)}, bf16[128,1536]{1,0:T(8,128)(2,1)S(1)}, u32[]{:S(2)}, u32[]{:S(2)}) %collective-permute-start.56) | collective-permute-done | bytes 393248 | tf_op jit(solution)/shard_map/ppermute | solution.py:93
  929.9 4.2 all-to-all-start.3
  940.7 16.5 %all-to-all-done.3 = bf16[8,48,1152]{2,1,0:T(8,128)(2,1)} async-done(((bf16[8,48,1152]{2,1,0:T(8,128)(2,1)}), bf16[8,48,1152]{2,1,0:T(8,128)(2,1)}, u32[]{:S(2)}, u32[]{:S(2)}) %all-to-all-start.3) | async-done | bytes 884768 | tf_op jit(solution)/shard_map/all_to_all | solution.py:992
  960.0 4.2 all-to-all-start.4
  972.9 6.8 collective-permute-done.60
  979.7 4.4 collective-permute-start.61
  (904 shorter events, 367.1 us)
Async XLA Ops:
  7.3 49.4 %all-gather.8.cloned.1.call-start = ((), (), s32[]{:S(2)}) async-start(), calls=%async_computation.13 | async-start | bytes 3932160 | tf_op jit(solution)/shard_map/all_gather | solution.py:661
  12.3 35.7 %all-to-all-start = ((bf16[8,48,1536]{2,1,0:T(8,128)(2,1)}), bf16[8,48,1536]{2,1,0:T(8,128)(2,1)S(1)}, u32[]{:S(2)}, u32[]{:S(2)}) async-start(bf16[8,48,1536]{2,1,0:T(8,128)(2,1)} %copy.606), calls=%async_computation | async-start | bytes 2359296 | tf_op jit(solution)/shard_map/all_to_all | solution.py:622
  18.7 114.5 %all-gather.10.cloned.1.call-start = ((), (), s32[]{:S(2)}) async-start(), calls=%async_computation.14 | async-start | bytes 5898240 | tf_op jit(solution)/shard_map/all_gather | solution.py:626
  56.7 211.3 %all-gather.12.cloned.1.call-start = ((), (), s32[]{:S(2)}) async-start(), calls=%async_computation.15 | async-start | bytes 7864320 | tf_op jit(solution)/shard_map/all_gather | solution.py:701
  58.4 14.7 %collective-permute-start = (bf16[128,1664]{1,0:T(8,128)(2,1)S(1)}, bf16[128,1664]{1,0:T(8,128)(2,1)S(1)}, u32[]{:S(2)}, u32[]{:S(2)}) collective-permute-start(bf16[128,1664]{1,0:T(8,128)(2,1)S(1)} %concatenate.200), channel_id=1, source_target_pairs={{0,2},{2,4},{4,6},{6,0},{1,3},{3,5},{5,7},{7,1},{8,10},{10,12},{12... | collective-permute-start | bytes 1277960 | tf_op jit(solution)/shard_map/ppermute | solution.py:93
  61.7 28.5 %collective-permute-start.1 = (bf16[128,1664]{1,0:T(8,128)(2,1)S(1)}, bf16[128,1664]{1,0:T(8,128)(2,1)S(1)}, u32[]{:S(2)}, u32[]{:S(2)}) collective-permute-start(bf16[128,1664]{1,0:T(8,128)(2,1)S(1)} %concatenate.200), channel_id=1, source_target_pairs={{0,4},{2,6},{4,0},{6,2},{1,5},{3,7},{5,1},{7,3},{8,12},{10,14},{12... | collective-permute-start | bytes 1277960 | tf_op jit(solution)/shard_map/ppermute | solution.py:93
  64.2 26.1 %collective-permute-start.2 = (bf16[128,1664]{1,0:T(8,128)(2,1)S(1)}, bf16[128,1664]{1,0:T(8,128)(2,1)S(1)}, u32[]{:S(2)}, u32[]{:S(2)}) collective-permute-start(bf16[128,1664]{1,0:T(8,128)(2,1)S(1)} %concatenate.200), channel_id=1, source_target_pairs={{0,6},{2,0},{4,2},{6,4},{1,7},{3,1},{5,3},{7,5},{8,14},{10,8},{12,... | collective-permute-start | bytes 1277960 | tf_op jit(solution)/shard_map/ppermute | solution.py:93
  98.4 28.5 %all-to-all-start.1 = ((bf16[8,48,768]{2,1,0:T(8,128)(2,1)}), bf16[8,48,768]{2,1,0:T(8,128)(2,1)S(1)}, u32[]{:S(2)}, u32[]{:S(2)}) async-start(bf16[8,48,768]{2,1,0:T(8,128)(2,1)} %copy.607), calls=%async_computation.1 | async-start | bytes 1179648 | tf_op jit(solution)/shard_map/all_to_all | solution.py:622
  110.2 168.7 %all-gather.14.cloned.1.call-start = ((), (), s32[]{:S(2)}) async-start(), calls=%async_computation.16 | async-start | bytes 2949120 | tf_op jit(solution)/shard_map/all_gather | solution.py:626
  131.0 24.9 %collective-permute-start.4 = (bf16[96,2048]{1,0:T(8,128)(2,1)S(1)}, bf16[96,2048]{1,0:T(8,128)(2,1)S(1)}, u32[]{:S(2)}, u32[]{:S(2)}) collective-permute-start(bf16[96,2048]{1,0:T(8,128)(2,1)S(1)} %bitcast.312), channel_id=1, source_target_pairs={{0,6},{2,0},{4,2},{6,4},{1,7},{3,1},{5,3},{7,5},{8,14},{10,8},{12,... | collective-permute-start | bytes 1179656 | tf_op jit(solution)/shard_map/ppermute | solution.py:93
  132.3 33.3 %collective-permute-start.5 = (bf16[96,2048]{1,0:T(8,128)(2,1)S(1)}, bf16[96,2048]{1,0:T(8,128)(2,1)}, u32[]{:S(2)}, u32[]{:S(2)}) collective-permute-start(bf16[96,2048]{1,0:T(8,128)(2,1)S(1)} %bitcast.313), channel_id=1, source_target_pairs={{0,4},{2,6},{4,0},{6,2},{1,5},{3,7},{5,1},{7,3},{8,12},{10,14},{12... | collective-permute-start | bytes 1179656 | tf_op jit(solution)/shard_map/ppermute | solution.py:93
  132.3 33.3 %collective-permute-start.6 = (bf16[96,2048]{1,0:T(8,128)(2,1)S(1)}, bf16[96,2048]{1,0:T(8,128)(2,1)}, u32[]{:S(2)}, u32[]{:S(2)}) collective-permute-start(bf16[96,2048]{1,0:T(8,128)(2,1)S(1)} %bitcast.314), channel_id=1, source_target_pairs={{0,2},{2,4},{4,6},{6,0},{1,3},{3,5},{5,7},{7,1},{8,10},{10,12},{12... | collective-permute-start | bytes 1179656 | tf_op jit(solution)/shard_map/ppermute | solution.py:93
  133.1 218.4 %all-gather.16.cloned.1.call-start = ((), (), s32[]{:S(2)}) async-start(), calls=%async_computation.17 | async-start | bytes 7864320 | tf_op jit(solution)/shard_map/all_gather | solution.py:771
  171.1 231.3 %all-gather.20.cloned.1.call-start = ((), (), s32[]{:S(2)}) async-start(), calls=%async_computation.19 | async-start | bytes 3932160 | tf_op jit(solution)/shard_map/all_gather | solution.py:661
  179.2 14.6 %collective-permute-start.10 = (bf16[128,1664]{1,0:T(8,128)(2,1)S(1)}, bf16[128,1664]{1,0:T(8,128)(2,1)S(1)}, u32[]{:S(2)}, u32[]{:S(2)}) collective-permute-start(bf16[128,1664]{1,0:T(8,128)(2,1)S(1)} %get-tuple-element.498), channel_id=1, source_target_pairs={{0,2},{2,4},{4,6},{6,0},{1,3},{3,5},{5,7},{7,1},{8,10},{10,12},{12... | collective-permute-start | bytes 1277960 | tf_op jit(solution)/shard_map/ppermute | solution.py:93
  180.8 21.3 %collective-permute-start.8 = (bf16[128,1664]{1,0:T(8,128)(2,1)S(1)}, bf16[128,1664]{1,0:T(8,128)(2,1)S(1)}, u32[]{:S(2)}, u32[]{:S(2)}) collective-permute-start(bf16[128,1664]{1,0:T(8,128)(2,1)S(1)} %get-tuple-element.497), channel_id=1, source_target_pairs={{0,6},{2,0},{4,2},{6,4},{1,7},{3,1},{5,3},{7,5},{8,14},{10,8},{12,... | collective-permute-start | bytes 1277960 | tf_op jit(solution)/shard_map/ppermute | solution.py:93
  183.1 37.2 %collective-permute-start.9 = (bf16[128,1664]{1,0:T(8,128)(2,1)S(1)}, bf16[128,1664]{1,0:T(8,128)(2,1)S(1)}, u32[]{:S(2)}, u32[]{:S(2)}) collective-permute-start(bf16[128,1664]{1,0:T(8,128)(2,1)S(1)} %get-tuple-element.499), channel_id=1, source_target_pairs={{0,4},{2,6},{4,0},{6,2},{1,5},{3,7},{5,1},{7,3},{8,12},{10,14},{12... | collective-permute-start | bytes 1277960 | tf_op jit(solution)/shard_map/ppermute | solution.py:93
  222.4 13.9 %collective-permute-start.14 = (bf16[128,1536]{1,0:T(8,128)(2,1)S(1)}, bf16[128,1536]{1,0:T(8,128)(2,1)S(1)}, u32[]{:S(2)}, u32[]{:S(2)}) collective-permute-start(bf16[128,1536]{1,0:T(8,128)(2,1)S(1)} %multiply_convert_fusion.11), channel_id=1, source_target_pairs={{0,2},{2,4},{4,6},{6,0},{1,3},{3,5},{5,7},{7,1},{8,10},{10,12},{12... | collective-permute-start | bytes 1179656 | tf_op jit(solution)/shard_map/ppermute | solution.py:93
  222.4 29.9 %collective-permute-start.15 = (bf16[128,1536]{1,0:T(8,128)(2,1)S(1)}, bf16[128,1536]{1,0:T(8,128)(2,1)S(1)}, u32[]{:S(2)}, u32[]{:S(2)}) collective-permute-start(bf16[128,1536]{1,0:T(8,128)(2,1)S(1)} %multiply_convert_fusion.11), channel_id=1, source_target_pairs={{0,4},{2,6},{4,0},{6,2},{1,5},{3,7},{5,1},{7,3},{8,12},{10,14},{12... | collective-permute-start | bytes 1179656 | tf_op jit(solution)/shard_map/ppermute | solution.py:93
  225.6 26.7 %collective-permute-start.16 = (bf16[128,1536]{1,0:T(8,128)(2,1)S(1)}, bf16[128,1536]{1,0:T(8,128)(2,1)S(1)}, u32[]{:S(2)}, u32[]{:S(2)}) collective-permute-start(bf16[128,1536]{1,0:T(8,128)(2,1)S(1)} %multiply_convert_fusion.11), channel_id=1, source_target_pairs={{0,6},{2,0},{4,2},{6,4},{1,7},{3,1},{5,3},{7,5},{8,14},{10,8},{12,... | collective-permute-start | bytes 1179656 | tf_op jit(solution)/shard_map/ppermute | solution.py:93
  253.6 14.4 %collective-permute-start.17 = (bf16[512,1536]{1,0:T(8,128)(2,1)}, bf16[512,1536]{1,0:T(8,128)(2,1)}, u32[]{:S(2)}, u32[]{:S(2)}) collective-permute-start(bf16[512,1536]{1,0:T(8,128)(2,1)} %pad_maximum_fusion.11), channel_id=1, source_target_pairs={{0,1},{1,0},{2,3},{3,2},{4,5},{5,4},{6,7},{7,6},{8,9},{9,8},{10,11... | collective-permute-start | bytes 4718600 | tf_op jit(solution)/shard_map/ppermute | solution.py:93
  253.6 25.3 %collective-permute-start.13 = (bf16[128,1536]{1,0:T(8,128)(2,1)S(1)}, bf16[128,1536]{1,0:T(8,128)(2,1)S(1)}, u32[]{:S(2)}, u32[]{:S(2)}) collective-permute-start(bf16[128,1536]{1,0:T(8,128)(2,1)S(1)} %bitcast.307), channel_id=1, source_target_pairs={{0,2},{2,4},{4,6},{6,0},{1,3},{3,5},{5,7},{7,1},{8,10},{10,12},{12... | collective-permute-start | bytes 1179656 | tf_op jit(solution)/shard_map/ppermute | solution.py:93
  261.6 33.2 %collective-permute-start.11 = (bf16[128,1536]{1,0:T(8,128)(2,1)S(1)}, bf16[128,1536]{1,0:T(8,128)(2,1)S(1)}, u32[]{:S(2)}, u32[]{:S(2)}) collective-permute-start(bf16[128,1536]{1,0:T(8,128)(2,1)S(1)} %bitcast.308), channel_id=1, source_target_pairs={{0,4},{2,6},{4,0},{6,2},{1,5},{3,7},{5,1},{7,3},{8,12},{10,14},{12... | collective-permute-start | bytes 1179656 | tf_op jit(solution)/shard_map/ppermute | solution.py:93
  261.6 33.2 %collective-permute-start.12 = (bf16[128,1536]{1,0:T(8,128)(2,1)S(1)}, bf16[128,1536]{1,0:T(8,128)(2,1)}, u32[]{:S(2)}, u32[]{:S(2)}) collective-permute-start(bf16[128,1536]{1,0:T(8,128)(2,1)S(1)} %bitcast.309), channel_id=1, source_target_pairs={{0,6},{2,0},{4,2},{6,4},{1,7},{3,1},{5,3},{7,5},{8,14},{10,8},{12,... | collective-permute-start | bytes 1179656 | tf_op jit(solution)/shard_map/ppermute | solution.py:93
  264.0 155.4 %all-gather.18.cloned.1.call-start = ((), (), s32[]{:S(2)}) async-start(), calls=%async_computation.18 | async-start | bytes 7864320 | tf_op jit(solution)/shard_map/all_gather | solution.py:701
  306.5 420.4 %reduce-scatter.10.cloned.1.call-start = ((), (), s32[]{:S(2)}) async-start(), calls=%async_computation.21 | async-start | bytes 3932160 | tf_op jit(solution)/shard_map/reduce_scatter | solution.py:821
  311.8 13.7 %collective-permute-start.19 = (bf16[128,1536]{1,0:T(8,128)(2,1)S(1)}, bf16[128,1536]{1,0:T(8,128)(2,1)S(1)}, u32[]{:S(2)}, u32[]{:S(2)}) collective-permute-start(bf16[128,1536]{1,0:T(8,128)(2,1)S(1)} %get-tuple-element.525), channel_id=1, source_target_pairs={{0,6},{2,0},{4,2},{6,4},{1,7},{3,1},{5,3},{7,5},{8,14},{10,8},{12,... | collective-permute-start | bytes 1179656 | tf_op jit(solution)/shard_map/ppermute | solution.py:93
  316.0 32.9 %collective-permute-start.20 = (bf16[128,1536]{1,0:T(8,128)(2,1)S(1)}, bf16[128,1536]{1,0:T(8,128)(2,1)S(1)}, u32[]{:S(2)}, u32[]{:S(2)}) collective-permute-start(bf16[128,1536]{1,0:T(8,128)(2,1)S(1)} %get-tuple-element.527), channel_id=1, source_target_pairs={{0,4},{2,6},{4,0},{6,2},{1,5},{3,7},{5,1},{7,3},{8,12},{10,14},{12... | collective-permute-start | bytes 1179656 | tf_op jit(solution)/shard_map/ppermute | solution.py:93
  316.0 32.9 %collective-permute-start.21 = (bf16[128,1536]{1,0:T(8,128)(2,1)S(1)}, bf16[128,1536]{1,0:T(8,128)(2,1)S(1)}, u32[]{:S(2)}, u32[]{:S(2)}) collective-permute-start(bf16[128,1536]{1,0:T(8,128)(2,1)S(1)} %get-tuple-element.526), channel_id=1, source_target_pairs={{0,2},{2,4},{4,6},{6,0},{1,3},{3,5},{5,7},{7,1},{8,10},{10,12},{12... | collective-permute-start | bytes 1179656 | tf_op jit(solution)/shard_map/ppermute | solution.py:93
  369.6 13.9 %collective-permute-start.24 = (bf16[128,1536]{1,0:T(8,128)(2,1)S(1)}, bf16[128,1536]{1,0:T(8,128)(2,1)S(1)}, u32[]{:S(2)}, u32[]{:S(2)}) collective-permute-start(bf16[128,1536]{1,0:T(8,128)(2,1)S(1)} %multiply_convert_fusion.9), channel_id=1, source_target_pairs={{0,2},{2,4},{4,6},{6,0},{1,3},{3,5},{5,7},{7,1},{8,10},{10,12},{12... | collective-permute-start | bytes 1179656 | tf_op jit(solution)/shard_map/ppermute | solution.py:93
  371.4 28.4 %collective-permute-start.25 = (bf16[128,1536]{1,0:T(8,128)(2,1)S(1)}, bf16[128,1536]{1,0:T(8,128)(2,1)S(1)}, u32[]{:S(2)}, u32[]{:S(2)}) collective-permute-start(bf16[128,1536]{1,0:T(8,128)(2,1)S(1)} %multiply_convert_fusion.9), channel_id=1, source_target_pairs={{0,4},{2,6},{4,0},{6,2},{1,5},{3,7},{5,1},{7,3},{8,12},{10,14},{12... | collective-permute-start | bytes 1179656 | tf_op jit(solution)/shard_map/ppermute | solution.py:93
  373.4 26.4 %collective-permute-start.26 = (bf16[128,1536]{1,0:T(8,128)(2,1)S(1)}, bf16[128,1536]{1,0:T(8,128)(2,1)S(1)}, u32[]{:S(2)}, u32[]{:S(2)}) collective-permute-start(bf16[128,1536]{1,0:T(8,128)(2,1)S(1)} %multiply_convert_fusion.9), channel_id=1, source_target_pairs={{0,6},{2,0},{4,2},{6,4},{1,7},{3,1},{5,3},{7,5},{8,14},{10,8},{12,... | collective-permute-start | bytes 1179656 | tf_op jit(solution)/shard_map/ppermute | solution.py:93
  378.5 41.0 %collective-permute-start.28 = (bf16[512,1536]{1,0:T(8,128)(2,1)}, bf16[512,1536]{1,0:T(8,128)(2,1)}, u32[]{:S(2)}, u32[]{:S(2)}) collective-permute-start(bf16[512,1536]{1,0:T(8,128)(2,1)} %pad_maximum_fusion.15), channel_id=1, source_target_pairs={{0,1},{1,0},{2,3},{3,2},{4,5},{5,4},{6,7},{7,6},{8,9},{9,8},{10,11... | collective-permute-start | bytes 4718600 | tf_op jit(solution)/shard_map/ppermute | solution.py:93
  401.3 20.0 %collective-permute-start.27 = (bf16[512,1536]{1,0:T(8,128)(2,1)}, bf16[512,1536]{1,0:T(8,128)(2,1)}, u32[]{:S(2)}, u32[]{:S(2)}) collective-permute-start(bf16[512,1536]{1,0:T(8,128)(2,1)} %pad_maximum_fusion.13), channel_id=1, source_target_pairs={{0,1},{1,0},{2,3},{3,2},{4,5},{5,4},{6,7},{7,6},{8,9},{9,8},{10,11... | collective-permute-start | bytes 4718600 | tf_op jit(solution)/shard_map/ppermute | solution.py:93
  494.4 232.4 %reduce-scatter.8.cloned.1.call-start = ((), (), s32[]{:S(2)}) async-start(), calls=%async_computation.20 | async-start | bytes 7864320 | tf_op jit(solution)/shard_map/reduce_scatter | solution.py:817
  494.5 30.6 %collective-permute-start.31 = (bf16[128,1664]{1,0:T(8,128)(2,1)}, bf16[128,1664]{1,0:T(8,128)(2,1)}, u32[]{:S(2)}, u32[]{:S(2)}) collective-permute-start(bf16[128,1664]{1,0:T(8,128)(2,1)} %get-tuple-element.496), channel_id=1, source_target_pairs={{0,4},{2,6},{4,0},{6,2},{1,5},{3,7},{5,1},{7,3},{8,12},{10,14},{12... | collective-permute-start | bytes 1277960 | tf_op jit(solution)/shard_map/ppermute | solution.py:93
  496.1 28.9 %collective-permute-start.32 = (bf16[128,1664]{1,0:T(8,128)(2,1)}, bf16[128,1664]{1,0:T(8,128)(2,1)}, u32[]{:S(2)}, u32[]{:S(2)}) collective-permute-start(bf16[128,1664]{1,0:T(8,128)(2,1)} %get-tuple-element.495), channel_id=1, source_target_pairs={{0,2},{2,4},{4,6},{6,0},{1,3},{3,5},{5,7},{7,1},{8,10},{10,12},{12... | collective-permute-start | bytes 1277960 | tf_op jit(solution)/shard_map/ppermute | solution.py:93
  525.1 278.7 %reduce-scatter.14.cloned.1.call-start = ((), (), s32[]{:S(2)}) async-start(), calls=%async_computation.23 | async-start | bytes 7864320 | tf_op jit(solution)/shard_map/reduce_scatter | solution.py:898
  541.4 61.9 %collective-permute-start.33 = (bf16[512,1536]{1,0:T(8,128)(2,1)}, bf16[512,1536]{1,0:T(8,128)(2,1)}, u32[]{:S(2)}, u32[]{:S(2)}) collective-permute-start(bf16[512,1536]{1,0:T(8,128)(2,1)} %slice.1149), channel_id=1, source_target_pairs={{0,1},{1,0},{2,3},{3,2},{4,5},{5,4},{6,7},{7,6},{8,9},{9,8},{10,11... | collective-permute-start | bytes 4718600 | tf_op jit(solution)/shard_map/ppermute | solution.py:93
  572.2 13.9 %collective-permute-start.37 = (bf16[128,1536]{1,0:T(8,128)(2,1)S(1)}, bf16[128,1536]{1,0:T(8,128)(2,1)S(1)}, u32[]{:S(2)}, u32[]{:S(2)}) collective-permute-start(bf16[128,1536]{1,0:T(8,128)(2,1)S(1)} %get-tuple-element.456), channel_id=1, source_target_pairs={{0,2},{2,4},{4,6},{6,0},{1,3},{3,5},{5,7},{7,1},{8,10},{10,12},{12... | collective-permute-start | bytes 1179656 | tf_op jit(solution)/shard_map/ppermute | solution.py:93
  572.2 29.7 %collective-permute-start.38 = (bf16[128,1536]{1,0:T(8,128)(2,1)S(1)}, bf16[128,1536]{1,0:T(8,128)(2,1)S(1)}, u32[]{:S(2)}, u32[]{:S(2)}) collective-permute-start(bf16[128,1536]{1,0:T(8,128)(2,1)S(1)} %get-tuple-element.456), channel_id=1, source_target_pairs={{0,4},{2,6},{4,0},{6,2},{1,5},{3,7},{5,1},{7,3},{8,12},{10,14},{12... | collective-permute-start | bytes 1179656 | tf_op jit(solution)/shard_map/ppermute | solution.py:93
  573.3 28.7 %collective-permute-start.39 = (bf16[128,1536]{1,0:T(8,128)(2,1)S(1)}, bf16[128,1536]{1,0:T(8,128)(2,1)S(1)}, u32[]{:S(2)}, u32[]{:S(2)}) collective-permute-start(bf16[128,1536]{1,0:T(8,128)(2,1)S(1)} %get-tuple-element.456), channel_id=1, source_target_pairs={{0,6},{2,0},{4,2},{6,4},{1,7},{3,1},{5,3},{7,5},{8,14},{10,8},{12,... | collective-permute-start | bytes 1179656 | tf_op jit(solution)/shard_map/ppermute | solution.py:93
  603.2 14.4 %collective-permute-start.40 = (bf16[512,1536]{1,0:T(8,128)(2,1)}, bf16[512,1536]{1,0:T(8,128)(2,1)}, u32[]{:S(2)}, u32[]{:S(2)}) collective-permute-start(bf16[512,1536]{1,0:T(8,128)(2,1)} %pad_maximum_fusion.16), channel_id=1, source_target_pairs={{0,1},{1,0},{2,3},{3,2},{4,5},{5,4},{6,7},{7,6},{8,9},{9,8},{10,11... | collective-permute-start | bytes 4718600 | tf_op jit(solution)/shard_map/ppermute | solution.py:93
  603.3 246.7 %reduce-scatter.16.cloned.1.call-start = ((), (), s32[]{:S(2)}) async-start(), calls=%async_computation.24 | async-start | bytes 7864320 | tf_op jit(solution)/shard_map/reduce_scatter | solution.py:817
  608.2 18.0 %collective-permute-start.34 = (bf16[128,1536]{1,0:T(8,128)(2,1)S(1)}, bf16[128,1536]{1,0:T(8,128)(2,1)S(1)}, u32[]{:S(2)}, u32[]{:S(2)}) collective-permute-start(bf16[128,1536]{1,0:T(8,128)(2,1)S(1)} %get-tuple-element.516), channel_id=1, source_target_pairs={{0,6},{2,0},{4,2},{6,4},{1,7},{3,1},{5,3},{7,5},{8,14},{10,8},{12,... | collective-permute-start | bytes 1179656 | tf_op jit(solution)/shard_map/ppermute | solution.py:93
  616.7 35.7 %collective-permute-start.41 = (bf16[128,1536]{1,0:T(8,128)(2,1)S(1)}, bf16[128,1536]{1,0:T(8,128)(2,1)S(1)}, u32[]{:S(2)}, u32[]{:S(2)}) collective-permute-start(bf16[128,1536]{1,0:T(8,128)(2,1)S(1)} %get-tuple-element.518), channel_id=1, source_target_pairs={{0,4},{2,6},{4,0},{6,2},{1,5},{3,7},{5,1},{7,3},{8,12},{10,14},{12... | collective-permute-start | bytes 1179656 | tf_op jit(solution)/shard_map/ppermute | solution.py:93
  617.6 34.9 %collective-permute-start.42 = (bf16[128,1536]{1,0:T(8,128)(2,1)S(1)}, bf16[128,1536]{1,0:T(8,128)(2,1)S(1)}, u32[]{:S(2)}, u32[]{:S(2)}) collective-permute-start(bf16[128,1536]{1,0:T(8,128)(2,1)S(1)} %get-tuple-element.517), channel_id=1, source_target_pairs={{0,2},{2,4},{4,6},{6,0},{1,3},{3,5},{5,7},{7,1},{8,10},{10,12},{12... | collective-permute-start | bytes 1179656 | tf_op jit(solution)/shard_map/ppermute | solution.py:93
  671.6 39.9 %collective-permute-start.45 = (bf16[128,1664]{1,0:T(8,128)(2,1)}, bf16[128,1664]{1,0:T(8,128)(2,1)}, u32[]{:S(2)}, u32[]{:S(2)}) collective-permute-start(bf16[128,1664]{1,0:T(8,128)(2,1)} %get-tuple-element.493), channel_id=1, source_target_pairs={{0,4},{2,6},{4,0},{6,2},{1,5},{3,7},{5,1},{7,3},{8,12},{10,14},{12... | collective-permute-start | bytes 1277960 | tf_op jit(solution)/shard_map/ppermute | solution.py:93
  682.9 28.7 %collective-permute-start.46 = (bf16[128,1664]{1,0:T(8,128)(2,1)S(1)}, bf16[128,1664]{1,0:T(8,128)(2,1)}, u32[]{:S(2)}, u32[]{:S(2)}) collective-permute-start(bf16[128,1664]{1,0:T(8,128)(2,1)S(1)} %get-tuple-element.492), channel_id=1, source_target_pairs={{0,2},{2,4},{4,6},{6,0},{1,3},{3,5},{5,7},{7,1},{8,10},{10,12},{12... | collective-permute-start | bytes 1277960 | tf_op jit(solution)/shard_map/ppermute | solution.py:93
  711.6 185.6 %reduce-scatter.20.cloned.1.call-start = ((), (), s32[]{:S(2)}) async-start(), calls=%async_computation.26 | async-start | bytes 3932160 | tf_op jit(solution)/shard_map/reduce_scatter | solution.py:821
  723.8 206.0 %reduce-scatter.12.cloned.1.call-start = ((), (), s32[]{:S(2)}) async-start(), calls=%async_computation.22 | async-start | bytes 4423680 | tf_op jit(solution)/shard_map/reduce_scatter | solution.py:989
  734.0 14.7 %collective-permute-start.47 = (bf16[128,1664]{1,0:T(8,128)(2,1)S(1)}, bf16[128,1664]{1,0:T(8,128)(2,1)S(1)}, u32[]{:S(2)}, u32[]{:S(2)}) collective-permute-start(bf16[128,1664]{1,0:T(8,128)(2,1)S(1)} %concatenate.234), channel_id=1, source_target_pairs={{0,2},{2,4},{4,6},{6,0},{1,3},{3,5},{5,7},{7,1},{8,10},{10,12},{12... | collective-permute-start | bytes 1277960 | tf_op jit(solution)/shard_map/ppermute | solution.py:93
  734.2 30.3 %collective-permute-start.48 = (bf16[128,1664]{1,0:T(8,128)(2,1)S(1)}, bf16[128,1664]{1,0:T(8,128)(2,1)S(1)}, u32[]{:S(2)}, u32[]{:S(2)}) collective-permute-start(bf16[128,1664]{1,0:T(8,128)(2,1)S(1)} %concatenate.234), channel_id=1, source_target_pairs={{0,4},{2,6},{4,0},{6,2},{1,5},{3,7},{5,1},{7,3},{8,12},{10,14},{12... | collective-permute-start | bytes 1277960 | tf_op jit(solution)/shard_map/ppermute | solution.py:93
  736.3 28.2 %collective-permute-start.49 = (bf16[128,1664]{1,0:T(8,128)(2,1)S(1)}, bf16[128,1664]{1,0:T(8,128)(2,1)S(1)}, u32[]{:S(2)}, u32[]{:S(2)}) collective-permute-start(bf16[128,1664]{1,0:T(8,128)(2,1)S(1)} %concatenate.234), channel_id=1, source_target_pairs={{0,6},{2,0},{4,2},{6,4},{1,7},{3,1},{5,3},{7,5},{8,14},{10,8},{12,... | collective-permute-start | bytes 1277960 | tf_op jit(solution)/shard_map/ppermute | solution.py:93
  800.3 158.2 %reduce-scatter.18.cloned.1.call-start = ((), (), s32[]{:S(2)}) async-start(), calls=%async_computation.25 | async-start | bytes 4423680 | tf_op jit(solution)/shard_map/reduce_scatter | solution.py:989
  805.2 33.3 %collective-permute-start.51 = (bf16[96,2048]{1,0:T(8,128)(2,1)S(1)}, bf16[96,2048]{1,0:T(8,128)(2,1)S(1)}, u32[]{:S(2)}, u32[]{:S(2)}) collective-permute-start(bf16[96,2048]{1,0:T(8,128)(2,1)S(1)} %get-tuple-element.509), channel_id=1, source_target_pairs={{0,2},{2,4},{4,6},{6,0},{1,3},{3,5},{5,7},{7,1},{8,10},{10,12},{12... | collective-permute-start | bytes 1179656 | tf_op jit(solution)/shard_map/ppermute | solution.py:93
  813.4 28.0 %collective-permute-start.52 = (bf16[96,2048]{1,0:T(8,128)(2,1)S(1)}, bf16[96,2048]{1,0:T(8,128)(2,1)S(1)}, u32[]{:S(2)}, u32[]{:S(2)}) collective-permute-start(bf16[96,2048]{1,0:T(8,128)(2,1)S(1)} %get-tuple-element.507), channel_id=1, source_target_pairs={{0,4},{2,6},{4,0},{6,2},{1,5},{3,7},{5,1},{7,3},{8,12},{10,14},{12... | collective-permute-start | bytes 1179656 | tf_op jit(solution)/shard_map/ppermute | solution.py:93
  815.3 34.6 %collective-permute-start.53 = (bf16[96,2048]{1,0:T(8,128)(2,1)S(1)}, bf16[96,2048]{1,0:T(8,128)(2,1)}, u32[]{:S(2)}, u32[]{:S(2)}) collective-permute-start(bf16[96,2048]{1,0:T(8,128)(2,1)S(1)} %get-tuple-element.508), channel_id=1, source_target_pairs={{0,6},{2,0},{4,2},{6,4},{1,7},{3,1},{5,3},{7,5},{8,14},{10,8},{12,... | collective-permute-start | bytes 1179656 | tf_op jit(solution)/shard_map/ppermute | solution.py:93
  853.2 14.6 %collective-permute-start.54 = (bf16[512,1536]{1,0:T(8,128)(2,1)}, bf16[512,1536]{1,0:T(8,128)(2,1)}, u32[]{:S(2)}, u32[]{:S(2)}) collective-permute-start(bf16[512,1536]{1,0:T(8,128)(2,1)} %slice.1148), channel_id=1, source_target_pairs={{0,1},{1,0},{2,3},{3,2},{4,5},{5,4},{6,7},{7,6},{8,9},{9,8},{10,11... | collective-permute-start | bytes 4718600 | tf_op jit(solution)/shard_map/ppermute | solution.py:93
  871.8 18.7 %collective-permute-start.55 = (bf16[128,1536]{1,0:T(8,128)(2,1)S(1)}, bf16[128,1536]{1,0:T(8,128)(2,1)S(1)}, u32[]{:S(2)}, u32[]{:S(2)}) collective-permute-start(bf16[128,1536]{1,0:T(8,128)(2,1)S(1)} %get-tuple-element.504), channel_id=1, source_target_pairs={{0,6},{2,0},{4,2},{6,4},{1,7},{3,1},{5,3},{7,5},{8,14},{10,8},{12,... | collective-permute-start | bytes 1179656 | tf_op jit(solution)/shard_map/ppermute | solution.py:93
  899.8 28.8 %collective-permute-start.56 = (bf16[128,1536]{1,0:T(8,128)(2,1)}, bf16[128,1536]{1,0:T(8,128)(2,1)S(1)}, u32[]{:S(2)}, u32[]{:S(2)}) collective-permute-start(bf16[128,1536]{1,0:T(8,128)(2,1)} %get-tuple-element.506), channel_id=1, source_target_pairs={{0,4},{2,6},{4,0},{6,2},{1,5},{3,7},{5,1},{7,3},{8,12},{10,14},{12... | collective-permute-start | bytes 1179656 | tf_op jit(solution)/shard_map/ppermute | solution.py:93
  901.2 27.5 %collective-permute-start.57 = (bf16[128,1536]{1,0:T(8,128)(2,1)S(1)}, bf16[128,1536]{1,0:T(8,128)(2,1)S(1)}, u32[]{:S(2)}, u32[]{:S(2)}) collective-permute-start(bf16[128,1536]{1,0:T(8,128)(2,1)S(1)} %get-tuple-element.505), channel_id=1, source_target_pairs={{0,2},{2,4},{4,6},{6,0},{1,3},{3,5},{5,7},{7,1},{8,10},{10,12},{12... | collective-permute-start | bytes 1179656 | tf_op jit(solution)/shard_map/ppermute | solution.py:93
  929.9 27.3 %all-to-all-start.3 = ((bf16[8,48,1152]{2,1,0:T(8,128)(2,1)}), bf16[8,48,1152]{2,1,0:T(8,128)(2,1)}, u32[]{:S(2)}, u32[]{:S(2)}) async-start(bf16[8,48,1152]{2,1,0:T(8,128)(2,1)} %bitcast.332), calls=%async_computation.9 | async-start | bytes 1769472 | tf_op jit(solution)/shard_map/all_to_all | solution.py:992
  960.0 31.0 %all-to-all-start.4 = ((bf16[8,48,1152]{2,1,0:T(8,128)(2,1)}), bf16[8,48,1152]{2,1,0:T(8,128)(2,1)}, u32[]{:S(2)}, u32[]{:S(2)}) async-start(bf16[8,48,1152]{2,1,0:T(8,128)(2,1)} %bitcast.333), calls=%async_computation.10 | async-start | bytes 1769472 | tf_op jit(solution)/shard_map/all_to_all | solution.py:992
  (228 other events, 2114.5 us)
Sparse Core Ops, SparseCore 0:
  10.0 46.6 all-gather.7
  59.1 57.0 all-gather.9
  118.7 70.1 all-gather.11
  191.2 37.4 all-gather.13
  230.9 70.1 all-gather.15
  302.8 43.9 all-gather.19
  349.2 70.1 all-gather.17
  494.6 44.8 reduce-scatter.9
  542.5 70.1 reduce-scatter.7
  615.5 70.2 reduce-scatter.13
  711.7 68.4 reduce-scatter.15
  783.0 43.9 reduce-scatter.19
  830.1 47.2 reduce-scatter.11
  893.7 47.6 reduce-scatter.17
